TPU v7x, 128 devices: a whole 4x4x4 slice. The times are simulated.
128 devices in a mesh: dp: 4 (over x), ctx: 32 (over z, y, core).
Axes of the slice: x: 4, y: 4, z: 4, core: 2. Of those that a mesh axis runs over, the one named last changes fastest.
Arguments:
- queries: bfloat16 [4, 8192, 2048], P('dp', 'ctx'), may hold values from -6 to 6
- keys: bfloat16 [4, 8192, 2048], P('dp', 'ctx'), may hold values from -6 to 6
- values: bfloat16 [4, 8192, 2048], P('dp', 'ctx'), may hold values from -6 to 6
- gain: float32 [2048], replicated, may hold values from 0.1 to 1.9
- out_weight: bfloat16 [2048, 4096], P('dp'), may hold values from -0.125 to 0.125
- grad_out: bfloat16 [4, 8192, 4096], P('dp', 'ctx'), may hold values from -6 to 6
Outputs:
- layer_out: bfloat16 [4, 8192, 4096], P('dp', 'ctx')
- grad_queries: bfloat16 [4, 8192, 2048], P('dp', 'ctx')
- grad_keys: bfloat16 [4, 8192, 2048], P('dp', 'ctx')
- grad_values: bfloat16 [4, 8192, 2048], P('dp', 'ctx')
- grad_weight: float32 [2048, 4096], P(('dp', 'ctx'))
All inputs are finite; a program needn't handle non-finite values.
Results may differ from a plain program's by a relative error of at most 0.015.
Values may be sent and summed in bfloat16 or wider, within the bound.
No kernel may reach another device: no remote copies, remote signals or barrier semaphores. Data moves between devices by JAX's collectives and lax.ppermute only.
A program may use at most 192 MiB of HBM per device.

v0:
```python
import math

import jax
import jax.numpy as jnp
from jax import lax
from jax.sharding import PartitionSpec as P

HD = 128


EPSILON = 1e-06
HIGHEST = lax.Precision.HIGHEST


def prefix(part, axis, combine, identity, reverse):
    count = lax.axis_size(axis)
    place = lax.axis_index(axis)
    ahead = count - 1 - place if reverse else place
    gathered = lax.all_gather(part, axis)
    state = jnp.zeros_like(part) + jnp.asarray(identity, part.dtype)

    def one(turn, state):
        source = count - 1 - turn if reverse else turn
        return combine(state, lax.dynamic_index_in_dim(gathered, source, 0, False))

    return lax.fori_loop(0, ahead, one, state)


def add_terms(earlier, later_part):
    return earlier + later_part


def shards(queries, keys, values, gain, out_weight, grad_out):
    tok_rows = queries.shape[1]
    feat_width = queries.shape[2]
    head_count = feat_width // HD
    model_width = grad_out.shape[2]
    query_rows = queries.reshape(tok_rows, head_count, HD)
    key_rows = keys.reshape(tok_rows, head_count, HD)
    value_rows = values.reshape(tok_rows, head_count, HD)
    causal = lax.broadcasted_iota(jnp.int32, (tok_rows, tok_rows), 0) >= lax.broadcasted_iota(
        jnp.int32, (tok_rows, tok_rows), 1
    )
    scores = jnp.einsum("thd,shd->hts", query_rows, key_rows, preferred_element_type=jnp.float32)
    weights = jnp.where(causal, scores, 0.0).astype(jnp.bfloat16)
    local_out = jnp.einsum("hts,shd->thd", weights, value_rows, preferred_element_type=jnp.float32)
    local_state = jnp.einsum(
        "shd,she->hde", key_rows, value_rows, preferred_element_type=jnp.float32
    )
    carried = prefix(local_state, "ctx", add_terms, jnp.zeros_like(local_state), False)
    state_out = jnp.einsum(
        "thd,hde->the", query_rows.astype(jnp.float32), carried, precision=HIGHEST
    )
    attended = local_out + state_out
    inv_rms = lax.rsqrt(jnp.mean(attended * attended, axis=-1, keepdims=True) + EPSILON)
    unit_out = attended * inv_rms
    gain_heads = gain.reshape(head_count, HD)
    normed = (unit_out * gain_heads).astype(jnp.bfloat16).reshape(tok_rows, feat_width)
    grad_rows = grad_out.reshape(tok_rows, model_width)
    full_weight = lax.all_gather(out_weight, "dp", axis=0, tiled=True)
    layer_rows = jnp.dot(normed, full_weight, preferred_element_type=jnp.float32)
    layer_out = layer_rows.astype(jnp.bfloat16).reshape(1, tok_rows, model_width)
    shared_cols = lax.all_to_all(normed, "dp", split_axis=1, concat_axis=0, tiled=True)
    grad_normed = lax.dot_general(
        grad_rows, full_weight, (((1,), (1,)), ((), ())), preferred_element_type=jnp.float32
    )
    weight_term = lax.dot_general(
        shared_cols,
        lax.all_gather(grad_rows, "dp", axis=0, tiled=True),
        (((0,), (0,)), ((), ())),
        preferred_element_type=jnp.float32,
    )
    token_count = lax.axis_size("dp") * lax.axis_size("ctx") * tok_rows
    grad_weight = lax.psum_scatter(
        weight_term.astype(jnp.bfloat16), "ctx", scatter_dimension=0, tiled=True
    ).astype(jnp.float32) * (1.0 / math.sqrt(token_count))
    grad_unit = grad_normed.reshape(tok_rows, head_count, HD) * gain_heads
    grad_attn = inv_rms * (
        grad_unit - unit_out * jnp.mean(grad_unit * unit_out, axis=-1, keepdims=True)
    )
    grad_attn = grad_attn.astype(jnp.bfloat16)
    grad_scores = jnp.einsum(
        "the,she->hts", grad_attn, value_rows, preferred_element_type=jnp.float32
    )
    grad_scores = jnp.where(causal, grad_scores, 0.0).astype(jnp.bfloat16)
    local_grad = jnp.einsum(
        "thd,the->hde", query_rows, grad_attn, preferred_element_type=jnp.float32
    )
    later = prefix(local_grad, "ctx", add_terms, jnp.zeros_like(local_grad), True)
    grad_query = jnp.einsum(
        "hts,shd->thd", grad_scores, key_rows, preferred_element_type=jnp.float32
    )
    grad_query = grad_query + jnp.einsum(
        "the,hde->thd", grad_attn.astype(jnp.float32), carried, precision=HIGHEST
    )
    grad_key = jnp.einsum(
        "hts,thd->shd", grad_scores, query_rows, preferred_element_type=jnp.float32
    )
    grad_key = grad_key + jnp.einsum(
        "she,hde->shd", value_rows.astype(jnp.float32), later, precision=HIGHEST
    )
    grad_value = jnp.einsum("hts,the->she", weights, grad_attn, preferred_element_type=jnp.float32)
    grad_value = grad_value + jnp.einsum(
        "shd,hde->she", key_rows.astype(jnp.float32), later, precision=HIGHEST
    )
    out_shape = (1, tok_rows, feat_width)
    return (
        layer_out,
        grad_query.astype(jnp.bfloat16).reshape(out_shape),
        grad_key.astype(jnp.bfloat16).reshape(out_shape),
        grad_value.astype(jnp.bfloat16).reshape(out_shape),
        grad_weight,
    )


def solution(mesh):
    in_specs = (
        P("dp", "ctx", None),
        P("dp", "ctx", None),
        P("dp", "ctx", None),
        P(),
        P("dp", None),
        P("dp", "ctx", None),
    )
    out_specs = (
        P("dp", "ctx", None),
        P("dp", "ctx", None),
        P("dp", "ctx", None),
        P("dp", "ctx", None),
        P(("dp", "ctx"), None),
    )
    return jax.shard_map(shards, mesh=mesh, in_specs=in_specs, out_specs=out_specs, check_vma=False)
```

profile of v0, /device:TPU:0, one launch (start us, length us, event | category | flops | bytes accessed | tf_op | source)
XLA Modules:
  0.0 650.7 jit_solution(872384761315528733)
XLA Ops:
  7.2 1.5 copy.78
  16.6 2.2 fusion.12
  18.7 109.2 %all-gather.10.cloned.1.call-done = f32[512,128,128]{2,1,0:T(8,128)} async-done(((f32[16,128,128]{2,1,0:T(8,128)}), f32[512,128,128]{2,1,0:T(8,128)}) %all-gather.10.cloned.1.call-update) | async-done | bytes 33554448 | tf_op jit(solution)/shard_map/all_gather | solution.py:19
  128.1 4.1 multiply_reduce_fusion.1
  132.2 150.6 %all-gather.8.cloned.1.call-done = bf16[2048,4096]{1,0:T(8,128)(2,1)} async-done(((bf16[512,4096]{1,0:T(8,128)(2,1)}), bf16[2048,4096]{1,0:T(8,128)(2,1)}) %all-gather.8.cloned.1.call-update) | async-done | bytes 16777232 | tf_op jit(solution)/shard_map/all_gather | solution.py:60
  282.8 12.6 %multiply_reduce_fusion = (f32[256,16]{0,1:T(8,128)S(1)}, f32[256,16,128]{0,2,1:T(8,128)S(1)}) fusion(f32[256,16,128]{0,2,1:T(8,128)} %get-tuple-element.128, f32[16,128]{1,0:T(8,128)S(1)} %bitcast.102, f32[256,16]{0,1:T(8,128)S(1)} %add_rsqrt_fusion, bf16[16,128,4096]{2,1,0:T(8,128)(2,1)} %bitcast.80, bf16[1,256,4096]{2,1,0:T(8,128)(2,1)} %param.15), kind=kOutput, calls=%fused_computation.18 | convolution fusion | flops 4297060352 | bytes 23109632 | tf_op jit(solution)/shard_map/dot_general | solution.py:64
  295.5 1.7 multiply_convert_fusion
  297.1 2.3 copy.69
  299.5 4.2 all-to-all-start
  303.9 75.8 %all-gather.14.cloned.1.call-done = bf16[1,1024,4096]{2,1,0:T(8,128)(2,1)} async-done(((bf16[1,256,4096]{2,1,0:T(8,128)(2,1)}), bf16[1,1024,4096]{2,1,0:T(8,128)(2,1)}) %all-gather.14.cloned.1.call-update) | async-done | bytes 8388624 | tf_op jit(solution)/shard_map/all_gather | solution.py:69
  379.8 10.2 %fusion.2 = bf16[512,4096]{1,0:T(8,128)(2,1)} fusion(bf16[1024,512]{1,0:T(8,128)(2,1)} %bitcast.23, bf16[1,1024,4096]{2,1,0:T(8,128)(2,1)} %all-gather.14.cloned.1.call-done), kind=kOutput, calls=%fused_computation.4 | convolution fusion | flops 4297064448 | bytes 13631488 | tf_op jit(solution)/shard_map/dot_general | solution.py:67
  390.1 2.7 convolution_bitcast_fusion
  392.7 2.6 copy.65
  397.9 2.1 fusion.7
  400.0 2.3 copy.70
  402.3 3.5 fusion.24
  405.8 11.9 %fusion.5 = bf16[1,256,4096]{2,1,0:T(8,128)(2,1)} fusion(bf16[256,2048]{0,1:T(8,128)(2,1)S(1)} %bitcast.90, bf16[2048,4096]{1,0:T(8,128)(2,1)} %all-gather.8.cloned.1.call-done), kind=kOutput, calls=%fused_computation.6 | convolution fusion | flops 4296015872 | bytes 19922944 | tf_op jit(solution)/shard_map/dot_general | solution.py:61
  417.8 56.0 %reduce-scatter.2.cloned.1.call-done = bf16[16,4096]{1,0:T(8,128)(2,1)} async-done(((bf16[512,4096]{1,0:T(8,128)(2,1)}), bf16[16,4096]{1,0:T(8,128)(2,1)}) %reduce-scatter.2.cloned.1.call-update) | async-done | bytes 131088 | tf_op jit(solution)/shard_map/reduce_scatter | solution.py:74
  473.7 1.6 convert_multiply_fusion
  475.3 113.5 %all-gather.12.cloned.1.call-done = f32[512,128,128]{2,1,0:T(8,128)} async-done(((f32[16,128,128]{2,1,0:T(8,128)}), f32[512,128,128]{2,1,0:T(8,128)}) %all-gather.12.cloned.1.call-update) | async-done | bytes 33554448 | tf_op jit(solution)/shard_map/all_gather | solution.py:19
  589.0 47.1 %while.23 = (s32[]{:T(128)}, f32[16,128,128]{2,1,0:T(8,128)S(1)}, s32[]{:T(128)}, f32[32,16,128,128]{3,2,1,0:T(8,128)}, s32[]{:T(128)}, /*index=5*/s32[]{:T(128)}, s32[]{:T(128)}, s32[]{:T(128)}) while((s32[]{:T(128)}, f32[16,128,128]{2,1,0:T(8,128)S(1)}, s32[]{:T(128)}, f32[32,16,128,128]{3,2,1,0:T(8,128)}, s32[]{:T(128)}, ...), condition=%wide.region_5.6_spmd, body=%wide.region_4.5_spmd.sunk | while | flops 262150 | bytes 3145871 | solution.py:26
  589.0 1.5 bitcast_add_fusion.8
  590.5 1.5 bitcast_add_fusion.8
  592.0 1.5 bitcast_add_fusion.8
  593.5 1.5 bitcast_add_fusion.8
  595.1 1.5 bitcast_add_fusion.8
  596.6 1.5 bitcast_add_fusion.8
  598.1 1.5 bitcast_add_fusion.8
  599.6 1.5 bitcast_add_fusion.8
  601.1 1.5 bitcast_add_fusion.8
  602.6 1.5 bitcast_add_fusion.8
  604.1 1.5 bitcast_add_fusion.8
  605.6 1.5 bitcast_add_fusion.8
  607.1 1.5 bitcast_add_fusion.8
  608.7 1.5 bitcast_add_fusion.8
  610.2 1.5 bitcast_add_fusion.8
  611.7 1.5 bitcast_add_fusion.8
  613.2 1.5 bitcast_add_fusion.8
  614.7 1.5 bitcast_add_fusion.8
  616.2 1.5 bitcast_add_fusion.8
  617.7 1.5 bitcast_add_fusion.8
  619.2 1.5 bitcast_add_fusion.8
  620.7 1.5 bitcast_add_fusion.8
  622.3 1.5 bitcast_add_fusion.8
  623.8 1.5 bitcast_add_fusion.8
  625.3 1.5 bitcast_add_fusion.8
  626.8 1.5 bitcast_add_fusion.8
  640.0 2.7 add_convert_fusion
  (61 shorter events, 23.6 us)
Async XLA Ops:
  7.2 120.8 %all-gather.10.cloned.1.call-start = ((), (), s32[]{:S(2)}) async-start(), calls=%async_computation.4 | async-start | bytes 34603008 | tf_op jit(solution)/shard_map/all_gather | solution.py:19
  7.2 2.5 copy-start.12
  8.8 1.0 copy-start.5
  9.7 1.7 copy-start.3
  11.4 271.4 %all-gather.8.cloned.1.call-start = ((), (), s32[]{:S(2)}) async-start(), calls=%async_computation.2 | async-start | bytes 20971520 | tf_op jit(solution)/shard_map/all_gather | solution.py:60
  12.2 2.3 copy-start.6
  12.2 367.6 %all-gather.14.cloned.1.call-start = ((), (), s32[]{:S(2)}) async-start(), calls=%async_computation.6 | async-start | bytes 10485760 | tf_op jit(solution)/shard_map/all_gather | solution.py:69
  14.4 113.6 %copy-start = (bf16[32,8,16,128]{3,2,1,0:T(8,128)(2,1)}, bf16[32,8,16,128]{3,2,1,0:T(8,128)(2,1)S(1)}, u32[]{:S(2)}) copy-start(bf16[32,8,16,128]{3,2,1,0:T(8,128)(2,1)S(1)} %copy.77) | copy-start | bytes 3145732
  15.2 1.3 copy-start.11
  128.0 154.8 %copy-start.13 = (f32[2048]{0:T(1024)S(1)}, f32[2048]{0:T(1024)}, u32[]{:S(2)}) copy-start(f32[2048]{0:T(1024)} %param.13) | copy-start | bytes 24580
  282.8 12.6 %copy-start.10 = (f32[256,16,128]{0,2,1:T(8,128)S(1)}, f32[256,16,128]{0,2,1:T(8,128)}, u32[]{:S(2)}) copy-start(f32[256,16,128]{0,2,1:T(8,128)} %get-tuple-element.128) | copy-start | bytes 6291460
  299.5 80.3 %all-to-all-start = ((bf16[256,4,512]{2,0,1:T(8,128)(2,1)}), bf16[256,4,512]{2,0,1:T(8,128)(2,1)}, u32[]{:S(2)}, u32[]{:S(2)}) async-start(bf16[256,4,512]{2,0,1:T(8,128)(2,1)} %copy.69), calls=%async_computation | async-start | bytes 2097152 | tf_op jit(solution)/shard_map/all_to_all | solution.py:63
  303.7 170.0 %reduce-scatter.2.cloned.1.call-start = ((), (), s32[]{:S(2)}) async-start(), calls=%async_computation.3 | async-start | bytes 4325376 | tf_op jit(solution)/shard_map/reduce_scatter | solution.py:74
  390.0 198.9 %all-gather.12.cloned.1.call-start = ((), (), s32[]{:S(2)}) async-start(), calls=%async_computation.5 | async-start | bytes 34603008 | tf_op jit(solution)/shard_map/all_gather | solution.py:19
  395.3 1.2 copy-start.4
  396.6 1.4 copy-start.8
  402.3 3.5 copy-start.2
  636.1 1.2 copy-start.1
  636.1 1.9 copy-start.9
  638.6 1.4 copy-start.7
Sparse Core Ops, SparseCore 0:
  11.6 116.3 all-gather.9
  129.6 153.2 all-gather.7
  284.5 95.2 all-gather.13
  390.1 83.5 reduce-scatter.1
  475.8 113.0 all-gather.11
where the time goes:
time: 652 us; the launch traced here: 651 us
  waiting for transfers between devices  507 us (78%)
  matrix products  57.5 us (9%)
  other arithmetic  49.5 us (8%)
  local copies, waits for them, and re-layouts  17.5 us (3%)
  between operations  14 us (2%)
    all_gather x2, waiting for transfers between devices, prefix(): gathered = lax.all_gather(part, axis)  223 us
    all_gather x1, waiting for transfers between devices, shards(): full_weight = lax.all_gather(out_weight, 'dp', axis=0, tiled=True)  151 us
    all_gather x1, waiting for transfers between devices, shards(): lax.all_gather(grad_rows, 'dp', axis=0, tiled=True)  75.8 us
    reduce_scatter x1, waiting for transfers between devices, shards(): lax.psum_scatter(weight_term.astype(jnp.bfloat16), 'ctx', scatter_dimensi...  56 us
    add x31, other arithmetic, add_terms(): return earlier + later_part  46.1 us
  transfers between devices with their start and end apart: 6, of which 5 were waited for; matrix products, arithmetic and copies ran while one was open for 8% of the time, Pallas kernels for 0%

commit v1 on v0

v1 whole, which is shorter than its diff:
```python
import functools
import math

import jax
import jax.numpy as jnp
from jax import lax
from jax.experimental import pallas as pl
from jax.experimental.pallas import tpu as pltpu
from jax.sharding import Mesh, PartitionSpec as P

HD = 128
EPSILON = 1e-06
BF = jnp.bfloat16
F32 = jnp.float32
CTX = ("z", "y", "c")
CH = 4
HC = 4


def mm(a, b, ca, cb):
    return lax.dot_general(a, b, (((ca,), (cb,)), ((), ())), preferred_element_type=F32)


def cost(flops, nbytes):
    return pl.CostEstimate(flops=flops, bytes_accessed=nbytes, transcendentals=0)


def head(ref, h):
    return ref[:, h * HD : (h + 1) * HD]


def causal(n):
    return lax.broadcasted_iota(jnp.int32, (n, n), 0) >= lax.broadcasted_iota(
        jnp.int32, (n, n), 1
    )


def state_body(k_ref, v_ref, s_ref):
    for h in range(HC):
        s_ref[h] = mm(head(k_ref, h), head(v_ref, h), 0, 0).astype(BF)


def local_state(k, v):
    t, f = k.shape
    w = f // CH
    blk = pl.BlockSpec((t, w), lambda g: (0, g))
    return pl.pallas_call(
        state_body,
        grid=(CH,),
        in_specs=[blk, blk],
        out_specs=pl.BlockSpec((HC, HD, HD), lambda g: (g, 0, 0)),
        out_shape=jax.ShapeDtypeStruct((CH * HC, HD, HD), BF),
        cost_estimate=cost(2 * t * f * HD, 4 * t * f),
        name="local_state",
    )(k, v)


def scan_body(reverse, s_ref, o_ref):
    n = s_ref.shape[0]
    total = jnp.zeros(s_ref.shape[1:], F32)
    for step in range(n):
        at = n - 1 - step if reverse else step
        o_ref[at] = total.astype(BF)
        if step < n - 1:
            total = total + s_ref[at].astype(F32)


def scan_blocks(s, reverse):
    return pl.pallas_call(
        functools.partial(scan_body, reverse),
        out_shape=jax.ShapeDtypeStruct(s.shape, BF),
        cost_estimate=cost(s.size, 4 * s.size),
        name="scan_blocks",
    )(s)


def carry(state, reverse):
    n = lax.axis_size(CTX)
    parts = state.reshape(n, -1, HD)
    theirs = lax.all_to_all(parts, CTX, 0, 0, tiled=True)
    sums = scan_blocks(theirs, reverse)
    mine = lax.all_to_all(sums, CTX, 0, 0, tiled=True)
    return mine.reshape(state.shape)


def scores_body(q_ref, k_ref, v_ref, w_ref, o_ref):
    keep = causal(q_ref.shape[0])
    for h in range(HC):
        w = jnp.where(keep, mm(head(q_ref, h), head(k_ref, h), 1, 1), 0.0).astype(BF)
        w_ref[h] = w
        o_ref[:, h * HD : (h + 1) * HD] = mm(w, head(v_ref, h), 1, 0)


def local_scores(q, k, v):
    t, f = q.shape
    w = f // CH
    blk = pl.BlockSpec((t, w), lambda g: (0, g))
    return pl.pallas_call(
        scores_body,
        grid=(CH,),
        in_specs=[blk, blk, blk],
        out_specs=[pl.BlockSpec((HC, t, t), lambda g: (g, 0, 0)), blk],
        out_shape=[
            jax.ShapeDtypeStruct((CH * HC, t, t), BF),
            jax.ShapeDtypeStruct((t, f), F32),
        ],
        cost_estimate=cost(4 * t * t * f, 14 * t * f),
        name="local_scores",
    )(q, k, v)


def attend_body(q_ref, o_ref, c_ref, g_ref, n_ref, a_ref):
    for h in range(HC):
        cols = slice(h * HD, (h + 1) * HD)
        a = o_ref[:, cols] + mm(head(q_ref, h), c_ref[h], 1, 0)
        a_ref[0, :, cols] = a
        inv = lax.rsqrt(jnp.mean(a * a, axis=-1, keepdims=True) + EPSILON)
        n_ref[0, :, cols] = (a * inv * g_ref[:, cols]).astype(BF)


def attend(q, out, carried, gain):
    t, f = q.shape
    w = f // CH
    blk = pl.BlockSpec((t, w), lambda g: (0, g))
    st = pl.BlockSpec((HC, HD, HD), lambda g: (g, 0, 0))
    chunk = pl.BlockSpec((1, t, w), lambda g: (g, 0, 0))
    return pl.pallas_call(
        attend_body,
        grid=(CH,),
        in_specs=[blk, blk, st, pl.BlockSpec((1, w), lambda g: (0, g))],
        out_specs=[chunk, chunk],
        out_shape=[
            jax.ShapeDtypeStruct((CH, t, w), BF),
            jax.ShapeDtypeStruct((CH, t, w), F32),
        ],
        cost_estimate=cost(2 * t * f * HD, 12 * t * f),
        name="attend",
    )(q, out, carried, gain)


def grad_attn_body(i_ref, q_ref, a_ref, gn_ref, g_ref, ga_ref, lg_ref):
    for h in range(HC):
        cols = slice(h * HD, (h + 1) * HD)
        a = a_ref[0, :, cols]
        inv = lax.rsqrt(jnp.mean(a * a, axis=-1, keepdims=True) + EPSILON)
        unit = a * inv
        gu = gn_ref[:, cols] * g_ref[:, cols]
        ga = inv * (gu - unit * jnp.mean(gu * unit, axis=-1, keepdims=True))
        ga = ga.astype(BF)
        ga_ref[:, cols] = ga
        lg_ref[h] = mm(head(q_ref, h), ga, 0, 0).astype(BF)


def grad_attn(which, q, attended, gn, gain):
    t, f = q.shape
    w = f // CH
    whole = pl.BlockSpec((t, w), lambda g, i: (0, 0))
    return pl.pallas_call(
        grad_attn_body,
        grid_spec=pltpu.PrefetchScalarGridSpec(
            num_scalar_prefetch=1,
            grid=(1,),
            in_specs=[
                pl.BlockSpec((t, w), lambda g, i: (0, i[0])),
                pl.BlockSpec((1, t, w), lambda g, i: (i[0], 0, 0)),
                whole,
                pl.BlockSpec((1, w), lambda g, i: (0, i[0])),
            ],
            out_specs=[whole, pl.BlockSpec((HC, HD, HD), lambda g, i: (0, 0, 0))],
        ),
        out_shape=[
            jax.ShapeDtypeStruct((t, w), BF),
            jax.ShapeDtypeStruct((HC, HD, HD), BF),
        ],
        cost_estimate=cost(2 * t * w * HD, 12 * t * w),
        name="grad_attn",
    )(which, q, attended, gn, gain)


def grads_body(i_ref, q_ref, k_ref, v_ref, w_ref, ga_ref, c_ref, gq_ref, gk_ref, gv_ref):
    keep = causal(q_ref.shape[0])
    for h in range(HC):
        cols = slice(h * HD, (h + 1) * HD)
        ga = ga_ref[0, :, cols]
        gs = jnp.where(keep, mm(ga, head(v_ref, h), 1, 1), 0.0).astype(BF)
        gq = mm(gs, head(k_ref, h), 1, 0) + mm(ga, c_ref[h], 1, 1)
        gq_ref[:, cols] = gq.astype(BF)
        gk_ref[0, :, cols] = mm(gs, head(q_ref, h), 0, 0)
        gv_ref[0, :, cols] = mm(w_ref[h], ga, 0, 0)


def local_grads(order, q, k, v, weights, ga, carried):
    t, f = q.shape
    w = f // CH
    nat = pl.BlockSpec((t, w), lambda g, i: (0, i[g]))
    chunk = pl.BlockSpec((1, t, w), lambda g, i: (g, 0, 0))
    return pl.pallas_call(
        grads_body,
        grid_spec=pltpu.PrefetchScalarGridSpec(
            num_scalar_prefetch=1,
            grid=(CH,),
            in_specs=[
                nat,
                nat,
                nat,
                pl.BlockSpec((HC, t, t), lambda g, i: (i[g], 0, 0)),
                chunk,
                pl.BlockSpec((HC, HD, HD), lambda g, i: (i[g], 0, 0)),
            ],
            out_specs=[nat, chunk, chunk],
        ),
        out_shape=[
            jax.ShapeDtypeStruct((t, f), BF),
            jax.ShapeDtypeStruct((CH, t, w), F32),
            jax.ShapeDtypeStruct((CH, t, w), F32),
        ],
        cost_estimate=cost(8 * t * t * f, 24 * t * f),
        name="local_grads",
    )(order, q, k, v, weights, ga, carried)


def later_body(i_ref, k_ref, v_ref, l_ref, pk_ref, pv_ref, gk_ref, gv_ref):
    for h in range(HC):
        cols = slice(h * HD, (h + 1) * HD)
        gk = pk_ref[0, :, cols] + mm(head(v_ref, h), l_ref[h], 1, 1)
        gv = pv_ref[0, :, cols] + mm(head(k_ref, h), l_ref[h], 1, 0)
        gk_ref[:, cols] = gk.astype(BF)
        gv_ref[:, cols] = gv.astype(BF)


def later_grads(order, k, v, later, pk, pv):
    t, f = k.shape
    w = f // CH
    nat = pl.BlockSpec((t, w), lambda g, i: (0, i[g]))
    chunk = pl.BlockSpec((1, t, w), lambda g, i: (g, 0, 0))
    return pl.pallas_call(
        later_body,
        grid_spec=pltpu.PrefetchScalarGridSpec(
            num_scalar_prefetch=1,
            grid=(CH,),
            in_specs=[
                nat,
                nat,
                pl.BlockSpec((HC, HD, HD), lambda g, i: (g, 0, 0)),
                chunk,
                chunk,
            ],
            out_specs=[nat, nat],
        ),
        out_shape=[jax.ShapeDtypeStruct((t, f), BF)] * 2,
        cost_estimate=cost(4 * t * f * HD, 16 * t * f),
        name="later_grads",
    )(order, k, v, later, pk, pv)


def layer_body(i_ref, n_ref, *refs):
    o_ref = refs[-1]
    total = None
    for k in range(CH):
        part = mm(n_ref[i_ref[k]], refs[k][...], 1, 0)
        total = part if total is None else total + part
    o_ref[...] = total.astype(BF)


def layer_rows(order, normed, blocks):
    _, t, w = normed.shape
    d = blocks[0].shape[1]
    tile = 512
    return pl.pallas_call(
        layer_body,
        grid_spec=pltpu.PrefetchScalarGridSpec(
            num_scalar_prefetch=1,
            grid=(d // tile,),
            in_specs=[pl.BlockSpec((CH, t, w), lambda g, i: (0, 0, 0))]
            + [pl.BlockSpec((w, tile), lambda g, i: (0, g))] * CH,
            out_specs=pl.BlockSpec((t, tile), lambda g, i: (0, g)),
        ),
        out_shape=jax.ShapeDtypeStruct((t, d), BF),
        cost_estimate=cost(2 * t * CH * w * d, 2 * (CH * w * d + CH * t * w + t * d)),
        name="layer_rows",
    )(order, normed, *blocks)


def weight_body(add, h_ref, n_ref, *refs):
    g_refs, rest = refs[:CH], refs[CH:]
    o_ref, nt = rest[-2], rest[-1]

    @pl.when(pl.program_id(0) == 0)
    def _():
        for s in range(CH):
            nt[s] = n_ref[s].T

    total = None
    for s in range(CH):
        part = mm(nt[s], g_refs[s][...], 1, 0)
        total = part if total is None else total + part
    if add:
        total = total + rest[0][...].astype(F32)
    o_ref[...] = total.astype(BF)


def weight_half(half, normed_all, grads_all, extra):
    _, t, w = normed_all.shape
    d = grads_all[0].shape[1]
    tile = 512
    steps = d // 2 // tile
    own = pl.BlockSpec((w, tile), lambda g, i: (0, g))
    add = extra is not None
    return pl.pallas_call(
        functools.partial(weight_body, add),
        grid_spec=pltpu.PrefetchScalarGridSpec(
            num_scalar_prefetch=1,
            grid=(steps,),
            in_specs=[pl.BlockSpec((CH, t, w), lambda g, i: (0, 0, 0))]
            + [pl.BlockSpec((t, tile), lambda g, i: (0, i[0] * steps + g))] * CH
            + [own] * add,
            out_specs=own,
            scratch_shapes=[pltpu.VMEM((CH, w, t), BF)],
        ),
        out_shape=jax.ShapeDtypeStruct((w, d // 2), BF),
        cost_estimate=cost(CH * t * w * d, CH * t * d + 2 * CH * t * w + w * d),
        name="weight_half",
    )(half, normed_all, *grads_all, *([extra] if add else []))


def sum_body(scale, s_ref, o_ref):
    total = s_ref[0].astype(F32)
    for step in range(1, s_ref.shape[0]):
        total = total + s_ref[step].astype(F32)
    o_ref[...] = total * scale


def sum_parts(parts, scale):
    n, r, w = parts.shape
    return pl.pallas_call(
        functools.partial(sum_body, scale),
        out_shape=jax.ShapeDtypeStruct((r, w), F32),
        cost_estimate=cost(parts.size, 2 * parts.size),
        name="sum_parts",
    )(parts)


def shift(x, axis, by):
    n = lax.axis_size(axis)
    return lax.ppermute(x, axis, [((d + by) % n, d) for d in range(n)])


def shards(queries, keys, values, gain, out_weight, grad_out):
    tok_rows, feat_width = queries.shape[1:]
    model_width = grad_out.shape[2]
    q = queries.reshape(tok_rows, feat_width)
    k = keys.reshape(tok_rows, feat_width)
    v = values.reshape(tok_rows, feat_width)
    grad_rows = grad_out.reshape(tok_rows, model_width)
    gain_row = gain.reshape(1, feat_width)
    seqs = lax.axis_size("x")
    blocks_n = lax.axis_size(CTX)
    at_x = lax.axis_index("x")
    at_ctx = lax.axis_index(CTX)
    at_core = lax.axis_index("c")
    order = (at_x + jnp.arange(CH, dtype=jnp.int32)) % CH

    piece = out_weight.shape[0] // blocks_n
    own_piece = lax.dynamic_slice_in_dim(out_weight, at_ctx * piece, piece, 0)
    blocks = [out_weight]
    for by in range(1, CH):
        blocks.append(lax.all_gather(shift(own_piece, "x", by), CTX, axis=0, tiled=True))

    right = shift(grad_rows, "x", 1)
    left = shift(grad_rows, "x", 3)
    half_cols = model_width // 2
    far_a = shift(right[:, :half_cols], "x", 1)
    far_b = shift(left[:, half_cols:], "x", 3)
    far = jnp.concatenate([far_a, far_b], axis=1)

    carried = carry(local_state(k, v), False)
    weights, local_out = local_scores(q, k, v)
    normed, attended = attend(q, local_out, carried, gain_row)

    ga, lg = [], []
    for n in range(CH):
        gn = mm(grad_rows, blocks[n], 1, 1)
        one_ga, one_lg = grad_attn(order[n : n + 1], q, attended, gn, gain_row)
        ga.append(one_ga)
        lg.append(one_lg)
    later = carry(jnp.concatenate(lg, axis=0), True)
    grad_query, pk, pv = local_grads(order, q, k, v, weights, jnp.stack(ga), carried)
    grad_key, grad_value = later_grads(order, k, v, later, pk, pv)

    layer_out = layer_rows(order, normed, blocks)

    normed_all = lax.all_to_all(normed, "x", 0, 0, tiled=True)
    rel = (jnp.arange(CH, dtype=jnp.int32) + at_x) % seqs
    normed_rot = jnp.take(normed_all, rel, axis=0)
    grads_all = [grad_rows, right, far, left]
    mine = at_core.reshape(1).astype(jnp.int32)
    for_partner = weight_half(1 - mine, normed_rot, grads_all, None)
    from_partner = shift(for_partner, "c", 1)
    partial = weight_half(mine, normed_rot, grads_all, from_partner)
    chips = blocks_n // 2
    rows = partial.shape[0] // chips
    parts = lax.all_to_all(
        partial.reshape(chips, rows, half_cols), ("z", "y"), 0, 0, tiled=True
    )
    token_count = seqs * blocks_n * tok_rows
    summed = sum_parts(parts, 1.0 / math.sqrt(token_count))
    out_rows = rows // 2
    keep = lax.dynamic_slice_in_dim(summed, at_core * out_rows, out_rows, 0)
    give = lax.dynamic_slice_in_dim(summed, (1 - at_core) * out_rows, out_rows, 0)
    got = shift(give, "c", 1)
    first = at_core == 0
    grad_weight = jnp.concatenate(
        [jnp.where(first, keep, got), jnp.where(first, got, keep)], axis=1
    )
    out_shape = (1, tok_rows, feat_width)
    return (
        layer_out.reshape(1, tok_rows, model_width),
        grad_query.reshape(out_shape),
        grad_key.reshape(out_shape),
        grad_value.reshape(out_shape),
        grad_weight,
    )


def solution(mesh):
    mesh = Mesh(mesh.devices.reshape(4, 4, 4, 2), ("x",) + CTX)
    tokens = P("x", CTX, None)
    in_specs = (tokens, tokens, tokens, P(), P("x", None), tokens)
    out_specs = (tokens, tokens, tokens, tokens, P(("x",) + CTX, None))
    return jax.shard_map(shards, mesh=mesh, in_specs=in_specs, out_specs=out_specs, check_vma=False)
```

time: 652 us -> 293 us (0.45)
  waiting for transfers between devices: 507 us -> 115 us
  Pallas kernels: 0 us -> 74.6 us
  other arithmetic: 49.5 us -> 4.8 us
  starting transfers between devices: 4.62 us -> 45.1 us
  matrix products: 57.5 us -> 18.4 us
    all_gather x4 -> x3, waiting for transfers between devices: 449 us -> 0.02 us  [shards(): lax.all_gather(shift(own_piece, 'x', by), CTX, axis=0, tiled=True)]
    pallas_call x0 -> x15, Pallas kernels: none -> 74.6 us  [the longest x2 13.6 us: weight_half(): pl.pallas_call(functools.partial(weight_body, add), grid_spec=pltpu.Prefe...]
    ppermute x0 -> x9, waiting for transfers between devices: none -> 63.6 us  [shift(): return lax.ppermute(x, axis, [((d + by) % n, d) for d in range(n)])]
    reduce_scatter x1 -> x0, waiting for transfers between devices: 56 us -> none  [shards(): lax.psum_scatter(weight_term.astype(jnp.bfloat16), 'ctx', scatter_dimensi...]
    all_to_all x1 -> x6, waiting for transfers between devices: 0.01 us -> 51.6 us  [the longest x1 24.8 us: shards(): lax.all_to_all(partial.reshape(chips, rows, half_cols), ('z', 'y'), 0, 0,...]
    add x31 -> x0, other arithmetic: 46.1 us -> none  [add_terms(): return earlier + later_part]
    dot_general x15 -> x4, matrix products: 57.5 us -> 18.4 us  [mm(): lax.dot_general(a, b, (((ca,), (cb,)), ((), ())), preferred_element_type=...]
    all_to_all x1 -> x6, starting transfers between devices: 4.24 us -> 32.6 us  [the longest x2 12.5 us: carry(): mine = lax.all_to_all(sums, CTX, 0, 0, tiled=True)]
  transfers between devices with their start and end apart: 6 -> 18, of which waited for: 5 -> 9; matrix products, arithmetic and copies ran while one was open for 8% -> 11% of each run, Pallas kernels for 0% -> 23%
where the time goes in v1:
time: 293 us; the launch traced here: 290 us
  waiting for transfers between devices  115 us (39%)
  Pallas kernels  74.6 us (25%)
  starting transfers between devices  45.1 us (15%)
  matrix products  18.4 us (6%)
  local copies, waits for them, and re-layouts  18.2 us (6%)
  between operations  14 us (5%)
  other arithmetic  4.8 us (2%)
    ppermute x9, waiting for transfers between devices, shift(): return lax.ppermute(x, axis, [((d + by) % n, d) for d in range(n)])  63.6 us
    all_to_all x1, waiting for transfers between devices, shards(): lax.all_to_all(partial.reshape(chips, rows, half_cols), ('z', 'y'), 0, 0,...  24.8 us
    dot_general x4, matrix products, mm(): lax.dot_general(a, b, (((ca,), (cb,)), ((), ())), preferred_element_type=...  18.4 us
    pallas_call x2, Pallas kernels, weight_half(): pl.pallas_call(functools.partial(weight_body, add), grid_spec=pltpu.Prefe...  13.6 us
    pallas_call x4, Pallas kernels, grad_attn(): pl.pallas_call(grad_attn_body, grid_spec=pltpu.PrefetchScalarGridSpec(num...  13.2 us
    pallas_call x1, Pallas kernels, layer_rows(): pl.pallas_call(layer_body, grid_spec=pltpu.PrefetchScalarGridSpec(num_sca...  12.5 us
    all_to_all x2, starting transfers between devices, carry(): mine = lax.all_to_all(sums, CTX, 0, 0, tiled=True)  12.5 us
    all_to_all x2, starting transfers between devices, carry(): theirs = lax.all_to_all(parts, CTX, 0, 0, tiled=True)  12.4 us
  transfers between devices with their start and end apart: 18, of which 9 were waited for; matrix products, arithmetic and copies ran while one was open for 11% of the time, Pallas kernels for 23%

profile of v1, /device:TPU:0, one launch (start us, length us, event | category | flops | bytes accessed | tf_op | source)
XLA Modules:
  0.0 290.3 jit_solution(4241920245270369752)
XLA Ops:
  8.1 1.7 collective-permute-start.2
  9.8 4.8 %collective-permute-done.2 = bf16[16,4096]{1,0:T(8,128)(2,1)S(1)} collective-permute-done((bf16[16,4096]{1,0:T(8,128)(2,1)S(1)}, bf16[16,4096]{1,0:T(8,128)(2,1)S(1)}, u32[]{:S(2)}, u32[]{:S(2)}) %collective-permute-start.2) | collective-permute-done | bytes 131104 | tf_op jit(solution)/shard_map/ppermute | solution.py:345
  15.3 2.1 collective-permute-start.1
  17.4 4.5 %collective-permute-done.1 = bf16[16,4096]{1,0:T(8,128)(2,1)S(1)} collective-permute-done((bf16[16,4096]{1,0:T(8,128)(2,1)S(1)}, bf16[16,4096]{1,0:T(8,128)(2,1)S(1)}, u32[]{:S(2)}, u32[]{:S(2)}) %collective-permute-start.1) | collective-permute-done | bytes 131104 | tf_op jit(solution)/shard_map/ppermute | solution.py:345
  22.5 1.8 collective-permute-start.3
  24.6 3.0 %collective-permute-start = (bf16[16,4096]{1,0:T(8,128)(2,1)S(1)}, bf16[16,4096]{1,0:T(8,128)(2,1)S(1)}, u32[]{:S(2)}, u32[]{:S(2)}) collective-permute-start(bf16[16,4096]{1,0:T(8,128)(2,1)S(1)} %constant_dynamic-slice_fusion.1), channel_id=1, source_target_pairs={{32,0},{64,32},{96,64},{0,96},{33,1},{65,33},{97,65},{1,97},{34,2}... | collective-permute-start | bytes 393224 | tf_op jit(solution)/shard_map/ppermute | solution.py:345
  27.6 4.0 %local_state.1 = bf16[16,128,128]{2,1,0:T(8,128)(2,1)} custom-call(bf16[256,2048]{1,0:T(8,128)(2,1)} %bitcast.46, bf16[256,2048]{1,0:T(8,128)(2,1)} %bitcast.50), custom_call_target="tpu_custom_call" | custom-call | flops 134217728 | bytes 2097152 | tf_op jit(solution)/shard_map/local_state/pallas_call | solution.py:47
  31.5 8.3 %all-to-all-start = ((bf16[32,64,128]{2,1,0:T(8,128)(2,1)}), bf16[32,64,128]{2,1,0:T(8,128)(2,1)S(1)}, u32[]{:S(2)}, u32[]{:S(2)}) async-start(bf16[32,64,128]{2,1,0:T(8,128)(2,1)} %bitcast.61), calls=%async_computation | async-start | bytes 1048576 | tf_op jit(solution)/shard_map/all_to_all | solution.py:80
  39.9 31.0 %collective-permute-done = bf16[16,4096]{1,0:T(8,128)(2,1)S(1)} collective-permute-done((bf16[16,4096]{1,0:T(8,128)(2,1)S(1)}, bf16[16,4096]{1,0:T(8,128)(2,1)S(1)}, u32[]{:S(2)}, u32[]{:S(2)}) %collective-permute-start) | collective-permute-done | bytes 131104 | tf_op jit(solution)/shard_map/ppermute | solution.py:345
  72.4 1.9 scan_blocks.2
  74.3 8.6 %all-to-all-start.1 = ((bf16[32,64,128]{2,1,0:T(8,128)(2,1)}), bf16[32,64,128]{2,1,0:T(8,128)(2,1)S(1)}, u32[]{:S(2)}, u32[]{:S(2)}) async-start(bf16[32,64,128]{2,1,0:T(8,128)(2,1)} %scan_blocks.2), calls=%async_computation.1 | async-start | bytes 1048576 | tf_op jit(solution)/shard_map/all_to_all | solution.py:82
  82.9 5.4 %local_scores.1 = (bf16[16,256,256]{2,1,0:T(8,128)(2,1)}, f32[256,2048]{1,0:T(8,128)}) custom-call(bf16[256,2048]{1,0:T(8,128)(2,1)} %bitcast.39, bf16[256,2048]{1,0:T(8,128)(2,1)} %bitcast.47, bf16[256,2048]{1,0:T(8,128)(2,1)} %bitcast.51), custom_call_target="tpu_custom_call" | custom-call | flops 536870912 | bytes 7340032 | tf_op jit(solution)/shard_map/local_scores/pallas_call | solution.py:98
  88.4 6.1 %all-to-all-done.1 = bf16[32,64,128]{2,1,0:T(8,128)(2,1)S(1)} async-done(((bf16[32,64,128]{2,1,0:T(8,128)(2,1)}), bf16[32,64,128]{2,1,0:T(8,128)(2,1)S(1)}, u32[]{:S(2)}, u32[]{:S(2)}) %all-to-all-start.1) | async-done | bytes 524320 | tf_op jit(solution)/shard_map/all_to_all | solution.py:82
  95.3 4.6 %attend.1 = (bf16[4,256,512]{2,1,0:T(8,128)(2,1)}, f32[4,256,512]{2,1,0:T(8,128)}) custom-call(bf16[256,2048]{1,0:T(8,128)(2,1)} %bitcast.40, f32[256,2048]{1,0:T(8,128)} %get-tuple-element.22.o_ref, bf16[16,128,128]{2,1,0:T(8,128)(2,1)} %bitcast.59, f32[1,2048]{1,0:T(1,128)} %bitcast.68), custom_call_target="tpu_custom_call" | custom-call | flops 134217728 | bytes 6291456 | tf_op jit(solution)/shard_map/attend/pallas_call | solution.py:127
  99.9 4.0 %all-to-all-start.4 = ((bf16[4,256,512]{2,1,0:T(8,128)(2,1)}), bf16[4,256,512]{2,1,0:T(8,128)(2,1)S(1)}, u32[]{:S(2)}, u32[]{:S(2)}) async-start(bf16[4,256,512]{2,1,0:T(8,128)(2,1)} %get-tuple-element.23.n_ref), calls=%async_computation.4 | async-start | bytes 2097152 | tf_op jit(solution)/shard_map/all_to_all | solution.py:392
  104.0 1.1 slice.26
  105.1 3.2 %collective-permute-start.4 = (bf16[256,2048]{1,0:T(8,128)(2,1)}, bf16[256,2048]{1,0:T(8,128)(2,1)}, u32[]{:S(2)}, u32[]{:S(2)}) collective-permute-start(bf16[256,2048]{1,0:T(8,128)(2,1)} %slice.26), channel_id=1, source_target_pairs={{32,0},{64,32},{96,64},{0,96},{33,1},{65,33},{97,65},{1,97},{34,2}... | collective-permute-start | bytes 3145736 | tf_op jit(solution)/shard_map/ppermute | solution.py:345
  108.3 2.3 slice.27
  110.7 9.8 %all-to-all-done.4 = bf16[4,256,512]{2,1,0:T(8,128)(2,1)S(1)} async-done(((bf16[4,256,512]{2,1,0:T(8,128)(2,1)}), bf16[4,256,512]{2,1,0:T(8,128)(2,1)S(1)}, u32[]{:S(2)}, u32[]{:S(2)}) %all-to-all-start.4) | async-done | bytes 1048608 | tf_op jit(solution)/shard_map/all_to_all | solution.py:392
  121.1 1.1 broadcast_select_fusion.n_ref
  122.3 18.2 %collective-permute-done.4 = bf16[256,2048]{1,0:T(8,128)(2,1)} collective-permute-done((bf16[256,2048]{1,0:T(8,128)(2,1)}, bf16[256,2048]{1,0:T(8,128)(2,1)}, u32[]{:S(2)}, u32[]{:S(2)}) %collective-permute-start.4) | collective-permute-done | bytes 1048608 | tf_op jit(solution)/shard_map/ppermute | solution.py:345
  140.4 1.3 constant_dynamic-update-slice_fusion.1
  141.7 1.3 constant_dynamic-update-slice_fusion.refs_2_
  143.0 1.4 copy-done.1
  144.4 6.5 %weight_half.2 = bf16[512,2048]{1,0:T(8,128)(2,1)} custom-call(s32[1]{0:T(128)S(6)} %sub.6.h_ref, bf16[4,256,512]{2,1,0:T(8,128)(2,1)} %broadcast_select_fusion.n_ref, bf16[256,4096]{1,0:T(8,128)(2,1)} %bitcast.57, bf16[256,4096]{1,0:T(8,128)(2,1)} %copy-done, bf16[256,4096]{1,0:T(8,128)(2,1)} %copy-done.1, bf16[256,4096]{1,0:T(8,128)(2,1)} %collective-permute-done.5.refs_3_), custom_call_target="tpu_custom_call" | custom-call | flops 2147483648 | bytes 7340032 | tf_op jit(solution)/shard_map/weight_half/pallas_call | solution.py:309
  150.9 5.2 %collective-permute-done.7.refs_4_ = bf16[512,2048]{1,0:T(8,128)(2,1)S(1)} collective-permute-done((bf16[512,2048]{1,0:T(8,128)(2,1)}, bf16[512,2048]{1,0:T(8,128)(2,1)S(1)}, u32[]{:S(2)}, u32[]{:S(2)}) %collective-permute-start.7) | collective-permute-done | bytes 2097184 | tf_op jit(solution)/shard_map/ppermute | solution.py:345
  156.1 1.4 copy-done.7
  157.5 7.1 %weight_half.3 = bf16[512,2048]{1,0:T(8,128)(2,1)} custom-call(s32[1]{0:T(128)} %bitcast.20.h_ref, bf16[4,256,512]{2,1,0:T(8,128)(2,1)} %broadcast_select_fusion.n_ref, bf16[256,4096]{1,0:T(8,128)(2,1)} %bitcast.58, bf16[256,4096]{1,0:T(8,128)(2,1)} %copy-done, bf16[256,4096]{1,0:T(8,128)(2,1)} %copy-done.1, ...), custom_call_target="tpu_custom_call" | custom-call | flops 2147483648 | bytes 7340032 | tf_op jit(solution)/shard_map/weight_half/pallas_call | solution.py:309
  164.6 3.7 %all-to-all-start.5 = ((bf16[16,32,2048]{2,1,0:T(8,128)(2,1)}), bf16[16,32,2048]{2,1,0:T(8,128)(2,1)S(1)}, u32[]{:S(2)}, u32[]{:S(2)}) async-start(bf16[16,32,2048]{2,1,0:T(8,128)(2,1)} %bitcast.54), calls=%async_computation.5 | async-start | bytes 4194304 | tf_op jit(solution)/shard_map/all_to_all | solution.py:402
  169.0 4.9 %fusion.6.gn_ref = f32[256,512]{1,0:T(8,128)} fusion(bf16[512,4096]{1,0:T(8,128)(2,1)} %refs_0_.1, bf16[1,256,4096]{2,1,0:T(8,128)(2,1)} %param.11), kind=kOutput, calls=%fused_computation.30 | convolution fusion | flops 1073741824 | bytes 6815744 | tf_op jit(solution)/shard_map/dot_general | solution.py:21
  173.9 3.3 %grad_attn.4 = (bf16[256,512]{1,0:T(8,128)(2,1)}, bf16[4,128,128]{2,1,0:T(8,128)(2,1)}) custom-call(s32[1]{0:T(128)} %get-tuple-element.41.i_ref, bf16[256,2048]{1,0:T(8,128)(2,1)} %bitcast.41, f32[4,256,512]{2,1,0:T(8,128)} %get-tuple-element.25.a_ref, f32[256,512]{1,0:T(8,128)} %fusion.6.gn_ref, f32[1,2048]{1,0:T(1,128)} %bitcast.69), custom_call_target="tpu_custom_call" | custom-call | flops 33554432 | bytes 1572864 | tf_op jit(solution)/shard_map/grad_attn/pallas_call | solution.py:158
  177.1 24.8 %all-to-all-done.5.s_ref = bf16[16,32,2048]{2,1,0:T(8,128)(2,1)S(1)} async-done(((bf16[16,32,2048]{2,1,0:T(8,128)(2,1)}), bf16[16,32,2048]{2,1,0:T(8,128)(2,1)S(1)}, u32[]{:S(2)}, u32[]{:S(2)}) %all-to-all-start.5) | async-done | bytes 2097184 | tf_op jit(solution)/shard_map/all_to_all | solution.py:402
  201.9 1.3 copy-done.2
  203.2 2.6 sum_parts.1
  207.0 4.9 %convolution_bitcast_fusion.gn_ref = f32[256,512]{1,0:T(8,128)} fusion(bf16[512,4096]{1,0:T(8,128)(2,1)} %all-gather.8.cloned.1.call-done.refs_3_, bf16[1,256,4096]{2,1,0:T(8,128)(2,1)} %param.11), kind=kOutput, calls=%fused_computation.1 | convolution fusion | flops 1073741824 | bytes 6815744 | tf_op jit(solution)/shard_map/dot_general | solution.py:21
  212.0 3.4 %grad_attn.7 = (bf16[256,512]{1,0:T(8,128)(2,1)}, bf16[4,128,128]{2,1,0:T(8,128)(2,1)}) custom-call(s32[1]{0:T(128)} %get-tuple-element.42.i_ref, bf16[256,2048]{1,0:T(8,128)(2,1)} %bitcast.42, f32[4,256,512]{2,1,0:T(8,128)} %get-tuple-element.25.a_ref, f32[256,512]{1,0:T(8,128)} %convolution_bitcast_fusion.gn_ref, f32[1,2048]{1,0:T(1,128)} %bitcast.70), custom_call_target="tpu_custom_call" | custom-call | flops 33554432 | bytes 1572864 | tf_op jit(solution)/shard_map/grad_attn/pallas_call | solution.py:158
  215.4 4.3 %convolution_bitcast_fusion.1.gn_ref = f32[256,512]{1,0:T(8,128)} fusion(bf16[512,4096]{1,0:T(8,128)(2,1)} %all-gather.6.cloned.1.call-done.refs_2_, bf16[1,256,4096]{2,1,0:T(8,128)(2,1)S(1)} %copy-done.3), kind=kOutput, calls=%fused_computation.2 | convolution fusion | flops 1073741824 | bytes 6815744 | tf_op jit(solution)/shard_map/dot_general | solution.py:21
  219.7 4.3 %convolution_bitcast_fusion.2.gn_ref = f32[256,512]{1,0:T(8,128)} fusion(bf16[512,4096]{1,0:T(8,128)(2,1)} %all-gather.4.cloned.1.call-done.refs_1_, bf16[1,256,4096]{2,1,0:T(8,128)(2,1)S(1)} %copy-done.3), kind=kOutput, calls=%fused_computation.3 | convolution fusion | flops 1073741824 | bytes 6815744 | tf_op jit(solution)/shard_map/dot_general | solution.py:21
  223.9 3.2 %grad_attn.6 = (bf16[256,512]{1,0:T(8,128)(2,1)}, bf16[4,128,128]{2,1,0:T(8,128)(2,1)}) custom-call(s32[1]{0:T(128)} %get-tuple-element.43.i_ref, bf16[256,2048]{1,0:T(8,128)(2,1)} %bitcast.43, f32[4,256,512]{2,1,0:T(8,128)} %get-tuple-element.25.a_ref, f32[256,512]{1,0:T(8,128)} %convolution_bitcast_fusion.1.gn_ref, f32[1,2048]{1,0:T(1,128)} %bitcast.71), custom_call_target="tpu_custom_call" | custom-call | flops 33554432 | bytes 1572864 | tf_op jit(solution)/shard_map/grad_attn/pallas_call | solution.py:158
  227.1 3.3 %grad_attn.5 = (bf16[256,512]{1,0:T(8,128)(2,1)}, bf16[4,128,128]{2,1,0:T(8,128)(2,1)}) custom-call(s32[1]{0:T(128)} %get-tuple-element.44.i_ref, bf16[256,2048]{1,0:T(8,128)(2,1)} %bitcast.44, f32[4,256,512]{2,1,0:T(8,128)} %get-tuple-element.25.a_ref, f32[256,512]{1,0:T(8,128)} %convolution_bitcast_fusion.2.gn_ref, f32[1,2048]{1,0:T(1,128)} %bitcast.72), custom_call_target="tpu_custom_call" | custom-call | flops 33554432 | bytes 1572864 | tf_op jit(solution)/shard_map/grad_attn/pallas_call | solution.py:158
  230.5 1.8 pad_maximum_fusion.1
  232.2 4.0 %all-to-all-start.2 = ((bf16[32,64,128]{2,1,0:T(8,128)(2,1)}), bf16[32,64,128]{2,1,0:T(8,128)(2,1)S(1)}, u32[]{:S(2)}, u32[]{:S(2)}) async-start(bf16[32,64,128]{2,1,0:T(8,128)(2,1)} %bitcast.16), calls=%async_computation.2 | async-start | bytes 1048576 | tf_op jit(solution)/shard_map/all_to_all | solution.py:80
  237.1 10.8 %all-to-all-done.2.s_ref = bf16[32,64,128]{2,1,0:T(8,128)(2,1)S(1)} async-done(((bf16[32,64,128]{2,1,0:T(8,128)(2,1)}), bf16[32,64,128]{2,1,0:T(8,128)(2,1)S(1)}, u32[]{:S(2)}, u32[]{:S(2)}) %all-to-all-start.2) | async-done | bytes 524320 | tf_op jit(solution)/shard_map/all_to_all | solution.py:80
  248.7 1.9 scan_blocks.3
  250.6 3.9 %all-to-all-start.3 = ((bf16[32,64,128]{2,1,0:T(8,128)(2,1)}), bf16[32,64,128]{2,1,0:T(8,128)(2,1)S(1)}, u32[]{:S(2)}, u32[]{:S(2)}) async-start(bf16[32,64,128]{2,1,0:T(8,128)(2,1)} %scan_blocks.3), calls=%async_computation.3 | async-start | bytes 1048576 | tf_op jit(solution)/shard_map/all_to_all | solution.py:82
  255.7 9.0 %local_grads.1 = (bf16[256,2048]{1,0:T(8,128)(2,1)}, f32[4,256,512]{2,1,0:T(8,128)}, f32[4,256,512]{2,1,0:T(8,128)}) custom-call(s32[4]{0:T(128)} %copy-done.20, bf16[256,2048]{1,0:T(8,128)(2,1)} %bitcast.45, bf16[256,2048]{1,0:T(8,128)(2,1)} %bitcast.48, bf16[256,2048]{1,0:T(8,128)(2,1)} %bitcast.52, bf16[16,256,256]{2,1,0:T(8,128)(2,1)} %get-tuple-element.24.w_ref, ...), custom_call_target="tpu_custom_call" | custom-call | flops 1073741824 | bytes 12582912 | tf_op jit(solution)/shard_map/local_grads/pallas_call | solution.py:197
  264.6 12.5 %layer_rows.1 = bf16[256,4096]{1,0:T(8,128)(2,1)} custom-call(s32[4]{0:T(128)} %copy-done.20, bf16[4,256,512]{2,1,0:T(8,128)(2,1)} %get-tuple-element.23.n_ref, bf16[512,4096]{1,0:T(8,128)(2,1)} %refs_0_.1, bf16[512,4096]{1,0:T(8,128)(2,1)} %all-gather.4.cloned.1.call-done.refs_1_, bf16[512,4096]{1,0:T(8,128)(2,1)} %all-gather.6.cloned.1.call-done.refs_2_, ...), custom_call_target="tpu_custom_call" | custom-call | flops 4294967296 | bytes 19922944 | tf_op jit(solution)/shard_map/layer_rows/pallas_call | solution.py:269
  278.0 5.8 %later_grads.1 = (bf16[256,2048]{1,0:T(8,128)(2,1)}, bf16[256,2048]{1,0:T(8,128)(2,1)}) custom-call(s32[4]{0:T(128)} %copy-done.20, bf16[256,2048]{1,0:T(8,128)(2,1)} %bitcast.49, bf16[256,2048]{1,0:T(8,128)(2,1)} %bitcast.53, bf16[16,128,128]{2,1,0:T(8,128)(2,1)} %bitcast.62, f32[4,256,512]{2,1,0:T(8,128)} %get-tuple-element.35.pk_ref, ...), custom_call_target="tpu_custom_call" | custom-call | flops 268435456 | bytes 8388608 | tf_op jit(solution)/shard_map/later_grads/pallas_call | solution.py:236
  (69 shorter events, 10.9 us)
Async XLA Ops:
  7.2 199.8 %all-gather.8.cloned.1.call-start = ((), (), s32[]{:S(2)}) async-start(), calls=%async_computation.8 | async-start | bytes 4325376 | tf_op jit(solution)/shard_map/all_gather | solution.py:367
  8.1 6.4 %collective-permute-start.2 = (bf16[16,4096]{1,0:T(8,128)(2,1)S(1)}, bf16[16,4096]{1,0:T(8,128)(2,1)S(1)}, u32[]{:S(2)}, u32[]{:S(2)}) collective-permute-start(bf16[16,4096]{1,0:T(8,128)(2,1)S(1)} %constant_dynamic-slice_fusion.1), channel_id=1, source_target_pairs={{96,0},{0,32},{32,64},{64,96},{97,1},{1,33},{33,65},{65,97},{98,2}... | collective-permute-start | bytes 393224 | tf_op jit(solution)/shard_map/ppermute | solution.py:345
  14.6 0.7 copy-start.14
  15.3 200.1 %all-gather.6.cloned.1.call-start = ((), (), s32[]{:S(2)}) async-start(), calls=%async_computation.7 | async-start | bytes 4325376 | tf_op jit(solution)/shard_map/all_gather | solution.py:367
  15.3 6.6 %collective-permute-start.1 = (bf16[16,4096]{1,0:T(8,128)(2,1)S(1)}, bf16[16,4096]{1,0:T(8,128)(2,1)S(1)}, u32[]{:S(2)}, u32[]{:S(2)}) collective-permute-start(bf16[16,4096]{1,0:T(8,128)(2,1)S(1)} %constant_dynamic-slice_fusion.1), channel_id=1, source_target_pairs={{64,0},{96,32},{0,64},{32,96},{65,1},{97,33},{1,65},{33,97},{66,2}... | collective-permute-start | bytes 393224 | tf_op jit(solution)/shard_map/ppermute | solution.py:345
  21.9 0.7 copy-start.15
  22.5 81.4 %collective-permute-start.3 = (bf16[256,4096]{1,0:T(8,128)(2,1)}, bf16[256,4096]{1,0:T(8,128)(2,1)S(1)}, u32[]{:S(2)}, u32[]{:S(2)}) collective-permute-start(bf16[256,4096]{1,0:T(8,128)(2,1)} %bitcast.55), channel_id=1, source_target_pairs={{32,0},{64,32},{96,64},{0,96},{33,1},{65,33},{97,65},{1,97},{34,2}... | collective-permute-start | bytes 6291464 | tf_op jit(solution)/shard_map/ppermute | solution.py:345
  24.4 83.9 %collective-permute-start.5 = (bf16[256,4096]{1,0:T(8,128)(2,1)}, bf16[256,4096]{1,0:T(8,128)(2,1)}, u32[]{:S(2)}, u32[]{:S(2)}) collective-permute-start(bf16[256,4096]{1,0:T(8,128)(2,1)} %bitcast.56), channel_id=1, source_target_pairs={{96,0},{0,32},{32,64},{64,96},{97,1},{1,33},{33,65},{65,97},{98,2}... | collective-permute-start | bytes 6291464 | tf_op jit(solution)/shard_map/ppermute | solution.py:345
  24.6 46.3 %collective-permute-start = (bf16[16,4096]{1,0:T(8,128)(2,1)S(1)}, bf16[16,4096]{1,0:T(8,128)(2,1)S(1)}, u32[]{:S(2)}, u32[]{:S(2)}) collective-permute-start(bf16[16,4096]{1,0:T(8,128)(2,1)S(1)} %constant_dynamic-slice_fusion.1), channel_id=1, source_target_pairs={{32,0},{64,32},{96,64},{0,96},{33,1},{65,33},{97,65},{1,97},{34,2}... | collective-permute-start | bytes 393224 | tf_op jit(solution)/shard_map/ppermute | solution.py:345
  31.5 40.0 %all-to-all-start = ((bf16[32,64,128]{2,1,0:T(8,128)(2,1)}), bf16[32,64,128]{2,1,0:T(8,128)(2,1)S(1)}, u32[]{:S(2)}, u32[]{:S(2)}) async-start(bf16[32,64,128]{2,1,0:T(8,128)(2,1)} %bitcast.61), calls=%async_computation | async-start | bytes 1048576 | tf_op jit(solution)/shard_map/all_to_all | solution.py:80
  39.9 179.8 %all-gather.4.cloned.1.call-start = ((), (), s32[]{:S(2)}) async-start(), calls=%async_computation.6 | async-start | bytes 4325376 | tf_op jit(solution)/shard_map/all_gather | solution.py:367
  70.9 0.6 copy-start.16
  71.6 0.8 copy-start.6
  74.3 20.2 %all-to-all-start.1 = ((bf16[32,64,128]{2,1,0:T(8,128)(2,1)}), bf16[32,64,128]{2,1,0:T(8,128)(2,1)S(1)}, u32[]{:S(2)}, u32[]{:S(2)}) async-start(bf16[32,64,128]{2,1,0:T(8,128)(2,1)} %scan_blocks.2), calls=%async_computation.1 | async-start | bytes 1048576 | tf_op jit(solution)/shard_map/all_to_all | solution.py:82
  94.5 0.8 copy-start.4
  99.9 20.6 %all-to-all-start.4 = ((bf16[4,256,512]{2,1,0:T(8,128)(2,1)}), bf16[4,256,512]{2,1,0:T(8,128)(2,1)S(1)}, u32[]{:S(2)}, u32[]{:S(2)}) async-start(bf16[4,256,512]{2,1,0:T(8,128)(2,1)} %get-tuple-element.23.n_ref), calls=%async_computation.4 | async-start | bytes 2097152 | tf_op jit(solution)/shard_map/all_to_all | solution.py:392
  103.9 6.7 %copy-start = (bf16[256,4096]{1,0:T(8,128)(2,1)}, bf16[256,4096]{1,0:T(8,128)(2,1)S(1)}, u32[]{:S(2)}) copy-start(bf16[256,4096]{1,0:T(8,128)(2,1)S(1)} %collective-permute-done.3.refs_1_) | copy-start | bytes 6291460
  105.1 35.4 %collective-permute-start.4 = (bf16[256,2048]{1,0:T(8,128)(2,1)}, bf16[256,2048]{1,0:T(8,128)(2,1)}, u32[]{:S(2)}, u32[]{:S(2)}) collective-permute-start(bf16[256,2048]{1,0:T(8,128)(2,1)} %slice.26), channel_id=1, source_target_pairs={{32,0},{64,32},{96,64},{0,96},{33,1},{65,33},{97,65},{1,97},{34,2}... | collective-permute-start | bytes 3145736 | tf_op jit(solution)/shard_map/ppermute | solution.py:345
  110.6 31.1 %collective-permute-start.6 = (bf16[256,2048]{1,0:T(8,128)(2,1)}, bf16[256,2048]{1,0:T(8,128)(2,1)}, u32[]{:S(2)}, u32[]{:S(2)}) collective-permute-start(bf16[256,2048]{1,0:T(8,128)(2,1)} %slice.27), channel_id=1, source_target_pairs={{96,0},{0,32},{32,64},{64,96},{97,1},{1,33},{33,65},{65,97},{98,2}... | collective-permute-start | bytes 3145736 | tf_op jit(solution)/shard_map/ppermute | solution.py:345
  143.0 1.4 copy-start.1
  150.9 5.2 %collective-permute-start.7 = (bf16[512,2048]{1,0:T(8,128)(2,1)}, bf16[512,2048]{1,0:T(8,128)(2,1)S(1)}, u32[]{:S(2)}, u32[]{:S(2)}) collective-permute-start(bf16[512,2048]{1,0:T(8,128)(2,1)} %weight_half.2), channel_id=1, source_target_pairs={{1,0},{0,1},{3,2},{2,3},{5,4},{4,5},{7,6},{6,7},{9,8},{8,9},{11,10... | collective-permute-start | bytes 6291464 | tf_op jit(solution)/shard_map/ppermute | solution.py:345
  156.1 1.4 copy-start.7
  164.6 37.3 %all-to-all-start.5 = ((bf16[16,32,2048]{2,1,0:T(8,128)(2,1)}), bf16[16,32,2048]{2,1,0:T(8,128)(2,1)S(1)}, u32[]{:S(2)}, u32[]{:S(2)}) async-start(bf16[16,32,2048]{2,1,0:T(8,128)(2,1)} %bitcast.54), calls=%async_computation.5 | async-start | bytes 4194304 | tf_op jit(solution)/shard_map/all_to_all | solution.py:402
  168.3 5.5 %copy-start.20 = (s32[4]{0:T(128)}, s32[4]{0:T(128)S(1)}, u32[]{:S(2)}) copy-start(s32[4]{0:T(128)S(1)} %and_select_fusion.1.i_ref) | copy-start | bytes 52
  201.9 1.3 copy-start.2
  206.7 29.6 %collective-permute-start.8 = (f32[16,2048]{1,0:T(8,128)S(1)}, f32[16,2048]{1,0:T(8,128)S(1)}, u32[]{:S(2)}, u32[]{:S(2)}) collective-permute-start(f32[16,2048]{1,0:T(8,128)S(1)} %constant_dynamic-slice_fusion), channel_id=1, source_target_pairs={{1,0},{0,1},{3,2},{2,3},{5,4},{4,5},{7,6},{6,7},{9,8},{8,9},{11,10... | collective-permute-start | bytes 393224 | tf_op jit(solution)/shard_map/ppermute | solution.py:345
  212.0 3.4 %copy-start.3 = (bf16[1,256,4096]{2,1,0:T(8,128)(2,1)S(1)}, bf16[1,256,4096]{2,1,0:T(8,128)(2,1)}, u32[]{:S(2)}) copy-start(bf16[1,256,4096]{2,1,0:T(8,128)(2,1)} %param.11) | copy-start | bytes 6291460
  227.1 3.3 %copy-start.17 = (bf16[4,128,128]{2,1,0:T(8,128)(2,1)S(1)}, bf16[4,128,128]{2,1,0:T(8,128)(2,1)}, u32[]{:S(2)}) copy-start(bf16[4,128,128]{2,1,0:T(8,128)(2,1)} %get-tuple-element.31) | copy-start | bytes 393220
  227.1 3.3 %copy-start.18 = (bf16[4,128,128]{2,1,0:T(8,128)(2,1)S(1)}, bf16[4,128,128]{2,1,0:T(8,128)(2,1)}, u32[]{:S(2)}) copy-start(bf16[4,128,128]{2,1,0:T(8,128)(2,1)} %get-tuple-element.34) | copy-start | bytes 393220
  227.1 3.3 %copy-start.19 = (bf16[4,128,128]{2,1,0:T(8,128)(2,1)S(1)}, bf16[4,128,128]{2,1,0:T(8,128)(2,1)}, u32[]{:S(2)}) copy-start(bf16[4,128,128]{2,1,0:T(8,128)(2,1)} %get-tuple-element.33) | copy-start | bytes 393220
  227.1 9.2 %copy-start.9 = (f32[32,2048]{1,0:T(8,128)S(1)}, f32[32,2048]{1,0:T(8,128)}, u32[]{:S(2)}) copy-start(f32[32,2048]{1,0:T(8,128)} %sum_parts.1) | copy-start | bytes 786436
  232.2 22.3 %copy-start.10 = (bf16[256,512]{1,0:T(8,128)(2,1)S(1)}, bf16[256,512]{1,0:T(8,128)(2,1)}, u32[]{:S(2)}) copy-start(bf16[256,512]{1,0:T(8,128)(2,1)} %get-tuple-element.26) | copy-start | bytes 786436
  232.2 22.3 %copy-start.11 = (bf16[256,512]{1,0:T(8,128)(2,1)S(1)}, bf16[256,512]{1,0:T(8,128)(2,1)}, u32[]{:S(2)}) copy-start(bf16[256,512]{1,0:T(8,128)(2,1)} %get-tuple-element.29) | copy-start | bytes 786436
  232.2 22.3 %copy-start.12 = (bf16[256,512]{1,0:T(8,128)(2,1)S(1)}, bf16[256,512]{1,0:T(8,128)(2,1)}, u32[]{:S(2)}) copy-start(bf16[256,512]{1,0:T(8,128)(2,1)} %get-tuple-element.28) | copy-start | bytes 786436
  232.2 22.3 %copy-start.13 = (bf16[256,512]{1,0:T(8,128)(2,1)S(1)}, bf16[256,512]{1,0:T(8,128)(2,1)}, u32[]{:S(2)}) copy-start(bf16[256,512]{1,0:T(8,128)(2,1)} %get-tuple-element.27) | copy-start | bytes 786436
  232.2 15.6 %all-to-all-start.2 = ((bf16[32,64,128]{2,1,0:T(8,128)(2,1)}), bf16[32,64,128]{2,1,0:T(8,128)(2,1)S(1)}, u32[]{:S(2)}, u32[]{:S(2)}) async-start(bf16[32,64,128]{2,1,0:T(8,128)(2,1)} %bitcast.16), calls=%async_computation.2 | async-start | bytes 1048576 | tf_op jit(solution)/shard_map/all_to_all | solution.py:80
  247.9 0.8 copy-start.5
  250.6 26.6 %all-to-all-start.3 = ((bf16[32,64,128]{2,1,0:T(8,128)(2,1)}), bf16[32,64,128]{2,1,0:T(8,128)(2,1)S(1)}, u32[]{:S(2)}, u32[]{:S(2)}) async-start(bf16[32,64,128]{2,1,0:T(8,128)(2,1)} %scan_blocks.3), calls=%async_computation.3 | async-start | bytes 1048576 | tf_op jit(solution)/shard_map/all_to_all | solution.py:82
  277.2 0.8 copy-start.8
Sparse Core Ops, SparseCore 0:
  15.4 47.5 all-gather.7
  65.3 50.1 all-gather.5
  117.7 45.4 all-gather.3

commit v2 on v1

v2 whole, which is shorter than its diff:
```python
import functools
import math

import jax
import jax.numpy as jnp
from jax import lax
from jax.experimental import pallas as pl
from jax.experimental.pallas import tpu as pltpu
from jax.sharding import Mesh, PartitionSpec as P

HD = 128
EPSILON = 1e-06
BF = jnp.bfloat16
F32 = jnp.float32
CTX = ("z", "y", "c")
CH = 4
HC = 4


def mm(a, b, ca, cb):
    return lax.dot_general(a, b, (((ca,), (cb,)), ((), ())), preferred_element_type=F32)


def cost(flops, nbytes):
    return pl.CostEstimate(flops=flops, bytes_accessed=nbytes, transcendentals=0)


def head(ref, h):
    return ref[:, h * HD : (h + 1) * HD]


def causal(n):
    return lax.broadcasted_iota(jnp.int32, (n, n), 0) >= lax.broadcasted_iota(
        jnp.int32, (n, n), 1
    )


def state_body(k_ref, v_ref, s_ref):
    for h in range(HC):
        s_ref[h] = mm(head(k_ref, h), head(v_ref, h), 0, 0).astype(BF)


def local_state(k, v):
    t, f = k.shape
    w = f // CH
    blk = pl.BlockSpec((t, w), lambda g: (0, g))
    return pl.pallas_call(
        state_body,
        grid=(CH,),
        in_specs=[blk, blk],
        out_specs=pl.BlockSpec((HC, HD, HD), lambda g: (g, 0, 0)),
        out_shape=jax.ShapeDtypeStruct((CH * HC, HD, HD), BF),
        cost_estimate=cost(2 * t * f * HD, 4 * t * f),
        compiler_params=pltpu.CompilerParams(vmem_limit_bytes=6 << 20),
        name="local_state",
    )(k, v)


def small_call(body, where, args, outs):
    return pl.pallas_call(
        body,
        in_specs=[pl.BlockSpec(memory_space=pltpu.SMEM)]
        + [pl.BlockSpec(memory_space=pltpu.VMEM)] * len(args),
        out_specs=[pl.BlockSpec(memory_space=pltpu.VMEM)] * len(outs),
        out_shape=outs,
        compiler_params=pltpu.CompilerParams(vmem_limit_bytes=6 << 20),
        cost_estimate=cost(1 << 18, 1 << 20),
    )(where, *args)


def chip_body(w_ref, s_ref, r_ref, own_ref, *out_refs):
    y, c = w_ref[6], w_ref[7]
    n = s_ref.shape[1]
    for k in range(n):
        at = lax.rem(y + k, n)
        part = s_ref[c, at].astype(F32) + r_ref[at].astype(F32)
        if k == 0:
            own_ref[...] = part
        else:
            out_refs[k - 1][...] = part.astype(BF)


def row_body(w_ref, own_ref, *refs):
    total = own_ref[...]
    for ref in refs[:-1]:
        total = total + ref[...].astype(F32)
    refs[-1][...] = total.astype(BF)


def plane_body(reverse, w_ref, own_ref, t1, t2, t3, z1, z2, z3, o_ref, o1, o2, o3):
    z, y = w_ref[5], w_ref[6]
    terms = [own_ref[...]] + [t[...].astype(F32) for t in (t1, t2, t3)]
    n = len(terms)
    base = jnp.zeros_like(terms[0])
    for k, ref in enumerate((z1, z2, z3), 1):
        use = z < k if reverse else z >= k
        base = base + jnp.where(use, ref[...].astype(F32), 0.0)
    for k in range(n):
        to = lax.rem(y + k, n)
        total = base
        for j in range(n):
            source = lax.rem(y - j + n, n)
            use = source > to if reverse else source < to
            total = total + jnp.where(use, terms[j], 0.0)
        if k == 0:
            o_ref[...] = total
        else:
            (o1, o2, o3)[k - 1][...] = total.astype(BF)


def core_body(reverse, w_ref, s_ref, r_ref, p0, p1, p2, p3, mine_ref, give_ref):
    y, c = w_ref[6], w_ref[7]
    n = s_ref.shape[1]
    first = c == (1 if reverse else 0)
    for j, p in enumerate((p0, p1, p2, p3)):
        at = lax.rem(y - j + n, n)
        base = p[...].astype(F32)
        mine_ref[at] = (base + jnp.where(first, 0.0, r_ref[at].astype(F32))).astype(BF)
        give_ref[at] = (base + jnp.where(first, s_ref[c, at].astype(F32), 0.0)).astype(BF)


def give_to(x, axis, by):
    n = lax.axis_size(axis)
    return lax.ppermute(x, axis, [(d, (d + by) % n) for d in range(n)])


def carry(state, where, core, reverse, fill_row, fill_plane, fill_core):
    heads, d, e = state.shape
    n = lax.axis_size("y")
    rows = heads * d // (2 * n)
    parts = state.reshape(2, n, rows, e)
    give = lax.dynamic_index_in_dim(parts, 1 - core, 0, False)
    other = give_to(give, "c", 1)
    one = jax.ShapeDtypeStruct((rows, e), F32)
    low = jax.ShapeDtypeStruct((rows, e), BF)
    half = jax.ShapeDtypeStruct((n, rows, e), BF)
    own, *out = small_call(chip_body, where, [parts, other], [one] + [low] * (n - 1))
    terms = [own] + [give_to(x, "y", k) for k, x in enumerate(out, 1)]
    filled_row = fill_row(out)
    terms = after(terms, filled_row)
    (row,) = small_call(row_body, where, terms, [low])
    rows_before = [give_to(row, "z", k) for k in range(1, n)]
    filled_plane = fill_plane(row, filled_row)
    rows_before = after(rows_before, filled_plane)
    own, *out = small_call(
        functools.partial(plane_body, reverse), where, terms + rows_before, [one] + [low] * (n - 1)
    )
    sums = [own] + [give_to(x, "y", k) for k, x in enumerate(out, 1)]
    filled_core = fill_core(out, filled_plane)
    mine, give = small_call(
        functools.partial(core_body, reverse), where, [parts, other] + sums, [half] * 2
    )
    filled_core = after(filled_core, give)
    got = give_to(give, "c", 1)
    shape = (heads // 2, d, e)
    return (mine.reshape(shape), got.reshape(shape)), filled_row, filled_plane, filled_core


def after(x, *others):
    return lax.optimization_barrier((x, others))[0]


def scores_body(q_ref, k_ref, v_ref, w_ref, o_ref):
    keep = causal(q_ref.shape[0])
    for h in range(HC):
        w = jnp.where(keep, mm(head(q_ref, h), head(k_ref, h), 1, 1), 0.0).astype(BF)
        w_ref[h] = w
        o_ref[:, h * HD : (h + 1) * HD] = mm(w, head(v_ref, h), 1, 0)


def local_scores(q, k, v):
    t, f = q.shape
    w = f // CH
    blk = pl.BlockSpec((t, w), lambda g: (0, g))
    return pl.pallas_call(
        scores_body,
        grid=(CH,),
        in_specs=[blk, blk, blk],
        out_specs=[pl.BlockSpec((HC, t, t), lambda g: (g, 0, 0)), blk],
        out_shape=[
            jax.ShapeDtypeStruct((CH * HC, t, t), BF),
            jax.ShapeDtypeStruct((t, f), F32),
        ],
        cost_estimate=cost(4 * t * t * f, 14 * t * f),
        compiler_params=pltpu.CompilerParams(vmem_limit_bytes=12 << 20),
        name="local_scores",
    )(q, k, v)


def pick(w_ref, chunk, m_ref, t_ref, h):
    return jnp.where(lax.div(chunk, CH // 2) == w_ref[7], m_ref[h], t_ref[h])


def attend_body(w_ref, q_ref, o_ref, m_ref, t_ref, g_ref, *refs):
    n_refs, a_ref = refs[:-1], refs[-1]
    g = pl.program_id(0)
    for h in range(HC):
        cols = slice(h * HD, (h + 1) * HD)
        state = pick(w_ref, w_ref[g], m_ref, t_ref, h)
        a = o_ref[:, cols] + mm(head(q_ref, h), state, 1, 0)
        a_ref[0, :, cols] = a
        inv = lax.rsqrt(jnp.mean(a * a, axis=-1, keepdims=True) + EPSILON)
        normed = (a * inv * g_ref[:, cols]).astype(BF)
        for k in range(CH):

            @pl.when(g == k)
            def _(k=k, normed=normed, cols=cols):
                n_refs[k][:, cols] = normed


def attend(where, q, out, carried, gain):
    t, f = q.shape
    w = f // CH
    blk = pl.BlockSpec((t, w), lambda g, i: (0, i[g]))
    st = pl.BlockSpec((HC, HD, HD), lambda g, i: (lax.rem(i[g], CH // 2), 0, 0))
    return pl.pallas_call(
        attend_body,
        grid_spec=pltpu.PrefetchScalarGridSpec(
            num_scalar_prefetch=1,
            grid=(CH,),
            in_specs=[blk, blk, st, st, pl.BlockSpec((1, w), lambda g, i: (0, i[g]))],
            out_specs=[pl.BlockSpec((t, w), lambda g, i: (0, 0))] * CH
            + [pl.BlockSpec((1, t, w), lambda g, i: (g, 0, 0))],
        ),
        out_shape=[jax.ShapeDtypeStruct((t, w), BF)] * CH
        + [jax.ShapeDtypeStruct((CH, t, w), F32)],
        cost_estimate=cost(2 * t * f * HD, 12 * t * f),
        compiler_params=pltpu.CompilerParams(vmem_limit_bytes=12 << 20),
        name="attend",
    )(where, q, out, *carried, gain)


def grad_attn_body(i_ref, q_ref, a_ref, gn_ref, g_ref, go_ref, w_ref, ga_ref, lg_ref):
    rows = w_ref.shape[0] * w_ref.shape[2]

    def finish(gn):
        for h in range(HC):
            cols = slice(h * HD, (h + 1) * HD)
            a = a_ref[0, :, cols]
            inv = lax.rsqrt(jnp.mean(a * a, axis=-1, keepdims=True) + EPSILON)
            unit = a * inv
            gu = gn[:, cols] * g_ref[:, cols]
            ga = inv * (gu - unit * jnp.mean(gu * unit, axis=-1, keepdims=True))
            ga = ga.astype(BF)
            ga_ref[0, :, cols] = ga
            lg_ref[h] = mm(head(q_ref, h), ga, 0, 0).astype(BF)

    @pl.when(pl.program_id(0) == 0)
    def _():
        finish(gn_ref[...])

    @pl.when(pl.program_id(0) > 0)
    def _():
        finish(mm(go_ref[...], w_ref[:, 0].reshape(rows, w_ref.shape[3]), 1, 1))


def grad_attn(order, q, attended, gn, gain, grad_rows, gathered):
    t, f = q.shape
    w = f // CH
    n, _, r, d = gathered.shape
    return pl.pallas_call(
        grad_attn_body,
        grid_spec=pltpu.PrefetchScalarGridSpec(
            num_scalar_prefetch=1,
            grid=(CH,),
            in_specs=[
                pl.BlockSpec((t, w), lambda g, i: (0, i[g])),
                pl.BlockSpec((1, t, w), lambda g, i: (g, 0, 0)),
                pl.BlockSpec((t, w), lambda g, i: (0, 0)),
                pl.BlockSpec((1, w), lambda g, i: (0, i[g])),
                pl.BlockSpec((t, d), lambda g, i: (0, 0)),
                pl.BlockSpec((n, 1, r, d), lambda g, i: (0, jnp.maximum(g - 1, 0), 0, 0)),
            ],
            out_specs=[
                pl.BlockSpec((1, t, w), lambda g, i: (g, 0, 0)),
                pl.BlockSpec((HC, HD, HD), lambda g, i: (g, 0, 0)),
            ],
        ),
        out_shape=[
            jax.ShapeDtypeStruct((CH, t, w), BF),
            jax.ShapeDtypeStruct((CH * HC, HD, HD), BF),
        ],
        cost_estimate=cost(2 * t * f * HD + 6 * t * w * d, 12 * t * f + 6 * w * d),
        compiler_params=pltpu.CompilerParams(vmem_limit_bytes=20 << 20),
        name="grad_attn",
    )(order, q, attended, gn, gain, grad_rows, gathered)


def grads_body(i_ref, q_ref, k_ref, v_ref, w_ref, ga_ref, m_ref, t_ref, gq_ref, gk_ref, gv_ref):
    chunk = i_ref[pl.program_id(0)]
    keep = causal(q_ref.shape[0])
    for h in range(HC):
        cols = slice(h * HD, (h + 1) * HD)
        ga = ga_ref[0, :, cols]
        gs = jnp.where(keep, mm(ga, head(v_ref, h), 1, 1), 0.0).astype(BF)
        gq = mm(gs, head(k_ref, h), 1, 0) + mm(ga, pick(i_ref, chunk, m_ref, t_ref, h), 1, 1)
        gq_ref[:, cols] = gq.astype(BF)
        gk_ref[0, :, cols] = mm(gs, head(q_ref, h), 0, 0)
        gv_ref[0, :, cols] = mm(w_ref[h], ga, 0, 0)


def local_grads(order, q, k, v, weights, ga, carried):
    t, f = q.shape
    w = f // CH
    nat = pl.BlockSpec((t, w), lambda g, i: (0, i[g]))
    chunk = pl.BlockSpec((1, t, w), lambda g, i: (g, 0, 0))
    return pl.pallas_call(
        grads_body,
        grid_spec=pltpu.PrefetchScalarGridSpec(
            num_scalar_prefetch=1,
            grid=(CH,),
            in_specs=[
                nat,
                nat,
                nat,
                pl.BlockSpec((HC, t, t), lambda g, i: (i[g], 0, 0)),
                chunk,
            ]
            + [pl.BlockSpec((HC, HD, HD), lambda g, i: (lax.rem(i[g], CH // 2), 0, 0))] * 2,
            out_specs=[nat, chunk, chunk],
        ),
        out_shape=[
            jax.ShapeDtypeStruct((t, f), BF),
            jax.ShapeDtypeStruct((CH, t, w), F32),
            jax.ShapeDtypeStruct((CH, t, w), F32),
        ],
        cost_estimate=cost(8 * t * t * f, 24 * t * f),
        compiler_params=pltpu.CompilerParams(vmem_limit_bytes=20 << 20),
        name="local_grads",
    )(order, q, k, v, weights, ga, *carried)


def later_body(i_ref, k_ref, v_ref, m_ref, t_ref, pk_ref, pv_ref, gk_ref, gv_ref):
    for h in range(HC):
        cols = slice(h * HD, (h + 1) * HD)
        state = pick(i_ref, pl.program_id(0), m_ref, t_ref, h)
        gk = pk_ref[0, :, cols] + mm(head(v_ref, h), state, 1, 1)
        gv = pv_ref[0, :, cols] + mm(head(k_ref, h), state, 1, 0)
        gk_ref[:, cols] = gk.astype(BF)
        gv_ref[:, cols] = gv.astype(BF)


def later_grads(order, k, v, later, pk, pv):
    t, f = k.shape
    w = f // CH
    nat = pl.BlockSpec((t, w), lambda g, i: (0, i[g]))
    chunk = pl.BlockSpec((1, t, w), lambda g, i: (g, 0, 0))
    return pl.pallas_call(
        later_body,
        grid_spec=pltpu.PrefetchScalarGridSpec(
            num_scalar_prefetch=1,
            grid=(CH,),
            in_specs=[
                nat,
                nat,
                pl.BlockSpec((HC, HD, HD), lambda g, i: (lax.rem(g, CH // 2), 0, 0)),
                pl.BlockSpec((HC, HD, HD), lambda g, i: (lax.rem(g, CH // 2), 0, 0)),
                chunk,
                chunk,
            ],
            out_specs=[nat, nat],
        ),
        out_shape=[jax.ShapeDtypeStruct((t, f), BF)] * 2,
        cost_estimate=cost(4 * t * f * HD, 16 * t * f),
        compiler_params=pltpu.CompilerParams(vmem_limit_bytes=12 << 20),
        name="later_grads",
    )(order, k, v, *later, pk, pv)


def layer_body(n0, n1, n2, n3, own_ref, w_ref, o_ref):
    normed = (n0, n1, n2, n3)
    total = mm(n0[...], own_ref[...], 1, 0)
    for k in range(1, CH):
        block = w_ref[:, k - 1].reshape(own_ref.shape)
        total = total + mm(normed[k][...], block, 1, 0)
    o_ref[...] = total.astype(BF)


def layer_rows(normed, own, gathered):
    t, w = normed[0].shape
    n, c, r, d = gathered.shape
    tile = 1024
    return pl.pallas_call(
        layer_body,
        grid=(d // tile,),
        in_specs=[pl.BlockSpec((t, w), lambda g: (0, 0))] * CH
        + [
            pl.BlockSpec((w, tile), lambda g: (0, g)),
            pl.BlockSpec((n, c, r, tile), lambda g: (0, 0, 0, g)),
        ],
        out_specs=pl.BlockSpec((t, tile), lambda g: (0, g)),
        out_shape=jax.ShapeDtypeStruct((t, d), BF),
        cost_estimate=cost(2 * t * CH * w * d, 2 * (CH * w * d + CH * t * w + t * d)),
        compiler_params=pltpu.CompilerParams(vmem_limit_bytes=20 << 20),
        name="layer_rows",
    )(*normed, own, gathered)


def weight_total(nt, g0_ref, g1_ref, fa_ref, fb_ref, g3_ref):
    total = mm(nt[0], g0_ref[...], 1, 0) + mm(nt[1], g1_ref[...], 1, 0)
    total = total + mm(nt[2], jnp.concatenate([fa_ref[...], fb_ref[...]], axis=0), 1, 0)
    return total + mm(nt[3], g3_ref[...], 1, 0)


def give_body(i_ref, n0, n1, n2, n3, *rest):
    *grads, o_ref, nt_ref = rest

    @pl.when(pl.program_id(0) == 0)
    def _():
        for s, n in enumerate((n0, n1, n2, n3)):
            nt_ref[s] = n[...].T

    o_ref[...] = weight_total(nt_ref, *grads).astype(BF)


def keep_body(i_ref, nt_ref, extra_ref, *rest):
    *grads, o_ref = rest
    o_ref[...] = (weight_total(nt_ref, *grads) + extra_ref[...].astype(F32)).astype(BF)


def weight_half(body, half, rows, grads_all, nt_out):
    t, d = grads_all[0].shape
    w = rows[0].shape[1]
    tile = 512
    steps = d // 2 // tile
    own = pl.BlockSpec((w, tile), lambda g, i: (0, g))
    whole = pl.BlockSpec((t, w), lambda g, i: (0, 0))
    turned = pl.BlockSpec((CH, w, t), lambda g, i: (0, 0, 0))
    out = jax.ShapeDtypeStruct((w, d // 2), BF)
    return pl.pallas_call(
        body,
        grid_spec=pltpu.PrefetchScalarGridSpec(
            num_scalar_prefetch=1,
            grid=(steps,),
            in_specs=([whole] * CH if nt_out else [turned, own])
            + [
                pl.BlockSpec((x.shape[0], tile), lambda g, i: (0, i[0] * steps + g))
                for x in grads_all
            ],
            out_specs=[own, turned] if nt_out else own,
        ),
        out_shape=[out, jax.ShapeDtypeStruct((CH, w, t), BF)] if nt_out else out,
        cost_estimate=cost(CH * t * w * d, CH * t * d + 2 * CH * t * w + w * d),
        compiler_params=pltpu.CompilerParams(vmem_limit_bytes=14 << 20),
        name="weight_half",
    )(half, *rows, *grads_all)


def sum_body(scale, s_ref, o_ref):
    total = s_ref[0].astype(F32)
    for step in range(1, s_ref.shape[0]):
        total = total + s_ref[step].astype(F32)
    o_ref[...] = total * scale


def sum_parts(parts, scale):
    _, r, w = parts.shape
    return pl.pallas_call(
        functools.partial(sum_body, scale),
        out_shape=jax.ShapeDtypeStruct((r, w), F32),
        cost_estimate=cost(parts.size, 2 * parts.size),
        compiler_params=pltpu.CompilerParams(vmem_limit_bytes=6 << 20),
        name="sum_parts",
    )(parts)


def shift(x, axis, by):
    n = lax.axis_size(axis)
    return lax.ppermute(x, axis, [((d + by) % n, d) for d in range(n)])


def layer(queries, keys, values, gain, out_weight, grad_out):
    tok_rows, feat_width = queries.shape[1:]
    model_width = grad_out.shape[2]
    q = queries.reshape(tok_rows, feat_width)
    k = keys.reshape(tok_rows, feat_width)
    v = values.reshape(tok_rows, feat_width)
    grad_rows = grad_out.reshape(tok_rows, model_width)
    gain_row = gain.reshape(1, feat_width)
    seqs = lax.axis_size("x")
    blocks_n = lax.axis_size(CTX)
    at_x = lax.axis_index("x")
    at_ctx = lax.axis_index(CTX)
    at_core = lax.axis_index("c")
    places = [at_x, lax.axis_index("z"), lax.axis_index("y"), at_core]
    order = [(at_x + n) % CH for n in range(CH)]
    where = jnp.stack(order + places).astype(jnp.int32)
    mine = at_core.reshape(1).astype(jnp.int32)
    others = 1 - mine

    piece = out_weight.shape[0] // blocks_n
    own_piece = lax.dynamic_slice_in_dim(out_weight, at_ctx * piece, piece, 0)
    pieces = [shift(own_piece, "x", by) for by in range(1, CH)]
    state = local_state(k, v)
    pieces, sent_rows, q_next = lax.optimization_barrier((pieces, grad_rows, q, state))[:3]
    gathered = lax.all_gather(jnp.concatenate(pieces, axis=0), CTX, axis=0, tiled=True)
    gathered = gathered.reshape(blocks_n, CH - 1, piece, model_width)
    gathered = pltpu.with_memory_space_constraint(gathered, pltpu.HBM)
    own_weight = pltpu.with_memory_space_constraint(out_weight, pltpu.HBM)

    right = shift(sent_rows, "x", 1)
    left = shift(sent_rows, "x", 3)
    half_rows = tok_rows // 2
    carried, (weights, local_out), gn, _ = carry(
        state,
        where,
        at_core,
        False,
        lambda sent: local_scores(after(q_next, sent), k, v),
        lambda sent, done: mm(after(sent_rows, sent, done), out_weight, 1, 1),
        lambda sent, done: (),
    )
    *normed, attended = attend(where, q, local_out, carried, gain_row)

    normed_all = [normed[0]] + [give_to(normed[n], "x", n) for n in range(1, CH)]
    right, left, attended = lax.optimization_barrier((right, left, attended))
    far_a = shift(right[:half_rows], "x", 1)
    far_b = shift(left[half_rows:], "x", 3)

    ga, lg = grad_attn(where, q, attended, gn, gain_row, grad_rows, gathered)
    half_cols = model_width // 2
    grads_all = [grad_rows, left, far_a, far_b, right]

    def first_half(sent, done):
        rows = after(normed_all, sent, done)
        return weight_half(give_body, others, rows, grads_all, True)

    def second_half(sent, done):
        for_partner, turned = done
        extra = give_to(for_partner, "c", 1)
        return weight_half(keep_body, mine, [after(turned, sent), extra], grads_all, False)

    later, (grad_query, pk, pv), _, partial = carry(
        lg,
        where,
        at_core,
        True,
        lambda sent: local_grads(where, q, k, v, weights, after(ga, sent), carried),
        first_half,
        second_half,
    )
    layer_out = layer_rows(after(normed, partial, later), own_weight, gathered)
    grad_key, grad_value = later_grads(where, k, v, later, pk, pv)

    chips = blocks_n // 2
    rows = partial.shape[0] // chips
    parts = lax.all_to_all(
        partial.reshape(chips, rows, half_cols), ("z", "y"), 0, 0, tiled=True
    )
    token_count = seqs * blocks_n * tok_rows
    parts = after(parts, layer_out, grad_key)
    summed = sum_parts(parts, 1.0 / math.sqrt(token_count))
    out_rows = rows // 2
    keep = lax.dynamic_slice_in_dim(summed, at_core * out_rows, out_rows, 0)
    give = lax.dynamic_slice_in_dim(summed, (1 - at_core) * out_rows, out_rows, 0)
    got = shift(give, "c", 1)
    first = at_core == 0
    grad_weight = jnp.concatenate(
        [jnp.where(first, keep, got), jnp.where(first, got, keep)], axis=1
    )
    out_shape = (1, tok_rows, feat_width)
    return (
        layer_out.reshape(1, tok_rows, model_width),
        grad_query.reshape(out_shape),
        grad_key.reshape(out_shape),
        grad_value.reshape(out_shape),
        grad_weight,
    )


def solution(mesh):
    mesh = Mesh(mesh.devices.reshape(4, 4, 4, 2), ("x",) + CTX)
    tokens = P("x", CTX, None)
    in_specs = (tokens, tokens, tokens, P(), P("x", None), tokens)
    out_specs = (tokens, tokens, tokens, tokens, P(("x",) + CTX, None))
    return jax.shard_map(layer, mesh=mesh, in_specs=in_specs, out_specs=out_specs, check_vma=False)
```

time: 293 us -> 201 us (0.69)
  waiting for transfers between devices: 115 us -> 46.6 us
  Pallas kernels: 74.6 us -> 55.7 us
  matrix products: 18.4 us -> 4.27 us
  local copies, waits for them, and re-layouts: 18.2 us -> 27 us
  starting transfers between devices: 45.1 us -> 49.6 us
  other arithmetic: 4.8 us -> 1.53 us
    ppermute x9 -> x8, waiting for transfers between devices: 63.6 us -> 1.39 us  [shift(): return lax.ppermute(x, axis, [((d + by) % n, d) for d in range(n)])]
    all_to_all x6 -> x1, waiting for transfers between devices: 51.6 us -> 12.2 us  [layer(): lax.all_to_all(partial.reshape(chips, rows, half_cols), ('z', 'y'), 0, 0,...]
    ppermute x0 -> x26, starting transfers between devices: none -> 33.7 us  [give_to(): return lax.ppermute(x, axis, [(d, (d + by) % n) for d in range(n)])]
    all_to_all x6 -> x1, starting transfers between devices: 32.6 us -> 4.58 us  [layer(): lax.all_to_all(partial.reshape(chips, rows, half_cols), ('z', 'y'), 0, 0,...]
    ppermute x0 -> x26, waiting for transfers between devices: none -> 25.1 us  [give_to(): return lax.ppermute(x, axis, [(d, (d + by) % n) for d in range(n)])]
    dot_general x4 -> x1, matrix products: 18.4 us -> 4.27 us  [mm(): lax.dot_general(a, b, (((ca,), (cb,)), ((), ())), preferred_element_type=...]
    unnamed x43 -> x82, local copies, waits for them, and re-layouts: 10.5 us -> 19.3 us
    all_gather x3 -> x1, waiting for transfers between devices: 0.02 us -> 7.94 us  [layer(): lax.all_gather(jnp.concatenate(pieces, axis=0), CTX, axis=0, tiled=True)]
  transfers between devices with their start and end apart: 18 -> 36, of which waited for: 9 -> 20; matrix products, arithmetic and copies ran while one was open for 11% -> 5% of each run, Pallas kernels for 23% -> 22%
where the time goes in v2:
time: 201 us; the launch traced here: 199 us
  Pallas kernels  55.7 us (28%)
  starting transfers between devices  49.6 us (25%)
  waiting for transfers between devices  46.6 us (23%)
  local copies, waits for them, and re-layouts  27 us (13%)
  between operations  14.5 us (7%)
  matrix products  4.27 us (2%)
    ppermute x26, starting transfers between devices, give_to(): return lax.ppermute(x, axis, [(d, (d + by) % n) for d in range(n)])  33.7 us
    ppermute x26, waiting for transfers between devices, give_to(): return lax.ppermute(x, axis, [(d, (d + by) % n) for d in range(n)])  25.1 us
    unnamed x82, local copies, waits for them, and re-layouts  19.3 us
    all_to_all x1, waiting for transfers between devices, layer(): lax.all_to_all(partial.reshape(chips, rows, half_cols), ('z', 'y'), 0, 0,...  12.2 us
    ppermute x8, starting transfers between devices, shift(): return lax.ppermute(x, axis, [((d + by) % n, d) for d in range(n)])  11.3 us
    pallas_call x2, Pallas kernels, weight_half(): pl.pallas_call(body, grid_spec=pltpu.PrefetchScalarGridSpec(num_scalar_pr...  9.98 us
    pallas_call x1, Pallas kernels, layer_rows(): pl.pallas_call(layer_body, grid=(d // tile,), in_specs=[pl.BlockSpec((t,...  9.55 us
    pallas_call x1, Pallas kernels, grad_attn(): pl.pallas_call(grad_attn_body, grid_spec=pltpu.PrefetchScalarGridSpec(num...  9.51 us
  transfers between devices with their start and end apart: 36, of which 20 were waited for; matrix products, arithmetic and copies ran while one was open for 5% of the time, Pallas kernels for 22%

profile of v2, /device:TPU:0, one launch (start us, length us, event | category | flops | bytes accessed | tf_op | source)
XLA Modules:
  0.0 199.2 jit_solution(3700896835607750998)
XLA Ops:
  8.3 1.7 collective-permute-start.2
  10.0 2.7 %collective-permute-start.1 = (bf16[16,4096]{1,0:T(8,128)(2,1)S(1)}, bf16[16,4096]{1,0:T(8,128)(2,1)S(1)}, u32[]{:S(2)}, u32[]{:S(2)}) collective-permute-start(bf16[16,4096]{1,0:T(8,128)(2,1)S(1)} %constant_dynamic-slice_fusion.1), channel_id=1, source_target_pairs={{64,0},{96,32},{0,64},{32,96},{65,1},{97,33},{1,65},{33,97},{66,2}... | collective-permute-start | bytes 393224 | tf_op jit(solution)/shard_map/ppermute | solution.py:469
  12.7 1.4 collective-permute-start
  20.8 2.0 %collective-permute-start.17 = (bf16[256,4096]{1,0:T(8,128)(2,1)S(1)}, bf16[256,4096]{1,0:T(8,128)(2,1)}, u32[]{:S(2)}, u32[]{:S(2)}) collective-permute-start(bf16[256,4096]{1,0:T(8,128)(2,1)S(1)} %bitcast.32), channel_id=1, source_target_pairs={{32,0},{64,32},{96,64},{0,96},{33,1},{65,33},{97,65},{1,97},{34,2}... | collective-permute-start | bytes 6291464 | tf_op jit(solution)/shard_map/ppermute | solution.py:469
  22.8 1.7 dynamic-slice_bitcast_fusion.1
  24.6 1.7 collective-permute-done.3.r_ref
  27.9 1.6 collective-permute-start.4
  29.6 2.9 %collective-permute-start.5 = (bf16[256,128]{1,0:T(8,128)(2,1)S(1)}, bf16[256,128]{1,0:T(8,128)(2,1)S(1)}, u32[]{:S(2)}, u32[]{:S(2)}) collective-permute-start(bf16[256,128]{1,0:T(8,128)(2,1)S(1)} %get-tuple-element.79), channel_id=1, source_target_pairs={{0,4},{2,6},{4,0},{6,2},{1,5},{3,7},{5,1},{7,3},{8,12},{10,14},{12... | collective-permute-start | bytes 196616 | tf_op jit(solution)/shard_map/ppermute | solution.py:124
  32.5 1.3 collective-permute-start.6
  36.3 3.0 %local_scores.1 = (bf16[16,256,256]{2,1,0:T(8,128)(2,1)S(1)}, f32[256,2048]{1,0:T(8,128)S(1)}) custom-call(bf16[256,2048]{1,0:T(8,128)(2,1)S(1)} %bitcast.37, bf16[256,2048]{1,0:T(8,128)(2,1)S(1)} %bitcast.42, bf16[256,2048]{1,0:T(8,128)(2,1)S(1)} %bitcast.46), custom_call_target="tpu_custom_call" | custom-call | flops 536870912 | bytes 7340032 | tf_op jit(solution)/shard_map/local_scores/pallas_call | solution.py:175
  39.3 1.3 copy-done.16
  41.2 4.1 %collective-permute-start.9 = (bf16[256,128]{1,0:T(8,128)(2,1)S(1)}, bf16[256,128]{1,0:T(8,128)(2,1)S(1)}, u32[]{:S(2)}, u32[]{:S(2)}) collective-permute-start(bf16[256,128]{1,0:T(8,128)(2,1)S(1)} %shard_map.102), channel_id=1, source_target_pairs={{0,24},{8,0},{16,8},{24,16},{1,25},{9,1},{17,9},{25,17},{2,26},{10... | collective-permute-start | bytes 196616 | tf_op jit(solution)/shard_map/ppermute | solution.py:124
  46.6 4.3 %fusion.gn_ref = f32[256,512]{1,0:T(8,128)} fusion(bf16[256,4096]{1,0:T(8,128)(2,1)S(1)} %bitcast.33, bf16[512,4096]{1,0:T(8,128)(2,1)} %own_ref.1), kind=kOutput, calls=%fused_computation.8 | convolution fusion | flops 1073741824 | bytes 6815744 | tf_op jit(solution)/shard_map/dot_general | solution.py:21
  53.9 2.0 %collective-permute-start.12 = (bf16[256,128]{1,0:T(8,128)(2,1)S(1)}, bf16[256,128]{1,0:T(8,128)(2,1)S(1)}, u32[]{:S(2)}, u32[]{:S(2)}) collective-permute-start(bf16[256,128]{1,0:T(8,128)(2,1)S(1)} %get-tuple-element.97), channel_id=1, source_target_pairs={{0,6},{2,0},{4,2},{6,4},{1,7},{3,1},{5,3},{7,5},{8,14},{10,8},{12,... | collective-permute-start | bytes 196616 | tf_op jit(solution)/shard_map/ppermute | solution.py:124
  55.9 1.9 collective-permute-done.10.p1
  58.7 3.3 %collective-permute-done.12.p3 = bf16[256,128]{1,0:T(8,128)(2,1)S(1)} collective-permute-done((bf16[256,128]{1,0:T(8,128)(2,1)S(1)}, bf16[256,128]{1,0:T(8,128)(2,1)S(1)}, u32[]{:S(2)}, u32[]{:S(2)}) %collective-permute-start.12) | collective-permute-done | bytes 65568 | tf_op jit(solution)/shard_map/ppermute | solution.py:124
  62.8 1.9 collective-permute-done.13
  64.7 5.3 %attend.1 = (bf16[256,512]{1,0:T(8,128)(2,1)S(1)}, bf16[256,512]{1,0:T(8,128)(2,1)S(1)}, bf16[256,512]{1,0:T(8,128)(2,1)S(1)}, bf16[256,512]{1,0:T(8,128)(2,1)S(1)}, f32[4,256,512]{2,1,0:T(8,128)S(1)}) custom-call(s32[8]{0:T(128)S(1)} %stack.35.w_ref.i_ref, bf16[256,2048]{1,0:T(8,128)(2,1)S(1)} %bitcast.38, f32[256,2048]{1,0:T(8,128)S(1)} %get-tuple-element.82.o_ref, ...), custom_call_target="tpu_custom_call" | custom-call | flops 134217728 | bytes 6291456 | tf_op jit(solution)/shard_map/attend/pallas_call | solution.py:216
  71.4 2.6 %slice.7 = bf16[128,4096]{1,0:T(8,128)(2,1)} slice(bf16[256,4096]{1,0:T(8,128)(2,1)} %collective-permute-done.18.rest_1_), slice={[128:256], [0:4096]} | slice | bytes 2097152 | tf_op jit(solution)/shard_map/slice | solution.py:518
  73.9 2.3 %slice.6 = bf16[128,4096]{1,0:T(8,128)(2,1)} slice(bf16[256,4096]{1,0:T(8,128)(2,1)} %collective-permute-done.17.rest_4_), slice={[0:128], [0:4096]} | slice | bytes 2097152 | tf_op jit(solution)/shard_map/slice | solution.py:517
  76.3 2.0 %collective-permute-start.24 = (bf16[128,4096]{1,0:T(8,128)(2,1)}, bf16[128,4096]{1,0:T(8,128)(2,1)}, u32[]{:S(2)}, u32[]{:S(2)}) collective-permute-start(bf16[128,4096]{1,0:T(8,128)(2,1)} %slice.7), channel_id=1, source_target_pairs={{96,0},{0,32},{32,64},{64,96},{97,1},{1,33},{33,65},{65,97},{98,2}... | collective-permute-start | bytes 3145736 | tf_op jit(solution)/shard_map/ppermute | solution.py:469
  78.3 7.9 %all-gather.2.cloned.1.call-done = bf16[1536,4096]{1,0:T(8,128)(2,1)} async-done(((bf16[48,4096]{1,0:T(8,128)(2,1)}), bf16[1536,4096]{1,0:T(8,128)(2,1)}) %all-gather.2.cloned.1.call-update) | async-done | bytes 12582928 | tf_op jit(solution)/shard_map/all_gather | solution.py:496
  86.3 1.6 copy-done.15
  89.0 9.5 %grad_attn.1 = (bf16[4,256,512]{2,1,0:T(8,128)(2,1)S(1)}, bf16[16,128,128]{2,1,0:T(8,128)(2,1)S(1)}) custom-call(s32[8]{0:T(128)S(1)} %stack.35.w_ref.i_ref, bf16[256,2048]{1,0:T(8,128)(2,1)S(1)} %bitcast.39, f32[4,256,512]{2,1,0:T(8,128)S(1)} %copy-done.15, f32[256,512]{1,0:T(8,128)S(1)} %copy-done.26, f32[1,2048]{1,0:T(1,128)S(1)} %bitcast.63, ...), custom_call_target="tpu_custom_call" | custom-call | flops 3355443200 | bytes 18874368 | tf_op jit(solution)/shard_map/grad_attn/pallas_call | solution.py:261
  100.7 1.6 collective-permute-start.20
  102.3 2.7 %collective-permute-start.21 = (bf16[256,128]{1,0:T(8,128)(2,1)S(1)}, bf16[256,128]{1,0:T(8,128)(2,1)S(1)}, u32[]{:S(2)}, u32[]{:S(2)}) collective-permute-start(bf16[256,128]{1,0:T(8,128)(2,1)S(1)} %get-tuple-element.112), channel_id=1, source_target_pairs={{0,4},{2,6},{4,0},{6,2},{1,5},{3,7},{5,1},{7,3},{8,12},{10,14},{12... | collective-permute-start | bytes 196616 | tf_op jit(solution)/shard_map/ppermute | solution.py:124
  105.0 1.4 collective-permute-start.22
  106.5 1.5 collective-permute-start.14
  108.6 3.0 %collective-permute-start.15 = (bf16[256,512]{1,0:T(8,128)(2,1)S(1)}, bf16[256,512]{1,0:T(8,128)(2,1)S(1)}, u32[]{:S(2)}, u32[]{:S(2)}) collective-permute-start(bf16[256,512]{1,0:T(8,128)(2,1)S(1)} %copy-done.31), channel_id=1, source_target_pairs={{0,64},{32,96},{64,0},{96,32},{1,65},{33,97},{65,1},{97,33},{2,66}... | collective-permute-start | bytes 786440 | tf_op jit(solution)/shard_map/ppermute | solution.py:124
  112.8 6.8 %local_grads.1 = (bf16[256,2048]{1,0:T(8,128)(2,1)}, f32[4,256,512]{2,1,0:T(8,128)S(1)}, f32[4,256,512]{2,1,0:T(8,128)S(1)}) custom-call(s32[8]{0:T(128)S(1)} %stack.35.w_ref.i_ref, bf16[256,2048]{1,0:T(8,128)(2,1)S(1)} %bitcast.40, bf16[256,2048]{1,0:T(8,128)(2,1)S(1)} %bitcast.43, bf16[256,2048]{1,0:T(8,128)(2,1)S(1)} %bitcast.47, ...), custom_call_target="tpu_custom_call" | custom-call | flops 1073741824 | bytes 12582912 | tf_op jit(solution)/shard_map/local_grads/pallas_call | solution.py:307
  119.6 1.3 copy-done.18
  123.1 5.1 %weight_half.2 = (bf16[512,2048]{1,0:T(8,128)(2,1)S(1)}, bf16[4,512,256]{2,1,0:T(8,128)(2,1)S(1)}) custom-call(s32[1]{0:T(128)S(6)} %sub.9.i_ref, bf16[256,512]{1,0:T(8,128)(2,1)S(1)} %get-tuple-element.142.n0, bf16[256,512]{1,0:T(8,128)(2,1)S(1)} %collective-permute-done.14.n1, bf16[256,512]{1,0:T(8,128)(2,1)S(1)} %collective-permute-done.15.n2, ...), custom_call_target="tpu_custom_call" | custom-call | flops 2147483648 | bytes 7340032 | tf_op jit(solution)/shard_map/weight_half/pallas_call | solution.py:430
  128.3 2.6 %collective-permute-start.27 = (bf16[256,128]{1,0:T(8,128)(2,1)S(1)}, bf16[256,128]{1,0:T(8,128)(2,1)S(1)}, u32[]{:S(2)}, u32[]{:S(2)}) collective-permute-start(bf16[256,128]{1,0:T(8,128)(2,1)S(1)} %shard_map.106), channel_id=1, source_target_pairs={{0,24},{8,0},{16,8},{24,16},{1,25},{9,1},{17,9},{25,17},{2,26},{10... | collective-permute-start | bytes 196616 | tf_op jit(solution)/shard_map/ppermute | solution.py:124
  131.9 2.4 %collective-permute-done.27.z3 = bf16[256,128]{1,0:T(8,128)(2,1)S(1)} collective-permute-done((bf16[256,128]{1,0:T(8,128)(2,1)S(1)}, bf16[256,128]{1,0:T(8,128)(2,1)S(1)}, u32[]{:S(2)}, u32[]{:S(2)}) %collective-permute-start.27) | collective-permute-done | bytes 65568 | tf_op jit(solution)/shard_map/ppermute | solution.py:124
  134.4 3.0 %collective-permute-done.26.z2 = bf16[256,128]{1,0:T(8,128)(2,1)S(1)} collective-permute-done((bf16[256,128]{1,0:T(8,128)(2,1)S(1)}, bf16[256,128]{1,0:T(8,128)(2,1)S(1)}, u32[]{:S(2)}, u32[]{:S(2)}) %collective-permute-start.26) | collective-permute-done | bytes 65568 | tf_op jit(solution)/shard_map/ppermute | solution.py:124
  138.5 2.6 %collective-permute-start.30 = (bf16[256,128]{1,0:T(8,128)(2,1)S(1)}, bf16[256,128]{1,0:T(8,128)(2,1)S(1)}, u32[]{:S(2)}, u32[]{:S(2)}) collective-permute-start(bf16[256,128]{1,0:T(8,128)(2,1)S(1)} %get-tuple-element.135), channel_id=1, source_target_pairs={{0,4},{2,6},{4,0},{6,2},{1,5},{3,7},{5,1},{7,3},{8,12},{10,14},{12... | collective-permute-start | bytes 196616 | tf_op jit(solution)/shard_map/ppermute | solution.py:124
  141.8 3.1 %collective-permute-done.29.p1 = bf16[256,128]{1,0:T(8,128)(2,1)S(1)} collective-permute-done((bf16[256,128]{1,0:T(8,128)(2,1)S(1)}, bf16[256,128]{1,0:T(8,128)(2,1)S(1)}, u32[]{:S(2)}, u32[]{:S(2)}) %collective-permute-start.29) | collective-permute-done | bytes 65568 | tf_op jit(solution)/shard_map/ppermute | solution.py:124
  147.7 4.9 %weight_half.3 = bf16[512,2048]{1,0:T(8,128)(2,1)S(1)} custom-call(s32[1]{0:T(128)} %bitcast.7.i_ref, bf16[4,512,256]{2,1,0:T(8,128)(2,1)S(1)} %get-tuple-element.137.nt_ref, bf16[512,2048]{1,0:T(8,128)(2,1)S(1)} %collective-permute-done.28.extra_ref, bf16[256,4096]{1,0:T(8,128)(2,1)S(1)} %bitcast.36, bf16[256,4096]{1,0:T(8,128)(2,1)} %collective-permute-done.18.rest_1_, ...), custom_call_target="tpu_custom_call" | custom-call | flops 2147483648 | bytes 7340032 | tf_op jit(solution)/shard_map/weight_half/pallas_call | solution.py:430
  152.6 1.3 copy-done.10
  153.9 4.6 %all-to-all-start = ((bf16[16,32,2048]{2,1,0:T(8,128)(2,1)}), bf16[16,32,2048]{2,1,0:T(8,128)(2,1)}, u32[]{:S(2)}, u32[]{:S(2)}) async-start(bf16[16,32,2048]{2,1,0:T(8,128)(2,1)} %bitcast.49), calls=%async_computation | async-start | bytes 4194304 | tf_op jit(solution)/shard_map/all_to_all | solution.py:547
  158.6 1.5 collective-permute-done.32
  160.1 1.6 copy-done.19
  161.7 1.6 copy-done.21
  163.3 3.2 %later_grads.1 = (bf16[256,2048]{1,0:T(8,128)(2,1)}, bf16[256,2048]{1,0:T(8,128)(2,1)}) custom-call(s32[8]{0:T(128)S(1)} %stack.35.w_ref.i_ref, bf16[256,2048]{1,0:T(8,128)(2,1)S(1)} %bitcast.44, bf16[256,2048]{1,0:T(8,128)(2,1)S(1)} %bitcast.48, bf16[8,128,128]{2,1,0:T(8,128)(2,1)S(1)} %bitcast.60, bf16[8,128,128]{2,1,0:T(8,128)(2,1)S(1)} %bitcast.61, ...), custom_call_target="tpu_custom_call" | custom-call | flops 268435456 | bytes 8388608 | tf_op jit(solution)/shard_map/later_grads/pallas_call | solution.py:348
  166.5 9.6 %layer_rows.1 = bf16[256,4096]{1,0:T(8,128)(2,1)} custom-call(bf16[256,512]{1,0:T(8,128)(2,1)S(1)} %get-tuple-element.142.n0, bf16[256,512]{1,0:T(8,128)(2,1)S(1)} %copy-done.29, bf16[256,512]{1,0:T(8,128)(2,1)S(1)} %copy-done.32, bf16[256,512]{1,0:T(8,128)(2,1)S(1)} %copy-done.35, bf16[512,4096]{1,0:T(8,128)(2,1)} %own_ref.1, bf16[32,3,16,4096]{3,2,1,0:T(8,128)(2,1)} %bitcast.65), custom_call_target="tpu_custom_call" | custom-call | flops 4294967296 | bytes 19922944 | tf_op jit(solution)/shard_map/layer_rows/pallas_call | solution.py:383
  176.1 12.2 %all-to-all-done.s_ref = bf16[16,32,2048]{2,1,0:T(8,128)(2,1)} async-done(((bf16[16,32,2048]{2,1,0:T(8,128)(2,1)}), bf16[16,32,2048]{2,1,0:T(8,128)(2,1)}, u32[]{:S(2)}, u32[]{:S(2)}) %all-to-all-start) | async-done | bytes 2097184 | tf_op jit(solution)/shard_map/all_to_all | solution.py:547
  188.2 1.9 sum_parts.1
  190.2 1.3 collective-permute-done.33
  (136 shorter events, 34.0 us)
Async XLA Ops:
  7.2 12.4 %copy-start = (bf16[1,256,4096]{2,1,0:T(8,128)(2,1)S(1)}, bf16[1,256,4096]{2,1,0:T(8,128)(2,1)}, u32[]{:S(2)}) copy-start(bf16[1,256,4096]{2,1,0:T(8,128)(2,1)} %param.11) | copy-start | bytes 6291460
  7.2 79.1 %all-gather.2.cloned.1.call-start = ((), (), s32[]{:S(2)}) async-start(), calls=%async_computation.1 | async-start | bytes 12976128 | tf_op jit(solution)/shard_map/all_gather | solution.py:496
  8.3 10.4 %collective-permute-start.2 = (bf16[16,4096]{1,0:T(8,128)(2,1)S(1)}, bf16[16,4096]{1,0:T(8,128)(2,1)S(1)}, u32[]{:S(2)}, u32[]{:S(2)}) collective-permute-start(bf16[16,4096]{1,0:T(8,128)(2,1)S(1)} %constant_dynamic-slice_fusion.1), channel_id=1, source_target_pairs={{96,0},{0,32},{32,64},{64,96},{97,1},{1,33},{33,65},{65,97},{98,2}... | collective-permute-start | bytes 393224 | tf_op jit(solution)/shard_map/ppermute | solution.py:469
  10.0 8.7 %collective-permute-start.1 = (bf16[16,4096]{1,0:T(8,128)(2,1)S(1)}, bf16[16,4096]{1,0:T(8,128)(2,1)S(1)}, u32[]{:S(2)}, u32[]{:S(2)}) collective-permute-start(bf16[16,4096]{1,0:T(8,128)(2,1)S(1)} %constant_dynamic-slice_fusion.1), channel_id=1, source_target_pairs={{64,0},{96,32},{0,64},{32,96},{65,1},{97,33},{1,65},{33,97},{66,2}... | collective-permute-start | bytes 393224 | tf_op jit(solution)/shard_map/ppermute | solution.py:469
  12.7 6.0 %collective-permute-start = (bf16[16,4096]{1,0:T(8,128)(2,1)S(1)}, bf16[16,4096]{1,0:T(8,128)(2,1)S(1)}, u32[]{:S(2)}, u32[]{:S(2)}) collective-permute-start(bf16[16,4096]{1,0:T(8,128)(2,1)S(1)} %constant_dynamic-slice_fusion.1), channel_id=1, source_target_pairs={{32,0},{64,32},{96,64},{0,96},{33,1},{65,33},{97,65},{1,97},{34,2}... | collective-permute-start | bytes 393224 | tf_op jit(solution)/shard_map/ppermute | solution.py:469
  16.6 17.2 %copy-start.1 = (bf16[1,256,2048]{2,1,0:T(8,128)(2,1)S(1)}, bf16[1,256,2048]{2,1,0:T(8,128)(2,1)}, u32[]{:S(2)}) copy-start(bf16[1,256,2048]{2,1,0:T(8,128)(2,1)} %param.6) | copy-start | bytes 3145732
  19.5 51.8 %collective-permute-start.18 = (bf16[256,4096]{1,0:T(8,128)(2,1)S(1)}, bf16[256,4096]{1,0:T(8,128)(2,1)}, u32[]{:S(2)}, u32[]{:S(2)}) collective-permute-start(bf16[256,4096]{1,0:T(8,128)(2,1)S(1)} %bitcast.31), channel_id=1, source_target_pairs={{96,0},{0,32},{32,64},{64,96},{97,1},{1,33},{33,65},{65,97},{98,2}... | collective-permute-start | bytes 6291464 | tf_op jit(solution)/shard_map/ppermute | solution.py:469
  20.8 50.5 %collective-permute-start.17 = (bf16[256,4096]{1,0:T(8,128)(2,1)S(1)}, bf16[256,4096]{1,0:T(8,128)(2,1)}, u32[]{:S(2)}, u32[]{:S(2)}) collective-permute-start(bf16[256,4096]{1,0:T(8,128)(2,1)S(1)} %bitcast.32), channel_id=1, source_target_pairs={{32,0},{64,32},{96,64},{0,96},{33,1},{65,33},{97,65},{1,97},{34,2}... | collective-permute-start | bytes 6291464 | tf_op jit(solution)/shard_map/ppermute | solution.py:469
  24.5 1.7 collective-permute-start.3
  27.9 12.7 %collective-permute-start.4 = (bf16[256,128]{1,0:T(8,128)(2,1)S(1)}, bf16[256,128]{1,0:T(8,128)(2,1)S(1)}, u32[]{:S(2)}, u32[]{:S(2)}) collective-permute-start(bf16[256,128]{1,0:T(8,128)(2,1)S(1)} %get-tuple-element.78), channel_id=1, source_target_pairs={{0,2},{2,4},{4,6},{6,0},{1,3},{3,5},{5,7},{7,1},{8,10},{10,12},{12... | collective-permute-start | bytes 196616 | tf_op jit(solution)/shard_map/ppermute | solution.py:124
  29.6 11.0 %collective-permute-start.5 = (bf16[256,128]{1,0:T(8,128)(2,1)S(1)}, bf16[256,128]{1,0:T(8,128)(2,1)S(1)}, u32[]{:S(2)}, u32[]{:S(2)}) collective-permute-start(bf16[256,128]{1,0:T(8,128)(2,1)S(1)} %get-tuple-element.79), channel_id=1, source_target_pairs={{0,4},{2,6},{4,0},{6,2},{1,5},{3,7},{5,1},{7,3},{8,12},{10,14},{12... | collective-permute-start | bytes 196616 | tf_op jit(solution)/shard_map/ppermute | solution.py:124
  32.5 8.1 %collective-permute-start.6 = (bf16[256,128]{1,0:T(8,128)(2,1)S(1)}, bf16[256,128]{1,0:T(8,128)(2,1)S(1)}, u32[]{:S(2)}, u32[]{:S(2)}) collective-permute-start(bf16[256,128]{1,0:T(8,128)(2,1)S(1)} %get-tuple-element.80), channel_id=1, source_target_pairs={{0,6},{2,0},{4,2},{6,4},{1,7},{3,1},{5,3},{7,5},{8,14},{10,8},{12,... | collective-permute-start | bytes 196616 | tf_op jit(solution)/shard_map/ppermute | solution.py:124
  41.2 20.8 %copy-start.13 = (bf16[16,128,128]{2,1,0:T(8,128)(2,1)S(1)}, bf16[16,128,128]{2,1,0:T(8,128)(2,1)}, u32[]{:S(2)}) copy-start(bf16[16,128,128]{2,1,0:T(8,128)(2,1)} %copy-done.11) | copy-start | bytes 1572868
  41.2 23.5 %copy-start.38 = (f32[2048]{0:T(1024)S(1)}, f32[2048]{0:T(1024)}, u32[]{:S(2)}) copy-start(f32[2048]{0:T(1024)} %param.9) | copy-start | bytes 24580
  41.2 9.6 %collective-permute-start.9 = (bf16[256,128]{1,0:T(8,128)(2,1)S(1)}, bf16[256,128]{1,0:T(8,128)(2,1)S(1)}, u32[]{:S(2)}, u32[]{:S(2)}) collective-permute-start(bf16[256,128]{1,0:T(8,128)(2,1)S(1)} %shard_map.102), channel_id=1, source_target_pairs={{0,24},{8,0},{16,8},{24,16},{1,25},{9,1},{17,9},{25,17},{2,26},{10... | collective-permute-start | bytes 196616 | tf_op jit(solution)/shard_map/ppermute | solution.py:124
  45.3 5.9 %collective-permute-start.8 = (bf16[256,128]{1,0:T(8,128)(2,1)S(1)}, bf16[256,128]{1,0:T(8,128)(2,1)S(1)}, u32[]{:S(2)}, u32[]{:S(2)}) collective-permute-start(bf16[256,128]{1,0:T(8,128)(2,1)S(1)} %shard_map.102), channel_id=1, source_target_pairs={{0,16},{8,24},{16,0},{24,8},{1,17},{9,25},{17,1},{25,9},{2,18},{10... | collective-permute-start | bytes 196616 | tf_op jit(solution)/shard_map/ppermute | solution.py:124
  45.3 6.2 %collective-permute-start.7 = (bf16[256,128]{1,0:T(8,128)(2,1)S(1)}, bf16[256,128]{1,0:T(8,128)(2,1)S(1)}, u32[]{:S(2)}, u32[]{:S(2)}) collective-permute-start(bf16[256,128]{1,0:T(8,128)(2,1)S(1)} %shard_map.102), channel_id=1, source_target_pairs={{0,8},{8,16},{16,24},{24,0},{1,9},{9,17},{17,25},{25,1},{2,10},{10... | collective-permute-start | bytes 196616 | tf_op jit(solution)/shard_map/ppermute | solution.py:124
  52.2 5.5 %collective-permute-start.10 = (bf16[256,128]{1,0:T(8,128)(2,1)S(1)}, bf16[256,128]{1,0:T(8,128)(2,1)S(1)}, u32[]{:S(2)}, u32[]{:S(2)}) collective-permute-start(bf16[256,128]{1,0:T(8,128)(2,1)S(1)} %get-tuple-element.95), channel_id=1, source_target_pairs={{0,2},{2,4},{4,6},{6,0},{1,3},{3,5},{5,7},{7,1},{8,10},{10,12},{12... | collective-permute-start | bytes 196616 | tf_op jit(solution)/shard_map/ppermute | solution.py:124
  53.0 5.8 %collective-permute-start.11 = (bf16[256,128]{1,0:T(8,128)(2,1)S(1)}, bf16[256,128]{1,0:T(8,128)(2,1)S(1)}, u32[]{:S(2)}, u32[]{:S(2)}) collective-permute-start(bf16[256,128]{1,0:T(8,128)(2,1)S(1)} %get-tuple-element.96), channel_id=1, source_target_pairs={{0,4},{2,6},{4,0},{6,2},{1,5},{3,7},{5,1},{7,3},{8,12},{10,14},{12... | collective-permute-start | bytes 196616 | tf_op jit(solution)/shard_map/ppermute | solution.py:124
  53.9 8.2 %collective-permute-start.12 = (bf16[256,128]{1,0:T(8,128)(2,1)S(1)}, bf16[256,128]{1,0:T(8,128)(2,1)S(1)}, u32[]{:S(2)}, u32[]{:S(2)}) collective-permute-start(bf16[256,128]{1,0:T(8,128)(2,1)S(1)} %get-tuple-element.97), channel_id=1, source_target_pairs={{0,6},{2,0},{4,2},{6,4},{1,7},{3,1},{5,3},{7,5},{8,14},{10,8},{12,... | collective-permute-start | bytes 196616 | tf_op jit(solution)/shard_map/ppermute | solution.py:124
  62.7 2.0 collective-permute-start.13
  76.2 46.9 %collective-permute-start.23 = (bf16[128,4096]{1,0:T(8,128)(2,1)}, bf16[128,4096]{1,0:T(8,128)(2,1)}, u32[]{:S(2)}, u32[]{:S(2)}) collective-permute-start(bf16[128,4096]{1,0:T(8,128)(2,1)} %slice.6), channel_id=1, source_target_pairs={{32,0},{64,32},{96,64},{0,96},{33,1},{65,33},{97,65},{1,97},{34,2}... | collective-permute-start | bytes 3145736 | tf_op jit(solution)/shard_map/ppermute | solution.py:469
  76.3 46.8 %collective-permute-start.24 = (bf16[128,4096]{1,0:T(8,128)(2,1)}, bf16[128,4096]{1,0:T(8,128)(2,1)}, u32[]{:S(2)}, u32[]{:S(2)}) collective-permute-start(bf16[128,4096]{1,0:T(8,128)(2,1)} %slice.7), channel_id=1, source_target_pairs={{96,0},{0,32},{32,64},{64,96},{97,1},{1,33},{33,65},{65,97},{98,2}... | collective-permute-start | bytes 3145736 | tf_op jit(solution)/shard_map/ppermute | solution.py:469
  88.9 17.6 %copy-start.28 = (bf16[256,512]{1,0:T(8,128)(2,1)S(1)}, bf16[256,512]{1,0:T(8,128)(2,1)}, u32[]{:S(2)}) copy-start(bf16[256,512]{1,0:T(8,128)(2,1)} %copy-done.27) | copy-start | bytes 786436
  88.9 19.7 %copy-start.31 = (bf16[256,512]{1,0:T(8,128)(2,1)S(1)}, bf16[256,512]{1,0:T(8,128)(2,1)}, u32[]{:S(2)}) copy-start(bf16[256,512]{1,0:T(8,128)(2,1)} %copy-done.30) | copy-start | bytes 786436
  88.9 22.7 %copy-start.34 = (bf16[256,512]{1,0:T(8,128)(2,1)S(1)}, bf16[256,512]{1,0:T(8,128)(2,1)}, u32[]{:S(2)}) copy-start(bf16[256,512]{1,0:T(8,128)(2,1)} %copy-done.33) | copy-start | bytes 786436
  88.9 23.9 %copy-start.4 = (bf16[1,256,2048]{2,1,0:T(8,128)(2,1)S(1)}, bf16[1,256,2048]{2,1,0:T(8,128)(2,1)}, u32[]{:S(2)}) copy-start(bf16[1,256,2048]{2,1,0:T(8,128)(2,1)} %param.7) | copy-start | bytes 3145732
  88.9 23.9 %copy-start.8 = (bf16[1,256,2048]{2,1,0:T(8,128)(2,1)S(1)}, bf16[1,256,2048]{2,1,0:T(8,128)(2,1)}, u32[]{:S(2)}) copy-start(bf16[1,256,2048]{2,1,0:T(8,128)(2,1)} %param.8) | copy-start | bytes 3145732
  88.9 23.9 %copy-start.17 = (bf16[16,256,256]{2,1,0:T(8,128)(2,1)S(1)}, bf16[16,256,256]{2,1,0:T(8,128)(2,1)}, u32[]{:S(2)}) copy-start(bf16[16,256,256]{2,1,0:T(8,128)(2,1)} %copy-done.16) | copy-start | bytes 6291460
  88.9 23.9 %copy-start.23 = (bf16[4,256,128]{2,1,0:T(8,128)(2,1)S(1)}, bf16[4,256,128]{2,1,0:T(8,128)(2,1)}, u32[]{:S(2)}) copy-start(bf16[4,256,128]{2,1,0:T(8,128)(2,1)} %copy-done.22) | copy-start | bytes 786436
  88.9 23.9 %copy-start.25 = (bf16[4,256,128]{2,1,0:T(8,128)(2,1)S(1)}, bf16[4,256,128]{2,1,0:T(8,128)(2,1)}, u32[]{:S(2)}) copy-start(bf16[4,256,128]{2,1,0:T(8,128)(2,1)} %copy-done.24) | copy-start | bytes 786436
  98.5 1.6 collective-permute-start.19
  100.7 5.7 %collective-permute-start.20 = (bf16[256,128]{1,0:T(8,128)(2,1)S(1)}, bf16[256,128]{1,0:T(8,128)(2,1)S(1)}, u32[]{:S(2)}, u32[]{:S(2)}) collective-permute-start(bf16[256,128]{1,0:T(8,128)(2,1)S(1)} %get-tuple-element.111), channel_id=1, source_target_pairs={{0,2},{2,4},{4,6},{6,0},{1,3},{3,5},{5,7},{7,1},{8,10},{10,12},{12... | collective-permute-start | bytes 196616 | tf_op jit(solution)/shard_map/ppermute | solution.py:124
  102.3 6.3 %collective-permute-start.21 = (bf16[256,128]{1,0:T(8,128)(2,1)S(1)}, bf16[256,128]{1,0:T(8,128)(2,1)S(1)}, u32[]{:S(2)}, u32[]{:S(2)}) collective-permute-start(bf16[256,128]{1,0:T(8,128)(2,1)S(1)} %get-tuple-element.112), channel_id=1, source_target_pairs={{0,4},{2,6},{4,0},{6,2},{1,5},{3,7},{5,1},{7,3},{8,12},{10,14},{12... | collective-permute-start | bytes 196616 | tf_op jit(solution)/shard_map/ppermute | solution.py:124
  105.0 6.6 %collective-permute-start.22 = (bf16[256,128]{1,0:T(8,128)(2,1)S(1)}, bf16[256,128]{1,0:T(8,128)(2,1)S(1)}, u32[]{:S(2)}, u32[]{:S(2)}) collective-permute-start(bf16[256,128]{1,0:T(8,128)(2,1)S(1)} %get-tuple-element.113), channel_id=1, source_target_pairs={{0,6},{2,0},{4,2},{6,4},{1,7},{3,1},{5,3},{7,5},{8,14},{10,8},{12,... | collective-permute-start | bytes 196616 | tf_op jit(solution)/shard_map/ppermute | solution.py:124
  106.5 15.1 %collective-permute-start.14 = (bf16[256,512]{1,0:T(8,128)(2,1)S(1)}, bf16[256,512]{1,0:T(8,128)(2,1)S(1)}, u32[]{:S(2)}, u32[]{:S(2)}) collective-permute-start(bf16[256,512]{1,0:T(8,128)(2,1)S(1)} %copy-done.28), channel_id=1, source_target_pairs={{0,32},{32,64},{64,96},{96,0},{1,33},{33,65},{65,97},{97,1},{2,34}... | collective-permute-start | bytes 786440 | tf_op jit(solution)/shard_map/ppermute | solution.py:124
  108.6 13.2 %collective-permute-start.15 = (bf16[256,512]{1,0:T(8,128)(2,1)S(1)}, bf16[256,512]{1,0:T(8,128)(2,1)S(1)}, u32[]{:S(2)}, u32[]{:S(2)}) collective-permute-start(bf16[256,512]{1,0:T(8,128)(2,1)S(1)} %copy-done.31), channel_id=1, source_target_pairs={{0,64},{32,96},{64,0},{96,32},{1,65},{33,97},{65,1},{97,33},{2,66}... | collective-permute-start | bytes 786440 | tf_op jit(solution)/shard_map/ppermute | solution.py:124
  111.6 11.5 %collective-permute-start.16 = (bf16[256,512]{1,0:T(8,128)(2,1)S(1)}, bf16[256,512]{1,0:T(8,128)(2,1)S(1)}, u32[]{:S(2)}, u32[]{:S(2)}) collective-permute-start(bf16[256,512]{1,0:T(8,128)(2,1)S(1)} %copy-done.34), channel_id=1, source_target_pairs={{0,96},{32,0},{64,32},{96,64},{1,97},{33,1},{65,33},{97,65},{2,98}... | collective-permute-start | bytes 786440 | tf_op jit(solution)/shard_map/ppermute | solution.py:124
  128.3 19.4 %collective-permute-start.28 = (bf16[512,2048]{1,0:T(8,128)(2,1)S(1)}, bf16[512,2048]{1,0:T(8,128)(2,1)S(1)}, u32[]{:S(2)}, u32[]{:S(2)}) collective-permute-start(bf16[512,2048]{1,0:T(8,128)(2,1)S(1)} %get-tuple-element.130), channel_id=1, source_target_pairs={{0,1},{1,0},{2,3},{3,2},{4,5},{5,4},{6,7},{7,6},{8,9},{9,8},{10,11... | collective-permute-start | bytes 6291464 | tf_op jit(solution)/shard_map/ppermute | solution.py:124
  128.3 6.0 %collective-permute-start.27 = (bf16[256,128]{1,0:T(8,128)(2,1)S(1)}, bf16[256,128]{1,0:T(8,128)(2,1)S(1)}, u32[]{:S(2)}, u32[]{:S(2)}) collective-permute-start(bf16[256,128]{1,0:T(8,128)(2,1)S(1)} %shard_map.106), channel_id=1, source_target_pairs={{0,24},{8,0},{16,8},{24,16},{1,25},{9,1},{17,9},{25,17},{2,26},{10... | collective-permute-start | bytes 196616 | tf_op jit(solution)/shard_map/ppermute | solution.py:124
  131.0 6.4 %collective-permute-start.26 = (bf16[256,128]{1,0:T(8,128)(2,1)S(1)}, bf16[256,128]{1,0:T(8,128)(2,1)S(1)}, u32[]{:S(2)}, u32[]{:S(2)}) collective-permute-start(bf16[256,128]{1,0:T(8,128)(2,1)S(1)} %shard_map.106), channel_id=1, source_target_pairs={{0,16},{8,24},{16,0},{24,8},{1,17},{9,25},{17,1},{25,9},{2,18},{10... | collective-permute-start | bytes 196616 | tf_op jit(solution)/shard_map/ppermute | solution.py:124
  131.0 6.8 %collective-permute-start.25 = (bf16[256,128]{1,0:T(8,128)(2,1)S(1)}, bf16[256,128]{1,0:T(8,128)(2,1)S(1)}, u32[]{:S(2)}, u32[]{:S(2)}) collective-permute-start(bf16[256,128]{1,0:T(8,128)(2,1)S(1)} %shard_map.106), channel_id=1, source_target_pairs={{0,8},{8,16},{16,24},{24,0},{1,9},{9,17},{17,25},{25,1},{2,10},{10... | collective-permute-start | bytes 196616 | tf_op jit(solution)/shard_map/ppermute | solution.py:124
  138.5 6.4 %collective-permute-start.29 = (bf16[256,128]{1,0:T(8,128)(2,1)S(1)}, bf16[256,128]{1,0:T(8,128)(2,1)S(1)}, u32[]{:S(2)}, u32[]{:S(2)}) collective-permute-start(bf16[256,128]{1,0:T(8,128)(2,1)S(1)} %get-tuple-element.134), channel_id=1, source_target_pairs={{0,2},{2,4},{4,6},{6,0},{1,3},{3,5},{5,7},{7,1},{8,10},{10,12},{12... | collective-permute-start | bytes 196616 | tf_op jit(solution)/shard_map/ppermute | solution.py:124
  138.5 6.3 %collective-permute-start.30 = (bf16[256,128]{1,0:T(8,128)(2,1)S(1)}, bf16[256,128]{1,0:T(8,128)(2,1)S(1)}, u32[]{:S(2)}, u32[]{:S(2)}) collective-permute-start(bf16[256,128]{1,0:T(8,128)(2,1)S(1)} %get-tuple-element.135), channel_id=1, source_target_pairs={{0,4},{2,6},{4,0},{6,2},{1,5},{3,7},{5,1},{7,3},{8,12},{10,14},{12... | collective-permute-start | bytes 196616 | tf_op jit(solution)/shard_map/ppermute | solution.py:124
  141.1 4.4 %collective-permute-start.31 = (bf16[256,128]{1,0:T(8,128)(2,1)S(1)}, bf16[256,128]{1,0:T(8,128)(2,1)S(1)}, u32[]{:S(2)}, u32[]{:S(2)}) collective-permute-start(bf16[256,128]{1,0:T(8,128)(2,1)S(1)} %get-tuple-element.136), channel_id=1, source_target_pairs={{0,6},{2,0},{4,2},{6,4},{1,7},{3,1},{5,3},{7,5},{8,14},{10,8},{12,... | collective-permute-start | bytes 196616 | tf_op jit(solution)/shard_map/ppermute | solution.py:124
  153.9 34.3 %all-to-all-start = ((bf16[16,32,2048]{2,1,0:T(8,128)(2,1)}), bf16[16,32,2048]{2,1,0:T(8,128)(2,1)}, u32[]{:S(2)}, u32[]{:S(2)}) async-start(bf16[16,32,2048]{2,1,0:T(8,128)(2,1)} %bitcast.49), calls=%async_computation | async-start | bytes 4194304 | tf_op jit(solution)/shard_map/all_to_all | solution.py:547
  158.5 1.6 collective-permute-start.32
  190.1 1.4 collective-permute-start.33
  (29 other events, 94.5 us)
Sparse Core Ops, SparseCore 0:
  19.6 66.5 all-gather.1

commit v3 on v2

--- a/solution.py
+++ b/solution.py
@@ -119,6 +119,10 @@
         give_ref[at] = (base + jnp.where(first, s_ref[c, at].astype(F32), 0.0)).astype(BF)
 
 
+def partner(x, axis, bits):
+    return lax.ppermute(x, axis, [(d, d ^ bits) for d in range(lax.axis_size(axis))])
+
+
 def give_to(x, axis, by):
     n = lax.axis_size(axis)
     return lax.ppermute(x, axis, [(d, (d + by) % n) for d in range(n)])
@@ -143,7 +147,10 @@
     filled_plane = fill_plane(row, filled_row)
     rows_before = after(rows_before, filled_plane)
     own, *out = small_call(
-        functools.partial(plane_body, reverse), where, terms + rows_before, [one] + [low] * (n - 1)
+        functools.partial(plane_body, reverse),
+        where,
+        terms + rows_before,
+        [one] + [low] * (n - 1),
     )
     sums = [own] + [give_to(x, "y", k) for k, x in enumerate(out, 1)]
     filled_core = fill_core(out, filled_plane)
@@ -191,38 +198,46 @@
     return jnp.where(lax.div(chunk, CH // 2) == w_ref[7], m_ref[h], t_ref[h])
 
 
-def attend_body(w_ref, q_ref, o_ref, m_ref, t_ref, g_ref, *refs):
-    n_refs, a_ref = refs[:-1], refs[-1]
+def attend_body(w_ref, q_ref, o_ref, m_ref, t_ref, g_ref, near_ref, far_ref, a_ref):
     g = pl.program_id(0)
+    normed = []
     for h in range(HC):
         cols = slice(h * HD, (h + 1) * HD)
         state = pick(w_ref, w_ref[g], m_ref, t_ref, h)
         a = o_ref[:, cols] + mm(head(q_ref, h), state, 1, 0)
         a_ref[0, :, cols] = a
         inv = lax.rsqrt(jnp.mean(a * a, axis=-1, keepdims=True) + EPSILON)
-        normed = (a * inv * g_ref[:, cols]).astype(BF)
-        for k in range(CH):
-
-            @pl.when(g == k)
-            def _(k=k, normed=normed, cols=cols):
-                n_refs[k][:, cols] = normed
+        normed.append((a * inv * g_ref[:, cols]).astype(BF))
+    normed = jnp.concatenate(normed, axis=1)
+
+    @pl.when(g < CH // 2)
+    def _():
+        near_ref[...] = normed
+
+    @pl.when(g >= CH // 2)
+    def _():
+        far_ref[...] = normed
 
 
 def attend(where, q, out, carried, gain):
     t, f = q.shape
     w = f // CH
+    two = CH // 2
     blk = pl.BlockSpec((t, w), lambda g, i: (0, i[g]))
-    st = pl.BlockSpec((HC, HD, HD), lambda g, i: (lax.rem(i[g], CH // 2), 0, 0))
+    st = pl.BlockSpec((HC, HD, HD), lambda g, i: (lax.rem(i[g], two), 0, 0))
     return pl.pallas_call(
         attend_body,
         grid_spec=pltpu.PrefetchScalarGridSpec(
             num_scalar_prefetch=1,
             grid=(CH,),
             in_specs=[blk, blk, st, st, pl.BlockSpec((1, w), lambda g, i: (0, i[g]))],
-            out_specs=[pl.BlockSpec((t, w), lambda g, i: (0, 0))] * CH
-            + [pl.BlockSpec((1, t, w), lambda g, i: (g, 0, 0))],
+            out_specs=[
+                pl.BlockSpec((t, w), lambda g, i: (0, jnp.minimum(g, two - 1))),
+                pl.BlockSpec((t, w), lambda g, i: (0, jnp.maximum(g - two, 0))),
+                pl.BlockSpec((1, t, w), lambda g, i: (i[g], 0, 0)),
+            ],
         ),
-        out_shape=[jax.ShapeDtypeStruct((t, w), BF)] * CH
+        out_shape=[jax.ShapeDtypeStruct((t, two * w), BF)] * 2
         + [jax.ShapeDtypeStruct((CH, t, w), F32)],
         cost_estimate=cost(2 * t * f * HD, 12 * t * f),
         compiler_params=pltpu.CompilerParams(vmem_limit_bytes=12 << 20),
@@ -265,7 +280,7 @@
             grid=(CH,),
             in_specs=[
                 pl.BlockSpec((t, w), lambda g, i: (0, i[g])),
-                pl.BlockSpec((1, t, w), lambda g, i: (g, 0, 0)),
+                pl.BlockSpec((1, t, w), lambda g, i: (i[g], 0, 0)),
                 pl.BlockSpec((t, w), lambda g, i: (0, 0)),
                 pl.BlockSpec((1, w), lambda g, i: (0, i[g])),
                 pl.BlockSpec((t, d), lambda g, i: (0, 0)),
@@ -367,39 +382,59 @@
     )(order, k, v, *later, pk, pv)
 
 
-def layer_body(n0, n1, n2, n3, own_ref, w_ref, o_ref):
-    normed = (n0, n1, n2, n3)
-    total = mm(n0[...], own_ref[...], 1, 0)
-    for k in range(1, CH):
-        block = w_ref[:, k - 1].reshape(own_ref.shape)
-        total = total + mm(normed[k][...], block, 1, 0)
+def layer_body(i_ref, near_ref, far_ref, own_ref, w_ref, o_ref):
+    w = own_ref.shape[0]
+    mine = lax.div(i_ref[4], CH // 2)
+    total = None
+    for k in range(CH):
+        chunk = i_ref[k]
+        cols = pl.ds(pl.multiple_of(lax.rem(chunk, CH // 2) * w, w), w)
+        is_near = lax.div(chunk, CH // 2) == mine
+        rows = jnp.where(is_near, near_ref[:, cols], far_ref[:, cols])
+        block = own_ref[...] if k == 0 else w_ref[:, k - 1].reshape(own_ref.shape)
+        part = mm(rows, block, 1, 0)
+        total = part if total is None else total + part
     o_ref[...] = total.astype(BF)
 
 
-def layer_rows(normed, own, gathered):
-    t, w = normed[0].shape
+def layer_rows(where, near, far, own, gathered):
+    t = near.shape[0]
+    w = own.shape[0]
     n, c, r, d = gathered.shape
     tile = 1024
+    half = pl.BlockSpec(near.shape, lambda g, i: (0, 0))
     return pl.pallas_call(
         layer_body,
-        grid=(d // tile,),
-        in_specs=[pl.BlockSpec((t, w), lambda g: (0, 0))] * CH
-        + [
-            pl.BlockSpec((w, tile), lambda g: (0, g)),
-            pl.BlockSpec((n, c, r, tile), lambda g: (0, 0, 0, g)),
-        ],
-        out_specs=pl.BlockSpec((t, tile), lambda g: (0, g)),
+        grid_spec=pltpu.PrefetchScalarGridSpec(
+            num_scalar_prefetch=1,
+            grid=(d // tile,),
+            in_specs=[
+                half,
+                half,
+                pl.BlockSpec((w, tile), lambda g, i: (0, g)),
+                pl.BlockSpec((n, c, r, tile), lambda g, i: (0, 0, 0, g)),
+            ],
+            out_specs=pl.BlockSpec((t, tile), lambda g, i: (0, g)),
+        ),
         out_shape=jax.ShapeDtypeStruct((t, d), BF),
         cost_estimate=cost(2 * t * CH * w * d, 2 * (CH * w * d + CH * t * w + t * d)),
         compiler_params=pltpu.CompilerParams(vmem_limit_bytes=20 << 20),
         name="layer_rows",
-    )(*normed, own, gathered)
-
-
-def weight_total(nt, g0_ref, g1_ref, fa_ref, fb_ref, g3_ref):
-    total = mm(nt[0], g0_ref[...], 1, 0) + mm(nt[1], g1_ref[...], 1, 0)
-    total = total + mm(nt[2], jnp.concatenate([fa_ref[...], fb_ref[...]], axis=0), 1, 0)
-    return total + mm(nt[3], g3_ref[...], 1, 0)
+    )(where, near, far, own, gathered)
+
+
+def weight_total(nt, grads, o_ref, extra_ref):
+    total = None
+    for s, g in enumerate(grads):
+        part = mm(nt[s], g[...], 1, 0)
+        total = part if total is None else total + part
+    chips, blocks, rows, w = o_ref.shape
+    span = chips * rows
+    for b in range(blocks):
+        one = total[b * span : (b + 1) * span].reshape(chips, rows, w)
+        if extra_ref is not None:
+            one = one + extra_ref[:, b].astype(F32)
+        o_ref[:, b] = one.astype(BF)
 
 
 def give_body(i_ref, n0, n1, n2, n3, *rest):
@@ -410,58 +445,81 @@
         for s, n in enumerate((n0, n1, n2, n3)):
             nt_ref[s] = n[...].T
 
-    o_ref[...] = weight_total(nt_ref, *grads).astype(BF)
+    weight_total(nt_ref, grads, o_ref, None)
 
 
 def keep_body(i_ref, nt_ref, extra_ref, *rest):
     *grads, o_ref = rest
-    o_ref[...] = (weight_total(nt_ref, *grads) + extra_ref[...].astype(F32)).astype(BF)
-
-
-def weight_half(body, half, rows, grads_all, nt_out):
+    weight_total(nt_ref, grads, o_ref, extra_ref)
+
+
+def weight_half(body, half, rows, grads_all, shape, nt_out):
     t, d = grads_all[0].shape
     w = rows[0].shape[1]
-    tile = 512
+    tile = 256
     steps = d // 2 // tile
-    own = pl.BlockSpec((w, tile), lambda g, i: (0, g))
+    own = pl.BlockSpec(shape[:-1] + (tile,), lambda g, i: (0, 0, 0, g))
     whole = pl.BlockSpec((t, w), lambda g, i: (0, 0))
     turned = pl.BlockSpec((CH, w, t), lambda g, i: (0, 0, 0))
-    out = jax.ShapeDtypeStruct((w, d // 2), BF)
+    out = jax.ShapeDtypeStruct(shape, BF)
+    cols = pl.BlockSpec((t, tile), lambda g, i: (0, i[0] * steps + g))
     return pl.pallas_call(
         body,
         grid_spec=pltpu.PrefetchScalarGridSpec(
             num_scalar_prefetch=1,
             grid=(steps,),
-            in_specs=([whole] * CH if nt_out else [turned, own])
-            + [
-                pl.BlockSpec((x.shape[0], tile), lambda g, i: (0, i[0] * steps + g))
-                for x in grads_all
-            ],
+            in_specs=([whole] * CH if nt_out else [turned, own]) + [cols] * CH,
             out_specs=[own, turned] if nt_out else own,
         ),
         out_shape=[out, jax.ShapeDtypeStruct((CH, w, t), BF)] if nt_out else out,
-        cost_estimate=cost(CH * t * w * d, CH * t * d + 2 * CH * t * w + w * d),
-        compiler_params=pltpu.CompilerParams(vmem_limit_bytes=14 << 20),
+        cost_estimate=cost(CH * t * w * d, 2 * CH * t * d + 2 * CH * t * w + w * d),
+        compiler_params=pltpu.CompilerParams(vmem_limit_bytes=20 << 20),
         name="weight_half",
     )(half, *rows, *grads_all)
 
 
-def sum_body(scale, s_ref, o_ref):
-    total = s_ref[0].astype(F32)
+def sum_body(scale, w_ref, s_ref, keep_ref, x_ref, c_ref, xc_ref, total):
+    acc = s_ref[0].astype(F32)
     for step in range(1, s_ref.shape[0]):
-        total = total + s_ref[step].astype(F32)
-    o_ref[...] = total * scale
-
-
-def sum_parts(parts, scale):
-    _, r, w = parts.shape
+        acc = acc + s_ref[step].astype(F32)
+    total[...] = acc * scale
+    rows = keep_ref.shape[0]
+    block, c = lax.rem(w_ref[4], 2), w_ref[7]
+    mine = pl.ds(pl.multiple_of(c * rows, rows), rows)
+    other = pl.ds(pl.multiple_of((1 - c) * rows, rows), rows)
+    keep_ref[...] = total[block, mine]
+    x_ref[...] = total[1 - block, mine]
+    c_ref[...] = total[block, other]
+    xc_ref[...] = total[1 - block, other]
+
+
+def sum_parts(where, parts, scale):
+    _, b, r, w = parts.shape
     return pl.pallas_call(
         functools.partial(sum_body, scale),
-        out_shape=jax.ShapeDtypeStruct((r, w), F32),
+        in_specs=[
+            pl.BlockSpec(memory_space=pltpu.SMEM),
+            pl.BlockSpec(memory_space=pltpu.VMEM),
+        ],
+        out_specs=[pl.BlockSpec(memory_space=pltpu.VMEM)] * 4,
+        out_shape=[jax.ShapeDtypeStruct((r // 2, w), F32)] * 4,
+        scratch_shapes=[pltpu.VMEM((b, r, w), F32)],
         cost_estimate=cost(parts.size, 2 * parts.size),
-        compiler_params=pltpu.CompilerParams(vmem_limit_bytes=6 << 20),
+        compiler_params=pltpu.CompilerParams(vmem_limit_bytes=8 << 20),
         name="sum_parts",
-    )(parts)
+    )(where, parts)
+
+
+def join_body(w_ref, own_ref, x_ref, c_ref, xc_ref, o_ref):
+    block, c = lax.rem(w_ref[4], 2), w_ref[7]
+    w = own_ref.shape[1]
+    for ref, b, h in (
+        (own_ref, block, c),
+        (x_ref, 1 - block, c),
+        (c_ref, block, 1 - c),
+        (xc_ref, 1 - block, 1 - c),
+    ):
+        o_ref[:, pl.ds(pl.multiple_of((2 * b + h) * w, w), w)] = ref[...]
 
 
 def shift(x, axis, by):
@@ -485,6 +543,9 @@
     places = [at_x, lax.axis_index("z"), lax.axis_index("y"), at_core]
     order = [(at_x + n) % CH for n in range(CH)]
     where = jnp.stack(order + places).astype(jnp.int32)
+    row_half = at_x // 2
+    turns = [2 * row_half, 2 * row_half + 1, 2 - 2 * row_half, 3 - 2 * row_half]
+    turns = jnp.stack(turns + places).astype(jnp.int32)
     mine = at_core.reshape(1).astype(jnp.int32)
     others = 1 - mine
 
@@ -498,9 +559,17 @@
     gathered = pltpu.with_memory_space_constraint(gathered, pltpu.HBM)
     own_weight = pltpu.with_memory_space_constraint(out_weight, pltpu.HBM)
 
-    right = shift(sent_rows, "x", 1)
-    left = shift(sent_rows, "x", 3)
-    half_rows = tok_rows // 2
+    half_cols = model_width // 2
+    side = at_x % 2
+    near_cols = lax.dynamic_slice_in_dim(sent_rows, side * half_cols, half_cols, 1)
+    far_cols = lax.dynamic_slice_in_dim(sent_rows, (1 - side) * half_cols, half_cols, 1)
+    grads_all = [
+        near_cols,
+        partner(far_cols, "x", 1),
+        partner(near_cols, "x", 2),
+        partner(far_cols, "x", 3),
+    ]
+
     carried, (weights, local_out), gn, _ = carry(
         state,
         where,
@@ -510,53 +579,49 @@
         lambda sent, done: mm(after(sent_rows, sent, done), out_weight, 1, 1),
         lambda sent, done: (),
     )
-    *normed, attended = attend(where, q, local_out, carried, gain_row)
-
-    normed_all = [normed[0]] + [give_to(normed[n], "x", n) for n in range(1, CH)]
-    right, left, attended = lax.optimization_barrier((right, left, attended))
-    far_a = shift(right[:half_rows], "x", 1)
-    far_b = shift(left[half_rows:], "x", 3)
+    near, far, attended = attend(turns, q, local_out, carried, gain_row)
+    normed_all = [
+        near,
+        partner(near, "x", 1),
+        partner(far, "x", 2),
+        partner(far, "x", 3),
+    ]
+    attended = pltpu.with_memory_space_constraint(attended, pltpu.HBM)
+    gn = pltpu.with_memory_space_constraint(gn, pltpu.HBM)
 
     ga, lg = grad_attn(where, q, attended, gn, gain_row, grad_rows, gathered)
-    half_cols = model_width // 2
-    grads_all = [grad_rows, left, far_a, far_b, right]
-
-    def first_half(sent, done):
-        rows = after(normed_all, sent, done)
-        return weight_half(give_body, others, rows, grads_all, True)
+    chips = blocks_n // 2
+    shape = (chips, 2, out_weight.shape[0] // chips, half_cols // 2)
+
+    def first_half(sent):
+        rows = after(normed_all, sent)
+        return weight_half(give_body, others, rows, grads_all, shape, True)
 
     def second_half(sent, done):
         for_partner, turned = done
         extra = give_to(for_partner, "c", 1)
-        return weight_half(keep_body, mine, [after(turned, sent), extra], grads_all, False)
-
-    later, (grad_query, pk, pv), _, partial = carry(
-        lg,
+        return weight_half(
+            keep_body, mine, [after(turned, sent), extra], grads_all, shape, False
+        )
+
+    later, _, _, partial = carry(
+        lg, where, at_core, True, first_half, second_half, lambda sent, done: done
+    )
+    ga = after(ga, partial)
+    grad_query, pk, pv = local_grads(where, q, k, v, weights, ga, carried)
+    layer_out = layer_rows(where, near, after(far, partial, later), own_weight, gathered)
+    grad_key, grad_value = later_grads(where, k, v, later, pk, pv)
+
+    parts = lax.all_to_all(partial, ("z", "y"), 0, 0, tiled=True)
+    parts = after(parts, layer_out, grad_key)
+    token_count = seqs * blocks_n * tok_rows
+    own, to_x, to_c, to_both = sum_parts(where, parts, 1.0 / math.sqrt(token_count))
+    both = lax.ppermute(to_both, ("x", "c"), [(d, d ^ 3) for d in range(2 * seqs)])
+    (grad_weight,) = small_call(
+        join_body,
         where,
-        at_core,
-        True,
-        lambda sent: local_grads(where, q, k, v, weights, after(ga, sent), carried),
-        first_half,
-        second_half,
-    )
-    layer_out = layer_rows(after(normed, partial, later), own_weight, gathered)
-    grad_key, grad_value = later_grads(where, k, v, later, pk, pv)
-
-    chips = blocks_n // 2
-    rows = partial.shape[0] // chips
-    parts = lax.all_to_all(
-        partial.reshape(chips, rows, half_cols), ("z", "y"), 0, 0, tiled=True
-    )
-    token_count = seqs * blocks_n * tok_rows
-    parts = after(parts, layer_out, grad_key)
-    summed = sum_parts(parts, 1.0 / math.sqrt(token_count))
-    out_rows = rows // 2
-    keep = lax.dynamic_slice_in_dim(summed, at_core * out_rows, out_rows, 0)
-    give = lax.dynamic_slice_in_dim(summed, (1 - at_core) * out_rows, out_rows, 0)
-    got = shift(give, "c", 1)
-    first = at_core == 0
-    grad_weight = jnp.concatenate(
-        [jnp.where(first, keep, got), jnp.where(first, got, keep)], axis=1
+        [own, partner(to_x, "x", 1), partner(to_c, "c", 1), both],
+        [jax.ShapeDtypeStruct((own.shape[0], model_width), F32)],
     )
     out_shape = (1, tok_rows, feat_width)
     return (

time: 201 us -> 235 us (1.17)
  waiting for transfers between devices: 46.6 us -> 82.8 us
  local copies, waits for them, and re-layouts: 27 us -> 24.2 us
    ppermute x0 -> x9, waiting for transfers between devices: none -> 50.8 us  [the longest x8 50.8 us: partner(): lax.ppermute(x, axis, [(d, d ^ bits) for d in range(lax.axis_size(axis))])]
    ppermute x26 -> x23, waiting for transfers between devices: 25.1 us -> 13.8 us  [give_to(): return lax.ppermute(x, axis, [(d, (d + by) % n) for d in range(n)])]
    ppermute x0 -> x9, starting transfers between devices: none -> 9.32 us  [the longest x8 7.36 us: partner(): lax.ppermute(x, axis, [(d, d ^ bits) for d in range(lax.axis_size(axis))])]
    all_to_all x1, waiting for transfers between devices: 12.2 us -> 2.99 us  [layer(): parts = lax.all_to_all(partial, ('z', 'y'), 0, 0, tiled=True)]
    ppermute x8 -> x3, starting transfers between devices: 11.3 us -> 4.62 us  [shift(): return lax.ppermute(x, axis, [((d + by) % n, d) for d in range(n)])]
    slice x2 -> x0, local copies, waits for them, and re-layouts: 4.85 us -> none  [the longest x1 2.57 us: layer(): far_b = shift(left[half_rows:], 'x', 3)]
    ppermute x26 -> x23, starting transfers between devices: 33.7 us -> 29 us  [give_to(): return lax.ppermute(x, axis, [(d, (d + by) % n) for d in range(n)])]
    all_gather x1, waiting for transfers between devices: 7.94 us -> 12.2 us  [layer(): lax.all_gather(jnp.concatenate(pieces, axis=0), CTX, axis=0, tiled=True)]
  transfers between devices with their start and end apart: 36 -> 37, of which waited for: 20 -> 17; matrix products, arithmetic and copies ran while one was open for 5% -> 4% of each run, Pallas kernels for 22% -> 20%
where the time goes in v3:
time: 235 us; the launch traced here: 233 us
  waiting for transfers between devices  82.8 us (35%)
  Pallas kernels  58 us (25%)
  starting transfers between devices  48.5 us (21%)
  local copies, waits for them, and re-layouts  24.2 us (10%)
  between operations  14.4 us (6%)
  matrix products  4.62 us (2%)
    ppermute x8, waiting for transfers between devices, partner(): lax.ppermute(x, axis, [(d, d ^ bits) for d in range(lax.axis_size(axis))])  50.8 us
    ppermute x23, starting transfers between devices, give_to(): return lax.ppermute(x, axis, [(d, (d + by) % n) for d in range(n)])  29 us
    unnamed x58, local copies, waits for them, and re-layouts  18.2 us
    ppermute x23, waiting for transfers between devices, give_to(): return lax.ppermute(x, axis, [(d, (d + by) % n) for d in range(n)])  13.8 us
    all_gather x1, waiting for transfers between devices, layer(): lax.all_gather(jnp.concatenate(pieces, axis=0), CTX, axis=0, tiled=True)  12.2 us
    pallas_call x1, Pallas kernels, layer_rows(): pl.pallas_call(layer_body, grid_spec=pltpu.PrefetchScalarGridSpec(num_sca...  10.6 us
    pallas_call x2, Pallas kernels, weight_half(): pl.pallas_call(body, grid_spec=pltpu.PrefetchScalarGridSpec(num_scalar_pr...  10.4 us
    pallas_call x1, Pallas kernels, grad_attn(): pl.pallas_call(grad_attn_body, grid_spec=pltpu.PrefetchScalarGridSpec(num...  9.72 us
  transfers between devices with their start and end apart: 37, of which 17 were waited for; matrix products, arithmetic and copies ran while one was open for 4% of the time, Pallas kernels for 20%

profile of v3, /device:TPU:0, one launch (start us, length us, event | category | flops | bytes accessed | tf_op | source)
XLA Modules:
  0.0 233.3 jit_solution(2900101103572588784)
XLA Ops:
  8.1 2.9 %collective-permute-start = (bf16[16,4096]{1,0:T(8,128)(2,1)S(1)}, bf16[16,4096]{1,0:T(8,128)(2,1)S(1)}, u32[]{:S(2)}, u32[]{:S(2)}) collective-permute-start(bf16[16,4096]{1,0:T(8,128)(2,1)S(1)} %constant_dynamic-slice_fusion.2), channel_id=1, source_target_pairs={{32,0},{64,32},{96,64},{0,96},{33,1},{65,33},{97,65},{1,97},{34,2}... | collective-permute-start | bytes 393224 | tf_op jit(solution)/shard_map/ppermute | solution.py:527
  17.3 1.6 collective-permute-done.1
  19.0 1.4 collective-permute-done.2
  21.2 1.7 dynamic-slice_bitcast_fusion.1
  22.9 1.7 collective-permute-done.3.r_ref
  26.3 1.6 collective-permute-start.4
  27.9 2.9 %collective-permute-start.5 = (bf16[256,128]{1,0:T(8,128)(2,1)S(1)}, bf16[256,128]{1,0:T(8,128)(2,1)S(1)}, u32[]{:S(2)}, u32[]{:S(2)}) collective-permute-start(bf16[256,128]{1,0:T(8,128)(2,1)S(1)} %get-tuple-element.75), channel_id=1, source_target_pairs={{0,4},{2,6},{4,0},{6,2},{1,5},{3,7},{5,1},{7,3},{8,12},{10,14},{12... | collective-permute-start | bytes 196616 | tf_op jit(solution)/shard_map/ppermute | solution.py:128
  30.8 1.3 collective-permute-start.6
  32.2 3.0 %local_scores.1 = (bf16[16,256,256]{2,1,0:T(8,128)(2,1)S(1)}, f32[256,2048]{1,0:T(8,128)S(1)}) custom-call(bf16[256,2048]{1,0:T(8,128)(2,1)S(1)} %bitcast.34, bf16[256,2048]{1,0:T(8,128)(2,1)S(1)} %bitcast.39, bf16[256,2048]{1,0:T(8,128)(2,1)S(1)} %bitcast.43), custom_call_target="tpu_custom_call" | custom-call | flops 536870912 | bytes 7340032 | tf_op jit(solution)/shard_map/local_scores/pallas_call | solution.py:182
  35.2 1.3 copy-done.12
  36.5 1.3 copy-done.14
  38.4 2.0 collective-permute-start.7
  40.4 3.6 %collective-permute-start.8 = (bf16[256,128]{1,0:T(8,128)(2,1)S(1)}, bf16[256,128]{1,0:T(8,128)(2,1)S(1)}, u32[]{:S(2)}, u32[]{:S(2)}) collective-permute-start(bf16[256,128]{1,0:T(8,128)(2,1)S(1)} %shard_map.102), channel_id=1, source_target_pairs={{0,16},{8,24},{16,0},{24,8},{1,17},{9,25},{17,1},{25,9},{2,18},{10... | collective-permute-start | bytes 196616 | tf_op jit(solution)/shard_map/ppermute | solution.py:128
  45.0 4.6 %fusion.gn_ref = f32[256,512]{1,0:T(8,128)} fusion(bf16[256,4096]{1,0:T(8,128)(2,1)S(1)} %bitcast.47, bf16[512,4096]{1,0:T(8,128)(2,1)} %own_ref.1), kind=kOutput, calls=%fused_computation.6 | convolution fusion | flops 1073741824 | bytes 6815744 | tf_op jit(solution)/shard_map/dot_general | solution.py:21
  49.6 1.3 shard_map.103
  51.6 1.8 collective-permute-start.11
  54.3 2.4 %collective-permute-done.10.p1 = bf16[256,128]{1,0:T(8,128)(2,1)} collective-permute-done((bf16[256,128]{1,0:T(8,128)(2,1)}, bf16[256,128]{1,0:T(8,128)(2,1)}, u32[]{:S(2)}, u32[]{:S(2)}) %collective-permute-start.10) | collective-permute-done | bytes 65568 | tf_op jit(solution)/shard_map/ppermute | solution.py:128
  61.2 3.3 %constant_dynamic-slice_fusion = (bf16[256,2048]{1,0:T(8,128)(2,1)}, bf16[256,2048]{1,0:T(8,128)(2,1)}) fusion(bf16[256,4096]{1,0:T(8,128)(2,1)} %bitcast.46, s32[]{:T(128)S(6)} %select_n.50, s32[]{:T(128)S(6)} %select_n.49), kind=kLoop, calls=%fused_computation.3 | loop fusion | bytes 4194312 | tf_op jit(solution)/shard_map/dynamic_slice | solution.py:565
  65.4 3.2 %collective-permute-start.19 = (bf16[256,2048]{1,0:T(8,128)(2,1)}, bf16[256,2048]{1,0:T(8,128)(2,1)}, u32[]{:S(2)}, u32[]{:S(2)}) collective-permute-start(bf16[256,2048]{1,0:T(8,128)(2,1)} %get-tuple-element.142.rest_0_), channel_id=1, source_target_pairs={{0,64},{32,96},{64,0},{96,32},{1,65},{33,97},{65,1},{97,33},{2,66}... | collective-permute-start | bytes 3145736 | tf_op jit(solution)/shard_map/ppermute | solution.py:123
  68.6 3.5 %attend.1 = (bf16[256,1024]{1,0:T(8,128)(2,1)}, bf16[256,1024]{1,0:T(8,128)(2,1)S(1)}, f32[4,256,512]{2,1,0:T(8,128)S(1)}) custom-call(s32[8]{0:T(128)S(1)} %stack.59.w_ref, bf16[256,2048]{1,0:T(8,128)(2,1)S(1)} %bitcast.35, f32[256,2048]{1,0:T(8,128)S(1)} %copy-done.15, bf16[8,128,128]{2,1,0:T(8,128)(2,1)S(1)} %bitcast.55, ...), custom_call_target="tpu_custom_call" | custom-call | flops 134217728 | bytes 6291456 | tf_op jit(solution)/shard_map/attend/pallas_call | solution.py:228
  72.1 1.3 copy-done.11
  74.2 12.2 %all-gather.2.cloned.1.call-done = bf16[1536,4096]{1,0:T(8,128)(2,1)} async-done(((bf16[48,4096]{1,0:T(8,128)(2,1)}), bf16[1536,4096]{1,0:T(8,128)(2,1)}) %all-gather.2.cloned.1.call-update) | async-done | bytes 12582928 | tf_op jit(solution)/shard_map/all_gather | solution.py:557
  86.5 1.6 copy-done.6
  88.1 9.7 %grad_attn.1 = (bf16[4,256,512]{2,1,0:T(8,128)(2,1)S(1)}, bf16[16,128,128]{2,1,0:T(8,128)(2,1)S(1)}) custom-call(s32[8]{0:T(128)S(1)} %stack.54.w_ref.i_ref, bf16[256,2048]{1,0:T(8,128)(2,1)S(1)} %bitcast.36, f32[4,256,512]{2,1,0:T(8,128)} %copy-done.11, f32[256,512]{1,0:T(8,128)} %fusion.gn_ref, f32[1,2048]{1,0:T(1,128)S(1)} %bitcast.62, ...), custom_call_target="tpu_custom_call" | custom-call | flops 3355443200 | bytes 18874368 | tf_op jit(solution)/shard_map/grad_attn/pallas_call | solution.py:276
  98.2 25.8 %collective-permute-done.14.n1 = bf16[256,1024]{1,0:T(8,128)(2,1)} collective-permute-done((bf16[256,1024]{1,0:T(8,128)(2,1)}, bf16[256,1024]{1,0:T(8,128)(2,1)}, u32[]{:S(2)}, u32[]{:S(2)}) %collective-permute-start.14) | collective-permute-done | bytes 524320 | tf_op jit(solution)/shard_map/ppermute | solution.py:123
  124.3 2.7 %collective-permute-start.16 = (bf16[256,1024]{1,0:T(8,128)(2,1)S(1)}, bf16[256,1024]{1,0:T(8,128)(2,1)S(1)}, u32[]{:S(2)}, u32[]{:S(2)}) collective-permute-start(bf16[256,1024]{1,0:T(8,128)(2,1)S(1)} %copy-done.23), channel_id=1, source_target_pairs={{0,96},{32,64},{64,32},{96,0},{1,97},{33,65},{65,33},{97,1},{2,98}... | collective-permute-start | bytes 1572872 | tf_op jit(solution)/shard_map/ppermute | solution.py:123
  127.6 11.4 %collective-permute-done.15.n2 = bf16[256,1024]{1,0:T(8,128)(2,1)S(1)} collective-permute-done((bf16[256,1024]{1,0:T(8,128)(2,1)S(1)}, bf16[256,1024]{1,0:T(8,128)(2,1)S(1)}, u32[]{:S(2)}, u32[]{:S(2)}) %collective-permute-start.15) | collective-permute-done | bytes 524320 | tf_op jit(solution)/shard_map/ppermute | solution.py:123
  139.0 10.9 %collective-permute-done.16.n3 = bf16[256,1024]{1,0:T(8,128)(2,1)S(1)} collective-permute-done((bf16[256,1024]{1,0:T(8,128)(2,1)S(1)}, bf16[256,1024]{1,0:T(8,128)(2,1)S(1)}, u32[]{:S(2)}, u32[]{:S(2)}) %collective-permute-start.16) | collective-permute-done | bytes 524320 | tf_op jit(solution)/shard_map/ppermute | solution.py:123
  149.9 5.6 %weight_half.2 = (bf16[16,2,32,1024]{3,2,1,0:T(8,128)(2,1)S(1)}, bf16[4,1024,256]{2,1,0:T(8,128)(2,1)S(1)}) custom-call(s32[1]{0:T(128)S(6)} %sub.24.i_ref, bf16[256,1024]{1,0:T(8,128)(2,1)} %get-tuple-element.106.n0.near_ref, bf16[256,1024]{1,0:T(8,128)(2,1)} %collective-permute-done.14.n1, bf16[256,1024]{1,0:T(8,128)(2,1)S(1)} %collective-permute-done.15.n2, ...), custom_call_target="tpu_custom_call" | custom-call | flops 2147483648 | bytes 8388608 | tf_op jit(solution)/shard_map/weight_half/pallas_call | solution.py:466
  155.7 1.3 collective-permute-start.21
  157.0 3.0 %collective-permute-start.22 = (bf16[256,128]{1,0:T(8,128)(2,1)S(1)}, bf16[256,128]{1,0:T(8,128)(2,1)S(1)}, u32[]{:S(2)}, u32[]{:S(2)}) collective-permute-start(bf16[256,128]{1,0:T(8,128)(2,1)S(1)} %get-tuple-element.104), channel_id=1, source_target_pairs={{0,4},{2,6},{4,0},{6,2},{1,5},{3,7},{5,1},{7,3},{8,12},{10,14},{12... | collective-permute-start | bytes 196616 | tf_op jit(solution)/shard_map/ppermute | solution.py:128
  160.0 1.4 collective-permute-done.21.refs_0_.t1
  161.4 2.4 %collective-permute-done.22.refs_1_.t2 = bf16[256,128]{1,0:T(8,128)(2,1)S(1)} collective-permute-done((bf16[256,128]{1,0:T(8,128)(2,1)S(1)}, bf16[256,128]{1,0:T(8,128)(2,1)S(1)}, u32[]{:S(2)}, u32[]{:S(2)}) %collective-permute-start.22) | collective-permute-done | bytes 65568 | tf_op jit(solution)/shard_map/ppermute | solution.py:128
  164.9 1.3 collective-permute-start.25
  167.0 1.9 collective-permute-start.27
  168.9 4.8 %weight_half.3 = bf16[16,2,32,1024]{3,2,1,0:T(8,128)(2,1)S(1)} custom-call(s32[1]{0:T(128)} %bitcast.7.i_ref, bf16[4,1024,256]{2,1,0:T(8,128)(2,1)S(1)} %get-tuple-element.117.nt_ref, bf16[16,2,32,1024]{3,2,1,0:T(8,128)(2,1)S(1)} %collective-permute-done.24.extra_ref, bf16[256,2048]{1,0:T(8,128)(2,1)} %get-tuple-element.142.rest_0_, ...), custom_call_target="tpu_custom_call" | custom-call | flops 2147483648 | bytes 8388608 | tf_op jit(solution)/shard_map/weight_half/pallas_call | solution.py:466
  173.8 1.3 copy-done.7
  175.9 3.1 %collective-permute-start.29 = (bf16[256,128]{1,0:T(8,128)(2,1)S(1)}, bf16[256,128]{1,0:T(8,128)(2,1)S(1)}, u32[]{:S(2)}, u32[]{:S(2)}) collective-permute-start(bf16[256,128]{1,0:T(8,128)(2,1)S(1)} %get-tuple-element.123), channel_id=1, source_target_pairs={{0,4},{2,6},{4,0},{6,2},{1,5},{3,7},{5,1},{7,3},{8,12},{10,14},{12... | collective-permute-start | bytes 196616 | tf_op jit(solution)/shard_map/ppermute | solution.py:128
  180.0 2.0 collective-permute-done.28.p1
  185.3 5.5 %all-to-all-start = ((bf16[16,2,32,1024]{3,2,1,0:T(8,128)(2,1)}), bf16[16,2,32,1024]{3,2,1,0:T(8,128)(2,1)}, u32[]{:S(2)}, u32[]{:S(2)}) async-start(bf16[16,2,32,1024]{3,2,1,0:T(8,128)(2,1)} %copy-done.7), calls=%async_computation | async-start | bytes 4194304 | tf_op jit(solution)/shard_map/all_to_all | solution.py:615
  190.9 1.6 copy-done.13
  194.7 6.8 %local_grads.1 = (bf16[256,2048]{1,0:T(8,128)(2,1)}, f32[4,256,512]{2,1,0:T(8,128)S(1)}, f32[4,256,512]{2,1,0:T(8,128)S(1)}) custom-call(s32[8]{0:T(128)S(1)} %stack.54.w_ref.i_ref, bf16[256,2048]{1,0:T(8,128)(2,1)S(1)} %bitcast.37, bf16[256,2048]{1,0:T(8,128)(2,1)S(1)} %bitcast.40, bf16[256,2048]{1,0:T(8,128)(2,1)S(1)} %bitcast.44, ...), custom_call_target="tpu_custom_call" | custom-call | flops 1073741824 | bytes 12582912 | tf_op jit(solution)/shard_map/local_grads/pallas_call | solution.py:322
  201.6 3.2 %later_grads.1 = (bf16[256,2048]{1,0:T(8,128)(2,1)}, bf16[256,2048]{1,0:T(8,128)(2,1)}) custom-call(s32[8]{0:T(128)S(1)} %stack.54.w_ref.i_ref, bf16[256,2048]{1,0:T(8,128)(2,1)S(1)} %bitcast.41, bf16[256,2048]{1,0:T(8,128)(2,1)S(1)} %bitcast.45, bf16[8,128,128]{2,1,0:T(8,128)(2,1)S(1)} %bitcast.59, bf16[8,128,128]{2,1,0:T(8,128)(2,1)S(1)} %bitcast.60, ...), custom_call_target="tpu_custom_call" | custom-call | flops 268435456 | bytes 8388608 | tf_op jit(solution)/shard_map/later_grads/pallas_call | solution.py:363
  204.8 10.6 %layer_rows.1 = bf16[256,4096]{1,0:T(8,128)(2,1)} custom-call(s32[8]{0:T(128)S(1)} %stack.54.w_ref.i_ref, bf16[256,1024]{1,0:T(8,128)(2,1)} %get-tuple-element.106.n0.near_ref, bf16[256,1024]{1,0:T(8,128)(2,1)S(1)} %copy-done.24, bf16[512,4096]{1,0:T(8,128)(2,1)} %own_ref.1, bf16[32,3,16,4096]{3,2,1,0:T(8,128)(2,1)} %bitcast.64), custom_call_target="tpu_custom_call" | custom-call | flops 4294967296 | bytes 19922944 | tf_op jit(solution)/shard_map/layer_rows/pallas_call | solution.py:406
  215.4 3.0 %all-to-all-done.s_ref = bf16[16,2,32,1024]{3,2,1,0:T(8,128)(2,1)} async-done(((bf16[16,2,32,1024]{3,2,1,0:T(8,128)(2,1)}), bf16[16,2,32,1024]{3,2,1,0:T(8,128)(2,1)}, u32[]{:S(2)}, u32[]{:S(2)}) %all-to-all-start) | async-done | bytes 2097184 | tf_op jit(solution)/shard_map/all_to_all | solution.py:615
  218.3 2.0 sum_parts.1
  220.6 2.0 collective-permute-start.34
  222.5 2.6 %collective-permute-done.32.x_ref = f32[16,1024]{1,0:T(8,128)S(1)} collective-permute-done((f32[16,1024]{1,0:T(8,128)S(1)}, f32[16,1024]{1,0:T(8,128)S(1)}, u32[]{:S(2)}, u32[]{:S(2)}) %collective-permute-start.32) | collective-permute-done | bytes 65568 | tf_op jit(solution)/shard_map/ppermute | solution.py:123
  (112 shorter events, 31.4 us)
Async XLA Ops:
  7.2 79.3 %all-gather.2.cloned.1.call-start = ((), (), s32[]{:S(2)}) async-start(), calls=%async_computation.1 | async-start | bytes 12976128 | tf_op jit(solution)/shard_map/all_gather | solution.py:557
  8.1 9.2 %collective-permute-start = (bf16[16,4096]{1,0:T(8,128)(2,1)S(1)}, bf16[16,4096]{1,0:T(8,128)(2,1)S(1)}, u32[]{:S(2)}, u32[]{:S(2)}) collective-permute-start(bf16[16,4096]{1,0:T(8,128)(2,1)S(1)} %constant_dynamic-slice_fusion.2), channel_id=1, source_target_pairs={{32,0},{64,32},{96,64},{0,96},{33,1},{65,33},{97,65},{1,97},{34,2}... | collective-permute-start | bytes 393224 | tf_op jit(solution)/shard_map/ppermute | solution.py:527
  11.1 7.9 %collective-permute-start.1 = (bf16[16,4096]{1,0:T(8,128)(2,1)S(1)}, bf16[16,4096]{1,0:T(8,128)(2,1)S(1)}, u32[]{:S(2)}, u32[]{:S(2)}) collective-permute-start(bf16[16,4096]{1,0:T(8,128)(2,1)S(1)} %constant_dynamic-slice_fusion.2), channel_id=1, source_target_pairs={{64,0},{96,32},{0,64},{32,96},{65,1},{97,33},{1,65},{33,97},{66,2}... | collective-permute-start | bytes 393224 | tf_op jit(solution)/shard_map/ppermute | solution.py:527
  11.9 8.5 %collective-permute-start.2 = (bf16[16,4096]{1,0:T(8,128)(2,1)S(1)}, bf16[16,4096]{1,0:T(8,128)(2,1)S(1)}, u32[]{:S(2)}, u32[]{:S(2)}) collective-permute-start(bf16[16,4096]{1,0:T(8,128)(2,1)S(1)} %constant_dynamic-slice_fusion.2), channel_id=1, source_target_pairs={{96,0},{0,32},{32,64},{64,96},{97,1},{1,33},{33,65},{65,97},{98,2}... | collective-permute-start | bytes 393224 | tf_op jit(solution)/shard_map/ppermute | solution.py:527
  15.2 16.9 %copy-start = (bf16[1,256,2048]{2,1,0:T(8,128)(2,1)S(1)}, bf16[1,256,2048]{2,1,0:T(8,128)(2,1)}, u32[]{:S(2)}) copy-start(bf16[1,256,2048]{2,1,0:T(8,128)(2,1)} %param.6) | copy-start | bytes 3145732
  15.2 16.9 %copy-start.2 = (bf16[1,256,2048]{2,1,0:T(8,128)(2,1)S(1)}, bf16[1,256,2048]{2,1,0:T(8,128)(2,1)}, u32[]{:S(2)}) copy-start(bf16[1,256,2048]{2,1,0:T(8,128)(2,1)} %param.7) | copy-start | bytes 3145732
  15.2 16.9 %copy-start.4 = (bf16[1,256,2048]{2,1,0:T(8,128)(2,1)S(1)}, bf16[1,256,2048]{2,1,0:T(8,128)(2,1)}, u32[]{:S(2)}) copy-start(bf16[1,256,2048]{2,1,0:T(8,128)(2,1)} %param.8) | copy-start | bytes 3145732
  22.8 1.7 collective-permute-start.3
  22.9 22.0 %copy-start.5 = (bf16[1,256,4096]{2,1,0:T(8,128)(2,1)S(1)}, bf16[1,256,4096]{2,1,0:T(8,128)(2,1)}, u32[]{:S(2)}) copy-start(bf16[1,256,4096]{2,1,0:T(8,128)(2,1)} %param.11) | copy-start | bytes 6291460
  26.3 11.5 %collective-permute-start.4 = (bf16[256,128]{1,0:T(8,128)(2,1)S(1)}, bf16[256,128]{1,0:T(8,128)(2,1)S(1)}, u32[]{:S(2)}, u32[]{:S(2)}) collective-permute-start(bf16[256,128]{1,0:T(8,128)(2,1)S(1)} %get-tuple-element.74), channel_id=1, source_target_pairs={{0,2},{2,4},{4,6},{6,0},{1,3},{3,5},{5,7},{7,1},{8,10},{10,12},{12... | collective-permute-start | bytes 196616 | tf_op jit(solution)/shard_map/ppermute | solution.py:128
  27.9 9.9 %collective-permute-start.5 = (bf16[256,128]{1,0:T(8,128)(2,1)S(1)}, bf16[256,128]{1,0:T(8,128)(2,1)S(1)}, u32[]{:S(2)}, u32[]{:S(2)}) collective-permute-start(bf16[256,128]{1,0:T(8,128)(2,1)S(1)} %get-tuple-element.75), channel_id=1, source_target_pairs={{0,4},{2,6},{4,0},{6,2},{1,5},{3,7},{5,1},{7,3},{8,12},{10,14},{12... | collective-permute-start | bytes 196616 | tf_op jit(solution)/shard_map/ppermute | solution.py:128
  30.8 7.0 %collective-permute-start.6 = (bf16[256,128]{1,0:T(8,128)(2,1)S(1)}, bf16[256,128]{1,0:T(8,128)(2,1)S(1)}, u32[]{:S(2)}, u32[]{:S(2)}) collective-permute-start(bf16[256,128]{1,0:T(8,128)(2,1)S(1)} %get-tuple-element.76), channel_id=1, source_target_pairs={{0,6},{2,0},{4,2},{6,4},{1,7},{3,1},{5,3},{7,5},{8,14},{10,8},{12,... | collective-permute-start | bytes 196616 | tf_op jit(solution)/shard_map/ppermute | solution.py:128
  38.4 11.2 %collective-permute-start.7 = (bf16[256,128]{1,0:T(8,128)(2,1)S(1)}, bf16[256,128]{1,0:T(8,128)(2,1)S(1)}, u32[]{:S(2)}, u32[]{:S(2)}) collective-permute-start(bf16[256,128]{1,0:T(8,128)(2,1)S(1)} %shard_map.102), channel_id=1, source_target_pairs={{0,8},{8,16},{16,24},{24,0},{1,9},{9,17},{17,25},{25,1},{2,10},{10... | collective-permute-start | bytes 196616 | tf_op jit(solution)/shard_map/ppermute | solution.py:128
  40.4 9.2 %collective-permute-start.8 = (bf16[256,128]{1,0:T(8,128)(2,1)S(1)}, bf16[256,128]{1,0:T(8,128)(2,1)S(1)}, u32[]{:S(2)}, u32[]{:S(2)}) collective-permute-start(bf16[256,128]{1,0:T(8,128)(2,1)S(1)} %shard_map.102), channel_id=1, source_target_pairs={{0,16},{8,24},{16,0},{24,8},{1,17},{9,25},{17,1},{25,9},{2,18},{10... | collective-permute-start | bytes 196616 | tf_op jit(solution)/shard_map/ppermute | solution.py:128
  44.0 5.6 %collective-permute-start.9 = (bf16[256,128]{1,0:T(8,128)(2,1)S(1)}, bf16[256,128]{1,0:T(8,128)(2,1)S(1)}, u32[]{:S(2)}, u32[]{:S(2)}) collective-permute-start(bf16[256,128]{1,0:T(8,128)(2,1)S(1)} %shard_map.102), channel_id=1, source_target_pairs={{0,24},{8,0},{16,8},{24,16},{1,25},{9,1},{17,9},{25,17},{2,26},{10... | collective-permute-start | bytes 196616 | tf_op jit(solution)/shard_map/ppermute | solution.py:128
  50.9 5.8 %collective-permute-start.10 = (bf16[256,128]{1,0:T(8,128)(2,1)}, bf16[256,128]{1,0:T(8,128)(2,1)}, u32[]{:S(2)}, u32[]{:S(2)}) collective-permute-start(bf16[256,128]{1,0:T(8,128)(2,1)} %get-tuple-element.91), channel_id=1, source_target_pairs={{0,2},{2,4},{4,6},{6,0},{1,3},{3,5},{5,7},{7,1},{8,10},{10,12},{12... | collective-permute-start | bytes 196616 | tf_op jit(solution)/shard_map/ppermute | solution.py:128
  51.6 6.1 %collective-permute-start.11 = (bf16[256,128]{1,0:T(8,128)(2,1)}, bf16[256,128]{1,0:T(8,128)(2,1)}, u32[]{:S(2)}, u32[]{:S(2)}) collective-permute-start(bf16[256,128]{1,0:T(8,128)(2,1)} %get-tuple-element.92), channel_id=1, source_target_pairs={{0,4},{2,6},{4,0},{6,2},{1,5},{3,7},{5,1},{7,3},{8,12},{10,14},{12... | collective-permute-start | bytes 196616 | tf_op jit(solution)/shard_map/ppermute | solution.py:128
  53.4 5.6 %collective-permute-start.12 = (bf16[256,128]{1,0:T(8,128)(2,1)}, bf16[256,128]{1,0:T(8,128)(2,1)}, u32[]{:S(2)}, u32[]{:S(2)}) collective-permute-start(bf16[256,128]{1,0:T(8,128)(2,1)} %get-tuple-element.93), channel_id=1, source_target_pairs={{0,6},{2,0},{4,2},{6,4},{1,7},{3,1},{5,3},{7,5},{8,14},{10,8},{12,... | collective-permute-start | bytes 196616 | tf_op jit(solution)/shard_map/ppermute | solution.py:128
  61.1 7.5 %copy-start.18 = (bf16[4,256,128]{2,1,0:T(8,128)(2,1)}, bf16[4,256,128]{2,1,0:T(8,128)(2,1)S(1)}, u32[]{:S(2)}) copy-start(bf16[4,256,128]{2,1,0:T(8,128)(2,1)S(1)} %get-tuple-element.94) | copy-start | bytes 786436
  61.1 7.5 %copy-start.15 = (f32[256,2048]{1,0:T(8,128)S(1)}, f32[256,2048]{1,0:T(8,128)}, u32[]{:S(2)}) copy-start(f32[256,2048]{1,0:T(8,128)} %copy-done.14) | copy-start | bytes 6291460
  61.1 7.5 %copy-start.27 = (f32[2048]{0:T(1024)S(1)}, f32[2048]{0:T(1024)}, u32[]{:S(2)}) copy-start(f32[2048]{0:T(1024)} %param.9) | copy-start | bytes 24580
  61.1 7.5 %collective-permute-start.13 = (bf16[4,256,128]{2,1,0:T(8,128)(2,1)S(1)}, bf16[4,256,128]{2,1,0:T(8,128)(2,1)S(1)}, u32[]{:S(2)}, u32[]{:S(2)}) collective-permute-start(bf16[4,256,128]{2,1,0:T(8,128)(2,1)S(1)} %get-tuple-element.95), channel_id=1, source_target_pairs={{0,1},{1,0},{2,3},{3,2},{4,5},{5,4},{6,7},{7,6},{8,9},{9,8},{10,11... | collective-permute-start | bytes 786440 | tf_op jit(solution)/shard_map/ppermute | solution.py:128
  64.5 85.4 %collective-permute-start.18 = (bf16[256,2048]{1,0:T(8,128)(2,1)}, bf16[256,2048]{1,0:T(8,128)(2,1)}, u32[]{:S(2)}, u32[]{:S(2)}) collective-permute-start(bf16[256,2048]{1,0:T(8,128)(2,1)} %get-tuple-element.141), channel_id=1, source_target_pairs={{0,32},{32,0},{64,96},{96,64},{1,33},{33,1},{65,97},{97,65},{2,34}... | collective-permute-start | bytes 3145736 | tf_op jit(solution)/shard_map/ppermute | solution.py:123
  64.5 85.4 %collective-permute-start.20 = (bf16[256,2048]{1,0:T(8,128)(2,1)}, bf16[256,2048]{1,0:T(8,128)(2,1)}, u32[]{:S(2)}, u32[]{:S(2)}) collective-permute-start(bf16[256,2048]{1,0:T(8,128)(2,1)} %get-tuple-element.141), channel_id=1, source_target_pairs={{0,96},{32,64},{64,32},{96,0},{1,97},{33,65},{65,33},{97,1},{2,98}... | collective-permute-start | bytes 3145736 | tf_op jit(solution)/shard_map/ppermute | solution.py:123
  65.4 84.5 %collective-permute-start.19 = (bf16[256,2048]{1,0:T(8,128)(2,1)}, bf16[256,2048]{1,0:T(8,128)(2,1)}, u32[]{:S(2)}, u32[]{:S(2)}) collective-permute-start(bf16[256,2048]{1,0:T(8,128)(2,1)} %get-tuple-element.142.rest_0_), channel_id=1, source_target_pairs={{0,64},{32,96},{64,0},{96,32},{1,65},{33,97},{65,1},{97,33},{2,66}... | collective-permute-start | bytes 3145736 | tf_op jit(solution)/shard_map/ppermute | solution.py:123
  74.2 49.8 %collective-permute-start.14 = (bf16[256,1024]{1,0:T(8,128)(2,1)}, bf16[256,1024]{1,0:T(8,128)(2,1)}, u32[]{:S(2)}, u32[]{:S(2)}) collective-permute-start(bf16[256,1024]{1,0:T(8,128)(2,1)} %get-tuple-element.106.n0.near_ref), channel_id=1, source_target_pairs={{0,32},{32,0},{64,96},{96,64},{1,33},{33,1},{65,97},{97,65},{2,34}... | collective-permute-start | bytes 1572872 | tf_op jit(solution)/shard_map/ppermute | solution.py:123
  88.1 35.9 %copy-start.23 = (bf16[256,1024]{1,0:T(8,128)(2,1)S(1)}, bf16[256,1024]{1,0:T(8,128)(2,1)}, u32[]{:S(2)}) copy-start(bf16[256,1024]{1,0:T(8,128)(2,1)} %copy-done.22) | copy-start | bytes 1572868
  97.8 57.8 %copy-start.16 = (bf16[4,256,512]{2,1,0:T(8,128)(2,1)}, bf16[4,256,512]{2,1,0:T(8,128)(2,1)S(1)}, u32[]{:S(2)}) copy-start(bf16[4,256,512]{2,1,0:T(8,128)(2,1)S(1)} %get-tuple-element.130.ga_ref) | copy-start | bytes 3145732
  97.8 26.5 %collective-permute-start.17 = (bf16[4,256,128]{2,1,0:T(8,128)(2,1)S(1)}, bf16[4,256,128]{2,1,0:T(8,128)(2,1)S(1)}, u32[]{:S(2)}, u32[]{:S(2)}) collective-permute-start(bf16[4,256,128]{2,1,0:T(8,128)(2,1)S(1)} %dynamic-slice_bitcast_fusion), channel_id=1, source_target_pairs={{0,1},{1,0},{2,3},{3,2},{4,5},{5,4},{6,7},{7,6},{8,9},{9,8},{10,11... | collective-permute-start | bytes 786440 | tf_op jit(solution)/shard_map/ppermute | solution.py:128
  124.0 15.0 %collective-permute-start.15 = (bf16[256,1024]{1,0:T(8,128)(2,1)S(1)}, bf16[256,1024]{1,0:T(8,128)(2,1)S(1)}, u32[]{:S(2)}, u32[]{:S(2)}) collective-permute-start(bf16[256,1024]{1,0:T(8,128)(2,1)S(1)} %copy-done.23), channel_id=1, source_target_pairs={{0,64},{32,96},{64,0},{96,32},{1,65},{33,97},{65,1},{97,33},{2,66}... | collective-permute-start | bytes 1572872 | tf_op jit(solution)/shard_map/ppermute | solution.py:123
  124.3 25.6 %collective-permute-start.16 = (bf16[256,1024]{1,0:T(8,128)(2,1)S(1)}, bf16[256,1024]{1,0:T(8,128)(2,1)S(1)}, u32[]{:S(2)}, u32[]{:S(2)}) collective-permute-start(bf16[256,1024]{1,0:T(8,128)(2,1)S(1)} %copy-done.23), channel_id=1, source_target_pairs={{0,96},{32,64},{64,32},{96,0},{1,97},{33,65},{65,33},{97,1},{2,98}... | collective-permute-start | bytes 1572872 | tf_op jit(solution)/shard_map/ppermute | solution.py:123
  155.6 13.4 %collective-permute-start.24 = (bf16[16,2,32,1024]{3,2,1,0:T(8,128)(2,1)S(1)}, bf16[16,2,32,1024]{3,2,1,0:T(8,128)(2,1)S(1)}, u32[]{:S(2)}, u32[]{:S(2)}) collective-permute-start(bf16[16,2,32,1024]{3,2,1,0:T(8,128)(2,1)S(1)} %get-tuple-element.112), channel_id=1, source_target_pairs={{0,1},{1,0},{2,3},{3,2},{4,5},{5,4},{6,7},{7,6},{8,9},{9,8},{10,11... | collective-permute-start | bytes 6291464 | tf_op jit(solution)/shard_map/ppermute | solution.py:128
  155.7 5.7 %collective-permute-start.21 = (bf16[256,128]{1,0:T(8,128)(2,1)S(1)}, bf16[256,128]{1,0:T(8,128)(2,1)S(1)}, u32[]{:S(2)}, u32[]{:S(2)}) collective-permute-start(bf16[256,128]{1,0:T(8,128)(2,1)S(1)} %get-tuple-element.103), channel_id=1, source_target_pairs={{0,2},{2,4},{4,6},{6,0},{1,3},{3,5},{5,7},{7,1},{8,10},{10,12},{12... | collective-permute-start | bytes 196616 | tf_op jit(solution)/shard_map/ppermute | solution.py:128
  157.0 6.8 %collective-permute-start.22 = (bf16[256,128]{1,0:T(8,128)(2,1)S(1)}, bf16[256,128]{1,0:T(8,128)(2,1)S(1)}, u32[]{:S(2)}, u32[]{:S(2)}) collective-permute-start(bf16[256,128]{1,0:T(8,128)(2,1)S(1)} %get-tuple-element.104), channel_id=1, source_target_pairs={{0,4},{2,6},{4,0},{6,2},{1,5},{3,7},{5,1},{7,3},{8,12},{10,14},{12... | collective-permute-start | bytes 196616 | tf_op jit(solution)/shard_map/ppermute | solution.py:128
  160.0 4.3 %collective-permute-start.23 = (bf16[256,128]{1,0:T(8,128)(2,1)S(1)}, bf16[256,128]{1,0:T(8,128)(2,1)S(1)}, u32[]{:S(2)}, u32[]{:S(2)}) collective-permute-start(bf16[256,128]{1,0:T(8,128)(2,1)S(1)} %get-tuple-element.105), channel_id=1, source_target_pairs={{0,6},{2,0},{4,2},{6,4},{1,7},{3,1},{5,3},{7,5},{8,14},{10,8},{12,... | collective-permute-start | bytes 196616 | tf_op jit(solution)/shard_map/ppermute | solution.py:128
  164.9 10.2 %collective-permute-start.25 = (bf16[256,128]{1,0:T(8,128)(2,1)S(1)}, bf16[256,128]{1,0:T(8,128)(2,1)S(1)}, u32[]{:S(2)}, u32[]{:S(2)}) collective-permute-start(bf16[256,128]{1,0:T(8,128)(2,1)S(1)} %shard_map.106), channel_id=1, source_target_pairs={{0,8},{8,16},{16,24},{24,0},{1,9},{9,17},{17,25},{25,1},{2,10},{10... | collective-permute-start | bytes 196616 | tf_op jit(solution)/shard_map/ppermute | solution.py:128
  166.2 8.9 %collective-permute-start.26 = (bf16[256,128]{1,0:T(8,128)(2,1)S(1)}, bf16[256,128]{1,0:T(8,128)(2,1)S(1)}, u32[]{:S(2)}, u32[]{:S(2)}) collective-permute-start(bf16[256,128]{1,0:T(8,128)(2,1)S(1)} %shard_map.106), channel_id=1, source_target_pairs={{0,16},{8,24},{16,0},{24,8},{1,17},{9,25},{17,1},{25,9},{2,18},{10... | collective-permute-start | bytes 196616 | tf_op jit(solution)/shard_map/ppermute | solution.py:128
  167.0 8.0 %collective-permute-start.27 = (bf16[256,128]{1,0:T(8,128)(2,1)S(1)}, bf16[256,128]{1,0:T(8,128)(2,1)S(1)}, u32[]{:S(2)}, u32[]{:S(2)}) collective-permute-start(bf16[256,128]{1,0:T(8,128)(2,1)S(1)} %shard_map.106), channel_id=1, source_target_pairs={{0,24},{8,0},{16,8},{24,16},{1,25},{9,1},{17,9},{25,17},{2,26},{10... | collective-permute-start | bytes 196616 | tf_op jit(solution)/shard_map/ppermute | solution.py:128
  175.8 6.2 %collective-permute-start.28 = (bf16[256,128]{1,0:T(8,128)(2,1)S(1)}, bf16[256,128]{1,0:T(8,128)(2,1)S(1)}, u32[]{:S(2)}, u32[]{:S(2)}) collective-permute-start(bf16[256,128]{1,0:T(8,128)(2,1)S(1)} %get-tuple-element.122), channel_id=1, source_target_pairs={{0,2},{2,4},{4,6},{6,0},{1,3},{3,5},{5,7},{7,1},{8,10},{10,12},{12... | collective-permute-start | bytes 196616 | tf_op jit(solution)/shard_map/ppermute | solution.py:128
  175.9 6.2 %collective-permute-start.29 = (bf16[256,128]{1,0:T(8,128)(2,1)S(1)}, bf16[256,128]{1,0:T(8,128)(2,1)S(1)}, u32[]{:S(2)}, u32[]{:S(2)}) collective-permute-start(bf16[256,128]{1,0:T(8,128)(2,1)S(1)} %get-tuple-element.123), channel_id=1, source_target_pairs={{0,4},{2,6},{4,0},{6,2},{1,5},{3,7},{5,1},{7,3},{8,12},{10,14},{12... | collective-permute-start | bytes 196616 | tf_op jit(solution)/shard_map/ppermute | solution.py:128
  178.9 4.3 %collective-permute-start.30 = (bf16[256,128]{1,0:T(8,128)(2,1)S(1)}, bf16[256,128]{1,0:T(8,128)(2,1)S(1)}, u32[]{:S(2)}, u32[]{:S(2)}) collective-permute-start(bf16[256,128]{1,0:T(8,128)(2,1)S(1)} %get-tuple-element.124), channel_id=1, source_target_pairs={{0,6},{2,0},{4,2},{6,4},{1,7},{3,1},{5,3},{7,5},{8,14},{10,8},{12,... | collective-permute-start | bytes 196616 | tf_op jit(solution)/shard_map/ppermute | solution.py:128
  185.3 5.6 %copy-start.19 = (bf16[4,256,128]{2,1,0:T(8,128)(2,1)S(1)}, bf16[4,256,128]{2,1,0:T(8,128)(2,1)}, u32[]{:S(2)}) copy-start(bf16[4,256,128]{2,1,0:T(8,128)(2,1)} %copy-done.18) | copy-start | bytes 786436
  185.3 33.0 %all-to-all-start = ((bf16[16,2,32,1024]{3,2,1,0:T(8,128)(2,1)}), bf16[16,2,32,1024]{3,2,1,0:T(8,128)(2,1)}, u32[]{:S(2)}, u32[]{:S(2)}) async-start(bf16[16,2,32,1024]{3,2,1,0:T(8,128)(2,1)} %copy-done.7), calls=%async_computation | async-start | bytes 4194304 | tf_op jit(solution)/shard_map/all_to_all | solution.py:615
  190.8 10.7 %collective-permute-start.31 = (bf16[4,256,128]{2,1,0:T(8,128)(2,1)}, bf16[4,256,128]{2,1,0:T(8,128)(2,1)S(1)}, u32[]{:S(2)}, u32[]{:S(2)}) collective-permute-start(bf16[4,256,128]{2,1,0:T(8,128)(2,1)} %copy-done.28), channel_id=1, source_target_pairs={{0,1},{1,0},{2,3},{3,2},{4,5},{5,4},{6,7},{7,6},{8,9},{9,8},{10,11... | collective-permute-start | bytes 786440 | tf_op jit(solution)/shard_map/ppermute | solution.py:128
  194.7 6.9 %copy-start.26 = (bf16[4,256,128]{2,1,0:T(8,128)(2,1)S(1)}, bf16[4,256,128]{2,1,0:T(8,128)(2,1)}, u32[]{:S(2)}) copy-start(bf16[4,256,128]{2,1,0:T(8,128)(2,1)} %copy-done.25) | copy-start | bytes 786436
  220.3 4.9 %collective-permute-start.32 = (f32[16,1024]{1,0:T(8,128)S(1)}, f32[16,1024]{1,0:T(8,128)S(1)}, u32[]{:S(2)}, u32[]{:S(2)}) collective-permute-start(f32[16,1024]{1,0:T(8,128)S(1)} %get-tuple-element.138), channel_id=1, source_target_pairs={{0,32},{32,0},{64,96},{96,64},{1,33},{33,1},{65,97},{97,65},{2,34}... | collective-permute-start | bytes 196616 | tf_op jit(solution)/shard_map/ppermute | solution.py:123
  220.6 4.6 %collective-permute-start.33 = (f32[16,1024]{1,0:T(8,128)S(1)}, f32[16,1024]{1,0:T(8,128)S(1)}, u32[]{:S(2)}, u32[]{:S(2)}) collective-permute-start(f32[16,1024]{1,0:T(8,128)S(1)} %get-tuple-element.139), channel_id=1, source_target_pairs={{0,1},{1,0},{2,3},{3,2},{4,5},{5,4},{6,7},{7,6},{8,9},{9,8},{10,11... | collective-permute-start | bytes 196616 | tf_op jit(solution)/shard_map/ppermute | solution.py:123
  220.6 4.6 %collective-permute-start.34 = (f32[16,1024]{1,0:T(8,128)S(1)}, f32[16,1024]{1,0:T(8,128)S(1)}, u32[]{:S(2)}, u32[]{:S(2)}) collective-permute-start(f32[16,1024]{1,0:T(8,128)S(1)} %get-tuple-element.140), channel_id=1, source_target_pairs={{0,33},{1,32},{32,1},{33,0},{64,97},{65,96},{96,65},{97,64},{2,35}... | collective-permute-start | bytes 196616 | tf_op jit(solution)/shard_map/ppermute | solution.py:619
  (18 other events, 24.9 us)
Sparse Core Ops, SparseCore 0:
  21.3 65.1 all-gather.1

commit v4 on v3

--- a/solution.py
+++ b/solution.py
@@ -145,7 +145,7 @@
     (row,) = small_call(row_body, where, terms, [low])
     rows_before = [give_to(row, "z", k) for k in range(1, n)]
     filled_plane = fill_plane(row, filled_row)
-    rows_before = after(rows_before, filled_plane)
+    rows_before = after(rows_before, filled_plane[-1] if reverse else filled_plane)
     own, *out = small_call(
         functools.partial(plane_body, reverse),
         where,
@@ -154,10 +154,10 @@
     )
     sums = [own] + [give_to(x, "y", k) for k, x in enumerate(out, 1)]
     filled_core = fill_core(out, filled_plane)
+    sums = after(sums, filled_core)
     mine, give = small_call(
         functools.partial(core_body, reverse), where, [parts, other] + sums, [half] * 2
     )
-    filled_core = after(filled_core, give)
     got = give_to(give, "c", 1)
     shape = (heads // 2, d, e)
     return (mine.reshape(shape), got.reshape(shape)), filled_row, filled_plane, filled_core
@@ -553,16 +553,18 @@
     own_piece = lax.dynamic_slice_in_dim(out_weight, at_ctx * piece, piece, 0)
     pieces = [shift(own_piece, "x", by) for by in range(1, CH)]
     state = local_state(k, v)
-    pieces, sent_rows, q_next = lax.optimization_barrier((pieces, grad_rows, q, state))[:3]
+    half_cols = model_width // 2
+    side = at_x % 2
+    near_cols = lax.dynamic_slice_in_dim(grad_rows, side * half_cols, half_cols, 1)
+    far_cols = lax.dynamic_slice_in_dim(grad_rows, (1 - side) * half_cols, half_cols, 1)
+    pieces, near_cols, far_cols, sent_rows, q_next = lax.optimization_barrier(
+        (pieces, near_cols, far_cols, grad_rows, q, state)
+    )[:5]
     gathered = lax.all_gather(jnp.concatenate(pieces, axis=0), CTX, axis=0, tiled=True)
     gathered = gathered.reshape(blocks_n, CH - 1, piece, model_width)
     gathered = pltpu.with_memory_space_constraint(gathered, pltpu.HBM)
     own_weight = pltpu.with_memory_space_constraint(out_weight, pltpu.HBM)
 
-    half_cols = model_width // 2
-    side = at_x % 2
-    near_cols = lax.dynamic_slice_in_dim(sent_rows, side * half_cols, half_cols, 1)
-    far_cols = lax.dynamic_slice_in_dim(sent_rows, (1 - side) * half_cols, half_cols, 1)
     grads_all = [
         near_cols,
         partner(far_cols, "x", 1),
@@ -604,16 +606,22 @@
             keep_body, mine, [after(turned, sent), extra], grads_all, shape, False
         )
 
-    later, _, _, partial = carry(
-        lg, where, at_core, True, first_half, second_half, lambda sent, done: done
+    def halves(sent, done):
+        partial = second_half(sent, done)
+        return lax.all_to_all(partial, ("z", "y"), 0, 0, tiled=True), partial
+
+    def rest(sent, done):
+        grads = local_grads(where, q, k, v, weights, after(ga, sent), carried)
+        rows = layer_rows(where, near, after(far, grads), own_weight, gathered)
+        return grads, rows
+
+    later, _, (parts, _), (grads, layer_out) = carry(
+        lg, where, at_core, True, first_half, halves, rest
     )
-    ga = after(ga, partial)
-    grad_query, pk, pv = local_grads(where, q, k, v, weights, ga, carried)
-    layer_out = layer_rows(where, near, after(far, partial, later), own_weight, gathered)
+    grad_query, pk, pv = grads
     grad_key, grad_value = later_grads(where, k, v, later, pk, pv)
 
-    parts = lax.all_to_all(partial, ("z", "y"), 0, 0, tiled=True)
-    parts = after(parts, layer_out, grad_key)
+    parts = after(parts, layer_out, later[0])
     token_count = seqs * blocks_n * tok_rows
     own, to_x, to_c, to_both = sum_parts(where, parts, 1.0 / math.sqrt(token_count))
     both = lax.ppermute(to_both, ("x", "c"), [(d, d ^ 3) for d in range(2 * seqs)])

time: 235 us -> 252 us (1.072)
  waiting for transfers between devices: 82.8 us -> 90.4 us
  starting transfers between devices: 48.5 us -> 53.3 us
  Pallas kernels: 58 us -> 61.2 us
    ppermute x23, waiting for transfers between devices: 13.8 us -> 30.6 us  [give_to(): return lax.ppermute(x, axis, [(d, (d + by) % n) for d in range(n)])]
    ppermute x8, waiting for transfers between devices: 50.8 us -> 43 us  [partner(): lax.ppermute(x, axis, [(d, d ^ bits) for d in range(lax.axis_size(axis))])]
    ppermute x23, starting transfers between devices: 29 us -> 34.5 us  [give_to(): return lax.ppermute(x, axis, [(d, (d + by) % n) for d in range(n)])]
    all_to_all x1, waiting for transfers between devices: 2.99 us -> 0.01 us  [halves(): return (lax.all_to_all(partial, ('z', 'y'), 0, 0, tiled=True), partial)]
    unnamed x58 -> x76, local copies, waits for them, and re-layouts: 18.2 us -> 18.8 us
  transfers between devices with their start and end apart: 37 -> 37, of which waited for: 17 -> 16; matrix products, arithmetic and copies ran while one was open for 4% -> 4% of each run, Pallas kernels for 20% -> 20%
where the time goes in v4:
time: 252 us; the launch traced here: 250 us
  waiting for transfers between devices  90.4 us (36%)
  Pallas kernels  61.2 us (24%)
  starting transfers between devices  53.3 us (21%)
  local copies, waits for them, and re-layouts  24.8 us (10%)
  between operations  14.4 us (6%)
  matrix products  4.61 us (2%)
    ppermute x8, waiting for transfers between devices, partner(): lax.ppermute(x, axis, [(d, d ^ bits) for d in range(lax.axis_size(axis))])  43 us
    ppermute x23, starting transfers between devices, give_to(): return lax.ppermute(x, axis, [(d, (d + by) % n) for d in range(n)])  34.5 us
    ppermute x23, waiting for transfers between devices, give_to(): return lax.ppermute(x, axis, [(d, (d + by) % n) for d in range(n)])  30.6 us
    unnamed x76, local copies, waits for them, and re-layouts  18.8 us
    all_gather x1, waiting for transfers between devices, layer(): lax.all_gather(jnp.concatenate(pieces, axis=0), CTX, axis=0, tiled=True)  14.4 us
    pallas_call x1, Pallas kernels, layer_rows(): pl.pallas_call(layer_body, grid_spec=pltpu.PrefetchScalarGridSpec(num_sca...  11.8 us
    pallas_call x2, Pallas kernels, weight_half(): pl.pallas_call(body, grid_spec=pltpu.PrefetchScalarGridSpec(num_scalar_pr...  10.4 us
    pallas_call x1, Pallas kernels, grad_attn(): pl.pallas_call(grad_attn_body, grid_spec=pltpu.PrefetchScalarGridSpec(num...  9.72 us
  transfers between devices with their start and end apart: 37, of which 16 were waited for; matrix products, arithmetic and copies ran while one was open for 4% of the time, Pallas kernels for 20%

profile of v4, /device:TPU:0, one launch (start us, length us, event | category | flops | bytes accessed | tf_op | source)
XLA Modules:
  0.0 250.4 jit_solution(16638774554411024651)
XLA Ops:
  8.1 2.9 %collective-permute-start = (bf16[16,4096]{1,0:T(8,128)(2,1)S(1)}, bf16[16,4096]{1,0:T(8,128)(2,1)S(1)}, u32[]{:S(2)}, u32[]{:S(2)}) collective-permute-start(bf16[16,4096]{1,0:T(8,128)(2,1)S(1)} %constant_dynamic-slice_fusion), channel_id=1, source_target_pairs={{32,0},{64,32},{96,64},{0,96},{33,1},{65,33},{97,65},{1,97},{34,2}... | collective-permute-start | bytes 393224 | tf_op jit(solution)/shard_map/ppermute | solution.py:527
  12.8 3.3 %dynamic-slice_bitcast_fusion = (bf16[256,2048]{1,0:T(8,128)(2,1)}, bf16[256,2048]{1,0:T(8,128)(2,1)}) fusion(bf16[1,256,4096]{2,1,0:T(8,128)(2,1)} %param.11, s32[]{:T(128)S(6)} %select_n.49, s32[]{:T(128)S(6)} %select_n.48), kind=kLoop, calls=%fused_computation | loop fusion | bytes 4194312 | tf_op jit(solution)/shard_map/dynamic_slice | solution.py:559
  19.0 1.5 collective-permute-done.2
  20.5 1.7 pad_maximum_fusion
  22.2 1.7 dynamic-slice_bitcast_fusion.3
  23.9 1.7 collective-permute-done.3.r_ref
  27.2 1.6 collective-permute-start.4
  28.9 2.9 %collective-permute-start.5 = (bf16[256,128]{1,0:T(8,128)(2,1)S(1)}, bf16[256,128]{1,0:T(8,128)(2,1)S(1)}, u32[]{:S(2)}, u32[]{:S(2)}) collective-permute-start(bf16[256,128]{1,0:T(8,128)(2,1)S(1)} %get-tuple-element.84), channel_id=1, source_target_pairs={{0,4},{2,6},{4,0},{6,2},{1,5},{3,7},{5,1},{7,3},{8,12},{10,14},{12... | collective-permute-start | bytes 196616 | tf_op jit(solution)/shard_map/ppermute | solution.py:128
  31.8 1.3 collective-permute-start.6
  33.1 3.0 %local_scores.1 = (bf16[16,256,256]{2,1,0:T(8,128)(2,1)S(1)}, f32[256,2048]{1,0:T(8,128)S(1)}) custom-call(bf16[256,2048]{1,0:T(8,128)(2,1)S(1)} %bitcast.38, bf16[256,2048]{1,0:T(8,128)(2,1)S(1)} %bitcast.43, bf16[256,2048]{1,0:T(8,128)(2,1)S(1)} %bitcast.47), custom_call_target="tpu_custom_call" | custom-call | flops 536870912 | bytes 7340032 | tf_op jit(solution)/shard_map/local_scores/pallas_call | solution.py:182
  36.1 1.3 copy-done.13
  37.5 1.3 copy-done.15
  39.4 2.0 collective-permute-start.7
  41.4 3.6 %collective-permute-start.8 = (bf16[256,128]{1,0:T(8,128)(2,1)S(1)}, bf16[256,128]{1,0:T(8,128)(2,1)S(1)}, u32[]{:S(2)}, u32[]{:S(2)}) collective-permute-start(bf16[256,128]{1,0:T(8,128)(2,1)S(1)} %shard_map.102), channel_id=1, source_target_pairs={{0,16},{8,24},{16,0},{24,8},{1,17},{9,25},{17,1},{25,9},{2,18},{10... | collective-permute-start | bytes 196616 | tf_op jit(solution)/shard_map/ppermute | solution.py:128
  46.0 4.6 %fusion.gn_ref = f32[256,512]{1,0:T(8,128)} fusion(bf16[256,4096]{1,0:T(8,128)(2,1)S(1)} %bitcast.50, bf16[512,4096]{1,0:T(8,128)(2,1)} %own_ref.1), kind=kOutput, calls=%fused_computation.6 | convolution fusion | flops 1073741824 | bytes 6815744 | tf_op jit(solution)/shard_map/dot_general | solution.py:21
  52.1 1.8 collective-permute-start.11
  54.9 2.0 collective-permute-done.10.p1
  58.5 1.4 shard_map.104
  60.0 1.6 collective-permute-start.23
  61.5 2.5 %collective-permute-start.22 = (bf16[256,2048]{1,0:T(8,128)(2,1)}, bf16[256,2048]{1,0:T(8,128)(2,1)}, u32[]{:S(2)}, u32[]{:S(2)}) collective-permute-start(bf16[256,2048]{1,0:T(8,128)(2,1)} %get-tuple-element.125.rest_0_), channel_id=1, source_target_pairs={{0,64},{32,96},{64,0},{96,32},{1,65},{33,97},{65,1},{97,33},{2,66}... | collective-permute-start | bytes 3145736 | tf_op jit(solution)/shard_map/ppermute | solution.py:123
  64.0 1.6 copy-done.16
  65.6 4.8 %attend.1 = (bf16[256,1024]{1,0:T(8,128)(2,1)}, bf16[256,1024]{1,0:T(8,128)(2,1)S(1)}, f32[4,256,512]{2,1,0:T(8,128)S(1)}) custom-call(s32[8]{0:T(128)S(1)} %stack.59.w_ref, bf16[256,2048]{1,0:T(8,128)(2,1)S(1)} %bitcast.39, f32[256,2048]{1,0:T(8,128)S(1)} %copy-done.16, bf16[8,128,128]{2,1,0:T(8,128)(2,1)S(1)} %bitcast.58, ...), custom_call_target="tpu_custom_call" | custom-call | flops 134217728 | bytes 6291456 | tf_op jit(solution)/shard_map/attend/pallas_call | solution.py:228
  73.0 14.4 %all-gather.2.cloned.1.call-done = bf16[1536,4096]{1,0:T(8,128)(2,1)} async-done(((bf16[48,4096]{1,0:T(8,128)(2,1)}), bf16[1536,4096]{1,0:T(8,128)(2,1)}) %all-gather.2.cloned.1.call-update) | async-done | bytes 12582928 | tf_op jit(solution)/shard_map/all_gather | solution.py:563
  87.4 1.6 copy-done.4
  89.0 9.7 %grad_attn.1 = (bf16[4,256,512]{2,1,0:T(8,128)(2,1)S(1)}, bf16[16,128,128]{2,1,0:T(8,128)(2,1)S(1)}) custom-call(s32[8]{0:T(128)S(1)} %stack.54.w_ref.i_ref, bf16[256,2048]{1,0:T(8,128)(2,1)S(1)} %bitcast.40, f32[4,256,512]{2,1,0:T(8,128)} %copy-done.12, f32[256,512]{1,0:T(8,128)} %fusion.gn_ref, f32[1,2048]{1,0:T(1,128)S(1)} %bitcast.63, ...), custom_call_target="tpu_custom_call" | custom-call | flops 3355443200 | bytes 18874368 | tf_op jit(solution)/shard_map/grad_attn/pallas_call | solution.py:276
  99.1 20.4 %collective-permute-done.18.n1 = bf16[256,1024]{1,0:T(8,128)(2,1)} collective-permute-done((bf16[256,1024]{1,0:T(8,128)(2,1)}, bf16[256,1024]{1,0:T(8,128)(2,1)}, u32[]{:S(2)}, u32[]{:S(2)}) %collective-permute-start.18) | collective-permute-done | bytes 524320 | tf_op jit(solution)/shard_map/ppermute | solution.py:123
  120.6 2.0 collective-permute-start.20
  123.2 11.4 %collective-permute-done.19.n2 = bf16[256,1024]{1,0:T(8,128)(2,1)S(1)} collective-permute-done((bf16[256,1024]{1,0:T(8,128)(2,1)S(1)}, bf16[256,1024]{1,0:T(8,128)(2,1)S(1)}, u32[]{:S(2)}, u32[]{:S(2)}) %collective-permute-start.19) | collective-permute-done | bytes 524320 | tf_op jit(solution)/shard_map/ppermute | solution.py:123
  134.6 11.1 %collective-permute-done.20.n3 = bf16[256,1024]{1,0:T(8,128)(2,1)S(1)} collective-permute-done((bf16[256,1024]{1,0:T(8,128)(2,1)S(1)}, bf16[256,1024]{1,0:T(8,128)(2,1)S(1)}, u32[]{:S(2)}, u32[]{:S(2)}) %collective-permute-start.20) | collective-permute-done | bytes 524320 | tf_op jit(solution)/shard_map/ppermute | solution.py:123
  145.8 5.6 %weight_half.2 = (bf16[16,2,32,1024]{3,2,1,0:T(8,128)(2,1)S(1)}, bf16[4,1024,256]{2,1,0:T(8,128)(2,1)S(1)}) custom-call(s32[1]{0:T(128)S(6)} %sub.25.i_ref, bf16[256,1024]{1,0:T(8,128)(2,1)} %get-tuple-element.121.n0.near_ref, bf16[256,1024]{1,0:T(8,128)(2,1)} %collective-permute-done.18.n1, bf16[256,1024]{1,0:T(8,128)(2,1)S(1)} %collective-permute-done.19.n2, ...), custom_call_target="tpu_custom_call" | custom-call | flops 2147483648 | bytes 8388608 | tf_op jit(solution)/shard_map/weight_half/pallas_call | solution.py:466
  151.5 1.4 collective-permute-start.15
  152.9 3.5 %collective-permute-start.16 = (bf16[256,128]{1,0:T(8,128)(2,1)S(1)}, bf16[256,128]{1,0:T(8,128)(2,1)S(1)}, u32[]{:S(2)}, u32[]{:S(2)}) collective-permute-start(bf16[256,128]{1,0:T(8,128)(2,1)S(1)} %get-tuple-element.119), channel_id=1, source_target_pairs={{0,4},{2,6},{4,0},{6,2},{1,5},{3,7},{5,1},{7,3},{8,12},{10,14},{12... | collective-permute-start | bytes 196616 | tf_op jit(solution)/shard_map/ppermute | solution.py:128
  157.6 2.6 %collective-permute-done.16.refs_1_.t2 = bf16[256,128]{1,0:T(8,128)(2,1)S(1)} collective-permute-done((bf16[256,128]{1,0:T(8,128)(2,1)S(1)}, bf16[256,128]{1,0:T(8,128)(2,1)S(1)}, u32[]{:S(2)}, u32[]{:S(2)}) %collective-permute-start.16) | collective-permute-done | bytes 65568 | tf_op jit(solution)/shard_map/ppermute | solution.py:128
  161.9 4.8 %weight_half.3 = bf16[16,2,32,1024]{3,2,1,0:T(8,128)(2,1)S(1)} custom-call(s32[1]{0:T(128)} %bitcast.7.i_ref, bf16[4,1024,256]{2,1,0:T(8,128)(2,1)S(1)} %get-tuple-element.133.nt_ref, bf16[16,2,32,1024]{3,2,1,0:T(8,128)(2,1)S(1)} %collective-permute-done.27.extra_ref, bf16[256,2048]{1,0:T(8,128)(2,1)S(1)} %copy-done.9, ...), custom_call_target="tpu_custom_call" | custom-call | flops 2147483648 | bytes 8388608 | tf_op jit(solution)/shard_map/weight_half/pallas_call | solution.py:466
  168.1 4.4 %all-to-all-start = ((bf16[16,2,32,1024]{3,2,1,0:T(8,128)(2,1)}), bf16[16,2,32,1024]{3,2,1,0:T(8,128)(2,1)}, u32[]{:S(2)}, u32[]{:S(2)}) async-start(bf16[16,2,32,1024]{3,2,1,0:T(8,128)(2,1)} %copy-done.5), calls=%async_computation | async-start | bytes 4194304 | tf_op jit(solution)/shard_map/all_to_all | solution.py:611
  172.6 1.8 collective-permute-start.24
  174.3 2.7 %collective-permute-start.25 = (bf16[256,128]{1,0:T(8,128)(2,1)}, bf16[256,128]{1,0:T(8,128)(2,1)S(1)}, u32[]{:S(2)}, u32[]{:S(2)}) collective-permute-start(bf16[256,128]{1,0:T(8,128)(2,1)} %copy-done.36), channel_id=1, source_target_pairs={{0,16},{8,24},{16,0},{24,8},{1,17},{9,25},{17,1},{25,9},{2,18},{10... | collective-permute-start | bytes 196616 | tf_op jit(solution)/shard_map/ppermute | solution.py:128
  177.0 1.4 collective-permute-start.26
  178.5 18.8 %collective-permute-done.24.z1 = bf16[256,128]{1,0:T(8,128)(2,1)S(1)} collective-permute-done((bf16[256,128]{1,0:T(8,128)(2,1)}, bf16[256,128]{1,0:T(8,128)(2,1)S(1)}, u32[]{:S(2)}, u32[]{:S(2)}) %collective-permute-start.24) | collective-permute-done | bytes 65568 | tf_op jit(solution)/shard_map/ppermute | solution.py:128
  202.8 3.2 %collective-permute-start.28 = (bf16[256,128]{1,0:T(8,128)(2,1)S(1)}, bf16[256,128]{1,0:T(8,128)(2,1)S(1)}, u32[]{:S(2)}, u32[]{:S(2)}) collective-permute-start(bf16[256,128]{1,0:T(8,128)(2,1)S(1)} %get-tuple-element.137), channel_id=1, source_target_pairs={{0,2},{2,4},{4,6},{6,0},{1,3},{3,5},{5,7},{7,1},{8,10},{10,12},{12... | collective-permute-start | bytes 196616 | tf_op jit(solution)/shard_map/ppermute | solution.py:128
  206.0 3.0 %collective-permute-start.29 = (bf16[256,128]{1,0:T(8,128)(2,1)S(1)}, bf16[256,128]{1,0:T(8,128)(2,1)S(1)}, u32[]{:S(2)}, u32[]{:S(2)}) collective-permute-start(bf16[256,128]{1,0:T(8,128)(2,1)S(1)} %get-tuple-element.138), channel_id=1, source_target_pairs={{0,4},{2,6},{4,0},{6,2},{1,5},{3,7},{5,1},{7,3},{8,12},{10,14},{12... | collective-permute-start | bytes 196616 | tf_op jit(solution)/shard_map/ppermute | solution.py:128
  209.9 1.6 copy-done.14
  212.8 7.7 %local_grads.1 = (bf16[256,2048]{1,0:T(8,128)(2,1)}, f32[4,256,512]{2,1,0:T(8,128)S(1)}, f32[4,256,512]{2,1,0:T(8,128)S(1)}) custom-call(s32[8]{0:T(128)S(1)} %stack.54.w_ref.i_ref, bf16[256,2048]{1,0:T(8,128)(2,1)S(1)} %bitcast.41, bf16[256,2048]{1,0:T(8,128)(2,1)S(1)} %bitcast.44, bf16[256,2048]{1,0:T(8,128)(2,1)S(1)} %bitcast.48, ...), custom_call_target="tpu_custom_call" | custom-call | flops 1073741824 | bytes 12582912 | tf_op jit(solution)/shard_map/local_grads/pallas_call | solution.py:322
  220.5 11.8 %layer_rows.1 = bf16[256,4096]{1,0:T(8,128)(2,1)} custom-call(s32[8]{0:T(128)S(1)} %stack.54.w_ref.i_ref, bf16[256,1024]{1,0:T(8,128)(2,1)} %get-tuple-element.121.n0.near_ref, bf16[256,1024]{1,0:T(8,128)(2,1)S(1)} %copy-done.29, bf16[512,4096]{1,0:T(8,128)(2,1)} %own_ref.1, bf16[32,3,16,4096]{3,2,1,0:T(8,128)(2,1)} %bitcast.65), custom_call_target="tpu_custom_call" | custom-call | flops 4294967296 | bytes 19922944 | tf_op jit(solution)/shard_map/layer_rows/pallas_call | solution.py:406
  233.1 2.1 sum_parts.1
  235.9 1.6 collective-permute-start.34
  237.5 1.6 copy-done.20
  239.1 3.2 %later_grads.1 = (bf16[256,2048]{1,0:T(8,128)(2,1)}, bf16[256,2048]{1,0:T(8,128)(2,1)}) custom-call(s32[8]{0:T(128)S(1)} %stack.54.w_ref.i_ref, bf16[256,2048]{1,0:T(8,128)(2,1)S(1)} %bitcast.45, bf16[256,2048]{1,0:T(8,128)(2,1)S(1)} %bitcast.49, bf16[8,128,128]{2,1,0:T(8,128)(2,1)S(1)} %bitcast.60, bf16[8,128,128]{2,1,0:T(8,128)(2,1)S(1)} %bitcast.61, ...), custom_call_target="tpu_custom_call" | custom-call | flops 268435456 | bytes 8388608 | tf_op jit(solution)/shard_map/later_grads/pallas_call | solution.py:363
  (130 shorter events, 32.4 us)
Async XLA Ops:
  7.2 80.2 %all-gather.2.cloned.1.call-start = ((), (), s32[]{:S(2)}) async-start(), calls=%async_computation.1 | async-start | bytes 12976128 | tf_op jit(solution)/shard_map/all_gather | solution.py:563
  8.1 10.0 %collective-permute-start = (bf16[16,4096]{1,0:T(8,128)(2,1)S(1)}, bf16[16,4096]{1,0:T(8,128)(2,1)S(1)}, u32[]{:S(2)}, u32[]{:S(2)}) collective-permute-start(bf16[16,4096]{1,0:T(8,128)(2,1)S(1)} %constant_dynamic-slice_fusion), channel_id=1, source_target_pairs={{32,0},{64,32},{96,64},{0,96},{33,1},{65,33},{97,65},{1,97},{34,2}... | collective-permute-start | bytes 393224 | tf_op jit(solution)/shard_map/ppermute | solution.py:527
  11.1 7.9 %collective-permute-start.1 = (bf16[16,4096]{1,0:T(8,128)(2,1)S(1)}, bf16[16,4096]{1,0:T(8,128)(2,1)S(1)}, u32[]{:S(2)}, u32[]{:S(2)}) collective-permute-start(bf16[16,4096]{1,0:T(8,128)(2,1)S(1)} %constant_dynamic-slice_fusion), channel_id=1, source_target_pairs={{64,0},{96,32},{0,64},{32,96},{65,1},{97,33},{1,65},{33,97},{66,2}... | collective-permute-start | bytes 393224 | tf_op jit(solution)/shard_map/ppermute | solution.py:527
  11.9 8.6 %collective-permute-start.2 = (bf16[16,4096]{1,0:T(8,128)(2,1)S(1)}, bf16[16,4096]{1,0:T(8,128)(2,1)}, u32[]{:S(2)}, u32[]{:S(2)}) collective-permute-start(bf16[16,4096]{1,0:T(8,128)(2,1)S(1)} %constant_dynamic-slice_fusion), channel_id=1, source_target_pairs={{96,0},{0,32},{32,64},{64,96},{97,1},{1,33},{33,65},{65,97},{98,2}... | collective-permute-start | bytes 393224 | tf_op jit(solution)/shard_map/ppermute | solution.py:527
  16.0 17.1 %copy-start = (bf16[1,256,2048]{2,1,0:T(8,128)(2,1)S(1)}, bf16[1,256,2048]{2,1,0:T(8,128)(2,1)}, u32[]{:S(2)}) copy-start(bf16[1,256,2048]{2,1,0:T(8,128)(2,1)} %param.6) | copy-start | bytes 3145732
  23.8 1.7 collective-permute-start.3
  23.9 22.1 %copy-start.3 = (bf16[1,256,4096]{2,1,0:T(8,128)(2,1)S(1)}, bf16[1,256,4096]{2,1,0:T(8,128)(2,1)}, u32[]{:S(2)}) copy-start(bf16[1,256,4096]{2,1,0:T(8,128)(2,1)} %param.11) | copy-start | bytes 6291460
  26.6 12.8 %copy-start.23 = (bf16[4,256,128]{2,1,0:T(8,128)(2,1)}, bf16[4,256,128]{2,1,0:T(8,128)(2,1)S(1)}, u32[]{:S(2)}) copy-start(bf16[4,256,128]{2,1,0:T(8,128)(2,1)S(1)} %collective-permute-done.3.r_ref) | copy-start | bytes 786436
  27.2 11.6 %collective-permute-start.4 = (bf16[256,128]{1,0:T(8,128)(2,1)S(1)}, bf16[256,128]{1,0:T(8,128)(2,1)S(1)}, u32[]{:S(2)}, u32[]{:S(2)}) collective-permute-start(bf16[256,128]{1,0:T(8,128)(2,1)S(1)} %get-tuple-element.83), channel_id=1, source_target_pairs={{0,2},{2,4},{4,6},{6,0},{1,3},{3,5},{5,7},{7,1},{8,10},{10,12},{12... | collective-permute-start | bytes 196616 | tf_op jit(solution)/shard_map/ppermute | solution.py:128
  28.9 9.9 %collective-permute-start.5 = (bf16[256,128]{1,0:T(8,128)(2,1)S(1)}, bf16[256,128]{1,0:T(8,128)(2,1)S(1)}, u32[]{:S(2)}, u32[]{:S(2)}) collective-permute-start(bf16[256,128]{1,0:T(8,128)(2,1)S(1)} %get-tuple-element.84), channel_id=1, source_target_pairs={{0,4},{2,6},{4,0},{6,2},{1,5},{3,7},{5,1},{7,3},{8,12},{10,14},{12... | collective-permute-start | bytes 196616 | tf_op jit(solution)/shard_map/ppermute | solution.py:128
  31.8 7.0 %collective-permute-start.6 = (bf16[256,128]{1,0:T(8,128)(2,1)S(1)}, bf16[256,128]{1,0:T(8,128)(2,1)S(1)}, u32[]{:S(2)}, u32[]{:S(2)}) collective-permute-start(bf16[256,128]{1,0:T(8,128)(2,1)S(1)} %get-tuple-element.85), channel_id=1, source_target_pairs={{0,6},{2,0},{4,2},{6,4},{1,7},{3,1},{5,3},{7,5},{8,14},{10,8},{12,... | collective-permute-start | bytes 196616 | tf_op jit(solution)/shard_map/ppermute | solution.py:128
  39.4 19.1 %copy-start.8 = (bf16[16,128,128]{2,1,0:T(8,128)(2,1)S(1)}, bf16[16,128,128]{2,1,0:T(8,128)(2,1)}, u32[]{:S(2)}) copy-start(bf16[16,128,128]{2,1,0:T(8,128)(2,1)} %copy-done.6) | copy-start | bytes 1572868
  39.4 24.6 %copy-start.37 = (f32[2048]{0:T(1024)S(1)}, f32[2048]{0:T(1024)}, u32[]{:S(2)}) copy-start(f32[2048]{0:T(1024)} %param.9) | copy-start | bytes 24580
  39.4 11.2 %collective-permute-start.7 = (bf16[256,128]{1,0:T(8,128)(2,1)S(1)}, bf16[256,128]{1,0:T(8,128)(2,1)S(1)}, u32[]{:S(2)}, u32[]{:S(2)}) collective-permute-start(bf16[256,128]{1,0:T(8,128)(2,1)S(1)} %shard_map.102), channel_id=1, source_target_pairs={{0,8},{8,16},{16,24},{24,0},{1,9},{9,17},{17,25},{25,1},{2,10},{10... | collective-permute-start | bytes 196616 | tf_op jit(solution)/shard_map/ppermute | solution.py:128
  41.4 17.1 %copy-start.24 = (bf16[4,256,128]{2,1,0:T(8,128)(2,1)S(1)}, bf16[4,256,128]{2,1,0:T(8,128)(2,1)}, u32[]{:S(2)}) copy-start(bf16[4,256,128]{2,1,0:T(8,128)(2,1)} %copy-done.23) | copy-start | bytes 786436
  41.4 9.2 %collective-permute-start.8 = (bf16[256,128]{1,0:T(8,128)(2,1)S(1)}, bf16[256,128]{1,0:T(8,128)(2,1)S(1)}, u32[]{:S(2)}, u32[]{:S(2)}) collective-permute-start(bf16[256,128]{1,0:T(8,128)(2,1)S(1)} %shard_map.102), channel_id=1, source_target_pairs={{0,16},{8,24},{16,0},{24,8},{1,17},{9,25},{17,1},{25,9},{2,18},{10... | collective-permute-start | bytes 196616 | tf_op jit(solution)/shard_map/ppermute | solution.py:128
  45.0 5.6 %collective-permute-start.9 = (bf16[256,128]{1,0:T(8,128)(2,1)S(1)}, bf16[256,128]{1,0:T(8,128)(2,1)S(1)}, u32[]{:S(2)}, u32[]{:S(2)}) collective-permute-start(bf16[256,128]{1,0:T(8,128)(2,1)S(1)} %shard_map.102), channel_id=1, source_target_pairs={{0,24},{8,0},{16,8},{24,16},{1,25},{9,1},{17,9},{25,17},{2,26},{10... | collective-permute-start | bytes 196616 | tf_op jit(solution)/shard_map/ppermute | solution.py:128
  51.4 5.5 %collective-permute-start.10 = (bf16[256,128]{1,0:T(8,128)(2,1)S(1)}, bf16[256,128]{1,0:T(8,128)(2,1)S(1)}, u32[]{:S(2)}, u32[]{:S(2)}) collective-permute-start(bf16[256,128]{1,0:T(8,128)(2,1)S(1)} %get-tuple-element.100), channel_id=1, source_target_pairs={{0,2},{2,4},{4,6},{6,0},{1,3},{3,5},{5,7},{7,1},{8,10},{10,12},{12... | collective-permute-start | bytes 196616 | tf_op jit(solution)/shard_map/ppermute | solution.py:128
  52.1 5.8 %collective-permute-start.11 = (bf16[256,128]{1,0:T(8,128)(2,1)S(1)}, bf16[256,128]{1,0:T(8,128)(2,1)S(1)}, u32[]{:S(2)}, u32[]{:S(2)}) collective-permute-start(bf16[256,128]{1,0:T(8,128)(2,1)S(1)} %get-tuple-element.101), channel_id=1, source_target_pairs={{0,4},{2,6},{4,0},{6,2},{1,5},{3,7},{5,1},{7,3},{8,12},{10,14},{12... | collective-permute-start | bytes 196616 | tf_op jit(solution)/shard_map/ppermute | solution.py:128
  53.9 4.6 %collective-permute-start.12 = (bf16[256,128]{1,0:T(8,128)(2,1)S(1)}, bf16[256,128]{1,0:T(8,128)(2,1)S(1)}, u32[]{:S(2)}, u32[]{:S(2)}) collective-permute-start(bf16[256,128]{1,0:T(8,128)(2,1)S(1)} %get-tuple-element.102), channel_id=1, source_target_pairs={{0,6},{2,0},{4,2},{6,4},{1,7},{3,1},{5,3},{7,5},{8,14},{10,8},{12,... | collective-permute-start | bytes 196616 | tf_op jit(solution)/shard_map/ppermute | solution.py:128
  59.8 4.2 %collective-permute-start.13 = (bf16[4,256,128]{2,1,0:T(8,128)(2,1)}, bf16[4,256,128]{2,1,0:T(8,128)(2,1)}, u32[]{:S(2)}, u32[]{:S(2)}) collective-permute-start(bf16[4,256,128]{2,1,0:T(8,128)(2,1)} %get-tuple-element.108), channel_id=1, source_target_pairs={{0,1},{1,0},{2,3},{3,2},{4,5},{5,4},{6,7},{7,6},{8,9},{9,8},{10,11... | collective-permute-start | bytes 786440 | tf_op jit(solution)/shard_map/ppermute | solution.py:128
  59.9 85.8 %collective-permute-start.21 = (bf16[256,2048]{1,0:T(8,128)(2,1)}, bf16[256,2048]{1,0:T(8,128)(2,1)}, u32[]{:S(2)}, u32[]{:S(2)}) collective-permute-start(bf16[256,2048]{1,0:T(8,128)(2,1)} %get-tuple-element.126), channel_id=1, source_target_pairs={{0,32},{32,0},{64,96},{96,64},{1,33},{33,1},{65,97},{97,65},{2,34}... | collective-permute-start | bytes 3145736 | tf_op jit(solution)/shard_map/ppermute | solution.py:123
  60.0 85.8 %collective-permute-start.23 = (bf16[256,2048]{1,0:T(8,128)(2,1)}, bf16[256,2048]{1,0:T(8,128)(2,1)}, u32[]{:S(2)}, u32[]{:S(2)}) collective-permute-start(bf16[256,2048]{1,0:T(8,128)(2,1)} %get-tuple-element.126), channel_id=1, source_target_pairs={{0,96},{32,64},{64,32},{96,0},{1,97},{33,65},{65,33},{97,1},{2,98}... | collective-permute-start | bytes 3145736 | tf_op jit(solution)/shard_map/ppermute | solution.py:123
  61.5 84.2 %collective-permute-start.22 = (bf16[256,2048]{1,0:T(8,128)(2,1)}, bf16[256,2048]{1,0:T(8,128)(2,1)}, u32[]{:S(2)}, u32[]{:S(2)}) collective-permute-start(bf16[256,2048]{1,0:T(8,128)(2,1)} %get-tuple-element.125.rest_0_), channel_id=1, source_target_pairs={{0,64},{32,96},{64,0},{96,32},{1,65},{33,97},{65,1},{97,33},{2,66}... | collective-permute-start | bytes 3145736 | tf_op jit(solution)/shard_map/ppermute | solution.py:123
  72.6 47.0 %collective-permute-start.18 = (bf16[256,1024]{1,0:T(8,128)(2,1)}, bf16[256,1024]{1,0:T(8,128)(2,1)}, u32[]{:S(2)}, u32[]{:S(2)}) collective-permute-start(bf16[256,1024]{1,0:T(8,128)(2,1)} %get-tuple-element.121.n0.near_ref), channel_id=1, source_target_pairs={{0,32},{32,0},{64,96},{96,64},{1,33},{33,1},{65,97},{97,65},{2,34}... | collective-permute-start | bytes 1572872 | tf_op jit(solution)/shard_map/ppermute | solution.py:123
  89.0 30.6 %copy-start.28 = (bf16[256,1024]{1,0:T(8,128)(2,1)S(1)}, bf16[256,1024]{1,0:T(8,128)(2,1)}, u32[]{:S(2)}) copy-start(bf16[256,1024]{1,0:T(8,128)(2,1)} %copy-done.27) | copy-start | bytes 1572868
  89.0 56.8 %copy-start.9 = (bf16[256,2048]{1,0:T(8,128)(2,1)S(1)}, bf16[256,2048]{1,0:T(8,128)(2,1)}, u32[]{:S(2)}) copy-start(bf16[256,2048]{1,0:T(8,128)(2,1)} %get-tuple-element.125.rest_0_) | copy-start | bytes 3145732
  98.7 23.8 %copy-start.10 = (bf16[16,128,128]{2,1,0:T(8,128)(2,1)}, bf16[16,128,128]{2,1,0:T(8,128)(2,1)S(1)}, u32[]{:S(2)}) copy-start(bf16[16,128,128]{2,1,0:T(8,128)(2,1)S(1)} %get-tuple-element.116) | copy-start | bytes 1572868
  98.7 52.7 %copy-start.21 = (bf16[4,256,512]{2,1,0:T(8,128)(2,1)}, bf16[4,256,512]{2,1,0:T(8,128)(2,1)S(1)}, u32[]{:S(2)}) copy-start(bf16[4,256,512]{2,1,0:T(8,128)(2,1)S(1)} %get-tuple-element.140.ga_ref) | copy-start | bytes 3145732
  98.8 21.8 %collective-permute-start.14 = (bf16[4,256,128]{2,1,0:T(8,128)(2,1)S(1)}, bf16[4,256,128]{2,1,0:T(8,128)(2,1)S(1)}, u32[]{:S(2)}, u32[]{:S(2)}) collective-permute-start(bf16[4,256,128]{2,1,0:T(8,128)(2,1)S(1)} %dynamic-slice_bitcast_fusion.2), channel_id=1, source_target_pairs={{0,1},{1,0},{2,3},{3,2},{4,5},{5,4},{6,7},{7,6},{8,9},{9,8},{10,11... | collective-permute-start | bytes 786440 | tf_op jit(solution)/shard_map/ppermute | solution.py:128
  119.5 15.1 %collective-permute-start.19 = (bf16[256,1024]{1,0:T(8,128)(2,1)S(1)}, bf16[256,1024]{1,0:T(8,128)(2,1)S(1)}, u32[]{:S(2)}, u32[]{:S(2)}) collective-permute-start(bf16[256,1024]{1,0:T(8,128)(2,1)S(1)} %copy-done.28), channel_id=1, source_target_pairs={{0,64},{32,96},{64,0},{96,32},{1,65},{33,97},{65,1},{97,33},{2,66}... | collective-permute-start | bytes 1572872 | tf_op jit(solution)/shard_map/ppermute | solution.py:123
  120.6 30.8 %copy-start.25 = (bf16[4,256,128]{2,1,0:T(8,128)(2,1)}, bf16[4,256,128]{2,1,0:T(8,128)(2,1)S(1)}, u32[]{:S(2)}) copy-start(bf16[4,256,128]{2,1,0:T(8,128)(2,1)S(1)} %collective-permute-done.14.r_ref) | copy-start | bytes 786436
  120.6 25.2 %collective-permute-start.20 = (bf16[256,1024]{1,0:T(8,128)(2,1)S(1)}, bf16[256,1024]{1,0:T(8,128)(2,1)S(1)}, u32[]{:S(2)}, u32[]{:S(2)}) collective-permute-start(bf16[256,1024]{1,0:T(8,128)(2,1)S(1)} %copy-done.28), channel_id=1, source_target_pairs={{0,96},{32,64},{64,32},{96,0},{1,97},{33,65},{65,33},{97,1},{2,98}... | collective-permute-start | bytes 1572872 | tf_op jit(solution)/shard_map/ppermute | solution.py:123
  151.4 10.5 %collective-permute-start.27 = (bf16[16,2,32,1024]{3,2,1,0:T(8,128)(2,1)S(1)}, bf16[16,2,32,1024]{3,2,1,0:T(8,128)(2,1)S(1)}, u32[]{:S(2)}, u32[]{:S(2)}) collective-permute-start(bf16[16,2,32,1024]{3,2,1,0:T(8,128)(2,1)S(1)} %get-tuple-element.127), channel_id=1, source_target_pairs={{0,1},{1,0},{2,3},{3,2},{4,5},{5,4},{6,7},{7,6},{8,9},{9,8},{10,11... | collective-permute-start | bytes 6291464 | tf_op jit(solution)/shard_map/ppermute | solution.py:128
  151.5 6.1 %collective-permute-start.15 = (bf16[256,128]{1,0:T(8,128)(2,1)S(1)}, bf16[256,128]{1,0:T(8,128)(2,1)S(1)}, u32[]{:S(2)}, u32[]{:S(2)}) collective-permute-start(bf16[256,128]{1,0:T(8,128)(2,1)S(1)} %get-tuple-element.118), channel_id=1, source_target_pairs={{0,2},{2,4},{4,6},{6,0},{1,3},{3,5},{5,7},{7,1},{8,10},{10,12},{12... | collective-permute-start | bytes 196616 | tf_op jit(solution)/shard_map/ppermute | solution.py:128
  152.9 7.3 %collective-permute-start.16 = (bf16[256,128]{1,0:T(8,128)(2,1)S(1)}, bf16[256,128]{1,0:T(8,128)(2,1)S(1)}, u32[]{:S(2)}, u32[]{:S(2)}) collective-permute-start(bf16[256,128]{1,0:T(8,128)(2,1)S(1)} %get-tuple-element.119), channel_id=1, source_target_pairs={{0,4},{2,6},{4,0},{6,2},{1,5},{3,7},{5,1},{7,3},{8,12},{10,14},{12... | collective-permute-start | bytes 196616 | tf_op jit(solution)/shard_map/ppermute | solution.py:128
  156.4 4.3 %collective-permute-start.17 = (bf16[256,128]{1,0:T(8,128)(2,1)S(1)}, bf16[256,128]{1,0:T(8,128)(2,1)S(1)}, u32[]{:S(2)}, u32[]{:S(2)}) collective-permute-start(bf16[256,128]{1,0:T(8,128)(2,1)S(1)} %get-tuple-element.120), channel_id=1, source_target_pairs={{0,6},{2,0},{4,2},{6,4},{1,7},{3,1},{5,3},{7,5},{8,14},{10,8},{12,... | collective-permute-start | bytes 196616 | tf_op jit(solution)/shard_map/ppermute | solution.py:128
  168.1 65.0 %all-to-all-start = ((bf16[16,2,32,1024]{3,2,1,0:T(8,128)(2,1)}), bf16[16,2,32,1024]{3,2,1,0:T(8,128)(2,1)}, u32[]{:S(2)}, u32[]{:S(2)}) async-start(bf16[16,2,32,1024]{3,2,1,0:T(8,128)(2,1)} %copy-done.5), calls=%async_computation | async-start | bytes 4194304 | tf_op jit(solution)/shard_map/all_to_all | solution.py:611
  172.6 24.7 %collective-permute-start.24 = (bf16[256,128]{1,0:T(8,128)(2,1)}, bf16[256,128]{1,0:T(8,128)(2,1)S(1)}, u32[]{:S(2)}, u32[]{:S(2)}) collective-permute-start(bf16[256,128]{1,0:T(8,128)(2,1)} %copy-done.36), channel_id=1, source_target_pairs={{0,8},{8,16},{16,24},{24,0},{1,9},{9,17},{17,25},{25,1},{2,10},{10... | collective-permute-start | bytes 196616 | tf_op jit(solution)/shard_map/ppermute | solution.py:128
  174.3 24.0 %collective-permute-start.25 = (bf16[256,128]{1,0:T(8,128)(2,1)}, bf16[256,128]{1,0:T(8,128)(2,1)S(1)}, u32[]{:S(2)}, u32[]{:S(2)}) collective-permute-start(bf16[256,128]{1,0:T(8,128)(2,1)} %copy-done.36), channel_id=1, source_target_pairs={{0,16},{8,24},{16,0},{24,8},{1,17},{9,25},{17,1},{25,9},{2,18},{10... | collective-permute-start | bytes 196616 | tf_op jit(solution)/shard_map/ppermute | solution.py:128
  177.0 22.5 %collective-permute-start.26 = (bf16[256,128]{1,0:T(8,128)(2,1)}, bf16[256,128]{1,0:T(8,128)(2,1)S(1)}, u32[]{:S(2)}, u32[]{:S(2)}) collective-permute-start(bf16[256,128]{1,0:T(8,128)(2,1)} %copy-done.36), channel_id=1, source_target_pairs={{0,24},{8,0},{16,8},{24,16},{1,25},{9,1},{17,9},{25,17},{2,26},{10... | collective-permute-start | bytes 196616 | tf_op jit(solution)/shard_map/ppermute | solution.py:128
  202.8 29.5 %collective-permute-start.28 = (bf16[256,128]{1,0:T(8,128)(2,1)S(1)}, bf16[256,128]{1,0:T(8,128)(2,1)S(1)}, u32[]{:S(2)}, u32[]{:S(2)}) collective-permute-start(bf16[256,128]{1,0:T(8,128)(2,1)S(1)} %get-tuple-element.137), channel_id=1, source_target_pairs={{0,2},{2,4},{4,6},{6,0},{1,3},{3,5},{5,7},{7,1},{8,10},{10,12},{12... | collective-permute-start | bytes 196616 | tf_op jit(solution)/shard_map/ppermute | solution.py:128
  206.0 26.3 %collective-permute-start.29 = (bf16[256,128]{1,0:T(8,128)(2,1)S(1)}, bf16[256,128]{1,0:T(8,128)(2,1)S(1)}, u32[]{:S(2)}, u32[]{:S(2)}) collective-permute-start(bf16[256,128]{1,0:T(8,128)(2,1)S(1)} %get-tuple-element.138), channel_id=1, source_target_pairs={{0,4},{2,6},{4,0},{6,2},{1,5},{3,7},{5,1},{7,3},{8,12},{10,14},{12... | collective-permute-start | bytes 196616 | tf_op jit(solution)/shard_map/ppermute | solution.py:128
  208.9 23.4 %collective-permute-start.30 = (bf16[256,128]{1,0:T(8,128)(2,1)S(1)}, bf16[256,128]{1,0:T(8,128)(2,1)S(1)}, u32[]{:S(2)}, u32[]{:S(2)}) collective-permute-start(bf16[256,128]{1,0:T(8,128)(2,1)S(1)} %get-tuple-element.139), channel_id=1, source_target_pairs={{0,6},{2,0},{4,2},{6,4},{1,7},{3,1},{5,3},{7,5},{8,14},{10,8},{12,... | collective-permute-start | bytes 196616 | tf_op jit(solution)/shard_map/ppermute | solution.py:128
  233.0 4.5 %collective-permute-start.31 = (bf16[4,256,128]{2,1,0:T(8,128)(2,1)S(1)}, bf16[4,256,128]{2,1,0:T(8,128)(2,1)S(1)}, u32[]{:S(2)}, u32[]{:S(2)}) collective-permute-start(bf16[4,256,128]{2,1,0:T(8,128)(2,1)S(1)} %get-tuple-element.151), channel_id=1, source_target_pairs={{0,1},{1,0},{2,3},{3,2},{4,5},{5,4},{6,7},{7,6},{8,9},{9,8},{10,11... | collective-permute-start | bytes 786440 | tf_op jit(solution)/shard_map/ppermute | solution.py:128
  235.3 7.0 %collective-permute-start.32 = (f32[16,1024]{1,0:T(8,128)S(1)}, f32[16,1024]{1,0:T(8,128)S(1)}, u32[]{:S(2)}, u32[]{:S(2)}) collective-permute-start(f32[16,1024]{1,0:T(8,128)S(1)} %get-tuple-element.156), channel_id=1, source_target_pairs={{0,32},{32,0},{64,96},{96,64},{1,33},{33,1},{65,97},{97,65},{2,34}... | collective-permute-start | bytes 196616 | tf_op jit(solution)/shard_map/ppermute | solution.py:123
  235.5 6.8 %collective-permute-start.33 = (f32[16,1024]{1,0:T(8,128)S(1)}, f32[16,1024]{1,0:T(8,128)S(1)}, u32[]{:S(2)}, u32[]{:S(2)}) collective-permute-start(f32[16,1024]{1,0:T(8,128)S(1)} %get-tuple-element.157), channel_id=1, source_target_pairs={{0,1},{1,0},{2,3},{3,2},{4,5},{5,4},{6,7},{7,6},{8,9},{9,8},{10,11... | collective-permute-start | bytes 196616 | tf_op jit(solution)/shard_map/ppermute | solution.py:123
  235.9 6.4 %collective-permute-start.34 = (f32[16,1024]{1,0:T(8,128)S(1)}, f32[16,1024]{1,0:T(8,128)S(1)}, u32[]{:S(2)}, u32[]{:S(2)}) collective-permute-start(f32[16,1024]{1,0:T(8,128)S(1)} %get-tuple-element.158), channel_id=1, source_target_pairs={{0,33},{1,32},{32,1},{33,0},{64,97},{65,96},{96,65},{97,64},{2,35}... | collective-permute-start | bytes 196616 | tf_op jit(solution)/shard_map/ppermute | solution.py:627
  (27 other events, 89.9 us)
Sparse Core Ops, SparseCore 0:
  22.3 65.0 all-gather.1

commit v5 on v4

--- a/solution.py
+++ b/solution.py
@@ -145,7 +145,7 @@
     (row,) = small_call(row_body, where, terms, [low])
     rows_before = [give_to(row, "z", k) for k in range(1, n)]
     filled_plane = fill_plane(row, filled_row)
-    rows_before = after(rows_before, filled_plane[-1] if reverse else filled_plane)
+    rows_before = after(rows_before, filled_plane)
     own, *out = small_call(
         functools.partial(plane_body, reverse),
         where,
@@ -154,7 +154,7 @@
     )
     sums = [own] + [give_to(x, "y", k) for k, x in enumerate(out, 1)]
     filled_core = fill_core(out, filled_plane)
-    sums = after(sums, filled_core)
+    sums = after(sums, filled_core[-1] if reverse else filled_core)
     mine, give = small_call(
         functools.partial(core_body, reverse), where, [parts, other] + sums, [half] * 2
     )
@@ -163,6 +163,10 @@
     return (mine.reshape(shape), got.reshape(shape)), filled_row, filled_plane, filled_core
 
 
+def hbm(x):
+    return pltpu.with_memory_space_constraint(x, pltpu.HBM)
+
+
 def after(x, *others):
     return lax.optimization_barrier((x, others))[0]
 
@@ -185,8 +189,8 @@
         in_specs=[blk, blk, blk],
         out_specs=[pl.BlockSpec((HC, t, t), lambda g: (g, 0, 0)), blk],
         out_shape=[
-            jax.ShapeDtypeStruct((CH * HC, t, t), BF),
-            jax.ShapeDtypeStruct((t, f), F32),
+            pltpu.HBM((CH * HC, t, t), BF),
+            pltpu.HBM((t, f), F32),
         ],
         cost_estimate=cost(4 * t * t * f, 14 * t * f),
         compiler_params=pltpu.CompilerParams(vmem_limit_bytes=12 << 20),
@@ -238,18 +242,34 @@
             ],
         ),
         out_shape=[jax.ShapeDtypeStruct((t, two * w), BF)] * 2
-        + [jax.ShapeDtypeStruct((CH, t, w), F32)],
+        + [pltpu.HBM((CH, t, w), F32)],
         cost_estimate=cost(2 * t * f * HD, 12 * t * f),
         compiler_params=pltpu.CompilerParams(vmem_limit_bytes=12 << 20),
         name="attend",
     )(where, q, out, *carried, gain)
 
 
-def grad_attn_body(i_ref, q_ref, a_ref, gn_ref, g_ref, go_ref, w_ref, ga_ref, lg_ref):
-    rows = w_ref.shape[0] * w_ref.shape[2]
+PARTS = 1
+SLOTS = 3
+
+
+def grad_attn_body(
+    i_ref, q_ref, a_ref, gn_ref, g_ref, go_hbm, w_hbm, ga_ref, lg_ref, go, w, go_sem, w_sem
+):
+    g = pl.program_id(0)
+    _, blocks, rows, d = w.shape
+    last = PARTS * (CH - 1)
+
+    def load(t):
+        at = pl.ds(lax.rem(t, PARTS) * blocks, blocks)
+        slot = lax.rem(t, SLOTS)
+        source = w_hbm.at[at, lax.div(t, PARTS)]
+        return pltpu.make_async_copy(source, w.at[slot], w_sem.at[slot])
+
+    whole = pltpu.make_async_copy(go_hbm, go, go_sem)
 
     def finish(gn):
-        for h in range(HC):
+        for h in range(HC // PARTS):
             cols = slice(h * HD, (h + 1) * HD)
             a = a_ref[0, :, cols]
             inv = lax.rsqrt(jnp.mean(a * a, axis=-1, keepdims=True) + EPSILON)
@@ -260,43 +280,71 @@
             ga_ref[0, :, cols] = ga
             lg_ref[h] = mm(head(q_ref, h), ga, 0, 0).astype(BF)
 
-    @pl.when(pl.program_id(0) == 0)
+    @pl.when(g == 0)
+    def _():
+        whole.start()
+        for t in range(SLOTS):
+            load(t).start()
+
+    @pl.when(g < PARTS)
     def _():
         finish(gn_ref[...])
 
-    @pl.when(pl.program_id(0) > 0)
+    @pl.when(g == PARTS)
     def _():
-        finish(mm(go_ref[...], w_ref[:, 0].reshape(rows, w_ref.shape[3]), 1, 1))
+        whole.wait()
+
+    @pl.when(g >= PARTS)
+    def _():
+        t = g - PARTS
+        load(t).wait()
+        finish(mm(go[...], w[lax.rem(t, SLOTS)].reshape(blocks * rows, d), 1, 1))
+
+        @pl.when(t + SLOTS < last)
+        def _():
+            load(t + SLOTS).start()
 
 
 def grad_attn(order, q, attended, gn, gain, grad_rows, gathered):
     t, f = q.shape
-    w = f // CH
+    w = f // CH // PARTS
     n, _, r, d = gathered.shape
+
+    def nat(g, i):
+        return (0, i[lax.div(g, PARTS)] * PARTS + lax.rem(g, PARTS))
+
     return pl.pallas_call(
         grad_attn_body,
         grid_spec=pltpu.PrefetchScalarGridSpec(
             num_scalar_prefetch=1,
-            grid=(CH,),
+            grid=(CH * PARTS,),
             in_specs=[
-                pl.BlockSpec((t, w), lambda g, i: (0, i[g])),
-                pl.BlockSpec((1, t, w), lambda g, i: (i[g], 0, 0)),
-                pl.BlockSpec((t, w), lambda g, i: (0, 0)),
-                pl.BlockSpec((1, w), lambda g, i: (0, i[g])),
-                pl.BlockSpec((t, d), lambda g, i: (0, 0)),
-                pl.BlockSpec((n, 1, r, d), lambda g, i: (0, jnp.maximum(g - 1, 0), 0, 0)),
+                pl.BlockSpec((t, w), nat),
+                pl.BlockSpec(
+                    (1, t, w), lambda g, i: (i[lax.div(g, PARTS)], 0, lax.rem(g, PARTS))
+                ),
+                pl.BlockSpec((t, w), lambda g, i: (0, jnp.minimum(g, PARTS - 1))),
+                pl.BlockSpec((1, w), nat),
+                pl.BlockSpec(memory_space=pltpu.HBM),
+                pl.BlockSpec(memory_space=pltpu.HBM),
             ],
             out_specs=[
-                pl.BlockSpec((1, t, w), lambda g, i: (g, 0, 0)),
-                pl.BlockSpec((HC, HD, HD), lambda g, i: (g, 0, 0)),
+                pl.BlockSpec((1, t, w), lambda g, i: (lax.div(g, PARTS), 0, lax.rem(g, PARTS))),
+                pl.BlockSpec((HC // PARTS, HD, HD), lambda g, i: (g, 0, 0)),
+            ],
+            scratch_shapes=[
+                pltpu.VMEM((t, d), BF),
+                pltpu.VMEM((SLOTS, n // PARTS, r, d), BF),
+                pltpu.SemaphoreType.DMA(()),
+                pltpu.SemaphoreType.DMA((SLOTS,)),
             ],
         ),
         out_shape=[
-            jax.ShapeDtypeStruct((CH, t, w), BF),
+            pltpu.HBM((CH, t, f // CH), BF),
             jax.ShapeDtypeStruct((CH * HC, HD, HD), BF),
         ],
         cost_estimate=cost(2 * t * f * HD + 6 * t * w * d, 12 * t * f + 6 * w * d),
-        compiler_params=pltpu.CompilerParams(vmem_limit_bytes=20 << 20),
+        compiler_params=pltpu.CompilerParams(vmem_limit_bytes=26 << 20),
         name="grad_attn",
     )(order, q, attended, gn, gain, grad_rows, gathered)
 
@@ -336,8 +384,8 @@
         ),
         out_shape=[
             jax.ShapeDtypeStruct((t, f), BF),
-            jax.ShapeDtypeStruct((CH, t, w), F32),
-            jax.ShapeDtypeStruct((CH, t, w), F32),
+            pltpu.HBM((CH, t, w), F32),
+            pltpu.HBM((CH, t, w), F32),
         ],
         cost_estimate=cost(8 * t * t * f, 24 * t * f),
         compiler_params=pltpu.CompilerParams(vmem_limit_bytes=20 << 20),
@@ -424,10 +472,7 @@
 
 
 def weight_total(nt, grads, o_ref, extra_ref):
-    total = None
-    for s, g in enumerate(grads):
-        part = mm(nt[s], g[...], 1, 0)
-        total = part if total is None else total + part
+    total = mm(nt[...], jnp.concatenate([g[...] for g in grads], axis=0), 1, 0)
     chips, blocks, rows, w = o_ref.shape
     span = chips * rows
     for b in range(blocks):
@@ -442,8 +487,9 @@
 
     @pl.when(pl.program_id(0) == 0)
     def _():
+        t = n0.shape[0]
         for s, n in enumerate((n0, n1, n2, n3)):
-            nt_ref[s] = n[...].T
+            nt_ref[:, s * t : (s + 1) * t] = n[...].T
 
     weight_total(nt_ref, grads, o_ref, None)
 
@@ -455,13 +501,13 @@
 
 def weight_half(body, half, rows, grads_all, shape, nt_out):
     t, d = grads_all[0].shape
-    w = rows[0].shape[1]
+    w = rows[0].shape[1] if nt_out else rows[0].shape[0]
     tile = 256
     steps = d // 2 // tile
     own = pl.BlockSpec(shape[:-1] + (tile,), lambda g, i: (0, 0, 0, g))
     whole = pl.BlockSpec((t, w), lambda g, i: (0, 0))
-    turned = pl.BlockSpec((CH, w, t), lambda g, i: (0, 0, 0))
-    out = jax.ShapeDtypeStruct(shape, BF)
+    turned = pl.BlockSpec((w, CH * t), lambda g, i: (0, 0))
+    out = pltpu.HBM(shape, BF)
     cols = pl.BlockSpec((t, tile), lambda g, i: (0, i[0] * steps + g))
     return pl.pallas_call(
         body,
@@ -471,7 +517,7 @@
             in_specs=([whole] * CH if nt_out else [turned, own]) + [cols] * CH,
             out_specs=[own, turned] if nt_out else own,
         ),
-        out_shape=[out, jax.ShapeDtypeStruct((CH, w, t), BF)] if nt_out else out,
+        out_shape=[out, jax.ShapeDtypeStruct((w, CH * t), BF)] if nt_out else out,
         cost_estimate=cost(CH * t * w * d, 2 * CH * t * d + 2 * CH * t * w + w * d),
         compiler_params=pltpu.CompilerParams(vmem_limit_bytes=20 << 20),
         name="weight_half",
@@ -555,11 +601,9 @@
     state = local_state(k, v)
     half_cols = model_width // 2
     side = at_x % 2
-    near_cols = lax.dynamic_slice_in_dim(grad_rows, side * half_cols, half_cols, 1)
-    far_cols = lax.dynamic_slice_in_dim(grad_rows, (1 - side) * half_cols, half_cols, 1)
-    pieces, near_cols, far_cols, sent_rows, q_next = lax.optimization_barrier(
-        (pieces, near_cols, far_cols, grad_rows, q, state)
-    )[:5]
+    pieces, sent_rows, q_next = lax.optimization_barrier((pieces, grad_rows, q, state))[:3]
+    near_cols = lax.dynamic_slice_in_dim(sent_rows, side * half_cols, half_cols, 1)
+    far_cols = lax.dynamic_slice_in_dim(sent_rows, (1 - side) * half_cols, half_cols, 1)
     gathered = lax.all_gather(jnp.concatenate(pieces, axis=0), CTX, axis=0, tiled=True)
     gathered = gathered.reshape(blocks_n, CH - 1, piece, model_width)
     gathered = pltpu.with_memory_space_constraint(gathered, pltpu.HBM)
@@ -572,13 +616,13 @@
         partner(far_cols, "x", 3),
     ]
 
-    carried, (weights, local_out), gn, _ = carry(
+    carried, (weights, local_out), _, _ = carry(
         state,
         where,
         at_core,
         False,
         lambda sent: local_scores(after(q_next, sent), k, v),
-        lambda sent, done: mm(after(sent_rows, sent, done), out_weight, 1, 1),
+        lambda sent, done: (),
         lambda sent, done: (),
     )
     near, far, attended = attend(turns, q, local_out, carried, gain_row)
@@ -588,10 +632,9 @@
         partner(far, "x", 2),
         partner(far, "x", 3),
     ]
-    attended = pltpu.with_memory_space_constraint(attended, pltpu.HBM)
-    gn = pltpu.with_memory_space_constraint(gn, pltpu.HBM)
-
-    ga, lg = grad_attn(where, q, attended, gn, gain_row, grad_rows, gathered)
+    gn = hbm(mm(after(sent_rows, near), out_weight, 1, 1))
+
+    ga, lg = grad_attn(where, q, attended, gn, gain_row, hbm(grad_rows), gathered)
     chips = blocks_n // 2
     shape = (chips, 2, out_weight.shape[0] // chips, half_cols // 2)
 
@@ -606,17 +649,14 @@
             keep_body, mine, [after(turned, sent), extra], grads_all, shape, False
         )
 
-    def halves(sent, done):
-        partial = second_half(sent, done)
-        return lax.all_to_all(partial, ("z", "y"), 0, 0, tiled=True), partial
-
-    def rest(sent, done):
+    def rest(sent, partial):
+        parts = lax.all_to_all(partial, ("z", "y"), 0, 0, tiled=True)
         grads = local_grads(where, q, k, v, weights, after(ga, sent), carried)
         rows = layer_rows(where, near, after(far, grads), own_weight, gathered)
-        return grads, rows
-
-    later, _, (parts, _), (grads, layer_out) = carry(
-        lg, where, at_core, True, first_half, halves, rest
+        return parts, (grads, rows)
+
+    later, _, _, (parts, (grads, layer_out)) = carry(
+        lg, where, at_core, True, first_half, second_half, rest
     )
     grad_query, pk, pv = grads
     grad_key, grad_value = later_grads(where, k, v, later, pk, pv)

time: 252 us -> 255 us (1.012)
  Pallas kernels: 61.2 us -> 63.8 us
    ppermute x23, waiting for transfers between devices: 30.6 us -> 34.9 us  [give_to(): return lax.ppermute(x, axis, [(d, (d + by) % n) for d in range(n)])]
    all_gather x1, waiting for transfers between devices: 14.4 us -> 10.3 us  [layer(): lax.all_gather(jnp.concatenate(pieces, axis=0), CTX, axis=0, tiled=True)]
    unnamed x76 -> x68, local copies, waits for them, and re-layouts: 18.8 us -> 16.9 us
  transfers between devices with their start and end apart: 37 -> 37, of which waited for: 16 -> 19; matrix products, arithmetic and copies ran while one was open for 4% -> 4% of each run, Pallas kernels for 20% -> 20%
where the time goes in v5:
time: 255 us; the launch traced here: 253 us
  waiting for transfers between devices  92.2 us (36%)
  Pallas kernels  63.8 us (25%)
  starting transfers between devices  54.5 us (21%)
  local copies, waits for them, and re-layouts  23 us (9%)
  between operations  14.3 us (6%)
  matrix products  4.77 us (2%)
    ppermute x8, waiting for transfers between devices, partner(): lax.ppermute(x, axis, [(d, d ^ bits) for d in range(lax.axis_size(axis))])  44 us
    ppermute x23, starting transfers between devices, give_to(): return lax.ppermute(x, axis, [(d, (d + by) % n) for d in range(n)])  35.3 us
    ppermute x23, waiting for transfers between devices, give_to(): return lax.ppermute(x, axis, [(d, (d + by) % n) for d in range(n)])  34.9 us
    unnamed x68, local copies, waits for them, and re-layouts  16.9 us
    pallas_call x2, Pallas kernels, weight_half(): pl.pallas_call(body, grid_spec=pltpu.PrefetchScalarGridSpec(num_scalar_pr...  12.2 us
    pallas_call x1, Pallas kernels, grad_attn(): pl.pallas_call(grad_attn_body, grid_spec=pltpu.PrefetchScalarGridSpec(num...  11.8 us
    pallas_call x1, Pallas kernels, layer_rows(): pl.pallas_call(layer_body, grid_spec=pltpu.PrefetchScalarGridSpec(num_sca...  10.6 us
    all_gather x1, waiting for transfers between devices, layer(): lax.all_gather(jnp.concatenate(pieces, axis=0), CTX, axis=0, tiled=True)  10.3 us
  transfers between devices with their start and end apart: 37, of which 19 were waited for; matrix products, arithmetic and copies ran while one was open for 4% of the time, Pallas kernels for 20%

profile of v5, /device:TPU:0, one launch (start us, length us, event | category | flops | bytes accessed | tf_op | source)
XLA Modules:
  0.0 253.3 jit_solution(8002672187818585995)
XLA Ops:
  8.1 2.9 %collective-permute-start = (bf16[16,4096]{1,0:T(8,128)(2,1)S(1)}, bf16[16,4096]{1,0:T(8,128)(2,1)S(1)}, u32[]{:S(2)}, u32[]{:S(2)}) collective-permute-start(bf16[16,4096]{1,0:T(8,128)(2,1)S(1)} %constant_dynamic-slice_fusion.2), channel_id=1, source_target_pairs={{32,0},{64,32},{96,64},{0,96},{33,1},{65,33},{97,65},{1,97},{34,2}... | collective-permute-start | bytes 393224 | tf_op jit(solution)/shard_map/ppermute | solution.py:573
  17.3 1.6 collective-permute-done.1
  18.9 1.4 collective-permute-done.2
  21.1 1.7 dynamic-slice_bitcast_fusion.1
  22.9 1.7 collective-permute-done.3.r_ref
  26.2 1.6 collective-permute-start.4
  27.9 2.9 %collective-permute-start.5 = (bf16[256,128]{1,0:T(8,128)(2,1)S(1)}, bf16[256,128]{1,0:T(8,128)(2,1)S(1)}, u32[]{:S(2)}, u32[]{:S(2)}) collective-permute-start(bf16[256,128]{1,0:T(8,128)(2,1)S(1)} %get-tuple-element.82), channel_id=1, source_target_pairs={{0,4},{2,6},{4,0},{6,2},{1,5},{3,7},{5,1},{7,3},{8,12},{10,14},{12... | collective-permute-start | bytes 196616 | tf_op jit(solution)/shard_map/ppermute | solution.py:128
  30.8 1.3 collective-permute-start.6
  32.1 4.0 %local_scores.1 = (bf16[16,256,256]{2,1,0:T(8,128)(2,1)}, f32[256,2048]{1,0:T(8,128)}) custom-call(bf16[256,2048]{1,0:T(8,128)(2,1)S(1)} %bitcast.34, bf16[256,2048]{1,0:T(8,128)(2,1)S(1)} %bitcast.39, bf16[256,2048]{1,0:T(8,128)(2,1)S(1)} %bitcast.43), custom_call_target="tpu_custom_call" | custom-call | flops 536870912 | bytes 7340032 | tf_op jit(solution)/shard_map/local_scores/pallas_call | solution.py:186
  36.8 2.1 collective-permute-start.7
  38.9 3.7 %collective-permute-start.8 = (bf16[256,128]{1,0:T(8,128)(2,1)S(1)}, bf16[256,128]{1,0:T(8,128)(2,1)S(1)}, u32[]{:S(2)}, u32[]{:S(2)}) collective-permute-start(bf16[256,128]{1,0:T(8,128)(2,1)S(1)} %shard_map.102), channel_id=1, source_target_pairs={{0,16},{8,24},{16,0},{24,8},{1,17},{9,25},{17,1},{25,9},{2,18},{10... | collective-permute-start | bytes 196616 | tf_op jit(solution)/shard_map/ppermute | solution.py:128
  43.4 1.8 collective-permute-done.7.z1
  45.2 2.5 collective-permute-done.8.z2
  47.7 1.3 shard_map.103
  49.8 2.4 collective-permute-start.11
  52.2 1.3 collective-permute-start.12
  59.0 3.3 %constant_dynamic-slice_fusion = (bf16[256,2048]{1,0:T(8,128)(2,1)}, bf16[256,2048]{1,0:T(8,128)(2,1)}) fusion(bf16[256,4096]{1,0:T(8,128)(2,1)} %bitcast.62, s32[]{:T(128)S(6)} %select_n.50, s32[]{:T(128)S(6)} %select_n.49), kind=kLoop, calls=%fused_computation.3 | loop fusion | bytes 4194312 | tf_op jit(solution)/shard_map/dynamic_slice | solution.py:606
  62.3 1.8 collective-permute-start.23
  64.1 2.3 collective-permute-start.22
  66.4 4.0 %attend.1 = (bf16[256,1024]{1,0:T(8,128)(2,1)}, bf16[256,1024]{1,0:T(8,128)(2,1)S(1)}, f32[4,256,512]{2,1,0:T(8,128)}) custom-call(s32[8]{0:T(128)S(1)} %stack.59.w_ref, bf16[256,2048]{1,0:T(8,128)(2,1)S(1)} %bitcast.35, f32[256,2048]{1,0:T(8,128)S(1)} %copy-done.12, bf16[8,128,128]{2,1,0:T(8,128)(2,1)S(1)} %bitcast.52, bf16[8,128,128]{2,1,0:T(8,128)(2,1)S(1)} %bitcast.54, ...), custom_call_target="tpu_custom_call" | custom-call | flops 134217728 | bytes 6291456 | tf_op jit(solution)/shard_map/attend/pallas_call | solution.py:232
  71.2 4.8 %fusion.gn_ref = f32[256,512]{1,0:T(8,128)} fusion(bf16[256,4096]{1,0:T(8,128)(2,1)S(1)} %bitcast.64, bf16[512,4096]{1,0:T(8,128)(2,1)} %own_ref.1), kind=kOutput, calls=%fused_computation.6 | convolution fusion | flops 1073741824 | bytes 6815744 | tf_op jit(solution)/shard_map/dot_general | solution.py:21
  75.9 10.3 %all-gather.2.cloned.1.call-done = bf16[1536,4096]{1,0:T(8,128)(2,1)} async-done(((bf16[48,4096]{1,0:T(8,128)(2,1)}), bf16[1536,4096]{1,0:T(8,128)(2,1)}) %all-gather.2.cloned.1.call-update) | async-done | bytes 12582928 | tf_op jit(solution)/shard_map/all_gather | solution.py:607
  86.2 1.6 copy-done.10
  87.8 11.8 %grad_attn.1 = (bf16[4,256,512]{2,1,0:T(8,128)(2,1)}, bf16[16,128,128]{2,1,0:T(8,128)(2,1)S(1)}) custom-call(s32[8]{0:T(128)S(1)} %stack.54.w_ref.i_ref, bf16[256,2048]{1,0:T(8,128)(2,1)S(1)} %bitcast.36, f32[4,256,512]{2,1,0:T(8,128)S(1)} %copy-done.10, f32[256,512]{1,0:T(8,128)} %fusion.gn_ref, f32[1,2048]{1,0:T(1,128)S(1)} %bitcast.59, ...), custom_call_target="tpu_custom_call" | custom-call | flops 3355443200 | bytes 18874368 | tf_op jit(solution)/shard_map/grad_attn/pallas_call | solution.py:316
  100.1 21.6 %collective-permute-done.18.n1 = bf16[256,1024]{1,0:T(8,128)(2,1)} collective-permute-done((bf16[256,1024]{1,0:T(8,128)(2,1)}, bf16[256,1024]{1,0:T(8,128)(2,1)}, u32[]{:S(2)}, u32[]{:S(2)}) %collective-permute-start.18) | collective-permute-done | bytes 524320 | tf_op jit(solution)/shard_map/ppermute | solution.py:123
  123.0 1.7 collective-permute-start.20
  125.3 11.3 %collective-permute-done.19.n2 = bf16[256,1024]{1,0:T(8,128)(2,1)S(1)} collective-permute-done((bf16[256,1024]{1,0:T(8,128)(2,1)S(1)}, bf16[256,1024]{1,0:T(8,128)(2,1)S(1)}, u32[]{:S(2)}, u32[]{:S(2)}) %collective-permute-start.19) | collective-permute-done | bytes 524320 | tf_op jit(solution)/shard_map/ppermute | solution.py:123
  136.6 11.1 %collective-permute-done.20.n3 = bf16[256,1024]{1,0:T(8,128)(2,1)S(1)} collective-permute-done((bf16[256,1024]{1,0:T(8,128)(2,1)S(1)}, bf16[256,1024]{1,0:T(8,128)(2,1)S(1)}, u32[]{:S(2)}, u32[]{:S(2)}) %collective-permute-start.20) | collective-permute-done | bytes 524320 | tf_op jit(solution)/shard_map/ppermute | solution.py:123
  147.7 6.6 %weight_half.2 = (bf16[16,2,32,1024]{3,2,1,0:T(8,128)(2,1)}, bf16[1024,1024]{1,0:T(8,128)(2,1)S(1)}) custom-call(s32[1]{0:T(128)S(6)} %sub.24.i_ref, bf16[256,1024]{1,0:T(8,128)(2,1)} %get-tuple-element.119.n0.near_ref, bf16[256,1024]{1,0:T(8,128)(2,1)} %collective-permute-done.18.n1, bf16[256,1024]{1,0:T(8,128)(2,1)S(1)} %collective-permute-done.19.n2, ...), custom_call_target="tpu_custom_call" | custom-call | flops 2147483648 | bytes 8388608 | tf_op jit(solution)/shard_map/weight_half/pallas_call | solution.py:512
  155.3 3.2 %collective-permute-start.16 = (bf16[256,128]{1,0:T(8,128)(2,1)S(1)}, bf16[256,128]{1,0:T(8,128)(2,1)S(1)}, u32[]{:S(2)}, u32[]{:S(2)}) collective-permute-start(bf16[256,128]{1,0:T(8,128)(2,1)S(1)} %get-tuple-element.117), channel_id=1, source_target_pairs={{0,4},{2,6},{4,0},{6,2},{1,5},{3,7},{5,1},{7,3},{8,12},{10,14},{12... | collective-permute-start | bytes 196616 | tf_op jit(solution)/shard_map/ppermute | solution.py:128
  158.7 1.4 collective-permute-done.15.refs_0_.t1
  160.0 2.3 collective-permute-done.16.refs_1_.t2
  164.7 5.6 %weight_half.3 = bf16[16,2,32,1024]{3,2,1,0:T(8,128)(2,1)} custom-call(s32[1]{0:T(128)} %bitcast.7.i_ref, bf16[1024,1024]{1,0:T(8,128)(2,1)S(1)} %get-tuple-element.129.nt_ref, bf16[16,2,32,1024]{3,2,1,0:T(8,128)(2,1)S(1)} %collective-permute-done.27.extra_ref, bf16[256,2048]{1,0:T(8,128)(2,1)} %get-tuple-element.156.rest_0_, ...), custom_call_target="tpu_custom_call" | custom-call | flops 2147483648 | bytes 8388608 | tf_op jit(solution)/shard_map/weight_half/pallas_call | solution.py:512
  170.3 5.3 %all-to-all-start = ((bf16[16,2,32,1024]{3,2,1,0:T(8,128)(2,1)}), bf16[16,2,32,1024]{3,2,1,0:T(8,128)(2,1)}, u32[]{:S(2)}, u32[]{:S(2)}) async-start(bf16[16,2,32,1024]{3,2,1,0:T(8,128)(2,1)} %weight_half.3), calls=%async_computation | async-start | bytes 4194304 | tf_op jit(solution)/shard_map/all_to_all | solution.py:653
  175.6 1.9 collective-permute-start.24
  177.5 2.7 %collective-permute-start.25 = (bf16[256,128]{1,0:T(8,128)(2,1)}, bf16[256,128]{1,0:T(8,128)(2,1)S(1)}, u32[]{:S(2)}, u32[]{:S(2)}) collective-permute-start(bf16[256,128]{1,0:T(8,128)(2,1)} %copy-done.31), channel_id=1, source_target_pairs={{0,16},{8,24},{16,0},{24,8},{1,17},{9,25},{17,1},{25,9},{2,18},{10... | collective-permute-start | bytes 196616 | tf_op jit(solution)/shard_map/ppermute | solution.py:128
  180.1 1.5 collective-permute-start.26
  181.6 19.2 %collective-permute-done.24.z1 = bf16[256,128]{1,0:T(8,128)(2,1)S(1)} collective-permute-done((bf16[256,128]{1,0:T(8,128)(2,1)}, bf16[256,128]{1,0:T(8,128)(2,1)S(1)}, u32[]{:S(2)}, u32[]{:S(2)}) %collective-permute-start.24) | collective-permute-done | bytes 65568 | tf_op jit(solution)/shard_map/ppermute | solution.py:128
  201.8 1.3 collective-permute-done.26.z3
  206.4 2.7 %collective-permute-start.28 = (bf16[256,128]{1,0:T(8,128)(2,1)S(1)}, bf16[256,128]{1,0:T(8,128)(2,1)S(1)}, u32[]{:S(2)}, u32[]{:S(2)}) collective-permute-start(bf16[256,128]{1,0:T(8,128)(2,1)S(1)} %get-tuple-element.133), channel_id=1, source_target_pairs={{0,2},{2,4},{4,6},{6,0},{1,3},{3,5},{5,7},{7,1},{8,10},{10,12},{12... | collective-permute-start | bytes 196616 | tf_op jit(solution)/shard_map/ppermute | solution.py:128
  209.1 3.4 %collective-permute-start.29 = (bf16[256,128]{1,0:T(8,128)(2,1)S(1)}, bf16[256,128]{1,0:T(8,128)(2,1)S(1)}, u32[]{:S(2)}, u32[]{:S(2)}) collective-permute-start(bf16[256,128]{1,0:T(8,128)(2,1)S(1)} %get-tuple-element.134), channel_id=1, source_target_pairs={{0,4},{2,6},{4,0},{6,2},{1,5},{3,7},{5,1},{7,3},{8,12},{10,14},{12... | collective-permute-start | bytes 196616 | tf_op jit(solution)/shard_map/ppermute | solution.py:128
  213.5 1.6 copy-done.11
  217.3 7.3 %local_grads.1 = (bf16[256,2048]{1,0:T(8,128)(2,1)}, f32[4,256,512]{2,1,0:T(8,128)}, f32[4,256,512]{2,1,0:T(8,128)}) custom-call(s32[8]{0:T(128)S(1)} %stack.54.w_ref.i_ref, bf16[256,2048]{1,0:T(8,128)(2,1)S(1)} %bitcast.37, bf16[256,2048]{1,0:T(8,128)(2,1)S(1)} %bitcast.40, bf16[256,2048]{1,0:T(8,128)(2,1)S(1)} %bitcast.44, ...), custom_call_target="tpu_custom_call" | custom-call | flops 1073741824 | bytes 12582912 | tf_op jit(solution)/shard_map/local_grads/pallas_call | solution.py:370
  224.6 10.6 %layer_rows.1 = bf16[256,4096]{1,0:T(8,128)(2,1)} custom-call(s32[8]{0:T(128)S(1)} %stack.54.w_ref.i_ref, bf16[256,1024]{1,0:T(8,128)(2,1)} %get-tuple-element.119.n0.near_ref, bf16[256,1024]{1,0:T(8,128)(2,1)S(1)} %copy-done.24, bf16[512,4096]{1,0:T(8,128)(2,1)} %own_ref.1, bf16[32,3,16,4096]{3,2,1,0:T(8,128)(2,1)} %bitcast.61), custom_call_target="tpu_custom_call" | custom-call | flops 4294967296 | bytes 19922944 | tf_op jit(solution)/shard_map/layer_rows/pallas_call | solution.py:454
  236.1 2.1 sum_parts.1
  238.8 1.6 collective-permute-start.34
  240.4 1.6 copy-done.14
  242.0 3.2 %later_grads.1 = (bf16[256,2048]{1,0:T(8,128)(2,1)}, bf16[256,2048]{1,0:T(8,128)(2,1)}) custom-call(s32[8]{0:T(128)S(1)} %stack.54.w_ref.i_ref, bf16[256,2048]{1,0:T(8,128)(2,1)S(1)} %bitcast.41, bf16[256,2048]{1,0:T(8,128)(2,1)S(1)} %bitcast.45, bf16[8,128,128]{2,1,0:T(8,128)(2,1)S(1)} %bitcast.56, bf16[8,128,128]{2,1,0:T(8,128)(2,1)S(1)} %bitcast.57, ...), custom_call_target="tpu_custom_call" | custom-call | flops 268435456 | bytes 8388608 | tf_op jit(solution)/shard_map/later_grads/pallas_call | solution.py:411
  (122 shorter events, 34.4 us)
Async XLA Ops:
  7.2 79.0 %all-gather.2.cloned.1.call-start = ((), (), s32[]{:S(2)}) async-start(), calls=%async_computation.1 | async-start | bytes 12976128 | tf_op jit(solution)/shard_map/all_gather | solution.py:607
  8.1 9.2 %collective-permute-start = (bf16[16,4096]{1,0:T(8,128)(2,1)S(1)}, bf16[16,4096]{1,0:T(8,128)(2,1)S(1)}, u32[]{:S(2)}, u32[]{:S(2)}) collective-permute-start(bf16[16,4096]{1,0:T(8,128)(2,1)S(1)} %constant_dynamic-slice_fusion.2), channel_id=1, source_target_pairs={{32,0},{64,32},{96,64},{0,96},{33,1},{65,33},{97,65},{1,97},{34,2}... | collective-permute-start | bytes 393224 | tf_op jit(solution)/shard_map/ppermute | solution.py:573
  11.1 7.9 %collective-permute-start.1 = (bf16[16,4096]{1,0:T(8,128)(2,1)S(1)}, bf16[16,4096]{1,0:T(8,128)(2,1)S(1)}, u32[]{:S(2)}, u32[]{:S(2)}) collective-permute-start(bf16[16,4096]{1,0:T(8,128)(2,1)S(1)} %constant_dynamic-slice_fusion.2), channel_id=1, source_target_pairs={{64,0},{96,32},{0,64},{32,96},{65,1},{97,33},{1,65},{33,97},{66,2}... | collective-permute-start | bytes 393224 | tf_op jit(solution)/shard_map/ppermute | solution.py:573
  11.9 8.5 %collective-permute-start.2 = (bf16[16,4096]{1,0:T(8,128)(2,1)S(1)}, bf16[16,4096]{1,0:T(8,128)(2,1)S(1)}, u32[]{:S(2)}, u32[]{:S(2)}) collective-permute-start(bf16[16,4096]{1,0:T(8,128)(2,1)S(1)} %constant_dynamic-slice_fusion.2), channel_id=1, source_target_pairs={{96,0},{0,32},{32,64},{64,96},{97,1},{1,33},{33,65},{65,97},{98,2}... | collective-permute-start | bytes 393224 | tf_op jit(solution)/shard_map/ppermute | solution.py:573
  15.2 16.9 %copy-start = (bf16[1,256,2048]{2,1,0:T(8,128)(2,1)S(1)}, bf16[1,256,2048]{2,1,0:T(8,128)(2,1)}, u32[]{:S(2)}) copy-start(bf16[1,256,2048]{2,1,0:T(8,128)(2,1)} %param.6) | copy-start | bytes 3145732
  15.2 16.9 %copy-start.2 = (bf16[1,256,2048]{2,1,0:T(8,128)(2,1)S(1)}, bf16[1,256,2048]{2,1,0:T(8,128)(2,1)}, u32[]{:S(2)}) copy-start(bf16[1,256,2048]{2,1,0:T(8,128)(2,1)} %param.7) | copy-start | bytes 3145732
  15.2 16.9 %copy-start.4 = (bf16[1,256,2048]{2,1,0:T(8,128)(2,1)S(1)}, bf16[1,256,2048]{2,1,0:T(8,128)(2,1)}, u32[]{:S(2)}) copy-start(bf16[1,256,2048]{2,1,0:T(8,128)(2,1)} %param.8) | copy-start | bytes 3145732
  22.8 1.7 collective-permute-start.3
  26.2 9.9 %collective-permute-start.4 = (bf16[256,128]{1,0:T(8,128)(2,1)S(1)}, bf16[256,128]{1,0:T(8,128)(2,1)S(1)}, u32[]{:S(2)}, u32[]{:S(2)}) collective-permute-start(bf16[256,128]{1,0:T(8,128)(2,1)S(1)} %get-tuple-element.81), channel_id=1, source_target_pairs={{0,2},{2,4},{4,6},{6,0},{1,3},{3,5},{5,7},{7,1},{8,10},{10,12},{12... | collective-permute-start | bytes 196616 | tf_op jit(solution)/shard_map/ppermute | solution.py:128
  27.9 8.3 %collective-permute-start.5 = (bf16[256,128]{1,0:T(8,128)(2,1)S(1)}, bf16[256,128]{1,0:T(8,128)(2,1)S(1)}, u32[]{:S(2)}, u32[]{:S(2)}) collective-permute-start(bf16[256,128]{1,0:T(8,128)(2,1)S(1)} %get-tuple-element.82), channel_id=1, source_target_pairs={{0,4},{2,6},{4,0},{6,2},{1,5},{3,7},{5,1},{7,3},{8,12},{10,14},{12... | collective-permute-start | bytes 196616 | tf_op jit(solution)/shard_map/ppermute | solution.py:128
  30.8 5.4 %collective-permute-start.6 = (bf16[256,128]{1,0:T(8,128)(2,1)S(1)}, bf16[256,128]{1,0:T(8,128)(2,1)S(1)}, u32[]{:S(2)}, u32[]{:S(2)}) collective-permute-start(bf16[256,128]{1,0:T(8,128)(2,1)S(1)} %get-tuple-element.83), channel_id=1, source_target_pairs={{0,6},{2,0},{4,2},{6,4},{1,7},{3,1},{5,3},{7,5},{8,14},{10,8},{12,... | collective-permute-start | bytes 196616 | tf_op jit(solution)/shard_map/ppermute | solution.py:128
  36.8 8.4 %collective-permute-start.7 = (bf16[256,128]{1,0:T(8,128)(2,1)S(1)}, bf16[256,128]{1,0:T(8,128)(2,1)S(1)}, u32[]{:S(2)}, u32[]{:S(2)}) collective-permute-start(bf16[256,128]{1,0:T(8,128)(2,1)S(1)} %shard_map.102), channel_id=1, source_target_pairs={{0,8},{8,16},{16,24},{24,0},{1,9},{9,17},{17,25},{25,1},{2,10},{10... | collective-permute-start | bytes 196616 | tf_op jit(solution)/shard_map/ppermute | solution.py:128
  38.9 8.8 %collective-permute-start.8 = (bf16[256,128]{1,0:T(8,128)(2,1)S(1)}, bf16[256,128]{1,0:T(8,128)(2,1)S(1)}, u32[]{:S(2)}, u32[]{:S(2)}) collective-permute-start(bf16[256,128]{1,0:T(8,128)(2,1)S(1)} %shard_map.102), channel_id=1, source_target_pairs={{0,16},{8,24},{16,0},{24,8},{1,17},{9,25},{17,1},{25,9},{2,18},{10... | collective-permute-start | bytes 196616 | tf_op jit(solution)/shard_map/ppermute | solution.py:128
  42.5 5.1 %collective-permute-start.9 = (bf16[256,128]{1,0:T(8,128)(2,1)S(1)}, bf16[256,128]{1,0:T(8,128)(2,1)S(1)}, u32[]{:S(2)}, u32[]{:S(2)}) collective-permute-start(bf16[256,128]{1,0:T(8,128)(2,1)S(1)} %shard_map.102), channel_id=1, source_target_pairs={{0,24},{8,0},{16,8},{24,16},{1,25},{9,1},{17,9},{25,17},{2,26},{10... | collective-permute-start | bytes 196616 | tf_op jit(solution)/shard_map/ppermute | solution.py:128
  49.0 5.8 %collective-permute-start.10 = (bf16[256,128]{1,0:T(8,128)(2,1)}, bf16[256,128]{1,0:T(8,128)(2,1)}, u32[]{:S(2)}, u32[]{:S(2)}) collective-permute-start(bf16[256,128]{1,0:T(8,128)(2,1)} %get-tuple-element.96), channel_id=1, source_target_pairs={{0,2},{2,4},{4,6},{6,0},{1,3},{3,5},{5,7},{7,1},{8,10},{10,12},{12... | collective-permute-start | bytes 196616 | tf_op jit(solution)/shard_map/ppermute | solution.py:128
  49.8 6.1 %collective-permute-start.11 = (bf16[256,128]{1,0:T(8,128)(2,1)}, bf16[256,128]{1,0:T(8,128)(2,1)}, u32[]{:S(2)}, u32[]{:S(2)}) collective-permute-start(bf16[256,128]{1,0:T(8,128)(2,1)} %get-tuple-element.97), channel_id=1, source_target_pairs={{0,4},{2,6},{4,0},{6,2},{1,5},{3,7},{5,1},{7,3},{8,12},{10,14},{12... | collective-permute-start | bytes 196616 | tf_op jit(solution)/shard_map/ppermute | solution.py:128
  52.2 4.6 %collective-permute-start.12 = (bf16[256,128]{1,0:T(8,128)(2,1)}, bf16[256,128]{1,0:T(8,128)(2,1)}, u32[]{:S(2)}, u32[]{:S(2)}) collective-permute-start(bf16[256,128]{1,0:T(8,128)(2,1)} %get-tuple-element.98), channel_id=1, source_target_pairs={{0,6},{2,0},{4,2},{6,4},{1,7},{3,1},{5,3},{7,5},{8,14},{10,8},{12,... | collective-permute-start | bytes 196616 | tf_op jit(solution)/shard_map/ppermute | solution.py:128
  58.9 7.5 %copy-start.16 = (bf16[4,256,128]{2,1,0:T(8,128)(2,1)}, bf16[4,256,128]{2,1,0:T(8,128)(2,1)S(1)}, u32[]{:S(2)}) copy-start(bf16[4,256,128]{2,1,0:T(8,128)(2,1)S(1)} %get-tuple-element.103) | copy-start | bytes 786436
  58.9 7.5 %collective-permute-start.13 = (bf16[4,256,128]{2,1,0:T(8,128)(2,1)S(1)}, bf16[4,256,128]{2,1,0:T(8,128)(2,1)S(1)}, u32[]{:S(2)}, u32[]{:S(2)}) collective-permute-start(bf16[4,256,128]{2,1,0:T(8,128)(2,1)S(1)} %get-tuple-element.104), channel_id=1, source_target_pairs={{0,1},{1,0},{2,3},{3,2},{4,5},{5,4},{6,7},{7,6},{8,9},{9,8},{10,11... | collective-permute-start | bytes 786440 | tf_op jit(solution)/shard_map/ppermute | solution.py:128
  62.3 8.9 %copy-start.33 = (bf16[1,256,4096]{2,1,0:T(8,128)(2,1)S(1)}, bf16[1,256,4096]{2,1,0:T(8,128)(2,1)}, u32[]{:S(2)}) copy-start(bf16[1,256,4096]{2,1,0:T(8,128)(2,1)} %param.11) | copy-start | bytes 6291460
  62.3 85.5 %collective-permute-start.21 = (bf16[256,2048]{1,0:T(8,128)(2,1)}, bf16[256,2048]{1,0:T(8,128)(2,1)}, u32[]{:S(2)}, u32[]{:S(2)}) collective-permute-start(bf16[256,2048]{1,0:T(8,128)(2,1)} %get-tuple-element.155), channel_id=1, source_target_pairs={{0,32},{32,0},{64,96},{96,64},{1,33},{33,1},{65,97},{97,65},{2,34}... | collective-permute-start | bytes 3145736 | tf_op jit(solution)/shard_map/ppermute | solution.py:123
  62.3 85.5 %collective-permute-start.23 = (bf16[256,2048]{1,0:T(8,128)(2,1)}, bf16[256,2048]{1,0:T(8,128)(2,1)}, u32[]{:S(2)}, u32[]{:S(2)}) collective-permute-start(bf16[256,2048]{1,0:T(8,128)(2,1)} %get-tuple-element.155), channel_id=1, source_target_pairs={{0,96},{32,64},{64,32},{96,0},{1,97},{33,65},{65,33},{97,1},{2,98}... | collective-permute-start | bytes 3145736 | tf_op jit(solution)/shard_map/ppermute | solution.py:123
  64.1 83.7 %collective-permute-start.22 = (bf16[256,2048]{1,0:T(8,128)(2,1)}, bf16[256,2048]{1,0:T(8,128)(2,1)}, u32[]{:S(2)}, u32[]{:S(2)}) collective-permute-start(bf16[256,2048]{1,0:T(8,128)(2,1)} %get-tuple-element.156.rest_0_), channel_id=1, source_target_pairs={{0,64},{32,96},{64,0},{96,32},{1,65},{33,97},{65,1},{97,33},{2,66}... | collective-permute-start | bytes 3145736 | tf_op jit(solution)/shard_map/ppermute | solution.py:123
  71.2 50.5 %collective-permute-start.18 = (bf16[256,1024]{1,0:T(8,128)(2,1)}, bf16[256,1024]{1,0:T(8,128)(2,1)}, u32[]{:S(2)}, u32[]{:S(2)}) collective-permute-start(bf16[256,1024]{1,0:T(8,128)(2,1)} %get-tuple-element.119.n0.near_ref), channel_id=1, source_target_pairs={{0,32},{32,0},{64,96},{96,64},{1,33},{33,1},{65,97},{97,65},{2,34}... | collective-permute-start | bytes 1572872 | tf_op jit(solution)/shard_map/ppermute | solution.py:123
  87.8 33.9 %copy-start.23 = (bf16[256,1024]{1,0:T(8,128)(2,1)S(1)}, bf16[256,1024]{1,0:T(8,128)(2,1)}, u32[]{:S(2)}) copy-start(bf16[256,1024]{1,0:T(8,128)(2,1)} %copy-done.22) | copy-start | bytes 1572868
  99.6 25.1 %copy-start.8 = (bf16[16,128,128]{2,1,0:T(8,128)(2,1)}, bf16[16,128,128]{2,1,0:T(8,128)(2,1)S(1)}, u32[]{:S(2)}) copy-start(bf16[16,128,128]{2,1,0:T(8,128)(2,1)S(1)} %get-tuple-element.114) | copy-start | bytes 1572868
  99.6 23.4 %collective-permute-start.14 = (bf16[4,256,128]{2,1,0:T(8,128)(2,1)S(1)}, bf16[4,256,128]{2,1,0:T(8,128)(2,1)S(1)}, u32[]{:S(2)}, u32[]{:S(2)}) collective-permute-start(bf16[4,256,128]{2,1,0:T(8,128)(2,1)S(1)} %dynamic-slice_bitcast_fusion), channel_id=1, source_target_pairs={{0,1},{1,0},{2,3},{3,2},{4,5},{5,4},{6,7},{7,6},{8,9},{9,8},{10,11... | collective-permute-start | bytes 786440 | tf_op jit(solution)/shard_map/ppermute | solution.py:128
  121.7 14.9 %collective-permute-start.19 = (bf16[256,1024]{1,0:T(8,128)(2,1)S(1)}, bf16[256,1024]{1,0:T(8,128)(2,1)S(1)}, u32[]{:S(2)}, u32[]{:S(2)}) collective-permute-start(bf16[256,1024]{1,0:T(8,128)(2,1)S(1)} %copy-done.23), channel_id=1, source_target_pairs={{0,64},{32,96},{64,0},{96,32},{1,65},{33,97},{65,1},{97,33},{2,66}... | collective-permute-start | bytes 1572872 | tf_op jit(solution)/shard_map/ppermute | solution.py:123
  123.0 24.8 %copy-start.20 = (bf16[4,256,128]{2,1,0:T(8,128)(2,1)}, bf16[4,256,128]{2,1,0:T(8,128)(2,1)S(1)}, u32[]{:S(2)}) copy-start(bf16[4,256,128]{2,1,0:T(8,128)(2,1)S(1)} %collective-permute-done.14.r_ref) | copy-start | bytes 786436
  123.0 24.8 %collective-permute-start.20 = (bf16[256,1024]{1,0:T(8,128)(2,1)S(1)}, bf16[256,1024]{1,0:T(8,128)(2,1)S(1)}, u32[]{:S(2)}, u32[]{:S(2)}) collective-permute-start(bf16[256,1024]{1,0:T(8,128)(2,1)S(1)} %copy-done.23), channel_id=1, source_target_pairs={{0,96},{32,64},{64,32},{96,0},{1,97},{33,65},{65,33},{97,1},{2,98}... | collective-permute-start | bytes 1572872 | tf_op jit(solution)/shard_map/ppermute | solution.py:123
  154.3 10.4 %collective-permute-start.27 = (bf16[16,2,32,1024]{3,2,1,0:T(8,128)(2,1)}, bf16[16,2,32,1024]{3,2,1,0:T(8,128)(2,1)S(1)}, u32[]{:S(2)}, u32[]{:S(2)}) collective-permute-start(bf16[16,2,32,1024]{3,2,1,0:T(8,128)(2,1)} %get-tuple-element.123), channel_id=1, source_target_pairs={{0,1},{1,0},{2,3},{3,2},{4,5},{5,4},{6,7},{7,6},{8,9},{9,8},{10,11... | collective-permute-start | bytes 6291464 | tf_op jit(solution)/shard_map/ppermute | solution.py:128
  154.3 5.7 %collective-permute-start.15 = (bf16[256,128]{1,0:T(8,128)(2,1)S(1)}, bf16[256,128]{1,0:T(8,128)(2,1)S(1)}, u32[]{:S(2)}, u32[]{:S(2)}) collective-permute-start(bf16[256,128]{1,0:T(8,128)(2,1)S(1)} %get-tuple-element.116), channel_id=1, source_target_pairs={{0,2},{2,4},{4,6},{6,0},{1,3},{3,5},{5,7},{7,1},{8,10},{10,12},{12... | collective-permute-start | bytes 196616 | tf_op jit(solution)/shard_map/ppermute | solution.py:128
  155.3 7.0 %collective-permute-start.16 = (bf16[256,128]{1,0:T(8,128)(2,1)S(1)}, bf16[256,128]{1,0:T(8,128)(2,1)S(1)}, u32[]{:S(2)}, u32[]{:S(2)}) collective-permute-start(bf16[256,128]{1,0:T(8,128)(2,1)S(1)} %get-tuple-element.117), channel_id=1, source_target_pairs={{0,4},{2,6},{4,0},{6,2},{1,5},{3,7},{5,1},{7,3},{8,12},{10,14},{12... | collective-permute-start | bytes 196616 | tf_op jit(solution)/shard_map/ppermute | solution.py:128
  158.6 4.3 %collective-permute-start.17 = (bf16[256,128]{1,0:T(8,128)(2,1)S(1)}, bf16[256,128]{1,0:T(8,128)(2,1)S(1)}, u32[]{:S(2)}, u32[]{:S(2)}) collective-permute-start(bf16[256,128]{1,0:T(8,128)(2,1)S(1)} %get-tuple-element.118), channel_id=1, source_target_pairs={{0,6},{2,0},{4,2},{6,4},{1,7},{3,1},{5,3},{7,5},{8,14},{10,8},{12,... | collective-permute-start | bytes 196616 | tf_op jit(solution)/shard_map/ppermute | solution.py:128
  170.3 43.2 %copy-start.17 = (bf16[4,256,128]{2,1,0:T(8,128)(2,1)S(1)}, bf16[4,256,128]{2,1,0:T(8,128)(2,1)}, u32[]{:S(2)}) copy-start(bf16[4,256,128]{2,1,0:T(8,128)(2,1)} %copy-done.16) | copy-start | bytes 786436
  170.3 65.7 %all-to-all-start = ((bf16[16,2,32,1024]{3,2,1,0:T(8,128)(2,1)}), bf16[16,2,32,1024]{3,2,1,0:T(8,128)(2,1)}, u32[]{:S(2)}, u32[]{:S(2)}) async-start(bf16[16,2,32,1024]{3,2,1,0:T(8,128)(2,1)} %weight_half.3), calls=%async_computation | async-start | bytes 4194304 | tf_op jit(solution)/shard_map/all_to_all | solution.py:653
  175.6 25.2 %collective-permute-start.24 = (bf16[256,128]{1,0:T(8,128)(2,1)}, bf16[256,128]{1,0:T(8,128)(2,1)S(1)}, u32[]{:S(2)}, u32[]{:S(2)}) collective-permute-start(bf16[256,128]{1,0:T(8,128)(2,1)} %copy-done.31), channel_id=1, source_target_pairs={{0,8},{8,16},{16,24},{24,0},{1,9},{9,17},{17,25},{25,1},{2,10},{10... | collective-permute-start | bytes 196616 | tf_op jit(solution)/shard_map/ppermute | solution.py:128
  177.5 24.4 %collective-permute-start.25 = (bf16[256,128]{1,0:T(8,128)(2,1)}, bf16[256,128]{1,0:T(8,128)(2,1)S(1)}, u32[]{:S(2)}, u32[]{:S(2)}) collective-permute-start(bf16[256,128]{1,0:T(8,128)(2,1)} %copy-done.31), channel_id=1, source_target_pairs={{0,16},{8,24},{16,0},{24,8},{1,17},{9,25},{17,1},{25,9},{2,18},{10... | collective-permute-start | bytes 196616 | tf_op jit(solution)/shard_map/ppermute | solution.py:128
  180.1 23.0 %collective-permute-start.26 = (bf16[256,128]{1,0:T(8,128)(2,1)}, bf16[256,128]{1,0:T(8,128)(2,1)S(1)}, u32[]{:S(2)}, u32[]{:S(2)}) collective-permute-start(bf16[256,128]{1,0:T(8,128)(2,1)} %copy-done.31), channel_id=1, source_target_pairs={{0,24},{8,0},{16,8},{24,16},{1,25},{9,1},{17,9},{25,17},{2,26},{10... | collective-permute-start | bytes 196616 | tf_op jit(solution)/shard_map/ppermute | solution.py:128
  206.4 28.8 %collective-permute-start.28 = (bf16[256,128]{1,0:T(8,128)(2,1)S(1)}, bf16[256,128]{1,0:T(8,128)(2,1)S(1)}, u32[]{:S(2)}, u32[]{:S(2)}) collective-permute-start(bf16[256,128]{1,0:T(8,128)(2,1)S(1)} %get-tuple-element.133), channel_id=1, source_target_pairs={{0,2},{2,4},{4,6},{6,0},{1,3},{3,5},{5,7},{7,1},{8,10},{10,12},{12... | collective-permute-start | bytes 196616 | tf_op jit(solution)/shard_map/ppermute | solution.py:128
  209.1 26.1 %collective-permute-start.29 = (bf16[256,128]{1,0:T(8,128)(2,1)S(1)}, bf16[256,128]{1,0:T(8,128)(2,1)S(1)}, u32[]{:S(2)}, u32[]{:S(2)}) collective-permute-start(bf16[256,128]{1,0:T(8,128)(2,1)S(1)} %get-tuple-element.134), channel_id=1, source_target_pairs={{0,4},{2,6},{4,0},{6,2},{1,5},{3,7},{5,1},{7,3},{8,12},{10,14},{12... | collective-permute-start | bytes 196616 | tf_op jit(solution)/shard_map/ppermute | solution.py:128
  212.5 22.7 %collective-permute-start.30 = (bf16[256,128]{1,0:T(8,128)(2,1)S(1)}, bf16[256,128]{1,0:T(8,128)(2,1)S(1)}, u32[]{:S(2)}, u32[]{:S(2)}) collective-permute-start(bf16[256,128]{1,0:T(8,128)(2,1)S(1)} %get-tuple-element.135), channel_id=1, source_target_pairs={{0,6},{2,0},{4,2},{6,4},{1,7},{3,1},{5,3},{7,5},{8,14},{10,8},{12,... | collective-permute-start | bytes 196616 | tf_op jit(solution)/shard_map/ppermute | solution.py:128
  224.6 10.6 %copy-start.9 = (bf16[16,128,128]{2,1,0:T(8,128)(2,1)S(1)}, bf16[16,128,128]{2,1,0:T(8,128)(2,1)}, u32[]{:S(2)}) copy-start(bf16[16,128,128]{2,1,0:T(8,128)(2,1)} %copy-done.8) | copy-start | bytes 1572868
  224.6 10.6 %copy-start.21 = (bf16[4,256,128]{2,1,0:T(8,128)(2,1)S(1)}, bf16[4,256,128]{2,1,0:T(8,128)(2,1)}, u32[]{:S(2)}) copy-start(bf16[4,256,128]{2,1,0:T(8,128)(2,1)} %copy-done.20) | copy-start | bytes 786436
  236.0 4.5 %collective-permute-start.31 = (bf16[4,256,128]{2,1,0:T(8,128)(2,1)S(1)}, bf16[4,256,128]{2,1,0:T(8,128)(2,1)S(1)}, u32[]{:S(2)}, u32[]{:S(2)}) collective-permute-start(bf16[4,256,128]{2,1,0:T(8,128)(2,1)S(1)} %get-tuple-element.147), channel_id=1, source_target_pairs={{0,1},{1,0},{2,3},{3,2},{4,5},{5,4},{6,7},{7,6},{8,9},{9,8},{10,11... | collective-permute-start | bytes 786440 | tf_op jit(solution)/shard_map/ppermute | solution.py:128
  238.2 7.0 %collective-permute-start.32 = (f32[16,1024]{1,0:T(8,128)S(1)}, f32[16,1024]{1,0:T(8,128)S(1)}, u32[]{:S(2)}, u32[]{:S(2)}) collective-permute-start(f32[16,1024]{1,0:T(8,128)S(1)} %get-tuple-element.152), channel_id=1, source_target_pairs={{0,32},{32,0},{64,96},{96,64},{1,33},{33,1},{65,97},{97,65},{2,34}... | collective-permute-start | bytes 196616 | tf_op jit(solution)/shard_map/ppermute | solution.py:123
  238.3 6.9 %collective-permute-start.33 = (f32[16,1024]{1,0:T(8,128)S(1)}, f32[16,1024]{1,0:T(8,128)S(1)}, u32[]{:S(2)}, u32[]{:S(2)}) collective-permute-start(f32[16,1024]{1,0:T(8,128)S(1)} %get-tuple-element.153), channel_id=1, source_target_pairs={{0,1},{1,0},{2,3},{3,2},{4,5},{5,4},{6,7},{7,6},{8,9},{9,8},{10,11... | collective-permute-start | bytes 196616 | tf_op jit(solution)/shard_map/ppermute | solution.py:123
  238.8 6.4 %collective-permute-start.34 = (f32[16,1024]{1,0:T(8,128)S(1)}, f32[16,1024]{1,0:T(8,128)S(1)}, u32[]{:S(2)}, u32[]{:S(2)}) collective-permute-start(f32[16,1024]{1,0:T(8,128)S(1)} %get-tuple-element.154), channel_id=1, source_target_pairs={{0,33},{1,32},{32,1},{33,0},{64,97},{65,96},{96,65},{97,64},{2,35}... | collective-permute-start | bytes 196616 | tf_op jit(solution)/shard_map/ppermute | solution.py:667
  (23 other events, 49.1 us)
Sparse Core Ops, SparseCore 0:
  21.3 64.8 all-gather.1

commit v6 on v5

--- a/solution.py
+++ b/solution.py
@@ -147,10 +147,7 @@
     filled_plane = fill_plane(row, filled_row)
     rows_before = after(rows_before, filled_plane)
     own, *out = small_call(
-        functools.partial(plane_body, reverse),
-        where,
-        terms + rows_before,
-        [one] + [low] * (n - 1),
+        functools.partial(plane_body, reverse), where, terms + rows_before, [one] + [low] * (n - 1)
     )
     sums = [own] + [give_to(x, "y", k) for k, x in enumerate(out, 1)]
     filled_core = fill_core(out, filled_plane)
@@ -250,7 +247,7 @@
 
 
 PARTS = 1
-SLOTS = 3
+SLOTS = 2
 
 
 def grad_attn_body(
@@ -283,8 +280,7 @@
     @pl.when(g == 0)
     def _():
         whole.start()
-        for t in range(SLOTS):
-            load(t).start()
+        load(0).start()
 
     @pl.when(g < PARTS)
     def _():
@@ -298,11 +294,12 @@
     def _():
         t = g - PARTS
         load(t).wait()
+
+        @pl.when(t + 1 < last)
+        def _():
+            load(t + 1).start()
+
         finish(mm(go[...], w[lax.rem(t, SLOTS)].reshape(blocks * rows, d), 1, 1))
-
-        @pl.when(t + SLOTS < last)
-        def _():
-            load(t + SLOTS).start()
 
 
 def grad_attn(order, q, attended, gn, gain, grad_rows, gathered):
@@ -625,7 +622,7 @@
         lambda sent, done: (),
         lambda sent, done: (),
     )
-    near, far, attended = attend(turns, q, local_out, carried, gain_row)
+    near, far, attended = attend(turns, q, hbm(local_out), carried, gain_row)
     normed_all = [
         near,
         partner(near, "x", 1),
@@ -634,7 +631,7 @@
     ]
     gn = hbm(mm(after(sent_rows, near), out_weight, 1, 1))
 
-    ga, lg = grad_attn(where, q, attended, gn, gain_row, hbm(grad_rows), gathered)
+    ga, lg = grad_attn(where, q, hbm(attended), gn, gain_row, hbm(grad_rows), gathered)
     chips = blocks_n // 2
     shape = (chips, 2, out_weight.shape[0] // chips, half_cols // 2)
 
@@ -645,13 +642,11 @@
     def second_half(sent, done):
         for_partner, turned = done
         extra = give_to(for_partner, "c", 1)
-        return weight_half(
-            keep_body, mine, [after(turned, sent), extra], grads_all, shape, False
-        )
+        return weight_half(keep_body, mine, [after(turned, sent), extra], grads_all, shape, False)
 
     def rest(sent, partial):
         parts = lax.all_to_all(partial, ("z", "y"), 0, 0, tiled=True)
-        grads = local_grads(where, q, k, v, weights, after(ga, sent), carried)
+        grads = local_grads(where, q, k, v, hbm(weights), hbm(after(ga, sent)), carried)
         rows = layer_rows(where, near, after(far, grads), own_weight, gathered)
         return parts, (grads, rows)
 
@@ -659,7 +654,7 @@
         lg, where, at_core, True, first_half, second_half, rest
     )
     grad_query, pk, pv = grads
-    grad_key, grad_value = later_grads(where, k, v, later, pk, pv)
+    grad_key, grad_value = later_grads(where, k, v, later, hbm(pk), hbm(pv))
 
     parts = after(parts, layer_out, later[0])
     token_count = seqs * blocks_n * tok_rows

time: 255 us -> 254 us (level)
  local copies, waits for them, and re-layouts: 23 us -> 17 us
  Pallas kernels: 63.8 us -> 68.1 us
  waiting for transfers between devices: 92.2 us -> 95.5 us
  matrix products: 4.77 us -> 2.09 us
    unnamed x68 -> x58, local copies, waits for them, and re-layouts: 16.9 us -> 11 us
    dot_general x1, matrix products: 4.77 us -> 2.09 us  [mm(): lax.dot_general(a, b, (((ca,), (cb,)), ((), ())), preferred_element_type=...]
  transfers between devices with their start and end apart: 37 -> 37, of which waited for: 19 -> 19; matrix products, arithmetic and copies ran while one was open for 4% -> 3% of each run, Pallas kernels for 20% -> 22%
where the time goes in v6:
time: 254 us; the launch traced here: 252 us
  waiting for transfers between devices  95.5 us (38%)
  Pallas kernels  68.1 us (27%)
  starting transfers between devices  54.5 us (21%)
  local copies, waits for them, and re-layouts  17 us (7%)
  between operations  14.3 us (6%)
    ppermute x8, waiting for transfers between devices, partner(): lax.ppermute(x, axis, [(d, d ^ bits) for d in range(lax.axis_size(axis))])  46 us
    ppermute x23, starting transfers between devices, give_to(): return lax.ppermute(x, axis, [(d, (d + by) % n) for d in range(n)])  35.2 us
    ppermute x23, waiting for transfers between devices, give_to(): return lax.ppermute(x, axis, [(d, (d + by) % n) for d in range(n)])  34.9 us
    pallas_call x2, Pallas kernels, weight_half(): pl.pallas_call(body, grid_spec=pltpu.PrefetchScalarGridSpec(num_scalar_pr...  12.2 us
    pallas_call x1, Pallas kernels, grad_attn(): pl.pallas_call(grad_attn_body, grid_spec=pltpu.PrefetchScalarGridSpec(num...  11.6 us
    all_gather x1, waiting for transfers between devices, layer(): lax.all_gather(jnp.concatenate(pieces, axis=0), CTX, axis=0, tiled=True)  11.5 us
    unnamed x58, local copies, waits for them, and re-layouts  11 us
    pallas_call x1, Pallas kernels, layer_rows(): pl.pallas_call(layer_body, grid_spec=pltpu.PrefetchScalarGridSpec(num_sca...  10.6 us
  transfers between devices with their start and end apart: 37, of which 19 were waited for; matrix products, arithmetic and copies ran while one was open for 3% of the time, Pallas kernels for 22%

profile of v6, /device:TPU:0, one launch (start us, length us, event | category | flops | bytes accessed | tf_op | source)
XLA Modules:
  0.0 252.3 jit_solution(15884170919728147009)
XLA Ops:
  8.1 2.9 %collective-permute-start = (bf16[16,4096]{1,0:T(8,128)(2,1)S(1)}, bf16[16,4096]{1,0:T(8,128)(2,1)S(1)}, u32[]{:S(2)}, u32[]{:S(2)}) collective-permute-start(bf16[16,4096]{1,0:T(8,128)(2,1)S(1)} %constant_dynamic-slice_fusion.2), channel_id=1, source_target_pairs={{32,0},{64,32},{96,64},{0,96},{33,1},{65,33},{97,65},{1,97},{34,2}... | collective-permute-start | bytes 393224 | tf_op jit(solution)/shard_map/ppermute | solution.py:570
  15.2 1.3 local_state.1
  17.3 1.6 collective-permute-done.1
  18.9 1.4 collective-permute-done.2
  21.2 1.7 dynamic-slice_bitcast_fusion.1
  22.9 1.7 collective-permute-done.3.r_ref
  26.3 1.6 collective-permute-start.4
  27.9 2.9 %collective-permute-start.5 = (bf16[256,128]{1,0:T(8,128)(2,1)S(1)}, bf16[256,128]{1,0:T(8,128)(2,1)S(1)}, u32[]{:S(2)}, u32[]{:S(2)}) collective-permute-start(bf16[256,128]{1,0:T(8,128)(2,1)S(1)} %get-tuple-element.82), channel_id=1, source_target_pairs={{0,4},{2,6},{4,0},{6,2},{1,5},{3,7},{5,1},{7,3},{8,12},{10,14},{12... | collective-permute-start | bytes 196616 | tf_op jit(solution)/shard_map/ppermute | solution.py:128
  30.8 1.3 collective-permute-start.6
  32.2 4.0 %local_scores.1 = (bf16[16,256,256]{2,1,0:T(8,128)(2,1)}, f32[256,2048]{1,0:T(8,128)}) custom-call(bf16[256,2048]{1,0:T(8,128)(2,1)S(1)} %bitcast.34, bf16[256,2048]{1,0:T(8,128)(2,1)S(1)} %bitcast.39, bf16[256,2048]{1,0:T(8,128)(2,1)S(1)} %bitcast.43), custom_call_target="tpu_custom_call" | custom-call | flops 536870912 | bytes 7340032 | tf_op jit(solution)/shard_map/local_scores/pallas_call | solution.py:183
  36.8 2.1 collective-permute-start.7
  38.9 3.7 %collective-permute-start.8 = (bf16[256,128]{1,0:T(8,128)(2,1)S(1)}, bf16[256,128]{1,0:T(8,128)(2,1)S(1)}, u32[]{:S(2)}, u32[]{:S(2)}) collective-permute-start(bf16[256,128]{1,0:T(8,128)(2,1)S(1)} %shard_map.102), channel_id=1, source_target_pairs={{0,16},{8,24},{16,0},{24,8},{1,17},{9,25},{17,1},{25,9},{2,18},{10... | collective-permute-start | bytes 196616 | tf_op jit(solution)/shard_map/ppermute | solution.py:128
  43.5 1.8 collective-permute-done.7.z1
  45.2 2.5 collective-permute-done.8.z2
  47.7 1.3 shard_map.103
  49.8 2.4 collective-permute-start.11
  52.2 1.3 collective-permute-start.12
  59.0 3.3 %constant_dynamic-slice_fusion = (bf16[256,2048]{1,0:T(8,128)(2,1)}, bf16[256,2048]{1,0:T(8,128)(2,1)}) fusion(bf16[256,4096]{1,0:T(8,128)(2,1)} %bitcast.62, s32[]{:T(128)S(6)} %select_n.50, s32[]{:T(128)S(6)} %select_n.49), kind=kLoop, calls=%fused_computation.3 | loop fusion | bytes 4194312 | tf_op jit(solution)/shard_map/dynamic_slice | solution.py:603
  62.3 1.8 collective-permute-start.23
  64.1 2.3 collective-permute-start.22
  66.4 5.4 %attend.1 = (bf16[256,1024]{1,0:T(8,128)(2,1)}, bf16[256,1024]{1,0:T(8,128)(2,1)S(1)}, f32[4,256,512]{2,1,0:T(8,128)}) custom-call(s32[8]{0:T(128)S(1)} %stack.59.w_ref, bf16[256,2048]{1,0:T(8,128)(2,1)S(1)} %bitcast.35, f32[256,2048]{1,0:T(8,128)} %get-tuple-element.85.o_ref, bf16[8,128,128]{2,1,0:T(8,128)(2,1)S(1)} %bitcast.52, ...), custom_call_target="tpu_custom_call" | custom-call | flops 134217728 | bytes 6291456 | tf_op jit(solution)/shard_map/attend/pallas_call | solution.py:229
  72.6 2.1 fusion.gn_ref
  74.7 11.5 %all-gather.2.cloned.1.call-done = bf16[1536,4096]{1,0:T(8,128)(2,1)} async-done(((bf16[48,4096]{1,0:T(8,128)(2,1)}), bf16[1536,4096]{1,0:T(8,128)(2,1)}) %all-gather.2.cloned.1.call-update) | async-done | bytes 12582928 | tf_op jit(solution)/shard_map/all_gather | solution.py:604
  86.2 11.6 %grad_attn.1 = (bf16[4,256,512]{2,1,0:T(8,128)(2,1)}, bf16[16,128,128]{2,1,0:T(8,128)(2,1)S(1)}) custom-call(s32[8]{0:T(128)S(1)} %stack.54.w_ref.i_ref, bf16[256,2048]{1,0:T(8,128)(2,1)S(1)} %bitcast.36, f32[4,256,512]{2,1,0:T(8,128)} %get-tuple-element.107.a_ref, f32[256,512]{1,0:T(8,128)} %fusion.gn_ref, f32[1,2048]{1,0:T(1,128)S(1)} %bitcast.59, ...), custom_call_target="tpu_custom_call" | custom-call | flops 3355443200 | bytes 18874368 | tf_op jit(solution)/shard_map/grad_attn/pallas_call | solution.py:313
  98.4 23.4 %collective-permute-done.18.n1 = bf16[256,1024]{1,0:T(8,128)(2,1)} collective-permute-done((bf16[256,1024]{1,0:T(8,128)(2,1)}, bf16[256,1024]{1,0:T(8,128)(2,1)}, u32[]{:S(2)}, u32[]{:S(2)}) %collective-permute-start.18) | collective-permute-done | bytes 524320 | tf_op jit(solution)/shard_map/ppermute | solution.py:123
  121.8 1.3 collective-permute-start.19
  123.1 1.7 collective-permute-start.20
  125.5 11.4 %collective-permute-done.19.n2 = bf16[256,1024]{1,0:T(8,128)(2,1)S(1)} collective-permute-done((bf16[256,1024]{1,0:T(8,128)(2,1)S(1)}, bf16[256,1024]{1,0:T(8,128)(2,1)S(1)}, u32[]{:S(2)}, u32[]{:S(2)}) %collective-permute-start.19) | collective-permute-done | bytes 524320 | tf_op jit(solution)/shard_map/ppermute | solution.py:123
  136.9 11.1 %collective-permute-done.20.n3 = bf16[256,1024]{1,0:T(8,128)(2,1)S(1)} collective-permute-done((bf16[256,1024]{1,0:T(8,128)(2,1)S(1)}, bf16[256,1024]{1,0:T(8,128)(2,1)S(1)}, u32[]{:S(2)}, u32[]{:S(2)}) %collective-permute-start.20) | collective-permute-done | bytes 524320 | tf_op jit(solution)/shard_map/ppermute | solution.py:123
  148.1 6.6 %weight_half.2 = (bf16[16,2,32,1024]{3,2,1,0:T(8,128)(2,1)}, bf16[1024,1024]{1,0:T(8,128)(2,1)S(1)}) custom-call(s32[1]{0:T(128)S(6)} %sub.24.i_ref, bf16[256,1024]{1,0:T(8,128)(2,1)} %get-tuple-element.119.n0.near_ref, bf16[256,1024]{1,0:T(8,128)(2,1)} %collective-permute-done.18.n1, bf16[256,1024]{1,0:T(8,128)(2,1)S(1)} %collective-permute-done.19.n2, ...), custom_call_target="tpu_custom_call" | custom-call | flops 2147483648 | bytes 8388608 | tf_op jit(solution)/shard_map/weight_half/pallas_call | solution.py:509
  155.7 3.2 %collective-permute-start.16 = (bf16[256,128]{1,0:T(8,128)(2,1)S(1)}, bf16[256,128]{1,0:T(8,128)(2,1)S(1)}, u32[]{:S(2)}, u32[]{:S(2)}) collective-permute-start(bf16[256,128]{1,0:T(8,128)(2,1)S(1)} %get-tuple-element.117), channel_id=1, source_target_pairs={{0,4},{2,6},{4,0},{6,2},{1,5},{3,7},{5,1},{7,3},{8,12},{10,14},{12... | collective-permute-start | bytes 196616 | tf_op jit(solution)/shard_map/ppermute | solution.py:128
  159.0 1.4 collective-permute-done.15.refs_0_.t1
  160.4 2.3 collective-permute-done.16.refs_1_.t2
  165.1 5.6 %weight_half.3 = bf16[16,2,32,1024]{3,2,1,0:T(8,128)(2,1)} custom-call(s32[1]{0:T(128)} %bitcast.7.i_ref, bf16[1024,1024]{1,0:T(8,128)(2,1)S(1)} %get-tuple-element.129.nt_ref, bf16[16,2,32,1024]{3,2,1,0:T(8,128)(2,1)S(1)} %collective-permute-done.27.extra_ref, bf16[256,2048]{1,0:T(8,128)(2,1)} %get-tuple-element.156.rest_0_, ...), custom_call_target="tpu_custom_call" | custom-call | flops 2147483648 | bytes 8388608 | tf_op jit(solution)/shard_map/weight_half/pallas_call | solution.py:509
  170.7 5.2 %all-to-all-start = ((bf16[16,2,32,1024]{3,2,1,0:T(8,128)(2,1)}), bf16[16,2,32,1024]{3,2,1,0:T(8,128)(2,1)}, u32[]{:S(2)}, u32[]{:S(2)}) async-start(bf16[16,2,32,1024]{3,2,1,0:T(8,128)(2,1)} %weight_half.3), calls=%async_computation | async-start | bytes 4194304 | tf_op jit(solution)/shard_map/all_to_all | solution.py:648
  176.0 1.9 collective-permute-start.24
  177.8 2.7 %collective-permute-start.25 = (bf16[256,128]{1,0:T(8,128)(2,1)}, bf16[256,128]{1,0:T(8,128)(2,1)S(1)}, u32[]{:S(2)}, u32[]{:S(2)}) collective-permute-start(bf16[256,128]{1,0:T(8,128)(2,1)} %copy-done.25), channel_id=1, source_target_pairs={{0,16},{8,24},{16,0},{24,8},{1,17},{9,25},{17,1},{25,9},{2,18},{10... | collective-permute-start | bytes 196616 | tf_op jit(solution)/shard_map/ppermute | solution.py:128
  180.5 1.5 collective-permute-start.26
  182.0 19.2 %collective-permute-done.24.z1 = bf16[256,128]{1,0:T(8,128)(2,1)S(1)} collective-permute-done((bf16[256,128]{1,0:T(8,128)(2,1)}, bf16[256,128]{1,0:T(8,128)(2,1)S(1)}, u32[]{:S(2)}, u32[]{:S(2)}) %collective-permute-start.24) | collective-permute-done | bytes 65568 | tf_op jit(solution)/shard_map/ppermute | solution.py:128
  202.2 1.3 collective-permute-done.26.z3
  206.8 2.7 %collective-permute-start.28 = (bf16[256,128]{1,0:T(8,128)(2,1)S(1)}, bf16[256,128]{1,0:T(8,128)(2,1)S(1)}, u32[]{:S(2)}, u32[]{:S(2)}) collective-permute-start(bf16[256,128]{1,0:T(8,128)(2,1)S(1)} %get-tuple-element.133), channel_id=1, source_target_pairs={{0,2},{2,4},{4,6},{6,0},{1,3},{3,5},{5,7},{7,1},{8,10},{10,12},{12... | collective-permute-start | bytes 196616 | tf_op jit(solution)/shard_map/ppermute | solution.py:128
  209.5 3.4 %collective-permute-start.29 = (bf16[256,128]{1,0:T(8,128)(2,1)S(1)}, bf16[256,128]{1,0:T(8,128)(2,1)S(1)}, u32[]{:S(2)}, u32[]{:S(2)}) collective-permute-start(bf16[256,128]{1,0:T(8,128)(2,1)S(1)} %get-tuple-element.134), channel_id=1, source_target_pairs={{0,4},{2,6},{4,0},{6,2},{1,5},{3,7},{5,1},{7,3},{8,12},{10,14},{12... | collective-permute-start | bytes 196616 | tf_op jit(solution)/shard_map/ppermute | solution.py:128
  214.9 8.4 %local_grads.1 = (bf16[256,2048]{1,0:T(8,128)(2,1)}, f32[4,256,512]{2,1,0:T(8,128)}, f32[4,256,512]{2,1,0:T(8,128)}) custom-call(s32[8]{0:T(128)S(1)} %stack.54.w_ref.i_ref, bf16[256,2048]{1,0:T(8,128)(2,1)S(1)} %bitcast.37, bf16[256,2048]{1,0:T(8,128)(2,1)S(1)} %bitcast.40, bf16[256,2048]{1,0:T(8,128)(2,1)S(1)} %bitcast.44, ...), custom_call_target="tpu_custom_call" | custom-call | flops 1073741824 | bytes 12582912 | tf_op jit(solution)/shard_map/local_grads/pallas_call | solution.py:367
  223.3 10.6 %layer_rows.1 = bf16[256,4096]{1,0:T(8,128)(2,1)} custom-call(s32[8]{0:T(128)S(1)} %stack.54.w_ref.i_ref, bf16[256,1024]{1,0:T(8,128)(2,1)} %get-tuple-element.119.n0.near_ref, bf16[256,1024]{1,0:T(8,128)(2,1)S(1)} %copy-done.18, bf16[512,4096]{1,0:T(8,128)(2,1)} %own_ref.1, bf16[32,3,16,4096]{3,2,1,0:T(8,128)(2,1)} %bitcast.61), custom_call_target="tpu_custom_call" | custom-call | flops 4294967296 | bytes 19922944 | tf_op jit(solution)/shard_map/layer_rows/pallas_call | solution.py:451
  234.7 2.0 sum_parts.1
  237.3 1.6 collective-permute-start.34
  238.9 5.3 %later_grads.1 = (bf16[256,2048]{1,0:T(8,128)(2,1)}, bf16[256,2048]{1,0:T(8,128)(2,1)}) custom-call(s32[8]{0:T(128)S(1)} %stack.54.w_ref.i_ref, bf16[256,2048]{1,0:T(8,128)(2,1)S(1)} %bitcast.41, bf16[256,2048]{1,0:T(8,128)(2,1)S(1)} %bitcast.45, bf16[8,128,128]{2,1,0:T(8,128)(2,1)S(1)} %bitcast.56, bf16[8,128,128]{2,1,0:T(8,128)(2,1)S(1)} %bitcast.57, ...), custom_call_target="tpu_custom_call" | custom-call | flops 268435456 | bytes 8388608 | tf_op jit(solution)/shard_map/later_grads/pallas_call | solution.py:408
  244.2 1.3 shard_map.109
  (112 shorter events, 29.4 us)
Async XLA Ops:
  7.2 79.0 %all-gather.2.cloned.1.call-start = ((), (), s32[]{:S(2)}) async-start(), calls=%async_computation.1 | async-start | bytes 12976128 | tf_op jit(solution)/shard_map/all_gather | solution.py:604
  8.1 9.2 %collective-permute-start = (bf16[16,4096]{1,0:T(8,128)(2,1)S(1)}, bf16[16,4096]{1,0:T(8,128)(2,1)S(1)}, u32[]{:S(2)}, u32[]{:S(2)}) collective-permute-start(bf16[16,4096]{1,0:T(8,128)(2,1)S(1)} %constant_dynamic-slice_fusion.2), channel_id=1, source_target_pairs={{32,0},{64,32},{96,64},{0,96},{33,1},{65,33},{97,65},{1,97},{34,2}... | collective-permute-start | bytes 393224 | tf_op jit(solution)/shard_map/ppermute | solution.py:570
  11.1 7.9 %collective-permute-start.1 = (bf16[16,4096]{1,0:T(8,128)(2,1)S(1)}, bf16[16,4096]{1,0:T(8,128)(2,1)S(1)}, u32[]{:S(2)}, u32[]{:S(2)}) collective-permute-start(bf16[16,4096]{1,0:T(8,128)(2,1)S(1)} %constant_dynamic-slice_fusion.2), channel_id=1, source_target_pairs={{64,0},{96,32},{0,64},{32,96},{65,1},{97,33},{1,65},{33,97},{66,2}... | collective-permute-start | bytes 393224 | tf_op jit(solution)/shard_map/ppermute | solution.py:570
  11.9 8.5 %collective-permute-start.2 = (bf16[16,4096]{1,0:T(8,128)(2,1)S(1)}, bf16[16,4096]{1,0:T(8,128)(2,1)S(1)}, u32[]{:S(2)}, u32[]{:S(2)}) collective-permute-start(bf16[16,4096]{1,0:T(8,128)(2,1)S(1)} %constant_dynamic-slice_fusion.2), channel_id=1, source_target_pairs={{96,0},{0,32},{32,64},{64,96},{97,1},{1,33},{33,65},{65,97},{98,2}... | collective-permute-start | bytes 393224 | tf_op jit(solution)/shard_map/ppermute | solution.py:570
  15.2 16.9 %copy-start = (bf16[1,256,2048]{2,1,0:T(8,128)(2,1)S(1)}, bf16[1,256,2048]{2,1,0:T(8,128)(2,1)}, u32[]{:S(2)}) copy-start(bf16[1,256,2048]{2,1,0:T(8,128)(2,1)} %param.6) | copy-start | bytes 3145732
  15.2 16.9 %copy-start.2 = (bf16[1,256,2048]{2,1,0:T(8,128)(2,1)S(1)}, bf16[1,256,2048]{2,1,0:T(8,128)(2,1)}, u32[]{:S(2)}) copy-start(bf16[1,256,2048]{2,1,0:T(8,128)(2,1)} %param.7) | copy-start | bytes 3145732
  15.2 16.9 %copy-start.4 = (bf16[1,256,2048]{2,1,0:T(8,128)(2,1)S(1)}, bf16[1,256,2048]{2,1,0:T(8,128)(2,1)}, u32[]{:S(2)}) copy-start(bf16[1,256,2048]{2,1,0:T(8,128)(2,1)} %param.8) | copy-start | bytes 3145732
  22.8 1.7 collective-permute-start.3
  26.3 9.9 %collective-permute-start.4 = (bf16[256,128]{1,0:T(8,128)(2,1)S(1)}, bf16[256,128]{1,0:T(8,128)(2,1)S(1)}, u32[]{:S(2)}, u32[]{:S(2)}) collective-permute-start(bf16[256,128]{1,0:T(8,128)(2,1)S(1)} %get-tuple-element.81), channel_id=1, source_target_pairs={{0,2},{2,4},{4,6},{6,0},{1,3},{3,5},{5,7},{7,1},{8,10},{10,12},{12... | collective-permute-start | bytes 196616 | tf_op jit(solution)/shard_map/ppermute | solution.py:128
  27.9 8.2 %collective-permute-start.5 = (bf16[256,128]{1,0:T(8,128)(2,1)S(1)}, bf16[256,128]{1,0:T(8,128)(2,1)S(1)}, u32[]{:S(2)}, u32[]{:S(2)}) collective-permute-start(bf16[256,128]{1,0:T(8,128)(2,1)S(1)} %get-tuple-element.82), channel_id=1, source_target_pairs={{0,4},{2,6},{4,0},{6,2},{1,5},{3,7},{5,1},{7,3},{8,12},{10,14},{12... | collective-permute-start | bytes 196616 | tf_op jit(solution)/shard_map/ppermute | solution.py:128
  30.8 5.4 %collective-permute-start.6 = (bf16[256,128]{1,0:T(8,128)(2,1)S(1)}, bf16[256,128]{1,0:T(8,128)(2,1)S(1)}, u32[]{:S(2)}, u32[]{:S(2)}) collective-permute-start(bf16[256,128]{1,0:T(8,128)(2,1)S(1)} %get-tuple-element.83), channel_id=1, source_target_pairs={{0,6},{2,0},{4,2},{6,4},{1,7},{3,1},{5,3},{7,5},{8,14},{10,8},{12,... | collective-permute-start | bytes 196616 | tf_op jit(solution)/shard_map/ppermute | solution.py:128
  36.8 8.4 %collective-permute-start.7 = (bf16[256,128]{1,0:T(8,128)(2,1)S(1)}, bf16[256,128]{1,0:T(8,128)(2,1)S(1)}, u32[]{:S(2)}, u32[]{:S(2)}) collective-permute-start(bf16[256,128]{1,0:T(8,128)(2,1)S(1)} %shard_map.102), channel_id=1, source_target_pairs={{0,8},{8,16},{16,24},{24,0},{1,9},{9,17},{17,25},{25,1},{2,10},{10... | collective-permute-start | bytes 196616 | tf_op jit(solution)/shard_map/ppermute | solution.py:128
  38.9 8.8 %collective-permute-start.8 = (bf16[256,128]{1,0:T(8,128)(2,1)S(1)}, bf16[256,128]{1,0:T(8,128)(2,1)S(1)}, u32[]{:S(2)}, u32[]{:S(2)}) collective-permute-start(bf16[256,128]{1,0:T(8,128)(2,1)S(1)} %shard_map.102), channel_id=1, source_target_pairs={{0,16},{8,24},{16,0},{24,8},{1,17},{9,25},{17,1},{25,9},{2,18},{10... | collective-permute-start | bytes 196616 | tf_op jit(solution)/shard_map/ppermute | solution.py:128
  42.6 5.1 %collective-permute-start.9 = (bf16[256,128]{1,0:T(8,128)(2,1)S(1)}, bf16[256,128]{1,0:T(8,128)(2,1)S(1)}, u32[]{:S(2)}, u32[]{:S(2)}) collective-permute-start(bf16[256,128]{1,0:T(8,128)(2,1)S(1)} %shard_map.102), channel_id=1, source_target_pairs={{0,24},{8,0},{16,8},{24,16},{1,25},{9,1},{17,9},{25,17},{2,26},{10... | collective-permute-start | bytes 196616 | tf_op jit(solution)/shard_map/ppermute | solution.py:128
  49.0 5.8 %collective-permute-start.10 = (bf16[256,128]{1,0:T(8,128)(2,1)}, bf16[256,128]{1,0:T(8,128)(2,1)}, u32[]{:S(2)}, u32[]{:S(2)}) collective-permute-start(bf16[256,128]{1,0:T(8,128)(2,1)} %get-tuple-element.96), channel_id=1, source_target_pairs={{0,2},{2,4},{4,6},{6,0},{1,3},{3,5},{5,7},{7,1},{8,10},{10,12},{12... | collective-permute-start | bytes 196616 | tf_op jit(solution)/shard_map/ppermute | solution.py:128
  49.8 6.1 %collective-permute-start.11 = (bf16[256,128]{1,0:T(8,128)(2,1)}, bf16[256,128]{1,0:T(8,128)(2,1)}, u32[]{:S(2)}, u32[]{:S(2)}) collective-permute-start(bf16[256,128]{1,0:T(8,128)(2,1)} %get-tuple-element.97), channel_id=1, source_target_pairs={{0,4},{2,6},{4,0},{6,2},{1,5},{3,7},{5,1},{7,3},{8,12},{10,14},{12... | collective-permute-start | bytes 196616 | tf_op jit(solution)/shard_map/ppermute | solution.py:128
  52.2 4.6 %collective-permute-start.12 = (bf16[256,128]{1,0:T(8,128)(2,1)}, bf16[256,128]{1,0:T(8,128)(2,1)}, u32[]{:S(2)}, u32[]{:S(2)}) collective-permute-start(bf16[256,128]{1,0:T(8,128)(2,1)} %get-tuple-element.98), channel_id=1, source_target_pairs={{0,6},{2,0},{4,2},{6,4},{1,7},{3,1},{5,3},{7,5},{8,14},{10,8},{12,... | collective-permute-start | bytes 196616 | tf_op jit(solution)/shard_map/ppermute | solution.py:128
  58.9 7.5 %collective-permute-start.13 = (bf16[4,256,128]{2,1,0:T(8,128)(2,1)S(1)}, bf16[4,256,128]{2,1,0:T(8,128)(2,1)S(1)}, u32[]{:S(2)}, u32[]{:S(2)}) collective-permute-start(bf16[4,256,128]{2,1,0:T(8,128)(2,1)S(1)} %get-tuple-element.104), channel_id=1, source_target_pairs={{0,1},{1,0},{2,3},{3,2},{4,5},{5,4},{6,7},{7,6},{8,9},{9,8},{10,11... | collective-permute-start | bytes 786440 | tf_op jit(solution)/shard_map/ppermute | solution.py:128
  59.0 13.6 %copy-start.28 = (bf16[512,4096]{1,0:T(8,128)(2,1)S(1)}, bf16[512,4096]{1,0:T(8,128)(2,1)}, u32[]{:S(2)}) copy-start(bf16[512,4096]{1,0:T(8,128)(2,1)} %own_ref.1) | copy-start | bytes 12582916
  62.3 10.3 %copy-start.27 = (bf16[1,256,4096]{2,1,0:T(8,128)(2,1)S(1)}, bf16[1,256,4096]{2,1,0:T(8,128)(2,1)}, u32[]{:S(2)}) copy-start(bf16[1,256,4096]{2,1,0:T(8,128)(2,1)} %param.11) | copy-start | bytes 6291460
  62.3 85.8 %collective-permute-start.21 = (bf16[256,2048]{1,0:T(8,128)(2,1)}, bf16[256,2048]{1,0:T(8,128)(2,1)}, u32[]{:S(2)}, u32[]{:S(2)}) collective-permute-start(bf16[256,2048]{1,0:T(8,128)(2,1)} %get-tuple-element.155), channel_id=1, source_target_pairs={{0,32},{32,0},{64,96},{96,64},{1,33},{33,1},{65,97},{97,65},{2,34}... | collective-permute-start | bytes 3145736 | tf_op jit(solution)/shard_map/ppermute | solution.py:123
  62.3 85.8 %collective-permute-start.23 = (bf16[256,2048]{1,0:T(8,128)(2,1)}, bf16[256,2048]{1,0:T(8,128)(2,1)}, u32[]{:S(2)}, u32[]{:S(2)}) collective-permute-start(bf16[256,2048]{1,0:T(8,128)(2,1)} %get-tuple-element.155), channel_id=1, source_target_pairs={{0,96},{32,64},{64,32},{96,0},{1,97},{33,65},{65,33},{97,1},{2,98}... | collective-permute-start | bytes 3145736 | tf_op jit(solution)/shard_map/ppermute | solution.py:123
  64.1 84.0 %collective-permute-start.22 = (bf16[256,2048]{1,0:T(8,128)(2,1)}, bf16[256,2048]{1,0:T(8,128)(2,1)}, u32[]{:S(2)}, u32[]{:S(2)}) collective-permute-start(bf16[256,2048]{1,0:T(8,128)(2,1)} %get-tuple-element.156.rest_0_), channel_id=1, source_target_pairs={{0,64},{32,96},{64,0},{96,32},{1,65},{33,97},{65,1},{97,33},{2,66}... | collective-permute-start | bytes 3145736 | tf_op jit(solution)/shard_map/ppermute | solution.py:123
  72.6 49.2 %collective-permute-start.18 = (bf16[256,1024]{1,0:T(8,128)(2,1)}, bf16[256,1024]{1,0:T(8,128)(2,1)}, u32[]{:S(2)}, u32[]{:S(2)}) collective-permute-start(bf16[256,1024]{1,0:T(8,128)(2,1)} %get-tuple-element.119.n0.near_ref), channel_id=1, source_target_pairs={{0,32},{32,0},{64,96},{96,64},{1,33},{33,1},{65,97},{97,65},{2,34}... | collective-permute-start | bytes 1572872 | tf_op jit(solution)/shard_map/ppermute | solution.py:123
  86.2 35.6 %copy-start.17 = (bf16[256,1024]{1,0:T(8,128)(2,1)S(1)}, bf16[256,1024]{1,0:T(8,128)(2,1)}, u32[]{:S(2)}) copy-start(bf16[256,1024]{1,0:T(8,128)(2,1)} %copy-done.16) | copy-start | bytes 1572868
  97.8 27.0 %copy-start.8 = (bf16[16,128,128]{2,1,0:T(8,128)(2,1)}, bf16[16,128,128]{2,1,0:T(8,128)(2,1)S(1)}, u32[]{:S(2)}) copy-start(bf16[16,128,128]{2,1,0:T(8,128)(2,1)S(1)} %get-tuple-element.114) | copy-start | bytes 1572868
  97.9 25.2 %collective-permute-start.14 = (bf16[4,256,128]{2,1,0:T(8,128)(2,1)S(1)}, bf16[4,256,128]{2,1,0:T(8,128)(2,1)S(1)}, u32[]{:S(2)}, u32[]{:S(2)}) collective-permute-start(bf16[4,256,128]{2,1,0:T(8,128)(2,1)S(1)} %dynamic-slice_bitcast_fusion), channel_id=1, source_target_pairs={{0,1},{1,0},{2,3},{3,2},{4,5},{5,4},{6,7},{7,6},{8,9},{9,8},{10,11... | collective-permute-start | bytes 786440 | tf_op jit(solution)/shard_map/ppermute | solution.py:128
  121.8 15.1 %collective-permute-start.19 = (bf16[256,1024]{1,0:T(8,128)(2,1)S(1)}, bf16[256,1024]{1,0:T(8,128)(2,1)S(1)}, u32[]{:S(2)}, u32[]{:S(2)}) collective-permute-start(bf16[256,1024]{1,0:T(8,128)(2,1)S(1)} %copy-done.17), channel_id=1, source_target_pairs={{0,64},{32,96},{64,0},{96,32},{1,65},{33,97},{65,1},{97,33},{2,66}... | collective-permute-start | bytes 1572872 | tf_op jit(solution)/shard_map/ppermute | solution.py:123
  123.1 24.9 %copy-start.14 = (bf16[4,256,128]{2,1,0:T(8,128)(2,1)}, bf16[4,256,128]{2,1,0:T(8,128)(2,1)S(1)}, u32[]{:S(2)}) copy-start(bf16[4,256,128]{2,1,0:T(8,128)(2,1)S(1)} %collective-permute-done.14.r_ref) | copy-start | bytes 786436
  123.1 24.9 %collective-permute-start.20 = (bf16[256,1024]{1,0:T(8,128)(2,1)S(1)}, bf16[256,1024]{1,0:T(8,128)(2,1)S(1)}, u32[]{:S(2)}, u32[]{:S(2)}) collective-permute-start(bf16[256,1024]{1,0:T(8,128)(2,1)S(1)} %copy-done.17), channel_id=1, source_target_pairs={{0,96},{32,64},{64,32},{96,0},{1,97},{33,65},{65,33},{97,1},{2,98}... | collective-permute-start | bytes 1572872 | tf_op jit(solution)/shard_map/ppermute | solution.py:123
  154.7 10.4 %collective-permute-start.27 = (bf16[16,2,32,1024]{3,2,1,0:T(8,128)(2,1)}, bf16[16,2,32,1024]{3,2,1,0:T(8,128)(2,1)S(1)}, u32[]{:S(2)}, u32[]{:S(2)}) collective-permute-start(bf16[16,2,32,1024]{3,2,1,0:T(8,128)(2,1)} %get-tuple-element.123), channel_id=1, source_target_pairs={{0,1},{1,0},{2,3},{3,2},{4,5},{5,4},{6,7},{7,6},{8,9},{9,8},{10,11... | collective-permute-start | bytes 6291464 | tf_op jit(solution)/shard_map/ppermute | solution.py:128
  154.7 5.7 %collective-permute-start.15 = (bf16[256,128]{1,0:T(8,128)(2,1)S(1)}, bf16[256,128]{1,0:T(8,128)(2,1)S(1)}, u32[]{:S(2)}, u32[]{:S(2)}) collective-permute-start(bf16[256,128]{1,0:T(8,128)(2,1)S(1)} %get-tuple-element.116), channel_id=1, source_target_pairs={{0,2},{2,4},{4,6},{6,0},{1,3},{3,5},{5,7},{7,1},{8,10},{10,12},{12... | collective-permute-start | bytes 196616 | tf_op jit(solution)/shard_map/ppermute | solution.py:128
  155.7 7.1 %collective-permute-start.16 = (bf16[256,128]{1,0:T(8,128)(2,1)S(1)}, bf16[256,128]{1,0:T(8,128)(2,1)S(1)}, u32[]{:S(2)}, u32[]{:S(2)}) collective-permute-start(bf16[256,128]{1,0:T(8,128)(2,1)S(1)} %get-tuple-element.117), channel_id=1, source_target_pairs={{0,4},{2,6},{4,0},{6,2},{1,5},{3,7},{5,1},{7,3},{8,12},{10,14},{12... | collective-permute-start | bytes 196616 | tf_op jit(solution)/shard_map/ppermute | solution.py:128
  158.9 4.3 %collective-permute-start.17 = (bf16[256,128]{1,0:T(8,128)(2,1)S(1)}, bf16[256,128]{1,0:T(8,128)(2,1)S(1)}, u32[]{:S(2)}, u32[]{:S(2)}) collective-permute-start(bf16[256,128]{1,0:T(8,128)(2,1)S(1)} %get-tuple-element.118), channel_id=1, source_target_pairs={{0,6},{2,0},{4,2},{6,4},{1,7},{3,1},{5,3},{7,5},{8,14},{10,8},{12,... | collective-permute-start | bytes 196616 | tf_op jit(solution)/shard_map/ppermute | solution.py:128
  170.7 43.2 %copy-start.11 = (bf16[4,256,128]{2,1,0:T(8,128)(2,1)S(1)}, bf16[4,256,128]{2,1,0:T(8,128)(2,1)}, u32[]{:S(2)}) copy-start(bf16[4,256,128]{2,1,0:T(8,128)(2,1)} %copy-done.10) | copy-start | bytes 786436
  170.7 64.0 %all-to-all-start = ((bf16[16,2,32,1024]{3,2,1,0:T(8,128)(2,1)}), bf16[16,2,32,1024]{3,2,1,0:T(8,128)(2,1)}, u32[]{:S(2)}, u32[]{:S(2)}) async-start(bf16[16,2,32,1024]{3,2,1,0:T(8,128)(2,1)} %weight_half.3), calls=%async_computation | async-start | bytes 4194304 | tf_op jit(solution)/shard_map/all_to_all | solution.py:648
  176.0 25.2 %collective-permute-start.24 = (bf16[256,128]{1,0:T(8,128)(2,1)}, bf16[256,128]{1,0:T(8,128)(2,1)S(1)}, u32[]{:S(2)}, u32[]{:S(2)}) collective-permute-start(bf16[256,128]{1,0:T(8,128)(2,1)} %copy-done.25), channel_id=1, source_target_pairs={{0,8},{8,16},{16,24},{24,0},{1,9},{9,17},{17,25},{25,1},{2,10},{10... | collective-permute-start | bytes 196616 | tf_op jit(solution)/shard_map/ppermute | solution.py:128
  177.8 24.4 %collective-permute-start.25 = (bf16[256,128]{1,0:T(8,128)(2,1)}, bf16[256,128]{1,0:T(8,128)(2,1)S(1)}, u32[]{:S(2)}, u32[]{:S(2)}) collective-permute-start(bf16[256,128]{1,0:T(8,128)(2,1)} %copy-done.25), channel_id=1, source_target_pairs={{0,16},{8,24},{16,0},{24,8},{1,17},{9,25},{17,1},{25,9},{2,18},{10... | collective-permute-start | bytes 196616 | tf_op jit(solution)/shard_map/ppermute | solution.py:128
  180.5 23.0 %collective-permute-start.26 = (bf16[256,128]{1,0:T(8,128)(2,1)}, bf16[256,128]{1,0:T(8,128)(2,1)S(1)}, u32[]{:S(2)}, u32[]{:S(2)}) collective-permute-start(bf16[256,128]{1,0:T(8,128)(2,1)} %copy-done.25), channel_id=1, source_target_pairs={{0,24},{8,0},{16,8},{24,16},{1,25},{9,1},{17,9},{25,17},{2,26},{10... | collective-permute-start | bytes 196616 | tf_op jit(solution)/shard_map/ppermute | solution.py:128
  206.8 27.1 %collective-permute-start.28 = (bf16[256,128]{1,0:T(8,128)(2,1)S(1)}, bf16[256,128]{1,0:T(8,128)(2,1)S(1)}, u32[]{:S(2)}, u32[]{:S(2)}) collective-permute-start(bf16[256,128]{1,0:T(8,128)(2,1)S(1)} %get-tuple-element.133), channel_id=1, source_target_pairs={{0,2},{2,4},{4,6},{6,0},{1,3},{3,5},{5,7},{7,1},{8,10},{10,12},{12... | collective-permute-start | bytes 196616 | tf_op jit(solution)/shard_map/ppermute | solution.py:128
  209.5 24.4 %collective-permute-start.29 = (bf16[256,128]{1,0:T(8,128)(2,1)S(1)}, bf16[256,128]{1,0:T(8,128)(2,1)S(1)}, u32[]{:S(2)}, u32[]{:S(2)}) collective-permute-start(bf16[256,128]{1,0:T(8,128)(2,1)S(1)} %get-tuple-element.134), channel_id=1, source_target_pairs={{0,4},{2,6},{4,0},{6,2},{1,5},{3,7},{5,1},{7,3},{8,12},{10,14},{12... | collective-permute-start | bytes 196616 | tf_op jit(solution)/shard_map/ppermute | solution.py:128
  212.9 21.0 %collective-permute-start.30 = (bf16[256,128]{1,0:T(8,128)(2,1)S(1)}, bf16[256,128]{1,0:T(8,128)(2,1)S(1)}, u32[]{:S(2)}, u32[]{:S(2)}) collective-permute-start(bf16[256,128]{1,0:T(8,128)(2,1)S(1)} %get-tuple-element.135), channel_id=1, source_target_pairs={{0,6},{2,0},{4,2},{6,4},{1,7},{3,1},{5,3},{7,5},{8,14},{10,8},{12,... | collective-permute-start | bytes 196616 | tf_op jit(solution)/shard_map/ppermute | solution.py:128
  223.2 10.6 %copy-start.9 = (bf16[16,128,128]{2,1,0:T(8,128)(2,1)S(1)}, bf16[16,128,128]{2,1,0:T(8,128)(2,1)}, u32[]{:S(2)}) copy-start(bf16[16,128,128]{2,1,0:T(8,128)(2,1)} %copy-done.8) | copy-start | bytes 1572868
  223.2 10.6 %copy-start.15 = (bf16[4,256,128]{2,1,0:T(8,128)(2,1)S(1)}, bf16[4,256,128]{2,1,0:T(8,128)(2,1)}, u32[]{:S(2)}) copy-start(bf16[4,256,128]{2,1,0:T(8,128)(2,1)} %copy-done.14) | copy-start | bytes 786436
  234.6 4.3 %collective-permute-start.31 = (bf16[4,256,128]{2,1,0:T(8,128)(2,1)S(1)}, bf16[4,256,128]{2,1,0:T(8,128)(2,1)S(1)}, u32[]{:S(2)}, u32[]{:S(2)}) collective-permute-start(bf16[4,256,128]{2,1,0:T(8,128)(2,1)S(1)} %get-tuple-element.147), channel_id=1, source_target_pairs={{0,1},{1,0},{2,3},{3,2},{4,5},{5,4},{6,7},{7,6},{8,9},{9,8},{10,11... | collective-permute-start | bytes 786440 | tf_op jit(solution)/shard_map/ppermute | solution.py:128
  236.7 7.5 %collective-permute-start.32 = (f32[16,1024]{1,0:T(8,128)S(1)}, f32[16,1024]{1,0:T(8,128)S(1)}, u32[]{:S(2)}, u32[]{:S(2)}) collective-permute-start(f32[16,1024]{1,0:T(8,128)S(1)} %get-tuple-element.152), channel_id=1, source_target_pairs={{0,32},{32,0},{64,96},{96,64},{1,33},{33,1},{65,97},{97,65},{2,34}... | collective-permute-start | bytes 196616 | tf_op jit(solution)/shard_map/ppermute | solution.py:123
  236.8 7.4 %collective-permute-start.33 = (f32[16,1024]{1,0:T(8,128)S(1)}, f32[16,1024]{1,0:T(8,128)S(1)}, u32[]{:S(2)}, u32[]{:S(2)}) collective-permute-start(f32[16,1024]{1,0:T(8,128)S(1)} %get-tuple-element.153), channel_id=1, source_target_pairs={{0,1},{1,0},{2,3},{3,2},{4,5},{5,4},{6,7},{7,6},{8,9},{9,8},{10,11... | collective-permute-start | bytes 196616 | tf_op jit(solution)/shard_map/ppermute | solution.py:123
  237.3 6.9 %collective-permute-start.34 = (f32[16,1024]{1,0:T(8,128)S(1)}, f32[16,1024]{1,0:T(8,128)S(1)}, u32[]{:S(2)}, u32[]{:S(2)}) collective-permute-start(f32[16,1024]{1,0:T(8,128)S(1)} %get-tuple-element.154), channel_id=1, source_target_pairs={{0,33},{1,32},{32,1},{33,0},{64,97},{65,96},{96,65},{97,64},{2,35}... | collective-permute-start | bytes 196616 | tf_op jit(solution)/shard_map/ppermute | solution.py:662
  (18 other events, 41.3 us)
Sparse Core Ops, SparseCore 0:
  21.3 64.8 all-gather.1

commit v7 on v6

--- a/solution.py
+++ b/solution.py
@@ -355,8 +355,8 @@
         gs = jnp.where(keep, mm(ga, head(v_ref, h), 1, 1), 0.0).astype(BF)
         gq = mm(gs, head(k_ref, h), 1, 0) + mm(ga, pick(i_ref, chunk, m_ref, t_ref, h), 1, 1)
         gq_ref[:, cols] = gq.astype(BF)
-        gk_ref[0, :, cols] = mm(gs, head(q_ref, h), 0, 0)
-        gv_ref[0, :, cols] = mm(w_ref[h], ga, 0, 0)
+        gk_ref[0, :, cols] = mm(gs, head(q_ref, h), 0, 0).astype(BF)
+        gv_ref[0, :, cols] = mm(w_ref[h], ga, 0, 0).astype(BF)
 
 
 def local_grads(order, q, k, v, weights, ga, carried):
@@ -381,8 +381,8 @@
         ),
         out_shape=[
             jax.ShapeDtypeStruct((t, f), BF),
-            pltpu.HBM((CH, t, w), F32),
-            pltpu.HBM((CH, t, w), F32),
+            jax.ShapeDtypeStruct((CH, t, w), BF),
+            jax.ShapeDtypeStruct((CH, t, w), BF),
         ],
         cost_estimate=cost(8 * t * t * f, 24 * t * f),
         compiler_params=pltpu.CompilerParams(vmem_limit_bytes=20 << 20),
@@ -394,8 +394,8 @@
     for h in range(HC):
         cols = slice(h * HD, (h + 1) * HD)
         state = pick(i_ref, pl.program_id(0), m_ref, t_ref, h)
-        gk = pk_ref[0, :, cols] + mm(head(v_ref, h), state, 1, 1)
-        gv = pv_ref[0, :, cols] + mm(head(k_ref, h), state, 1, 0)
+        gk = pk_ref[0, :, cols].astype(F32) + mm(head(v_ref, h), state, 1, 1)
+        gv = pv_ref[0, :, cols].astype(F32) + mm(head(k_ref, h), state, 1, 0)
         gk_ref[:, cols] = gk.astype(BF)
         gv_ref[:, cols] = gv.astype(BF)
 
@@ -654,7 +654,7 @@
         lg, where, at_core, True, first_half, second_half, rest
     )
     grad_query, pk, pv = grads
-    grad_key, grad_value = later_grads(where, k, v, later, hbm(pk), hbm(pv))
+    grad_key, grad_value = later_grads(where, k, v, later, pk, pv)
 
     parts = after(parts, layer_out, later[0])
     token_count = seqs * blocks_n * tok_rows

time: 254 us -> 256 us (level)
  local copies, waits for them, and re-layouts: 17 us -> 20.9 us
    unnamed x58 -> x70, local copies, waits for them, and re-layouts: 11 us -> 14.8 us
  transfers between devices with their start and end apart: 37 -> 37, of which waited for: 19 -> 19; matrix products, arithmetic and copies ran while one was open for 3% -> 3% of each run, Pallas kernels for 22% -> 21%
where the time goes in v7:
time: 256 us; the launch traced here: 254 us
  waiting for transfers between devices  95.5 us (37%)
  Pallas kernels  65.6 us (26%)
  starting transfers between devices  54.5 us (21%)
  local copies, waits for them, and re-layouts  20.9 us (8%)
  between operations  14.3 us (6%)
    ppermute x8, waiting for transfers between devices, partner(): lax.ppermute(x, axis, [(d, d ^ bits) for d in range(lax.axis_size(axis))])  46 us
    ppermute x23, starting transfers between devices, give_to(): return lax.ppermute(x, axis, [(d, (d + by) % n) for d in range(n)])  35.3 us
    ppermute x23, waiting for transfers between devices, give_to(): return lax.ppermute(x, axis, [(d, (d + by) % n) for d in range(n)])  34.9 us
    unnamed x70, local copies, waits for them, and re-layouts  14.8 us
    pallas_call x2, Pallas kernels, weight_half(): pl.pallas_call(body, grid_spec=pltpu.PrefetchScalarGridSpec(num_scalar_pr...  12.2 us
    pallas_call x1, Pallas kernels, grad_attn(): pl.pallas_call(grad_attn_body, grid_spec=pltpu.PrefetchScalarGridSpec(num...  11.6 us
    all_gather x1, waiting for transfers between devices, layer(): lax.all_gather(jnp.concatenate(pieces, axis=0), CTX, axis=0, tiled=True)  11.6 us
    pallas_call x1, Pallas kernels, layer_rows(): pl.pallas_call(layer_body, grid_spec=pltpu.PrefetchScalarGridSpec(num_sca...  10.7 us
  transfers between devices with their start and end apart: 37, of which 19 were waited for; matrix products, arithmetic and copies ran while one was open for 3% of the time, Pallas kernels for 21%

profile of v7, /device:TPU:0, one launch (start us, length us, event | category | flops | bytes accessed | tf_op | source)
XLA Modules:
  0.0 253.7 jit_solution(12271436667930877994)
XLA Ops:
  8.1 2.9 %collective-permute-start = (bf16[16,4096]{1,0:T(8,128)(2,1)S(1)}, bf16[16,4096]{1,0:T(8,128)(2,1)S(1)}, u32[]{:S(2)}, u32[]{:S(2)}) collective-permute-start(bf16[16,4096]{1,0:T(8,128)(2,1)S(1)} %constant_dynamic-slice_fusion.2), channel_id=1, source_target_pairs={{32,0},{64,32},{96,64},{0,96},{33,1},{65,33},{97,65},{1,97},{34,2}... | collective-permute-start | bytes 393224 | tf_op jit(solution)/shard_map/ppermute | solution.py:570
  15.2 1.3 local_state.1
  17.3 1.6 collective-permute-done.1
  18.9 1.4 collective-permute-done.2
  21.2 1.7 dynamic-slice_bitcast_fusion.1
  22.9 1.7 collective-permute-done.3.r_ref
  26.2 1.6 collective-permute-start.4
  27.9 2.9 %collective-permute-start.5 = (bf16[256,128]{1,0:T(8,128)(2,1)S(1)}, bf16[256,128]{1,0:T(8,128)(2,1)S(1)}, u32[]{:S(2)}, u32[]{:S(2)}) collective-permute-start(bf16[256,128]{1,0:T(8,128)(2,1)S(1)} %get-tuple-element.82), channel_id=1, source_target_pairs={{0,4},{2,6},{4,0},{6,2},{1,5},{3,7},{5,1},{7,3},{8,12},{10,14},{12... | collective-permute-start | bytes 196616 | tf_op jit(solution)/shard_map/ppermute | solution.py:128
  30.8 1.3 collective-permute-start.6
  32.2 3.9 %local_scores.1 = (bf16[16,256,256]{2,1,0:T(8,128)(2,1)}, f32[256,2048]{1,0:T(8,128)}) custom-call(bf16[256,2048]{1,0:T(8,128)(2,1)S(1)} %bitcast.42, bf16[256,2048]{1,0:T(8,128)(2,1)S(1)} %bitcast.35, bf16[256,2048]{1,0:T(8,128)(2,1)S(1)} %bitcast.39), custom_call_target="tpu_custom_call" | custom-call | flops 536870912 | bytes 7340032 | tf_op jit(solution)/shard_map/local_scores/pallas_call | solution.py:183
  36.8 2.1 collective-permute-start.7
  38.9 3.7 %collective-permute-start.8 = (bf16[256,128]{1,0:T(8,128)(2,1)S(1)}, bf16[256,128]{1,0:T(8,128)(2,1)S(1)}, u32[]{:S(2)}, u32[]{:S(2)}) collective-permute-start(bf16[256,128]{1,0:T(8,128)(2,1)S(1)} %shard_map.102), channel_id=1, source_target_pairs={{0,16},{8,24},{16,0},{24,8},{1,17},{9,25},{17,1},{25,9},{2,18},{10... | collective-permute-start | bytes 196616 | tf_op jit(solution)/shard_map/ppermute | solution.py:128
  43.4 1.7 collective-permute-done.7.z1
  45.2 2.5 collective-permute-done.8.z2
  47.7 1.3 shard_map.103
  49.8 2.4 collective-permute-start.11
  52.2 1.3 collective-permute-start.12
  59.0 3.3 %constant_dynamic-slice_fusion = (bf16[256,2048]{1,0:T(8,128)(2,1)}, bf16[256,2048]{1,0:T(8,128)(2,1)}) fusion(bf16[256,4096]{1,0:T(8,128)(2,1)} %bitcast.62, s32[]{:T(128)S(6)} %select_n.50, s32[]{:T(128)S(6)} %select_n.49), kind=kLoop, calls=%fused_computation.3 | loop fusion | bytes 4194312 | tf_op jit(solution)/shard_map/dynamic_slice | solution.py:603
  62.3 1.8 collective-permute-start.23
  64.1 2.3 collective-permute-start.22
  66.4 5.4 %attend.1 = (bf16[256,1024]{1,0:T(8,128)(2,1)}, bf16[256,1024]{1,0:T(8,128)(2,1)S(1)}, f32[4,256,512]{2,1,0:T(8,128)}) custom-call(s32[8]{0:T(128)S(1)} %stack.59.w_ref, bf16[256,2048]{1,0:T(8,128)(2,1)S(1)} %bitcast.43, f32[256,2048]{1,0:T(8,128)} %get-tuple-element.85.o_ref, bf16[8,128,128]{2,1,0:T(8,128)(2,1)S(1)} %bitcast.52, ...), custom_call_target="tpu_custom_call" | custom-call | flops 134217728 | bytes 6291456 | tf_op jit(solution)/shard_map/attend/pallas_call | solution.py:229
  72.6 2.1 fusion.gn_ref
  74.6 11.6 %all-gather.2.cloned.1.call-done = bf16[1536,4096]{1,0:T(8,128)(2,1)} async-done(((bf16[48,4096]{1,0:T(8,128)(2,1)}), bf16[1536,4096]{1,0:T(8,128)(2,1)}) %all-gather.2.cloned.1.call-update) | async-done | bytes 12582928 | tf_op jit(solution)/shard_map/all_gather | solution.py:604
  86.2 11.6 %grad_attn.1 = (bf16[4,256,512]{2,1,0:T(8,128)(2,1)}, bf16[16,128,128]{2,1,0:T(8,128)(2,1)S(1)}) custom-call(s32[8]{0:T(128)S(1)} %stack.54.w_ref.i_ref, bf16[256,2048]{1,0:T(8,128)(2,1)S(1)} %bitcast.44, f32[4,256,512]{2,1,0:T(8,128)} %get-tuple-element.107.a_ref, f32[256,512]{1,0:T(8,128)} %fusion.gn_ref, f32[1,2048]{1,0:T(1,128)S(1)} %bitcast.59, ...), custom_call_target="tpu_custom_call" | custom-call | flops 3355443200 | bytes 18874368 | tf_op jit(solution)/shard_map/grad_attn/pallas_call | solution.py:313
  98.4 23.4 %collective-permute-done.18.n1 = bf16[256,1024]{1,0:T(8,128)(2,1)} collective-permute-done((bf16[256,1024]{1,0:T(8,128)(2,1)}, bf16[256,1024]{1,0:T(8,128)(2,1)}, u32[]{:S(2)}, u32[]{:S(2)}) %collective-permute-start.18) | collective-permute-done | bytes 524320 | tf_op jit(solution)/shard_map/ppermute | solution.py:123
  121.8 1.3 collective-permute-start.19
  123.1 1.7 collective-permute-start.20
  125.5 11.4 %collective-permute-done.19.n2 = bf16[256,1024]{1,0:T(8,128)(2,1)S(1)} collective-permute-done((bf16[256,1024]{1,0:T(8,128)(2,1)S(1)}, bf16[256,1024]{1,0:T(8,128)(2,1)S(1)}, u32[]{:S(2)}, u32[]{:S(2)}) %collective-permute-start.19) | collective-permute-done | bytes 524320 | tf_op jit(solution)/shard_map/ppermute | solution.py:123
  136.9 11.1 %collective-permute-done.20.n3 = bf16[256,1024]{1,0:T(8,128)(2,1)S(1)} collective-permute-done((bf16[256,1024]{1,0:T(8,128)(2,1)S(1)}, bf16[256,1024]{1,0:T(8,128)(2,1)S(1)}, u32[]{:S(2)}, u32[]{:S(2)}) %collective-permute-start.20) | collective-permute-done | bytes 524320 | tf_op jit(solution)/shard_map/ppermute | solution.py:123
  148.1 6.6 %weight_half.2 = (bf16[16,2,32,1024]{3,2,1,0:T(8,128)(2,1)}, bf16[1024,1024]{1,0:T(8,128)(2,1)S(1)}) custom-call(s32[1]{0:T(128)S(6)} %sub.24.i_ref, bf16[256,1024]{1,0:T(8,128)(2,1)} %get-tuple-element.119.n0.near_ref, bf16[256,1024]{1,0:T(8,128)(2,1)} %collective-permute-done.18.n1, bf16[256,1024]{1,0:T(8,128)(2,1)S(1)} %collective-permute-done.19.n2, ...), custom_call_target="tpu_custom_call" | custom-call | flops 2147483648 | bytes 8388608 | tf_op jit(solution)/shard_map/weight_half/pallas_call | solution.py:509
  155.6 3.2 %collective-permute-start.16 = (bf16[256,128]{1,0:T(8,128)(2,1)S(1)}, bf16[256,128]{1,0:T(8,128)(2,1)S(1)}, u32[]{:S(2)}, u32[]{:S(2)}) collective-permute-start(bf16[256,128]{1,0:T(8,128)(2,1)S(1)} %get-tuple-element.117), channel_id=1, source_target_pairs={{0,4},{2,6},{4,0},{6,2},{1,5},{3,7},{5,1},{7,3},{8,12},{10,14},{12... | collective-permute-start | bytes 196616 | tf_op jit(solution)/shard_map/ppermute | solution.py:128
  159.0 1.4 collective-permute-done.15.refs_0_.t1
  160.3 2.3 collective-permute-done.16.refs_1_.t2
  165.0 5.6 %weight_half.3 = bf16[16,2,32,1024]{3,2,1,0:T(8,128)(2,1)} custom-call(s32[1]{0:T(128)} %bitcast.7.i_ref, bf16[1024,1024]{1,0:T(8,128)(2,1)S(1)} %get-tuple-element.129.nt_ref, bf16[16,2,32,1024]{3,2,1,0:T(8,128)(2,1)S(1)} %collective-permute-done.27.extra_ref, bf16[256,2048]{1,0:T(8,128)(2,1)} %get-tuple-element.156.rest_0_, ...), custom_call_target="tpu_custom_call" | custom-call | flops 2147483648 | bytes 8388608 | tf_op jit(solution)/shard_map/weight_half/pallas_call | solution.py:509
  170.6 5.3 %all-to-all-start = ((bf16[16,2,32,1024]{3,2,1,0:T(8,128)(2,1)}), bf16[16,2,32,1024]{3,2,1,0:T(8,128)(2,1)}, u32[]{:S(2)}, u32[]{:S(2)}) async-start(bf16[16,2,32,1024]{3,2,1,0:T(8,128)(2,1)} %weight_half.3), calls=%async_computation | async-start | bytes 4194304 | tf_op jit(solution)/shard_map/all_to_all | solution.py:648
  175.9 1.9 collective-permute-start.24
  177.8 2.7 %collective-permute-start.25 = (bf16[256,128]{1,0:T(8,128)(2,1)}, bf16[256,128]{1,0:T(8,128)(2,1)S(1)}, u32[]{:S(2)}, u32[]{:S(2)}) collective-permute-start(bf16[256,128]{1,0:T(8,128)(2,1)} %copy-done.31), channel_id=1, source_target_pairs={{0,16},{8,24},{16,0},{24,8},{1,17},{9,25},{17,1},{25,9},{2,18},{10... | collective-permute-start | bytes 196616 | tf_op jit(solution)/shard_map/ppermute | solution.py:128
  180.5 1.5 collective-permute-start.26
  181.9 19.2 %collective-permute-done.24.z1 = bf16[256,128]{1,0:T(8,128)(2,1)S(1)} collective-permute-done((bf16[256,128]{1,0:T(8,128)(2,1)}, bf16[256,128]{1,0:T(8,128)(2,1)S(1)}, u32[]{:S(2)}, u32[]{:S(2)}) %collective-permute-start.24) | collective-permute-done | bytes 65568 | tf_op jit(solution)/shard_map/ppermute | solution.py:128
  202.1 1.3 collective-permute-done.26.z3
  206.7 2.7 %collective-permute-start.28 = (bf16[256,128]{1,0:T(8,128)(2,1)S(1)}, bf16[256,128]{1,0:T(8,128)(2,1)S(1)}, u32[]{:S(2)}, u32[]{:S(2)}) collective-permute-start(bf16[256,128]{1,0:T(8,128)(2,1)S(1)} %get-tuple-element.133), channel_id=1, source_target_pairs={{0,2},{2,4},{4,6},{6,0},{1,3},{3,5},{5,7},{7,1},{8,10},{10,12},{12... | collective-permute-start | bytes 196616 | tf_op jit(solution)/shard_map/ppermute | solution.py:128
  209.4 3.4 %collective-permute-start.29 = (bf16[256,128]{1,0:T(8,128)(2,1)S(1)}, bf16[256,128]{1,0:T(8,128)(2,1)S(1)}, u32[]{:S(2)}, u32[]{:S(2)}) collective-permute-start(bf16[256,128]{1,0:T(8,128)(2,1)S(1)} %get-tuple-element.134), channel_id=1, source_target_pairs={{0,4},{2,6},{4,0},{6,2},{1,5},{3,7},{5,1},{7,3},{8,12},{10,14},{12... | collective-permute-start | bytes 196616 | tf_op jit(solution)/shard_map/ppermute | solution.py:128
  214.8 7.9 %local_grads.1 = (bf16[256,2048]{1,0:T(8,128)(2,1)}, bf16[4,256,512]{2,1,0:T(8,128)(2,1)S(1)}, bf16[4,256,512]{2,1,0:T(8,128)(2,1)S(1)}) custom-call(s32[8]{0:T(128)S(1)} %stack.54.w_ref.i_ref, bf16[256,2048]{1,0:T(8,128)(2,1)S(1)} %bitcast.45, bf16[256,2048]{1,0:T(8,128)(2,1)S(1)} %bitcast.36, bf16[256,2048]{1,0:T(8,128)(2,1)S(1)} %bitcast.40, ...), custom_call_target="tpu_custom_call" | custom-call | flops 1073741824 | bytes 12582912 | tf_op jit(solution)/shard_map/local_grads/pallas_call | solution.py:367
  223.7 10.7 %layer_rows.1 = bf16[256,4096]{1,0:T(8,128)(2,1)} custom-call(s32[8]{0:T(128)S(1)} %stack.54.w_ref.i_ref, bf16[256,1024]{1,0:T(8,128)(2,1)} %get-tuple-element.119.n0.near_ref, bf16[256,1024]{1,0:T(8,128)(2,1)S(1)} %copy-done.22, bf16[512,4096]{1,0:T(8,128)(2,1)} %own_ref.1, bf16[32,3,16,4096]{3,2,1,0:T(8,128)(2,1)} %bitcast.61), custom_call_target="tpu_custom_call" | custom-call | flops 4294967296 | bytes 19922944 | tf_op jit(solution)/shard_map/layer_rows/pallas_call | solution.py:451
  235.3 2.1 sum_parts.1
  238.0 1.6 collective-permute-start.34
  242.4 3.2 %later_grads.1 = (bf16[256,2048]{1,0:T(8,128)(2,1)}, bf16[256,2048]{1,0:T(8,128)(2,1)}) custom-call(s32[8]{0:T(128)S(1)} %stack.54.w_ref.i_ref, bf16[256,2048]{1,0:T(8,128)(2,1)S(1)} %bitcast.37, bf16[256,2048]{1,0:T(8,128)(2,1)S(1)} %bitcast.41, bf16[8,128,128]{2,1,0:T(8,128)(2,1)S(1)} %bitcast.56, bf16[8,128,128]{2,1,0:T(8,128)(2,1)S(1)} %bitcast.57, ...), custom_call_target="tpu_custom_call" | custom-call | flops 268435456 | bytes 8388608 | tf_op jit(solution)/shard_map/later_grads/pallas_call | solution.py:408
  245.6 1.3 shard_map.109
  (124 shorter events, 33.2 us)
Async XLA Ops:
  7.2 79.1 %all-gather.2.cloned.1.call-start = ((), (), s32[]{:S(2)}) async-start(), calls=%async_computation.1 | async-start | bytes 12976128 | tf_op jit(solution)/shard_map/all_gather | solution.py:604
  8.1 9.2 %collective-permute-start = (bf16[16,4096]{1,0:T(8,128)(2,1)S(1)}, bf16[16,4096]{1,0:T(8,128)(2,1)S(1)}, u32[]{:S(2)}, u32[]{:S(2)}) collective-permute-start(bf16[16,4096]{1,0:T(8,128)(2,1)S(1)} %constant_dynamic-slice_fusion.2), channel_id=1, source_target_pairs={{32,0},{64,32},{96,64},{0,96},{33,1},{65,33},{97,65},{1,97},{34,2}... | collective-permute-start | bytes 393224 | tf_op jit(solution)/shard_map/ppermute | solution.py:570
  11.1 7.9 %collective-permute-start.1 = (bf16[16,4096]{1,0:T(8,128)(2,1)S(1)}, bf16[16,4096]{1,0:T(8,128)(2,1)S(1)}, u32[]{:S(2)}, u32[]{:S(2)}) collective-permute-start(bf16[16,4096]{1,0:T(8,128)(2,1)S(1)} %constant_dynamic-slice_fusion.2), channel_id=1, source_target_pairs={{64,0},{96,32},{0,64},{32,96},{65,1},{97,33},{1,65},{33,97},{66,2}... | collective-permute-start | bytes 393224 | tf_op jit(solution)/shard_map/ppermute | solution.py:570
  11.9 8.5 %collective-permute-start.2 = (bf16[16,4096]{1,0:T(8,128)(2,1)S(1)}, bf16[16,4096]{1,0:T(8,128)(2,1)S(1)}, u32[]{:S(2)}, u32[]{:S(2)}) collective-permute-start(bf16[16,4096]{1,0:T(8,128)(2,1)S(1)} %constant_dynamic-slice_fusion.2), channel_id=1, source_target_pairs={{96,0},{0,32},{32,64},{64,96},{97,1},{1,33},{33,65},{65,97},{98,2}... | collective-permute-start | bytes 393224 | tf_op jit(solution)/shard_map/ppermute | solution.py:570
  15.2 16.9 %copy-start.1 = (bf16[1,256,2048]{2,1,0:T(8,128)(2,1)S(1)}, bf16[1,256,2048]{2,1,0:T(8,128)(2,1)}, u32[]{:S(2)}) copy-start(bf16[1,256,2048]{2,1,0:T(8,128)(2,1)} %param.7) | copy-start | bytes 3145732
  15.2 16.9 %copy-start.3 = (bf16[1,256,2048]{2,1,0:T(8,128)(2,1)S(1)}, bf16[1,256,2048]{2,1,0:T(8,128)(2,1)}, u32[]{:S(2)}) copy-start(bf16[1,256,2048]{2,1,0:T(8,128)(2,1)} %param.8) | copy-start | bytes 3145732
  15.2 16.9 %copy-start.4 = (bf16[1,256,2048]{2,1,0:T(8,128)(2,1)S(1)}, bf16[1,256,2048]{2,1,0:T(8,128)(2,1)}, u32[]{:S(2)}) copy-start(bf16[1,256,2048]{2,1,0:T(8,128)(2,1)} %param.6) | copy-start | bytes 3145732
  22.8 1.7 collective-permute-start.3
  26.2 9.8 %collective-permute-start.4 = (bf16[256,128]{1,0:T(8,128)(2,1)S(1)}, bf16[256,128]{1,0:T(8,128)(2,1)S(1)}, u32[]{:S(2)}, u32[]{:S(2)}) collective-permute-start(bf16[256,128]{1,0:T(8,128)(2,1)S(1)} %get-tuple-element.81), channel_id=1, source_target_pairs={{0,2},{2,4},{4,6},{6,0},{1,3},{3,5},{5,7},{7,1},{8,10},{10,12},{12... | collective-permute-start | bytes 196616 | tf_op jit(solution)/shard_map/ppermute | solution.py:128
  27.9 8.2 %collective-permute-start.5 = (bf16[256,128]{1,0:T(8,128)(2,1)S(1)}, bf16[256,128]{1,0:T(8,128)(2,1)S(1)}, u32[]{:S(2)}, u32[]{:S(2)}) collective-permute-start(bf16[256,128]{1,0:T(8,128)(2,1)S(1)} %get-tuple-element.82), channel_id=1, source_target_pairs={{0,4},{2,6},{4,0},{6,2},{1,5},{3,7},{5,1},{7,3},{8,12},{10,14},{12... | collective-permute-start | bytes 196616 | tf_op jit(solution)/shard_map/ppermute | solution.py:128
  30.8 5.4 %collective-permute-start.6 = (bf16[256,128]{1,0:T(8,128)(2,1)S(1)}, bf16[256,128]{1,0:T(8,128)(2,1)S(1)}, u32[]{:S(2)}, u32[]{:S(2)}) collective-permute-start(bf16[256,128]{1,0:T(8,128)(2,1)S(1)} %get-tuple-element.83), channel_id=1, source_target_pairs={{0,6},{2,0},{4,2},{6,4},{1,7},{3,1},{5,3},{7,5},{8,14},{10,8},{12,... | collective-permute-start | bytes 196616 | tf_op jit(solution)/shard_map/ppermute | solution.py:128
  36.8 8.4 %collective-permute-start.7 = (bf16[256,128]{1,0:T(8,128)(2,1)S(1)}, bf16[256,128]{1,0:T(8,128)(2,1)S(1)}, u32[]{:S(2)}, u32[]{:S(2)}) collective-permute-start(bf16[256,128]{1,0:T(8,128)(2,1)S(1)} %shard_map.102), channel_id=1, source_target_pairs={{0,8},{8,16},{16,24},{24,0},{1,9},{9,17},{17,25},{25,1},{2,10},{10... | collective-permute-start | bytes 196616 | tf_op jit(solution)/shard_map/ppermute | solution.py:128
  38.9 8.8 %collective-permute-start.8 = (bf16[256,128]{1,0:T(8,128)(2,1)S(1)}, bf16[256,128]{1,0:T(8,128)(2,1)S(1)}, u32[]{:S(2)}, u32[]{:S(2)}) collective-permute-start(bf16[256,128]{1,0:T(8,128)(2,1)S(1)} %shard_map.102), channel_id=1, source_target_pairs={{0,16},{8,24},{16,0},{24,8},{1,17},{9,25},{17,1},{25,9},{2,18},{10... | collective-permute-start | bytes 196616 | tf_op jit(solution)/shard_map/ppermute | solution.py:128
  42.6 5.1 %collective-permute-start.9 = (bf16[256,128]{1,0:T(8,128)(2,1)S(1)}, bf16[256,128]{1,0:T(8,128)(2,1)S(1)}, u32[]{:S(2)}, u32[]{:S(2)}) collective-permute-start(bf16[256,128]{1,0:T(8,128)(2,1)S(1)} %shard_map.102), channel_id=1, source_target_pairs={{0,24},{8,0},{16,8},{24,16},{1,25},{9,1},{17,9},{25,17},{2,26},{10... | collective-permute-start | bytes 196616 | tf_op jit(solution)/shard_map/ppermute | solution.py:128
  49.0 5.8 %collective-permute-start.10 = (bf16[256,128]{1,0:T(8,128)(2,1)}, bf16[256,128]{1,0:T(8,128)(2,1)}, u32[]{:S(2)}, u32[]{:S(2)}) collective-permute-start(bf16[256,128]{1,0:T(8,128)(2,1)} %get-tuple-element.96), channel_id=1, source_target_pairs={{0,2},{2,4},{4,6},{6,0},{1,3},{3,5},{5,7},{7,1},{8,10},{10,12},{12... | collective-permute-start | bytes 196616 | tf_op jit(solution)/shard_map/ppermute | solution.py:128
  49.8 6.1 %collective-permute-start.11 = (bf16[256,128]{1,0:T(8,128)(2,1)}, bf16[256,128]{1,0:T(8,128)(2,1)}, u32[]{:S(2)}, u32[]{:S(2)}) collective-permute-start(bf16[256,128]{1,0:T(8,128)(2,1)} %get-tuple-element.97), channel_id=1, source_target_pairs={{0,4},{2,6},{4,0},{6,2},{1,5},{3,7},{5,1},{7,3},{8,12},{10,14},{12... | collective-permute-start | bytes 196616 | tf_op jit(solution)/shard_map/ppermute | solution.py:128
  52.2 4.6 %collective-permute-start.12 = (bf16[256,128]{1,0:T(8,128)(2,1)}, bf16[256,128]{1,0:T(8,128)(2,1)}, u32[]{:S(2)}, u32[]{:S(2)}) collective-permute-start(bf16[256,128]{1,0:T(8,128)(2,1)} %get-tuple-element.98), channel_id=1, source_target_pairs={{0,6},{2,0},{4,2},{6,4},{1,7},{3,1},{5,3},{7,5},{8,14},{10,8},{12,... | collective-permute-start | bytes 196616 | tf_op jit(solution)/shard_map/ppermute | solution.py:128
  58.9 7.5 %collective-permute-start.13 = (bf16[4,256,128]{2,1,0:T(8,128)(2,1)S(1)}, bf16[4,256,128]{2,1,0:T(8,128)(2,1)S(1)}, u32[]{:S(2)}, u32[]{:S(2)}) collective-permute-start(bf16[4,256,128]{2,1,0:T(8,128)(2,1)S(1)} %get-tuple-element.104), channel_id=1, source_target_pairs={{0,1},{1,0},{2,3},{3,2},{4,5},{5,4},{6,7},{7,6},{8,9},{9,8},{10,11... | collective-permute-start | bytes 786440 | tf_op jit(solution)/shard_map/ppermute | solution.py:128
  59.0 13.6 %copy-start.34 = (bf16[512,4096]{1,0:T(8,128)(2,1)S(1)}, bf16[512,4096]{1,0:T(8,128)(2,1)}, u32[]{:S(2)}) copy-start(bf16[512,4096]{1,0:T(8,128)(2,1)} %own_ref.1) | copy-start | bytes 12582916
  62.3 85.8 %collective-permute-start.21 = (bf16[256,2048]{1,0:T(8,128)(2,1)}, bf16[256,2048]{1,0:T(8,128)(2,1)}, u32[]{:S(2)}, u32[]{:S(2)}) collective-permute-start(bf16[256,2048]{1,0:T(8,128)(2,1)} %get-tuple-element.155), channel_id=1, source_target_pairs={{0,32},{32,0},{64,96},{96,64},{1,33},{33,1},{65,97},{97,65},{2,34}... | collective-permute-start | bytes 3145736 | tf_op jit(solution)/shard_map/ppermute | solution.py:123
  62.3 85.8 %collective-permute-start.23 = (bf16[256,2048]{1,0:T(8,128)(2,1)}, bf16[256,2048]{1,0:T(8,128)(2,1)}, u32[]{:S(2)}, u32[]{:S(2)}) collective-permute-start(bf16[256,2048]{1,0:T(8,128)(2,1)} %get-tuple-element.155), channel_id=1, source_target_pairs={{0,96},{32,64},{64,32},{96,0},{1,97},{33,65},{65,33},{97,1},{2,98}... | collective-permute-start | bytes 3145736 | tf_op jit(solution)/shard_map/ppermute | solution.py:123
  64.1 84.0 %collective-permute-start.22 = (bf16[256,2048]{1,0:T(8,128)(2,1)}, bf16[256,2048]{1,0:T(8,128)(2,1)}, u32[]{:S(2)}, u32[]{:S(2)}) collective-permute-start(bf16[256,2048]{1,0:T(8,128)(2,1)} %get-tuple-element.156.rest_0_), channel_id=1, source_target_pairs={{0,64},{32,96},{64,0},{96,32},{1,65},{33,97},{65,1},{97,33},{2,66}... | collective-permute-start | bytes 3145736 | tf_op jit(solution)/shard_map/ppermute | solution.py:123
  72.6 49.3 %collective-permute-start.18 = (bf16[256,1024]{1,0:T(8,128)(2,1)}, bf16[256,1024]{1,0:T(8,128)(2,1)}, u32[]{:S(2)}, u32[]{:S(2)}) collective-permute-start(bf16[256,1024]{1,0:T(8,128)(2,1)} %get-tuple-element.119.n0.near_ref), channel_id=1, source_target_pairs={{0,32},{32,0},{64,96},{96,64},{1,33},{33,1},{65,97},{97,65},{2,34}... | collective-permute-start | bytes 1572872 | tf_op jit(solution)/shard_map/ppermute | solution.py:123
  86.2 35.6 %copy-start.21 = (bf16[256,1024]{1,0:T(8,128)(2,1)S(1)}, bf16[256,1024]{1,0:T(8,128)(2,1)}, u32[]{:S(2)}) copy-start(bf16[256,1024]{1,0:T(8,128)(2,1)} %copy-done.20) | copy-start | bytes 1572868
  97.8 27.0 %copy-start.8 = (bf16[16,128,128]{2,1,0:T(8,128)(2,1)}, bf16[16,128,128]{2,1,0:T(8,128)(2,1)S(1)}, u32[]{:S(2)}) copy-start(bf16[16,128,128]{2,1,0:T(8,128)(2,1)S(1)} %get-tuple-element.114) | copy-start | bytes 1572868
  97.9 25.2 %collective-permute-start.14 = (bf16[4,256,128]{2,1,0:T(8,128)(2,1)S(1)}, bf16[4,256,128]{2,1,0:T(8,128)(2,1)S(1)}, u32[]{:S(2)}, u32[]{:S(2)}) collective-permute-start(bf16[4,256,128]{2,1,0:T(8,128)(2,1)S(1)} %dynamic-slice_bitcast_fusion), channel_id=1, source_target_pairs={{0,1},{1,0},{2,3},{3,2},{4,5},{5,4},{6,7},{7,6},{8,9},{9,8},{10,11... | collective-permute-start | bytes 786440 | tf_op jit(solution)/shard_map/ppermute | solution.py:128
  121.8 15.1 %collective-permute-start.19 = (bf16[256,1024]{1,0:T(8,128)(2,1)S(1)}, bf16[256,1024]{1,0:T(8,128)(2,1)S(1)}, u32[]{:S(2)}, u32[]{:S(2)}) collective-permute-start(bf16[256,1024]{1,0:T(8,128)(2,1)S(1)} %copy-done.21), channel_id=1, source_target_pairs={{0,64},{32,96},{64,0},{96,32},{1,65},{33,97},{65,1},{97,33},{2,66}... | collective-permute-start | bytes 1572872 | tf_op jit(solution)/shard_map/ppermute | solution.py:123
  123.1 24.9 %copy-start.18 = (bf16[4,256,128]{2,1,0:T(8,128)(2,1)}, bf16[4,256,128]{2,1,0:T(8,128)(2,1)S(1)}, u32[]{:S(2)}) copy-start(bf16[4,256,128]{2,1,0:T(8,128)(2,1)S(1)} %collective-permute-done.14.r_ref) | copy-start | bytes 786436
  123.1 24.9 %collective-permute-start.20 = (bf16[256,1024]{1,0:T(8,128)(2,1)S(1)}, bf16[256,1024]{1,0:T(8,128)(2,1)S(1)}, u32[]{:S(2)}, u32[]{:S(2)}) collective-permute-start(bf16[256,1024]{1,0:T(8,128)(2,1)S(1)} %copy-done.21), channel_id=1, source_target_pairs={{0,96},{32,64},{64,32},{96,0},{1,97},{33,65},{65,33},{97,1},{2,98}... | collective-permute-start | bytes 1572872 | tf_op jit(solution)/shard_map/ppermute | solution.py:123
  154.6 10.4 %collective-permute-start.27 = (bf16[16,2,32,1024]{3,2,1,0:T(8,128)(2,1)}, bf16[16,2,32,1024]{3,2,1,0:T(8,128)(2,1)S(1)}, u32[]{:S(2)}, u32[]{:S(2)}) collective-permute-start(bf16[16,2,32,1024]{3,2,1,0:T(8,128)(2,1)} %get-tuple-element.123), channel_id=1, source_target_pairs={{0,1},{1,0},{2,3},{3,2},{4,5},{5,4},{6,7},{7,6},{8,9},{9,8},{10,11... | collective-permute-start | bytes 6291464 | tf_op jit(solution)/shard_map/ppermute | solution.py:128
  154.6 5.7 %collective-permute-start.15 = (bf16[256,128]{1,0:T(8,128)(2,1)S(1)}, bf16[256,128]{1,0:T(8,128)(2,1)S(1)}, u32[]{:S(2)}, u32[]{:S(2)}) collective-permute-start(bf16[256,128]{1,0:T(8,128)(2,1)S(1)} %get-tuple-element.116), channel_id=1, source_target_pairs={{0,2},{2,4},{4,6},{6,0},{1,3},{3,5},{5,7},{7,1},{8,10},{10,12},{12... | collective-permute-start | bytes 196616 | tf_op jit(solution)/shard_map/ppermute | solution.py:128
  155.6 7.0 %collective-permute-start.16 = (bf16[256,128]{1,0:T(8,128)(2,1)S(1)}, bf16[256,128]{1,0:T(8,128)(2,1)S(1)}, u32[]{:S(2)}, u32[]{:S(2)}) collective-permute-start(bf16[256,128]{1,0:T(8,128)(2,1)S(1)} %get-tuple-element.117), channel_id=1, source_target_pairs={{0,4},{2,6},{4,0},{6,2},{1,5},{3,7},{5,1},{7,3},{8,12},{10,14},{12... | collective-permute-start | bytes 196616 | tf_op jit(solution)/shard_map/ppermute | solution.py:128
  158.8 4.3 %collective-permute-start.17 = (bf16[256,128]{1,0:T(8,128)(2,1)S(1)}, bf16[256,128]{1,0:T(8,128)(2,1)S(1)}, u32[]{:S(2)}, u32[]{:S(2)}) collective-permute-start(bf16[256,128]{1,0:T(8,128)(2,1)S(1)} %get-tuple-element.118), channel_id=1, source_target_pairs={{0,6},{2,0},{4,2},{6,4},{1,7},{3,1},{5,3},{7,5},{8,14},{10,8},{12,... | collective-permute-start | bytes 196616 | tf_op jit(solution)/shard_map/ppermute | solution.py:128
  170.6 43.3 %copy-start.15 = (bf16[4,256,128]{2,1,0:T(8,128)(2,1)S(1)}, bf16[4,256,128]{2,1,0:T(8,128)(2,1)}, u32[]{:S(2)}) copy-start(bf16[4,256,128]{2,1,0:T(8,128)(2,1)} %copy-done.14) | copy-start | bytes 786436
  170.6 64.6 %all-to-all-start = ((bf16[16,2,32,1024]{3,2,1,0:T(8,128)(2,1)}), bf16[16,2,32,1024]{3,2,1,0:T(8,128)(2,1)}, u32[]{:S(2)}, u32[]{:S(2)}) async-start(bf16[16,2,32,1024]{3,2,1,0:T(8,128)(2,1)} %weight_half.3), calls=%async_computation | async-start | bytes 4194304 | tf_op jit(solution)/shard_map/all_to_all | solution.py:648
  175.9 25.2 %collective-permute-start.24 = (bf16[256,128]{1,0:T(8,128)(2,1)}, bf16[256,128]{1,0:T(8,128)(2,1)S(1)}, u32[]{:S(2)}, u32[]{:S(2)}) collective-permute-start(bf16[256,128]{1,0:T(8,128)(2,1)} %copy-done.31), channel_id=1, source_target_pairs={{0,8},{8,16},{16,24},{24,0},{1,9},{9,17},{17,25},{25,1},{2,10},{10... | collective-permute-start | bytes 196616 | tf_op jit(solution)/shard_map/ppermute | solution.py:128
  177.8 24.4 %collective-permute-start.25 = (bf16[256,128]{1,0:T(8,128)(2,1)}, bf16[256,128]{1,0:T(8,128)(2,1)S(1)}, u32[]{:S(2)}, u32[]{:S(2)}) collective-permute-start(bf16[256,128]{1,0:T(8,128)(2,1)} %copy-done.31), channel_id=1, source_target_pairs={{0,16},{8,24},{16,0},{24,8},{1,17},{9,25},{17,1},{25,9},{2,18},{10... | collective-permute-start | bytes 196616 | tf_op jit(solution)/shard_map/ppermute | solution.py:128
  180.5 23.0 %collective-permute-start.26 = (bf16[256,128]{1,0:T(8,128)(2,1)}, bf16[256,128]{1,0:T(8,128)(2,1)S(1)}, u32[]{:S(2)}, u32[]{:S(2)}) collective-permute-start(bf16[256,128]{1,0:T(8,128)(2,1)} %copy-done.31), channel_id=1, source_target_pairs={{0,24},{8,0},{16,8},{24,16},{1,25},{9,1},{17,9},{25,17},{2,26},{10... | collective-permute-start | bytes 196616 | tf_op jit(solution)/shard_map/ppermute | solution.py:128
  206.7 27.7 %collective-permute-start.28 = (bf16[256,128]{1,0:T(8,128)(2,1)S(1)}, bf16[256,128]{1,0:T(8,128)(2,1)S(1)}, u32[]{:S(2)}, u32[]{:S(2)}) collective-permute-start(bf16[256,128]{1,0:T(8,128)(2,1)S(1)} %get-tuple-element.133), channel_id=1, source_target_pairs={{0,2},{2,4},{4,6},{6,0},{1,3},{3,5},{5,7},{7,1},{8,10},{10,12},{12... | collective-permute-start | bytes 196616 | tf_op jit(solution)/shard_map/ppermute | solution.py:128
  209.4 25.0 %collective-permute-start.29 = (bf16[256,128]{1,0:T(8,128)(2,1)S(1)}, bf16[256,128]{1,0:T(8,128)(2,1)S(1)}, u32[]{:S(2)}, u32[]{:S(2)}) collective-permute-start(bf16[256,128]{1,0:T(8,128)(2,1)S(1)} %get-tuple-element.134), channel_id=1, source_target_pairs={{0,4},{2,6},{4,0},{6,2},{1,5},{3,7},{5,1},{7,3},{8,12},{10,14},{12... | collective-permute-start | bytes 196616 | tf_op jit(solution)/shard_map/ppermute | solution.py:128
  212.8 21.6 %collective-permute-start.30 = (bf16[256,128]{1,0:T(8,128)(2,1)S(1)}, bf16[256,128]{1,0:T(8,128)(2,1)S(1)}, u32[]{:S(2)}, u32[]{:S(2)}) collective-permute-start(bf16[256,128]{1,0:T(8,128)(2,1)S(1)} %get-tuple-element.135), channel_id=1, source_target_pairs={{0,6},{2,0},{4,2},{6,4},{1,7},{3,1},{5,3},{7,5},{8,14},{10,8},{12,... | collective-permute-start | bytes 196616 | tf_op jit(solution)/shard_map/ppermute | solution.py:128
  223.7 10.7 %copy-start.12 = (bf16[4,256,512]{2,1,0:T(8,128)(2,1)}, bf16[4,256,512]{2,1,0:T(8,128)(2,1)S(1)}, u32[]{:S(2)}) copy-start(bf16[4,256,512]{2,1,0:T(8,128)(2,1)S(1)} %get-tuple-element.139.pv_ref) | copy-start | bytes 3145732
  223.7 10.7 %copy-start.9 = (bf16[16,128,128]{2,1,0:T(8,128)(2,1)S(1)}, bf16[16,128,128]{2,1,0:T(8,128)(2,1)}, u32[]{:S(2)}) copy-start(bf16[16,128,128]{2,1,0:T(8,128)(2,1)} %copy-done.8) | copy-start | bytes 1572868
  223.7 10.7 %copy-start.19 = (bf16[4,256,128]{2,1,0:T(8,128)(2,1)S(1)}, bf16[4,256,128]{2,1,0:T(8,128)(2,1)}, u32[]{:S(2)}) copy-start(bf16[4,256,128]{2,1,0:T(8,128)(2,1)} %copy-done.18) | copy-start | bytes 786436
  235.1 4.4 %collective-permute-start.31 = (bf16[4,256,128]{2,1,0:T(8,128)(2,1)S(1)}, bf16[4,256,128]{2,1,0:T(8,128)(2,1)S(1)}, u32[]{:S(2)}, u32[]{:S(2)}) collective-permute-start(bf16[4,256,128]{2,1,0:T(8,128)(2,1)S(1)} %get-tuple-element.147), channel_id=1, source_target_pairs={{0,1},{1,0},{2,3},{3,2},{4,5},{5,4},{6,7},{7,6},{8,9},{9,8},{10,11... | collective-permute-start | bytes 786440 | tf_op jit(solution)/shard_map/ppermute | solution.py:128
  237.3 8.3 %collective-permute-start.32 = (f32[16,1024]{1,0:T(8,128)S(1)}, f32[16,1024]{1,0:T(8,128)S(1)}, u32[]{:S(2)}, u32[]{:S(2)}) collective-permute-start(f32[16,1024]{1,0:T(8,128)S(1)} %get-tuple-element.152), channel_id=1, source_target_pairs={{0,32},{32,0},{64,96},{96,64},{1,33},{33,1},{65,97},{97,65},{2,34}... | collective-permute-start | bytes 196616 | tf_op jit(solution)/shard_map/ppermute | solution.py:123
  237.4 8.2 %collective-permute-start.33 = (f32[16,1024]{1,0:T(8,128)S(1)}, f32[16,1024]{1,0:T(8,128)S(1)}, u32[]{:S(2)}, u32[]{:S(2)}) collective-permute-start(f32[16,1024]{1,0:T(8,128)S(1)} %get-tuple-element.153), channel_id=1, source_target_pairs={{0,1},{1,0},{2,3},{3,2},{4,5},{5,4},{6,7},{7,6},{8,9},{9,8},{10,11... | collective-permute-start | bytes 196616 | tf_op jit(solution)/shard_map/ppermute | solution.py:123
  238.0 7.7 %collective-permute-start.34 = (f32[16,1024]{1,0:T(8,128)S(1)}, f32[16,1024]{1,0:T(8,128)S(1)}, u32[]{:S(2)}, u32[]{:S(2)}) collective-permute-start(f32[16,1024]{1,0:T(8,128)S(1)} %get-tuple-element.154), channel_id=1, source_target_pairs={{0,33},{1,32},{32,1},{33,0},{64,97},{65,96},{96,65},{97,64},{2,35}... | collective-permute-start | bytes 196616 | tf_op jit(solution)/shard_map/ppermute | solution.py:662
  (24 other events, 61.0 us)
Sparse Core Ops, SparseCore 0:
  21.3 64.8 all-gather.1

commit v8 on v6

--- a/solution.py
+++ b/solution.py
@@ -199,7 +199,7 @@
     return jnp.where(lax.div(chunk, CH // 2) == w_ref[7], m_ref[h], t_ref[h])
 
 
-def attend_body(w_ref, q_ref, o_ref, m_ref, t_ref, g_ref, near_ref, far_ref, a_ref):
+def attend_body(w_ref, q_ref, o_ref, m_ref, t_ref, g_ref, near_ref, far_ref, near_t_ref, far_t_ref, a_ref):
     g = pl.program_id(0)
     normed = []
     for h in range(HC):
@@ -214,10 +214,12 @@
     @pl.when(g < CH // 2)
     def _():
         near_ref[...] = normed
+        near_t_ref[...] = normed.T
 
     @pl.when(g >= CH // 2)
     def _():
         far_ref[...] = normed
+        far_t_ref[...] = normed.T
 
 
 def attend(where, q, out, carried, gain):
@@ -235,10 +237,13 @@
             out_specs=[
                 pl.BlockSpec((t, w), lambda g, i: (0, jnp.minimum(g, two - 1))),
                 pl.BlockSpec((t, w), lambda g, i: (0, jnp.maximum(g - two, 0))),
+                pl.BlockSpec((w, t), lambda g, i: (jnp.minimum(g, two - 1), 0)),
+                pl.BlockSpec((w, t), lambda g, i: (jnp.maximum(g - two, 0), 0)),
                 pl.BlockSpec((1, t, w), lambda g, i: (i[g], 0, 0)),
             ],
         ),
         out_shape=[jax.ShapeDtypeStruct((t, two * w), BF)] * 2
+        + [jax.ShapeDtypeStruct((two * w, t), BF)] * 2
         + [pltpu.HBM((CH, t, w), F32)],
         cost_estimate=cost(2 * t * f * HD, 12 * t * f),
         compiler_params=pltpu.CompilerParams(vmem_limit_bytes=12 << 20),
@@ -468,57 +473,42 @@
     )(where, near, far, own, gathered)
 
 
-def weight_total(nt, grads, o_ref, extra_ref):
-    total = mm(nt[...], jnp.concatenate([g[...] for g in grads], axis=0), 1, 0)
-    chips, blocks, rows, w = o_ref.shape
-    span = chips * rows
+def weight_body(add, i_ref, *refs):
+    rows, grads = refs[:CH], refs[CH : 2 * CH]
+    o_ref = refs[-1]
+    left = jnp.concatenate([n[...] for n in rows], axis=1)
+    total = mm(left, jnp.concatenate([g[...] for g in grads], axis=0), 1, 0)
+    chips, blocks, r, w = o_ref.shape
+    span = chips * r
     for b in range(blocks):
-        one = total[b * span : (b + 1) * span].reshape(chips, rows, w)
-        if extra_ref is not None:
-            one = one + extra_ref[:, b].astype(F32)
+        one = total[b * span : (b + 1) * span].reshape(chips, r, w)
+        if add:
+            one = one + refs[2 * CH][:, b].astype(F32)
         o_ref[:, b] = one.astype(BF)
 
 
-def give_body(i_ref, n0, n1, n2, n3, *rest):
-    *grads, o_ref, nt_ref = rest
-
-    @pl.when(pl.program_id(0) == 0)
-    def _():
-        t = n0.shape[0]
-        for s, n in enumerate((n0, n1, n2, n3)):
-            nt_ref[:, s * t : (s + 1) * t] = n[...].T
-
-    weight_total(nt_ref, grads, o_ref, None)
-
-
-def keep_body(i_ref, nt_ref, extra_ref, *rest):
-    *grads, o_ref = rest
-    weight_total(nt_ref, grads, o_ref, extra_ref)
-
-
-def weight_half(body, half, rows, grads_all, shape, nt_out):
+def weight_half(half, rows, grads_all, shape, extra):
     t, d = grads_all[0].shape
-    w = rows[0].shape[1] if nt_out else rows[0].shape[0]
+    w = rows[0].shape[0]
     tile = 256
     steps = d // 2 // tile
+    add = extra is not None
     own = pl.BlockSpec(shape[:-1] + (tile,), lambda g, i: (0, 0, 0, g))
-    whole = pl.BlockSpec((t, w), lambda g, i: (0, 0))
-    turned = pl.BlockSpec((w, CH * t), lambda g, i: (0, 0))
-    out = pltpu.HBM(shape, BF)
+    whole = pl.BlockSpec((w, t), lambda g, i: (0, 0))
     cols = pl.BlockSpec((t, tile), lambda g, i: (0, i[0] * steps + g))
     return pl.pallas_call(
-        body,
+        functools.partial(weight_body, add),
         grid_spec=pltpu.PrefetchScalarGridSpec(
             num_scalar_prefetch=1,
             grid=(steps,),
-            in_specs=([whole] * CH if nt_out else [turned, own]) + [cols] * CH,
-            out_specs=[own, turned] if nt_out else own,
+            in_specs=[whole] * CH + [cols] * CH + [own] * add,
+            out_specs=own,
         ),
-        out_shape=[out, jax.ShapeDtypeStruct((w, CH * t), BF)] if nt_out else out,
+        out_shape=pltpu.HBM(shape, BF),
         cost_estimate=cost(CH * t * w * d, 2 * CH * t * d + 2 * CH * t * w + w * d),
         compiler_params=pltpu.CompilerParams(vmem_limit_bytes=20 << 20),
         name="weight_half",
-    )(half, *rows, *grads_all)
+    )(half, *rows, *grads_all, *([extra] if add else []))
 
 
 def sum_body(scale, w_ref, s_ref, keep_ref, x_ref, c_ref, xc_ref, total):
@@ -622,13 +612,8 @@
         lambda sent, done: (),
         lambda sent, done: (),
     )
-    near, far, attended = attend(turns, q, hbm(local_out), carried, gain_row)
-    normed_all = [
-        near,
-        partner(near, "x", 1),
-        partner(far, "x", 2),
-        partner(far, "x", 3),
-    ]
+    near, far, near_t, far_t, attended = attend(turns, q, hbm(local_out), carried, gain_row)
+    normed_all = [near_t, partner(near_t, "x", 1), partner(far_t, "x", 2), partner(far_t, "x", 3)]
     gn = hbm(mm(after(sent_rows, near), out_weight, 1, 1))
 
     ga, lg = grad_attn(where, q, hbm(attended), gn, gain_row, hbm(grad_rows), gathered)
@@ -637,12 +622,12 @@
 
     def first_half(sent):
         rows = after(normed_all, sent)
-        return weight_half(give_body, others, rows, grads_all, shape, True)
-
-    def second_half(sent, done):
-        for_partner, turned = done
+        return weight_half(others, rows, grads_all, shape, None)
+
+    def second_half(sent, for_partner):
         extra = give_to(for_partner, "c", 1)
-        return weight_half(keep_body, mine, [after(turned, sent), extra], grads_all, shape, False)
+        rows = after(normed_all, sent)
+        return weight_half(mine, rows, grads_all, shape, extra)
 
     def rest(sent, partial):
         parts = lax.all_to_all(partial, ("z", "y"), 0, 0, tiled=True)

time: 254 us -> 254 us (level)
    unnamed x58 -> x64, local copies, waits for them, and re-layouts: 11 us -> 12.6 us
where the time goes in v8:
time: 254 us; the launch traced here: 251 us
  waiting for transfers between devices  93.6 us (37%)
  Pallas kernels  67.5 us (27%)
  starting transfers between devices  54.5 us (21%)
  local copies, waits for them, and re-layouts  18.6 us (7%)
  between operations  14.3 us (6%)
    ppermute x8, waiting for transfers between devices, partner(): lax.ppermute(x, axis, [(d, d ^ bits) for d in range(lax.axis_size(axis))])  46 us
    ppermute x23, starting transfers between devices, give_to(): return lax.ppermute(x, axis, [(d, (d + by) % n) for d in range(n)])  35.3 us
    ppermute x23, waiting for transfers between devices, give_to(): return lax.ppermute(x, axis, [(d, (d + by) % n) for d in range(n)])  34.8 us
    unnamed x64, local copies, waits for them, and re-layouts  12.6 us
    pallas_call x2, Pallas kernels, weight_half(): pl.pallas_call(functools.partial(weight_body, add), grid_spec=pltpu.Prefe...  11.9 us
    pallas_call x1, Pallas kernels, grad_attn(): pl.pallas_call(grad_attn_body, grid_spec=pltpu.PrefetchScalarGridSpec(num...  11.6 us
    pallas_call x1, Pallas kernels, layer_rows(): pl.pallas_call(layer_body, grid_spec=pltpu.PrefetchScalarGridSpec(num_sca...  10.1 us
    all_gather x1, waiting for transfers between devices, layer(): lax.all_gather(jnp.concatenate(pieces, axis=0), CTX, axis=0, tiled=True)  9.69 us
  transfers between devices with their start and end apart: 37, of which 19 were waited for; matrix products, arithmetic and copies ran while one was open for 3% of the time, Pallas kernels for 22%

profile of v8, /device:TPU:0, one launch (start us, length us, event | category | flops | bytes accessed | tf_op | source)
XLA Modules:
  0.0 251.4 jit_solution(8417306093721187092)
XLA Ops:
  8.1 2.9 %collective-permute-start = (bf16[16,4096]{1,0:T(8,128)(2,1)S(1)}, bf16[16,4096]{1,0:T(8,128)(2,1)S(1)}, u32[]{:S(2)}, u32[]{:S(2)}) collective-permute-start(bf16[16,4096]{1,0:T(8,128)(2,1)S(1)} %constant_dynamic-slice_fusion.2), channel_id=1, source_target_pairs={{32,0},{64,32},{96,64},{0,96},{33,1},{65,33},{97,65},{1,97},{34,2}... | collective-permute-start | bytes 393224 | tf_op jit(solution)/shard_map/ppermute | solution.py:560
  15.2 1.3 local_state.1
  17.3 1.6 collective-permute-done.1
  18.9 1.4 collective-permute-done.2
  21.2 1.7 dynamic-slice_bitcast_fusion.1
  22.9 1.7 collective-permute-done.3.r_ref
  26.2 1.6 collective-permute-start.4
  27.9 2.9 %collective-permute-start.5 = (bf16[256,128]{1,0:T(8,128)(2,1)S(1)}, bf16[256,128]{1,0:T(8,128)(2,1)S(1)}, u32[]{:S(2)}, u32[]{:S(2)}) collective-permute-start(bf16[256,128]{1,0:T(8,128)(2,1)S(1)} %get-tuple-element.85), channel_id=1, source_target_pairs={{0,4},{2,6},{4,0},{6,2},{1,5},{3,7},{5,1},{7,3},{8,12},{10,14},{12... | collective-permute-start | bytes 196616 | tf_op jit(solution)/shard_map/ppermute | solution.py:128
  30.8 1.3 collective-permute-start.6
  32.1 4.0 %local_scores.1 = (bf16[16,256,256]{2,1,0:T(8,128)(2,1)}, f32[256,2048]{1,0:T(8,128)}) custom-call(bf16[256,2048]{1,0:T(8,128)(2,1)S(1)} %bitcast.34, bf16[256,2048]{1,0:T(8,128)(2,1)S(1)} %bitcast.39, bf16[256,2048]{1,0:T(8,128)(2,1)S(1)} %bitcast.43), custom_call_target="tpu_custom_call" | custom-call | flops 536870912 | bytes 7340032 | tf_op jit(solution)/shard_map/local_scores/pallas_call | solution.py:183
  36.8 2.1 collective-permute-start.7
  38.9 3.7 %collective-permute-start.8 = (bf16[256,128]{1,0:T(8,128)(2,1)S(1)}, bf16[256,128]{1,0:T(8,128)(2,1)S(1)}, u32[]{:S(2)}, u32[]{:S(2)}) collective-permute-start(bf16[256,128]{1,0:T(8,128)(2,1)S(1)} %shard_map.102), channel_id=1, source_target_pairs={{0,16},{8,24},{16,0},{24,8},{1,17},{9,25},{17,1},{25,9},{2,18},{10... | collective-permute-start | bytes 196616 | tf_op jit(solution)/shard_map/ppermute | solution.py:128
  43.4 1.8 collective-permute-done.7.z1
  45.2 2.5 collective-permute-done.8.z2
  47.7 1.3 shard_map.103
  49.8 2.4 collective-permute-start.11
  52.2 1.3 collective-permute-start.12
  59.0 3.3 %constant_dynamic-slice_fusion = (bf16[256,2048]{1,0:T(8,128)(2,1)}, bf16[256,2048]{1,0:T(8,128)(2,1)}) fusion(bf16[256,4096]{1,0:T(8,128)(2,1)} %bitcast.62, s32[]{:T(128)S(6)} %select_n.50, s32[]{:T(128)S(6)} %select_n.49), kind=kLoop, calls=%fused_computation.3 | loop fusion | bytes 4194312 | tf_op jit(solution)/shard_map/dynamic_slice | solution.py:593
  62.3 1.8 collective-permute-start.23
  64.1 2.3 collective-permute-start.22
  66.4 5.6 %attend.1 = (bf16[256,1024]{1,0:T(8,128)(2,1)S(1)}, bf16[256,1024]{1,0:T(8,128)(2,1)S(1)}, bf16[1024,256]{1,0:T(8,128)(2,1)}, bf16[1024,256]{1,0:T(8,128)(2,1)S(1)}, f32[4,256,512]{2,1,0:T(8,128)}) custom-call(s32[8]{0:T(128)S(1)} %stack.59.w_ref, bf16[256,2048]{1,0:T(8,128)(2,1)S(1)} %bitcast.35, f32[256,2048]{1,0:T(8,128)} %get-tuple-element.88.o_ref, ...), custom_call_target="tpu_custom_call" | custom-call | flops 134217728 | bytes 6291456 | tf_op jit(solution)/shard_map/attend/pallas_call | solution.py:231
  74.4 2.1 fusion.gn_ref
  76.5 9.7 %all-gather.2.cloned.1.call-done = bf16[1536,4096]{1,0:T(8,128)(2,1)} async-done(((bf16[48,4096]{1,0:T(8,128)(2,1)}), bf16[1536,4096]{1,0:T(8,128)(2,1)}) %all-gather.2.cloned.1.call-update) | async-done | bytes 12582928 | tf_op jit(solution)/shard_map/all_gather | solution.py:594
  86.2 11.6 %grad_attn.1 = (bf16[4,256,512]{2,1,0:T(8,128)(2,1)}, bf16[16,128,128]{2,1,0:T(8,128)(2,1)S(1)}) custom-call(s32[8]{0:T(128)S(1)} %stack.54.w_ref.i_ref, bf16[256,2048]{1,0:T(8,128)(2,1)S(1)} %bitcast.36, f32[4,256,512]{2,1,0:T(8,128)} %get-tuple-element.110.a_ref, f32[256,512]{1,0:T(8,128)} %fusion.gn_ref, f32[1,2048]{1,0:T(1,128)S(1)} %bitcast.59, ...), custom_call_target="tpu_custom_call" | custom-call | flops 3355443200 | bytes 18874368 | tf_op jit(solution)/shard_map/grad_attn/pallas_call | solution.py:318
  98.4 23.4 %collective-permute-done.18.refs_1_ = bf16[1024,256]{1,0:T(8,128)(2,1)} collective-permute-done((bf16[1024,256]{1,0:T(8,128)(2,1)}, bf16[1024,256]{1,0:T(8,128)(2,1)}, u32[]{:S(2)}, u32[]{:S(2)}) %collective-permute-start.18) | collective-permute-done | bytes 524320 | tf_op jit(solution)/shard_map/ppermute | solution.py:123
  121.8 1.3 collective-permute-start.19
  123.1 1.7 collective-permute-start.20
  125.5 11.4 %collective-permute-done.19.refs_2_ = bf16[1024,256]{1,0:T(8,128)(2,1)S(1)} collective-permute-done((bf16[1024,256]{1,0:T(8,128)(2,1)S(1)}, bf16[1024,256]{1,0:T(8,128)(2,1)S(1)}, u32[]{:S(2)}, u32[]{:S(2)}) %collective-permute-start.19) | collective-permute-done | bytes 524320 | tf_op jit(solution)/shard_map/ppermute | solution.py:123
  136.9 11.1 %collective-permute-done.20.refs_3_ = bf16[1024,256]{1,0:T(8,128)(2,1)S(1)} collective-permute-done((bf16[1024,256]{1,0:T(8,128)(2,1)S(1)}, bf16[1024,256]{1,0:T(8,128)(2,1)S(1)}, u32[]{:S(2)}, u32[]{:S(2)}) %collective-permute-start.20) | collective-permute-done | bytes 524320 | tf_op jit(solution)/shard_map/ppermute | solution.py:123
  148.0 5.9 %weight_half.2 = bf16[16,2,32,1024]{3,2,1,0:T(8,128)(2,1)} custom-call(s32[1]{0:T(128)S(6)} %sub.24.i_ref, bf16[1024,256]{1,0:T(8,128)(2,1)} %get-tuple-element.132.refs_0_, bf16[1024,256]{1,0:T(8,128)(2,1)} %collective-permute-done.18.refs_1_, bf16[1024,256]{1,0:T(8,128)(2,1)S(1)} %collective-permute-done.19.refs_2_, ...), custom_call_target="tpu_custom_call" | custom-call | flops 2147483648 | bytes 8388608 | tf_op jit(solution)/shard_map/weight_half/pallas_call | solution.py:499
  155.0 3.2 %collective-permute-start.16 = (bf16[256,128]{1,0:T(8,128)(2,1)S(1)}, bf16[256,128]{1,0:T(8,128)(2,1)S(1)}, u32[]{:S(2)}, u32[]{:S(2)}) collective-permute-start(bf16[256,128]{1,0:T(8,128)(2,1)S(1)} %get-tuple-element.120), channel_id=1, source_target_pairs={{0,4},{2,6},{4,0},{6,2},{1,5},{3,7},{5,1},{7,3},{8,12},{10,14},{12... | collective-permute-start | bytes 196616 | tf_op jit(solution)/shard_map/ppermute | solution.py:128
  158.3 1.3 collective-permute-done.15.refs_0_.t1
  159.7 2.3 collective-permute-done.16.refs_1_.t2
  164.3 6.0 %weight_half.3 = bf16[16,2,32,1024]{3,2,1,0:T(8,128)(2,1)} custom-call(s32[1]{0:T(128)} %bitcast.7.i_ref, bf16[1024,256]{1,0:T(8,128)(2,1)} %get-tuple-element.132.refs_0_, bf16[1024,256]{1,0:T(8,128)(2,1)} %collective-permute-done.18.refs_1_, bf16[1024,256]{1,0:T(8,128)(2,1)S(1)} %collective-permute-done.19.refs_2_, ...), custom_call_target="tpu_custom_call" | custom-call | flops 2147483648 | bytes 8388608 | tf_op jit(solution)/shard_map/weight_half/pallas_call | solution.py:499
  170.3 5.3 %all-to-all-start = ((bf16[16,2,32,1024]{3,2,1,0:T(8,128)(2,1)}), bf16[16,2,32,1024]{3,2,1,0:T(8,128)(2,1)}, u32[]{:S(2)}, u32[]{:S(2)}) async-start(bf16[16,2,32,1024]{3,2,1,0:T(8,128)(2,1)} %weight_half.3), calls=%async_computation | async-start | bytes 4194304 | tf_op jit(solution)/shard_map/all_to_all | solution.py:633
  175.6 1.9 collective-permute-start.24
  177.5 2.7 %collective-permute-start.25 = (bf16[256,128]{1,0:T(8,128)(2,1)}, bf16[256,128]{1,0:T(8,128)(2,1)S(1)}, u32[]{:S(2)}, u32[]{:S(2)}) collective-permute-start(bf16[256,128]{1,0:T(8,128)(2,1)} %copy-done.26), channel_id=1, source_target_pairs={{0,16},{8,24},{16,0},{24,8},{1,17},{9,25},{17,1},{25,9},{2,18},{10... | collective-permute-start | bytes 196616 | tf_op jit(solution)/shard_map/ppermute | solution.py:128
  180.2 1.5 collective-permute-start.26
  181.6 19.2 %collective-permute-done.24.z1 = bf16[256,128]{1,0:T(8,128)(2,1)S(1)} collective-permute-done((bf16[256,128]{1,0:T(8,128)(2,1)}, bf16[256,128]{1,0:T(8,128)(2,1)S(1)}, u32[]{:S(2)}, u32[]{:S(2)}) %collective-permute-start.24) | collective-permute-done | bytes 65568 | tf_op jit(solution)/shard_map/ppermute | solution.py:128
  201.8 1.3 collective-permute-done.26.z3
  206.4 3.3 %collective-permute-start.28 = (bf16[256,128]{1,0:T(8,128)(2,1)S(1)}, bf16[256,128]{1,0:T(8,128)(2,1)S(1)}, u32[]{:S(2)}, u32[]{:S(2)}) collective-permute-start(bf16[256,128]{1,0:T(8,128)(2,1)S(1)} %get-tuple-element.139), channel_id=1, source_target_pairs={{0,2},{2,4},{4,6},{6,0},{1,3},{3,5},{5,7},{7,1},{8,10},{10,12},{12... | collective-permute-start | bytes 196616 | tf_op jit(solution)/shard_map/ppermute | solution.py:128
  209.7 2.8 %collective-permute-start.29 = (bf16[256,128]{1,0:T(8,128)(2,1)S(1)}, bf16[256,128]{1,0:T(8,128)(2,1)S(1)}, u32[]{:S(2)}, u32[]{:S(2)}) collective-permute-start(bf16[256,128]{1,0:T(8,128)(2,1)S(1)} %get-tuple-element.140), channel_id=1, source_target_pairs={{0,4},{2,6},{4,0},{6,2},{1,5},{3,7},{5,1},{7,3},{8,12},{10,14},{12... | collective-permute-start | bytes 196616 | tf_op jit(solution)/shard_map/ppermute | solution.py:128
  214.5 8.4 %local_grads.1 = (bf16[256,2048]{1,0:T(8,128)(2,1)}, f32[4,256,512]{2,1,0:T(8,128)}, f32[4,256,512]{2,1,0:T(8,128)}) custom-call(s32[8]{0:T(128)S(1)} %stack.54.w_ref.i_ref, bf16[256,2048]{1,0:T(8,128)(2,1)S(1)} %bitcast.37, bf16[256,2048]{1,0:T(8,128)(2,1)S(1)} %bitcast.40, bf16[256,2048]{1,0:T(8,128)(2,1)S(1)} %bitcast.44, ...), custom_call_target="tpu_custom_call" | custom-call | flops 1073741824 | bytes 12582912 | tf_op jit(solution)/shard_map/local_grads/pallas_call | solution.py:372
  222.9 10.1 %layer_rows.1 = bf16[256,4096]{1,0:T(8,128)(2,1)} custom-call(s32[8]{0:T(128)S(1)} %stack.54.w_ref.i_ref, bf16[256,1024]{1,0:T(8,128)(2,1)S(1)} %copy-done.17, bf16[256,1024]{1,0:T(8,128)(2,1)S(1)} %copy-done.19, bf16[512,4096]{1,0:T(8,128)(2,1)} %own_ref.1, bf16[32,3,16,4096]{3,2,1,0:T(8,128)(2,1)} %bitcast.61), custom_call_target="tpu_custom_call" | custom-call | flops 4294967296 | bytes 19922944 | tf_op jit(solution)/shard_map/layer_rows/pallas_call | solution.py:456
  233.8 2.0 sum_parts.1
  236.5 1.6 collective-permute-start.34
  238.0 5.3 %later_grads.1 = (bf16[256,2048]{1,0:T(8,128)(2,1)}, bf16[256,2048]{1,0:T(8,128)(2,1)}) custom-call(s32[8]{0:T(128)S(1)} %stack.54.w_ref.i_ref, bf16[256,2048]{1,0:T(8,128)(2,1)S(1)} %bitcast.41, bf16[256,2048]{1,0:T(8,128)(2,1)S(1)} %bitcast.45, bf16[8,128,128]{2,1,0:T(8,128)(2,1)S(1)} %bitcast.56, bf16[8,128,128]{2,1,0:T(8,128)(2,1)S(1)} %bitcast.57, ...), custom_call_target="tpu_custom_call" | custom-call | flops 268435456 | bytes 8388608 | tf_op jit(solution)/shard_map/later_grads/pallas_call | solution.py:413
  243.3 1.3 shard_map.109
  (118 shorter events, 31.0 us)
Async XLA Ops:
  7.2 79.0 %all-gather.2.cloned.1.call-start = ((), (), s32[]{:S(2)}) async-start(), calls=%async_computation.1 | async-start | bytes 12976128 | tf_op jit(solution)/shard_map/all_gather | solution.py:594
  8.1 9.2 %collective-permute-start = (bf16[16,4096]{1,0:T(8,128)(2,1)S(1)}, bf16[16,4096]{1,0:T(8,128)(2,1)S(1)}, u32[]{:S(2)}, u32[]{:S(2)}) collective-permute-start(bf16[16,4096]{1,0:T(8,128)(2,1)S(1)} %constant_dynamic-slice_fusion.2), channel_id=1, source_target_pairs={{32,0},{64,32},{96,64},{0,96},{33,1},{65,33},{97,65},{1,97},{34,2}... | collective-permute-start | bytes 393224 | tf_op jit(solution)/shard_map/ppermute | solution.py:560
  11.1 7.9 %collective-permute-start.1 = (bf16[16,4096]{1,0:T(8,128)(2,1)S(1)}, bf16[16,4096]{1,0:T(8,128)(2,1)S(1)}, u32[]{:S(2)}, u32[]{:S(2)}) collective-permute-start(bf16[16,4096]{1,0:T(8,128)(2,1)S(1)} %constant_dynamic-slice_fusion.2), channel_id=1, source_target_pairs={{64,0},{96,32},{0,64},{32,96},{65,1},{97,33},{1,65},{33,97},{66,2}... | collective-permute-start | bytes 393224 | tf_op jit(solution)/shard_map/ppermute | solution.py:560
  11.9 8.5 %collective-permute-start.2 = (bf16[16,4096]{1,0:T(8,128)(2,1)S(1)}, bf16[16,4096]{1,0:T(8,128)(2,1)S(1)}, u32[]{:S(2)}, u32[]{:S(2)}) collective-permute-start(bf16[16,4096]{1,0:T(8,128)(2,1)S(1)} %constant_dynamic-slice_fusion.2), channel_id=1, source_target_pairs={{96,0},{0,32},{32,64},{64,96},{97,1},{1,33},{33,65},{65,97},{98,2}... | collective-permute-start | bytes 393224 | tf_op jit(solution)/shard_map/ppermute | solution.py:560
  15.2 16.9 %copy-start = (bf16[1,256,2048]{2,1,0:T(8,128)(2,1)S(1)}, bf16[1,256,2048]{2,1,0:T(8,128)(2,1)}, u32[]{:S(2)}) copy-start(bf16[1,256,2048]{2,1,0:T(8,128)(2,1)} %param.6) | copy-start | bytes 3145732
  15.2 16.9 %copy-start.2 = (bf16[1,256,2048]{2,1,0:T(8,128)(2,1)S(1)}, bf16[1,256,2048]{2,1,0:T(8,128)(2,1)}, u32[]{:S(2)}) copy-start(bf16[1,256,2048]{2,1,0:T(8,128)(2,1)} %param.7) | copy-start | bytes 3145732
  15.2 16.9 %copy-start.4 = (bf16[1,256,2048]{2,1,0:T(8,128)(2,1)S(1)}, bf16[1,256,2048]{2,1,0:T(8,128)(2,1)}, u32[]{:S(2)}) copy-start(bf16[1,256,2048]{2,1,0:T(8,128)(2,1)} %param.8) | copy-start | bytes 3145732
  22.8 1.7 collective-permute-start.3
  26.2 9.9 %collective-permute-start.4 = (bf16[256,128]{1,0:T(8,128)(2,1)S(1)}, bf16[256,128]{1,0:T(8,128)(2,1)S(1)}, u32[]{:S(2)}, u32[]{:S(2)}) collective-permute-start(bf16[256,128]{1,0:T(8,128)(2,1)S(1)} %get-tuple-element.84), channel_id=1, source_target_pairs={{0,2},{2,4},{4,6},{6,0},{1,3},{3,5},{5,7},{7,1},{8,10},{10,12},{12... | collective-permute-start | bytes 196616 | tf_op jit(solution)/shard_map/ppermute | solution.py:128
  27.9 8.2 %collective-permute-start.5 = (bf16[256,128]{1,0:T(8,128)(2,1)S(1)}, bf16[256,128]{1,0:T(8,128)(2,1)S(1)}, u32[]{:S(2)}, u32[]{:S(2)}) collective-permute-start(bf16[256,128]{1,0:T(8,128)(2,1)S(1)} %get-tuple-element.85), channel_id=1, source_target_pairs={{0,4},{2,6},{4,0},{6,2},{1,5},{3,7},{5,1},{7,3},{8,12},{10,14},{12... | collective-permute-start | bytes 196616 | tf_op jit(solution)/shard_map/ppermute | solution.py:128
  30.8 5.4 %collective-permute-start.6 = (bf16[256,128]{1,0:T(8,128)(2,1)S(1)}, bf16[256,128]{1,0:T(8,128)(2,1)S(1)}, u32[]{:S(2)}, u32[]{:S(2)}) collective-permute-start(bf16[256,128]{1,0:T(8,128)(2,1)S(1)} %get-tuple-element.86), channel_id=1, source_target_pairs={{0,6},{2,0},{4,2},{6,4},{1,7},{3,1},{5,3},{7,5},{8,14},{10,8},{12,... | collective-permute-start | bytes 196616 | tf_op jit(solution)/shard_map/ppermute | solution.py:128
  36.8 8.4 %collective-permute-start.7 = (bf16[256,128]{1,0:T(8,128)(2,1)S(1)}, bf16[256,128]{1,0:T(8,128)(2,1)S(1)}, u32[]{:S(2)}, u32[]{:S(2)}) collective-permute-start(bf16[256,128]{1,0:T(8,128)(2,1)S(1)} %shard_map.102), channel_id=1, source_target_pairs={{0,8},{8,16},{16,24},{24,0},{1,9},{9,17},{17,25},{25,1},{2,10},{10... | collective-permute-start | bytes 196616 | tf_op jit(solution)/shard_map/ppermute | solution.py:128
  38.9 8.8 %collective-permute-start.8 = (bf16[256,128]{1,0:T(8,128)(2,1)S(1)}, bf16[256,128]{1,0:T(8,128)(2,1)S(1)}, u32[]{:S(2)}, u32[]{:S(2)}) collective-permute-start(bf16[256,128]{1,0:T(8,128)(2,1)S(1)} %shard_map.102), channel_id=1, source_target_pairs={{0,16},{8,24},{16,0},{24,8},{1,17},{9,25},{17,1},{25,9},{2,18},{10... | collective-permute-start | bytes 196616 | tf_op jit(solution)/shard_map/ppermute | solution.py:128
  42.6 5.1 %collective-permute-start.9 = (bf16[256,128]{1,0:T(8,128)(2,1)S(1)}, bf16[256,128]{1,0:T(8,128)(2,1)S(1)}, u32[]{:S(2)}, u32[]{:S(2)}) collective-permute-start(bf16[256,128]{1,0:T(8,128)(2,1)S(1)} %shard_map.102), channel_id=1, source_target_pairs={{0,24},{8,0},{16,8},{24,16},{1,25},{9,1},{17,9},{25,17},{2,26},{10... | collective-permute-start | bytes 196616 | tf_op jit(solution)/shard_map/ppermute | solution.py:128
  49.0 5.8 %collective-permute-start.10 = (bf16[256,128]{1,0:T(8,128)(2,1)}, bf16[256,128]{1,0:T(8,128)(2,1)}, u32[]{:S(2)}, u32[]{:S(2)}) collective-permute-start(bf16[256,128]{1,0:T(8,128)(2,1)} %get-tuple-element.99), channel_id=1, source_target_pairs={{0,2},{2,4},{4,6},{6,0},{1,3},{3,5},{5,7},{7,1},{8,10},{10,12},{12... | collective-permute-start | bytes 196616 | tf_op jit(solution)/shard_map/ppermute | solution.py:128
  49.8 6.1 %collective-permute-start.11 = (bf16[256,128]{1,0:T(8,128)(2,1)}, bf16[256,128]{1,0:T(8,128)(2,1)}, u32[]{:S(2)}, u32[]{:S(2)}) collective-permute-start(bf16[256,128]{1,0:T(8,128)(2,1)} %get-tuple-element.100), channel_id=1, source_target_pairs={{0,4},{2,6},{4,0},{6,2},{1,5},{3,7},{5,1},{7,3},{8,12},{10,14},{12... | collective-permute-start | bytes 196616 | tf_op jit(solution)/shard_map/ppermute | solution.py:128
  52.2 4.6 %collective-permute-start.12 = (bf16[256,128]{1,0:T(8,128)(2,1)}, bf16[256,128]{1,0:T(8,128)(2,1)}, u32[]{:S(2)}, u32[]{:S(2)}) collective-permute-start(bf16[256,128]{1,0:T(8,128)(2,1)} %get-tuple-element.101), channel_id=1, source_target_pairs={{0,6},{2,0},{4,2},{6,4},{1,7},{3,1},{5,3},{7,5},{8,14},{10,8},{12,... | collective-permute-start | bytes 196616 | tf_op jit(solution)/shard_map/ppermute | solution.py:128
  58.9 7.5 %collective-permute-start.13 = (bf16[4,256,128]{2,1,0:T(8,128)(2,1)S(1)}, bf16[4,256,128]{2,1,0:T(8,128)(2,1)S(1)}, u32[]{:S(2)}, u32[]{:S(2)}) collective-permute-start(bf16[4,256,128]{2,1,0:T(8,128)(2,1)S(1)} %get-tuple-element.107), channel_id=1, source_target_pairs={{0,1},{1,0},{2,3},{3,2},{4,5},{5,4},{6,7},{7,6},{8,9},{9,8},{10,11... | collective-permute-start | bytes 786440 | tf_op jit(solution)/shard_map/ppermute | solution.py:128
  59.0 15.4 %copy-start.31 = (bf16[512,4096]{1,0:T(8,128)(2,1)S(1)}, bf16[512,4096]{1,0:T(8,128)(2,1)}, u32[]{:S(2)}) copy-start(bf16[512,4096]{1,0:T(8,128)(2,1)} %own_ref.1) | copy-start | bytes 12582916
  62.3 12.2 %copy-start.30 = (bf16[1,256,4096]{2,1,0:T(8,128)(2,1)S(1)}, bf16[1,256,4096]{2,1,0:T(8,128)(2,1)}, u32[]{:S(2)}) copy-start(bf16[1,256,4096]{2,1,0:T(8,128)(2,1)} %param.11) | copy-start | bytes 6291460
  62.3 85.8 %collective-permute-start.21 = (bf16[256,2048]{1,0:T(8,128)(2,1)}, bf16[256,2048]{1,0:T(8,128)(2,1)}, u32[]{:S(2)}, u32[]{:S(2)}) collective-permute-start(bf16[256,2048]{1,0:T(8,128)(2,1)} %get-tuple-element.161), channel_id=1, source_target_pairs={{0,32},{32,0},{64,96},{96,64},{1,33},{33,1},{65,97},{97,65},{2,34}... | collective-permute-start | bytes 3145736 | tf_op jit(solution)/shard_map/ppermute | solution.py:123
  62.3 85.8 %collective-permute-start.23 = (bf16[256,2048]{1,0:T(8,128)(2,1)}, bf16[256,2048]{1,0:T(8,128)(2,1)}, u32[]{:S(2)}, u32[]{:S(2)}) collective-permute-start(bf16[256,2048]{1,0:T(8,128)(2,1)} %get-tuple-element.161), channel_id=1, source_target_pairs={{0,96},{32,64},{64,32},{96,0},{1,97},{33,65},{65,33},{97,1},{2,98}... | collective-permute-start | bytes 3145736 | tf_op jit(solution)/shard_map/ppermute | solution.py:123
  64.1 84.0 %collective-permute-start.22 = (bf16[256,2048]{1,0:T(8,128)(2,1)}, bf16[256,2048]{1,0:T(8,128)(2,1)}, u32[]{:S(2)}, u32[]{:S(2)}) collective-permute-start(bf16[256,2048]{1,0:T(8,128)(2,1)} %get-tuple-element.162.refs_4_), channel_id=1, source_target_pairs={{0,64},{32,96},{64,0},{96,32},{1,65},{33,97},{65,1},{97,33},{2,66}... | collective-permute-start | bytes 3145736 | tf_op jit(solution)/shard_map/ppermute | solution.py:123
  74.4 47.4 %collective-permute-start.18 = (bf16[1024,256]{1,0:T(8,128)(2,1)}, bf16[1024,256]{1,0:T(8,128)(2,1)}, u32[]{:S(2)}, u32[]{:S(2)}) collective-permute-start(bf16[1024,256]{1,0:T(8,128)(2,1)} %get-tuple-element.132.refs_0_), channel_id=1, source_target_pairs={{0,32},{32,0},{64,96},{96,64},{1,33},{33,1},{65,97},{97,65},{2,34}... | collective-permute-start | bytes 1572872 | tf_op jit(solution)/shard_map/ppermute | solution.py:123
  86.2 35.6 %copy-start.29 = (bf16[1024,256]{1,0:T(8,128)(2,1)S(1)}, bf16[1024,256]{1,0:T(8,128)(2,1)}, u32[]{:S(2)}) copy-start(bf16[1024,256]{1,0:T(8,128)(2,1)} %copy-done.28) | copy-start | bytes 1572868
  97.8 27.0 %copy-start.8 = (bf16[16,128,128]{2,1,0:T(8,128)(2,1)}, bf16[16,128,128]{2,1,0:T(8,128)(2,1)S(1)}, u32[]{:S(2)}) copy-start(bf16[16,128,128]{2,1,0:T(8,128)(2,1)S(1)} %get-tuple-element.117) | copy-start | bytes 1572868
  97.9 25.2 %collective-permute-start.14 = (bf16[4,256,128]{2,1,0:T(8,128)(2,1)S(1)}, bf16[4,256,128]{2,1,0:T(8,128)(2,1)S(1)}, u32[]{:S(2)}, u32[]{:S(2)}) collective-permute-start(bf16[4,256,128]{2,1,0:T(8,128)(2,1)S(1)} %dynamic-slice_bitcast_fusion), channel_id=1, source_target_pairs={{0,1},{1,0},{2,3},{3,2},{4,5},{5,4},{6,7},{7,6},{8,9},{9,8},{10,11... | collective-permute-start | bytes 786440 | tf_op jit(solution)/shard_map/ppermute | solution.py:128
  121.8 15.1 %collective-permute-start.19 = (bf16[1024,256]{1,0:T(8,128)(2,1)S(1)}, bf16[1024,256]{1,0:T(8,128)(2,1)S(1)}, u32[]{:S(2)}, u32[]{:S(2)}) collective-permute-start(bf16[1024,256]{1,0:T(8,128)(2,1)S(1)} %copy-done.29), channel_id=1, source_target_pairs={{0,64},{32,96},{64,0},{96,32},{1,65},{33,97},{65,1},{97,33},{2,66}... | collective-permute-start | bytes 1572872 | tf_op jit(solution)/shard_map/ppermute | solution.py:123
  123.1 30.8 %copy-start.14 = (bf16[4,256,128]{2,1,0:T(8,128)(2,1)}, bf16[4,256,128]{2,1,0:T(8,128)(2,1)S(1)}, u32[]{:S(2)}) copy-start(bf16[4,256,128]{2,1,0:T(8,128)(2,1)S(1)} %collective-permute-done.14.r_ref) | copy-start | bytes 786436
  123.1 24.9 %collective-permute-start.20 = (bf16[1024,256]{1,0:T(8,128)(2,1)S(1)}, bf16[1024,256]{1,0:T(8,128)(2,1)S(1)}, u32[]{:S(2)}, u32[]{:S(2)}) collective-permute-start(bf16[1024,256]{1,0:T(8,128)(2,1)S(1)} %copy-done.29), channel_id=1, source_target_pairs={{0,96},{32,64},{64,32},{96,0},{1,97},{33,65},{65,33},{97,1},{2,98}... | collective-permute-start | bytes 1572872 | tf_op jit(solution)/shard_map/ppermute | solution.py:123
  154.0 10.4 %collective-permute-start.27 = (bf16[16,2,32,1024]{3,2,1,0:T(8,128)(2,1)}, bf16[16,2,32,1024]{3,2,1,0:T(8,128)(2,1)S(1)}, u32[]{:S(2)}, u32[]{:S(2)}) collective-permute-start(bf16[16,2,32,1024]{3,2,1,0:T(8,128)(2,1)} %weight_half.2), channel_id=1, source_target_pairs={{0,1},{1,0},{2,3},{3,2},{4,5},{5,4},{6,7},{7,6},{8,9},{9,8},{10,11... | collective-permute-start | bytes 6291464 | tf_op jit(solution)/shard_map/ppermute | solution.py:128
  154.0 5.7 %collective-permute-start.15 = (bf16[256,128]{1,0:T(8,128)(2,1)S(1)}, bf16[256,128]{1,0:T(8,128)(2,1)S(1)}, u32[]{:S(2)}, u32[]{:S(2)}) collective-permute-start(bf16[256,128]{1,0:T(8,128)(2,1)S(1)} %get-tuple-element.119), channel_id=1, source_target_pairs={{0,2},{2,4},{4,6},{6,0},{1,3},{3,5},{5,7},{7,1},{8,10},{10,12},{12... | collective-permute-start | bytes 196616 | tf_op jit(solution)/shard_map/ppermute | solution.py:128
  155.0 7.0 %collective-permute-start.16 = (bf16[256,128]{1,0:T(8,128)(2,1)S(1)}, bf16[256,128]{1,0:T(8,128)(2,1)S(1)}, u32[]{:S(2)}, u32[]{:S(2)}) collective-permute-start(bf16[256,128]{1,0:T(8,128)(2,1)S(1)} %get-tuple-element.120), channel_id=1, source_target_pairs={{0,4},{2,6},{4,0},{6,2},{1,5},{3,7},{5,1},{7,3},{8,12},{10,14},{12... | collective-permute-start | bytes 196616 | tf_op jit(solution)/shard_map/ppermute | solution.py:128
  158.2 4.3 %collective-permute-start.17 = (bf16[256,128]{1,0:T(8,128)(2,1)S(1)}, bf16[256,128]{1,0:T(8,128)(2,1)S(1)}, u32[]{:S(2)}, u32[]{:S(2)}) collective-permute-start(bf16[256,128]{1,0:T(8,128)(2,1)S(1)} %get-tuple-element.121), channel_id=1, source_target_pairs={{0,6},{2,0},{4,2},{6,4},{1,7},{3,1},{5,3},{7,5},{8,14},{10,8},{12,... | collective-permute-start | bytes 196616 | tf_op jit(solution)/shard_map/ppermute | solution.py:128
  170.3 43.2 %copy-start.11 = (bf16[4,256,128]{2,1,0:T(8,128)(2,1)S(1)}, bf16[4,256,128]{2,1,0:T(8,128)(2,1)}, u32[]{:S(2)}) copy-start(bf16[4,256,128]{2,1,0:T(8,128)(2,1)} %copy-done.10) | copy-start | bytes 786436
  170.3 63.5 %all-to-all-start = ((bf16[16,2,32,1024]{3,2,1,0:T(8,128)(2,1)}), bf16[16,2,32,1024]{3,2,1,0:T(8,128)(2,1)}, u32[]{:S(2)}, u32[]{:S(2)}) async-start(bf16[16,2,32,1024]{3,2,1,0:T(8,128)(2,1)} %weight_half.3), calls=%async_computation | async-start | bytes 4194304 | tf_op jit(solution)/shard_map/all_to_all | solution.py:633
  175.6 25.2 %collective-permute-start.24 = (bf16[256,128]{1,0:T(8,128)(2,1)}, bf16[256,128]{1,0:T(8,128)(2,1)S(1)}, u32[]{:S(2)}, u32[]{:S(2)}) collective-permute-start(bf16[256,128]{1,0:T(8,128)(2,1)} %copy-done.26), channel_id=1, source_target_pairs={{0,8},{8,16},{16,24},{24,0},{1,9},{9,17},{17,25},{25,1},{2,10},{10... | collective-permute-start | bytes 196616 | tf_op jit(solution)/shard_map/ppermute | solution.py:128
  177.5 24.3 %collective-permute-start.25 = (bf16[256,128]{1,0:T(8,128)(2,1)}, bf16[256,128]{1,0:T(8,128)(2,1)S(1)}, u32[]{:S(2)}, u32[]{:S(2)}) collective-permute-start(bf16[256,128]{1,0:T(8,128)(2,1)} %copy-done.26), channel_id=1, source_target_pairs={{0,16},{8,24},{16,0},{24,8},{1,17},{9,25},{17,1},{25,9},{2,18},{10... | collective-permute-start | bytes 196616 | tf_op jit(solution)/shard_map/ppermute | solution.py:128
  180.2 23.0 %collective-permute-start.26 = (bf16[256,128]{1,0:T(8,128)(2,1)}, bf16[256,128]{1,0:T(8,128)(2,1)S(1)}, u32[]{:S(2)}, u32[]{:S(2)}) collective-permute-start(bf16[256,128]{1,0:T(8,128)(2,1)} %copy-done.26), channel_id=1, source_target_pairs={{0,24},{8,0},{16,8},{24,16},{1,25},{9,1},{17,9},{25,17},{2,26},{10... | collective-permute-start | bytes 196616 | tf_op jit(solution)/shard_map/ppermute | solution.py:128
  206.4 26.6 %collective-permute-start.28 = (bf16[256,128]{1,0:T(8,128)(2,1)S(1)}, bf16[256,128]{1,0:T(8,128)(2,1)S(1)}, u32[]{:S(2)}, u32[]{:S(2)}) collective-permute-start(bf16[256,128]{1,0:T(8,128)(2,1)S(1)} %get-tuple-element.139), channel_id=1, source_target_pairs={{0,2},{2,4},{4,6},{6,0},{1,3},{3,5},{5,7},{7,1},{8,10},{10,12},{12... | collective-permute-start | bytes 196616 | tf_op jit(solution)/shard_map/ppermute | solution.py:128
  209.7 23.3 %collective-permute-start.29 = (bf16[256,128]{1,0:T(8,128)(2,1)S(1)}, bf16[256,128]{1,0:T(8,128)(2,1)S(1)}, u32[]{:S(2)}, u32[]{:S(2)}) collective-permute-start(bf16[256,128]{1,0:T(8,128)(2,1)S(1)} %get-tuple-element.140), channel_id=1, source_target_pairs={{0,4},{2,6},{4,0},{6,2},{1,5},{3,7},{5,1},{7,3},{8,12},{10,14},{12... | collective-permute-start | bytes 196616 | tf_op jit(solution)/shard_map/ppermute | solution.py:128
  212.5 20.5 %collective-permute-start.30 = (bf16[256,128]{1,0:T(8,128)(2,1)S(1)}, bf16[256,128]{1,0:T(8,128)(2,1)S(1)}, u32[]{:S(2)}, u32[]{:S(2)}) collective-permute-start(bf16[256,128]{1,0:T(8,128)(2,1)S(1)} %get-tuple-element.141), channel_id=1, source_target_pairs={{0,6},{2,0},{4,2},{6,4},{1,7},{3,1},{5,3},{7,5},{8,14},{10,8},{12,... | collective-permute-start | bytes 196616 | tf_op jit(solution)/shard_map/ppermute | solution.py:128
  222.9 10.2 %copy-start.9 = (bf16[16,128,128]{2,1,0:T(8,128)(2,1)S(1)}, bf16[16,128,128]{2,1,0:T(8,128)(2,1)}, u32[]{:S(2)}) copy-start(bf16[16,128,128]{2,1,0:T(8,128)(2,1)} %copy-done.8) | copy-start | bytes 1572868
  222.9 10.2 %copy-start.15 = (bf16[4,256,128]{2,1,0:T(8,128)(2,1)S(1)}, bf16[4,256,128]{2,1,0:T(8,128)(2,1)}, u32[]{:S(2)}) copy-start(bf16[4,256,128]{2,1,0:T(8,128)(2,1)} %copy-done.14) | copy-start | bytes 786436
  233.7 4.3 %collective-permute-start.31 = (bf16[4,256,128]{2,1,0:T(8,128)(2,1)S(1)}, bf16[4,256,128]{2,1,0:T(8,128)(2,1)S(1)}, u32[]{:S(2)}, u32[]{:S(2)}) collective-permute-start(bf16[4,256,128]{2,1,0:T(8,128)(2,1)S(1)} %get-tuple-element.153), channel_id=1, source_target_pairs={{0,1},{1,0},{2,3},{3,2},{4,5},{5,4},{6,7},{7,6},{8,9},{9,8},{10,11... | collective-permute-start | bytes 786440 | tf_op jit(solution)/shard_map/ppermute | solution.py:128
  235.8 7.5 %collective-permute-start.32 = (f32[16,1024]{1,0:T(8,128)S(1)}, f32[16,1024]{1,0:T(8,128)S(1)}, u32[]{:S(2)}, u32[]{:S(2)}) collective-permute-start(f32[16,1024]{1,0:T(8,128)S(1)} %get-tuple-element.158), channel_id=1, source_target_pairs={{0,32},{32,0},{64,96},{96,64},{1,33},{33,1},{65,97},{97,65},{2,34}... | collective-permute-start | bytes 196616 | tf_op jit(solution)/shard_map/ppermute | solution.py:123
  235.9 7.4 %collective-permute-start.33 = (f32[16,1024]{1,0:T(8,128)S(1)}, f32[16,1024]{1,0:T(8,128)S(1)}, u32[]{:S(2)}, u32[]{:S(2)}) collective-permute-start(f32[16,1024]{1,0:T(8,128)S(1)} %get-tuple-element.159), channel_id=1, source_target_pairs={{0,1},{1,0},{2,3},{3,2},{4,5},{5,4},{6,7},{7,6},{8,9},{9,8},{10,11... | collective-permute-start | bytes 196616 | tf_op jit(solution)/shard_map/ppermute | solution.py:123
  236.5 6.9 %collective-permute-start.34 = (f32[16,1024]{1,0:T(8,128)S(1)}, f32[16,1024]{1,0:T(8,128)S(1)}, u32[]{:S(2)}, u32[]{:S(2)}) collective-permute-start(f32[16,1024]{1,0:T(8,128)S(1)} %get-tuple-element.160), channel_id=1, source_target_pairs={{0,33},{1,32},{32,1},{33,0},{64,97},{65,96},{96,65},{97,64},{2,35}... | collective-permute-start | bytes 196616 | tf_op jit(solution)/shard_map/ppermute | solution.py:647
  (21 other events, 51.4 us)
Sparse Core Ops, SparseCore 0:
  21.3 64.8 all-gather.1

commit v9 on v8

--- a/solution.py
+++ b/solution.py
@@ -360,8 +360,8 @@
         gs = jnp.where(keep, mm(ga, head(v_ref, h), 1, 1), 0.0).astype(BF)
         gq = mm(gs, head(k_ref, h), 1, 0) + mm(ga, pick(i_ref, chunk, m_ref, t_ref, h), 1, 1)
         gq_ref[:, cols] = gq.astype(BF)
-        gk_ref[0, :, cols] = mm(gs, head(q_ref, h), 0, 0)
-        gv_ref[0, :, cols] = mm(w_ref[h], ga, 0, 0)
+        gk_ref[0, :, cols] = mm(gs, head(q_ref, h), 0, 0).astype(BF)
+        gv_ref[0, :, cols] = mm(w_ref[h], ga, 0, 0).astype(BF)
 
 
 def local_grads(order, q, k, v, weights, ga, carried):
@@ -386,8 +386,8 @@
         ),
         out_shape=[
             jax.ShapeDtypeStruct((t, f), BF),
-            pltpu.HBM((CH, t, w), F32),
-            pltpu.HBM((CH, t, w), F32),
+            pltpu.HBM((CH, t, w), BF),
+            pltpu.HBM((CH, t, w), BF),
         ],
         cost_estimate=cost(8 * t * t * f, 24 * t * f),
         compiler_params=pltpu.CompilerParams(vmem_limit_bytes=20 << 20),
@@ -399,8 +399,8 @@
     for h in range(HC):
         cols = slice(h * HD, (h + 1) * HD)
         state = pick(i_ref, pl.program_id(0), m_ref, t_ref, h)
-        gk = pk_ref[0, :, cols] + mm(head(v_ref, h), state, 1, 1)
-        gv = pv_ref[0, :, cols] + mm(head(k_ref, h), state, 1, 0)
+        gk = pk_ref[0, :, cols].astype(F32) + mm(head(v_ref, h), state, 1, 1)
+        gv = pv_ref[0, :, cols].astype(F32) + mm(head(k_ref, h), state, 1, 0)
         gk_ref[:, cols] = gk.astype(BF)
         gv_ref[:, cols] = gv.astype(BF)
 

time: 254 us -> 253 us (level)
  transfers between devices with their start and end apart: 37 -> 37, of which waited for: 19 -> 18; matrix products, arithmetic and copies ran while one was open for 3% -> 3% of each run, Pallas kernels for 22% -> 21%
where the time goes in v9:
time: 253 us; the launch traced here: 251 us
  waiting for transfers between devices  93.6 us (37%)
  Pallas kernels  67 us (26%)
  starting transfers between devices  54.5 us (22%)
  local copies, waits for them, and re-layouts  18.6 us (7%)
  between operations  14.3 us (6%)
    ppermute x8, waiting for transfers between devices, partner(): lax.ppermute(x, axis, [(d, d ^ bits) for d in range(lax.axis_size(axis))])  46.1 us
    ppermute x23, starting transfers between devices, give_to(): return lax.ppermute(x, axis, [(d, (d + by) % n) for d in range(n)])  35.3 us
    ppermute x23, waiting for transfers between devices, give_to(): return lax.ppermute(x, axis, [(d, (d + by) % n) for d in range(n)])  34.9 us
    unnamed x64, local copies, waits for them, and re-layouts  12.5 us
    pallas_call x2, Pallas kernels, weight_half(): pl.pallas_call(functools.partial(weight_body, add), grid_spec=pltpu.Prefe...  11.8 us
    pallas_call x1, Pallas kernels, grad_attn(): pl.pallas_call(grad_attn_body, grid_spec=pltpu.PrefetchScalarGridSpec(num...  11.6 us
    pallas_call x1, Pallas kernels, layer_rows(): pl.pallas_call(layer_body, grid_spec=pltpu.PrefetchScalarGridSpec(num_sca...  10.1 us
    all_gather x1, waiting for transfers between devices, layer(): lax.all_gather(jnp.concatenate(pieces, axis=0), CTX, axis=0, tiled=True)  9.57 us
  transfers between devices with their start and end apart: 37, of which 18 were waited for; matrix products, arithmetic and copies ran while one was open for 3% of the time, Pallas kernels for 21%

profile of v9, /device:TPU:0, one launch (start us, length us, event | category | flops | bytes accessed | tf_op | source)
XLA Modules:
  0.0 250.8 jit_solution(7487486260567109705)
XLA Ops:
  8.1 2.9 %collective-permute-start = (bf16[16,4096]{1,0:T(8,128)(2,1)S(1)}, bf16[16,4096]{1,0:T(8,128)(2,1)S(1)}, u32[]{:S(2)}, u32[]{:S(2)}) collective-permute-start(bf16[16,4096]{1,0:T(8,128)(2,1)S(1)} %constant_dynamic-slice_fusion.2), channel_id=1, source_target_pairs={{32,0},{64,32},{96,64},{0,96},{33,1},{65,33},{97,65},{1,97},{34,2}... | collective-permute-start | bytes 393224 | tf_op jit(solution)/shard_map/ppermute | solution.py:560
  15.2 1.3 local_state.1
  17.3 1.6 collective-permute-done.1
  18.9 1.4 collective-permute-done.2
  21.2 1.7 dynamic-slice_bitcast_fusion.1
  22.9 1.7 collective-permute-done.3.r_ref
  26.2 1.6 collective-permute-start.4
  27.9 2.9 %collective-permute-start.5 = (bf16[256,128]{1,0:T(8,128)(2,1)S(1)}, bf16[256,128]{1,0:T(8,128)(2,1)S(1)}, u32[]{:S(2)}, u32[]{:S(2)}) collective-permute-start(bf16[256,128]{1,0:T(8,128)(2,1)S(1)} %get-tuple-element.85), channel_id=1, source_target_pairs={{0,4},{2,6},{4,0},{6,2},{1,5},{3,7},{5,1},{7,3},{8,12},{10,14},{12... | collective-permute-start | bytes 196616 | tf_op jit(solution)/shard_map/ppermute | solution.py:128
  30.8 1.3 collective-permute-start.6
  32.2 4.0 %local_scores.1 = (bf16[16,256,256]{2,1,0:T(8,128)(2,1)}, f32[256,2048]{1,0:T(8,128)}) custom-call(bf16[256,2048]{1,0:T(8,128)(2,1)S(1)} %bitcast.42, bf16[256,2048]{1,0:T(8,128)(2,1)S(1)} %bitcast.35, bf16[256,2048]{1,0:T(8,128)(2,1)S(1)} %bitcast.39), custom_call_target="tpu_custom_call" | custom-call | flops 536870912 | bytes 7340032 | tf_op jit(solution)/shard_map/local_scores/pallas_call | solution.py:183
  36.8 2.1 collective-permute-start.7
  38.9 3.7 %collective-permute-start.8 = (bf16[256,128]{1,0:T(8,128)(2,1)S(1)}, bf16[256,128]{1,0:T(8,128)(2,1)S(1)}, u32[]{:S(2)}, u32[]{:S(2)}) collective-permute-start(bf16[256,128]{1,0:T(8,128)(2,1)S(1)} %shard_map.102), channel_id=1, source_target_pairs={{0,16},{8,24},{16,0},{24,8},{1,17},{9,25},{17,1},{25,9},{2,18},{10... | collective-permute-start | bytes 196616 | tf_op jit(solution)/shard_map/ppermute | solution.py:128
  43.4 1.7 collective-permute-done.7.z1
  45.2 2.5 collective-permute-done.8.z2
  47.7 1.3 shard_map.103
  49.8 2.4 collective-permute-start.11
  52.2 1.3 collective-permute-start.12
  59.0 3.3 %constant_dynamic-slice_fusion = (bf16[256,2048]{1,0:T(8,128)(2,1)}, bf16[256,2048]{1,0:T(8,128)(2,1)}) fusion(bf16[256,4096]{1,0:T(8,128)(2,1)} %bitcast.62, s32[]{:T(128)S(6)} %select_n.50, s32[]{:T(128)S(6)} %select_n.49), kind=kLoop, calls=%fused_computation.3 | loop fusion | bytes 4194312 | tf_op jit(solution)/shard_map/dynamic_slice | solution.py:593
  62.3 1.8 collective-permute-start.23
  64.1 2.3 collective-permute-start.22
  66.4 5.6 %attend.1 = (bf16[256,1024]{1,0:T(8,128)(2,1)S(1)}, bf16[256,1024]{1,0:T(8,128)(2,1)S(1)}, bf16[1024,256]{1,0:T(8,128)(2,1)}, bf16[1024,256]{1,0:T(8,128)(2,1)S(1)}, f32[4,256,512]{2,1,0:T(8,128)}) custom-call(s32[8]{0:T(128)S(1)} %stack.59.w_ref, bf16[256,2048]{1,0:T(8,128)(2,1)S(1)} %bitcast.43, f32[256,2048]{1,0:T(8,128)} %get-tuple-element.88.o_ref, ...), custom_call_target="tpu_custom_call" | custom-call | flops 134217728 | bytes 6291456 | tf_op jit(solution)/shard_map/attend/pallas_call | solution.py:231
  74.5 2.1 fusion.gn_ref
  76.6 9.6 %all-gather.2.cloned.1.call-done = bf16[1536,4096]{1,0:T(8,128)(2,1)} async-done(((bf16[48,4096]{1,0:T(8,128)(2,1)}), bf16[1536,4096]{1,0:T(8,128)(2,1)}) %all-gather.2.cloned.1.call-update) | async-done | bytes 12582928 | tf_op jit(solution)/shard_map/all_gather | solution.py:594
  86.2 11.6 %grad_attn.1 = (bf16[4,256,512]{2,1,0:T(8,128)(2,1)}, bf16[16,128,128]{2,1,0:T(8,128)(2,1)S(1)}) custom-call(s32[8]{0:T(128)S(1)} %stack.54.w_ref.i_ref, bf16[256,2048]{1,0:T(8,128)(2,1)S(1)} %bitcast.44, f32[4,256,512]{2,1,0:T(8,128)} %get-tuple-element.110.a_ref, f32[256,512]{1,0:T(8,128)} %fusion.gn_ref, f32[1,2048]{1,0:T(1,128)S(1)} %bitcast.59, ...), custom_call_target="tpu_custom_call" | custom-call | flops 3355443200 | bytes 18874368 | tf_op jit(solution)/shard_map/grad_attn/pallas_call | solution.py:318
  98.3 23.5 %collective-permute-done.18.refs_1_ = bf16[1024,256]{1,0:T(8,128)(2,1)} collective-permute-done((bf16[1024,256]{1,0:T(8,128)(2,1)}, bf16[1024,256]{1,0:T(8,128)(2,1)}, u32[]{:S(2)}, u32[]{:S(2)}) %collective-permute-start.18) | collective-permute-done | bytes 524320 | tf_op jit(solution)/shard_map/ppermute | solution.py:123
  121.8 1.3 collective-permute-start.19
  123.1 1.7 collective-permute-start.20
  125.5 11.4 %collective-permute-done.19.refs_2_ = bf16[1024,256]{1,0:T(8,128)(2,1)S(1)} collective-permute-done((bf16[1024,256]{1,0:T(8,128)(2,1)S(1)}, bf16[1024,256]{1,0:T(8,128)(2,1)S(1)}, u32[]{:S(2)}, u32[]{:S(2)}) %collective-permute-start.19) | collective-permute-done | bytes 524320 | tf_op jit(solution)/shard_map/ppermute | solution.py:123
  136.9 11.1 %collective-permute-done.20.refs_3_ = bf16[1024,256]{1,0:T(8,128)(2,1)S(1)} collective-permute-done((bf16[1024,256]{1,0:T(8,128)(2,1)S(1)}, bf16[1024,256]{1,0:T(8,128)(2,1)S(1)}, u32[]{:S(2)}, u32[]{:S(2)}) %collective-permute-start.20) | collective-permute-done | bytes 524320 | tf_op jit(solution)/shard_map/ppermute | solution.py:123
  148.0 5.9 %weight_half.2 = bf16[16,2,32,1024]{3,2,1,0:T(8,128)(2,1)} custom-call(s32[1]{0:T(128)S(6)} %sub.24.i_ref, bf16[1024,256]{1,0:T(8,128)(2,1)} %get-tuple-element.132.refs_0_, bf16[1024,256]{1,0:T(8,128)(2,1)} %collective-permute-done.18.refs_1_, bf16[1024,256]{1,0:T(8,128)(2,1)S(1)} %collective-permute-done.19.refs_2_, ...), custom_call_target="tpu_custom_call" | custom-call | flops 2147483648 | bytes 8388608 | tf_op jit(solution)/shard_map/weight_half/pallas_call | solution.py:499
  155.0 3.3 %collective-permute-start.16 = (bf16[256,128]{1,0:T(8,128)(2,1)S(1)}, bf16[256,128]{1,0:T(8,128)(2,1)S(1)}, u32[]{:S(2)}, u32[]{:S(2)}) collective-permute-start(bf16[256,128]{1,0:T(8,128)(2,1)S(1)} %get-tuple-element.120), channel_id=1, source_target_pairs={{0,4},{2,6},{4,0},{6,2},{1,5},{3,7},{5,1},{7,3},{8,12},{10,14},{12... | collective-permute-start | bytes 196616 | tf_op jit(solution)/shard_map/ppermute | solution.py:128
  158.3 1.4 collective-permute-done.15.refs_0_.t1
  159.7 2.4 collective-permute-done.16.refs_1_.t2
  164.4 6.0 %weight_half.3 = bf16[16,2,32,1024]{3,2,1,0:T(8,128)(2,1)} custom-call(s32[1]{0:T(128)} %bitcast.7.i_ref, bf16[1024,256]{1,0:T(8,128)(2,1)} %get-tuple-element.132.refs_0_, bf16[1024,256]{1,0:T(8,128)(2,1)} %collective-permute-done.18.refs_1_, bf16[1024,256]{1,0:T(8,128)(2,1)S(1)} %collective-permute-done.19.refs_2_, ...), custom_call_target="tpu_custom_call" | custom-call | flops 2147483648 | bytes 8388608 | tf_op jit(solution)/shard_map/weight_half/pallas_call | solution.py:499
  170.4 5.1 %all-to-all-start = ((bf16[16,2,32,1024]{3,2,1,0:T(8,128)(2,1)}), bf16[16,2,32,1024]{3,2,1,0:T(8,128)(2,1)}, u32[]{:S(2)}, u32[]{:S(2)}) async-start(bf16[16,2,32,1024]{3,2,1,0:T(8,128)(2,1)} %weight_half.3), calls=%async_computation | async-start | bytes 4194304 | tf_op jit(solution)/shard_map/all_to_all | solution.py:633
  175.5 1.9 collective-permute-start.24
  177.4 2.7 %collective-permute-start.25 = (bf16[256,128]{1,0:T(8,128)(2,1)}, bf16[256,128]{1,0:T(8,128)(2,1)S(1)}, u32[]{:S(2)}, u32[]{:S(2)}) collective-permute-start(bf16[256,128]{1,0:T(8,128)(2,1)} %copy-done.26), channel_id=1, source_target_pairs={{0,16},{8,24},{16,0},{24,8},{1,17},{9,25},{17,1},{25,9},{2,18},{10... | collective-permute-start | bytes 196616 | tf_op jit(solution)/shard_map/ppermute | solution.py:128
  180.1 1.5 collective-permute-start.26
  181.5 19.2 %collective-permute-done.24.z1 = bf16[256,128]{1,0:T(8,128)(2,1)S(1)} collective-permute-done((bf16[256,128]{1,0:T(8,128)(2,1)}, bf16[256,128]{1,0:T(8,128)(2,1)S(1)}, u32[]{:S(2)}, u32[]{:S(2)}) %collective-permute-start.24) | collective-permute-done | bytes 65568 | tf_op jit(solution)/shard_map/ppermute | solution.py:128
  201.7 1.3 collective-permute-done.26.z3
  206.3 3.2 %collective-permute-start.28 = (bf16[256,128]{1,0:T(8,128)(2,1)S(1)}, bf16[256,128]{1,0:T(8,128)(2,1)S(1)}, u32[]{:S(2)}, u32[]{:S(2)}) collective-permute-start(bf16[256,128]{1,0:T(8,128)(2,1)S(1)} %get-tuple-element.139), channel_id=1, source_target_pairs={{0,2},{2,4},{4,6},{6,0},{1,3},{3,5},{5,7},{7,1},{8,10},{10,12},{12... | collective-permute-start | bytes 196616 | tf_op jit(solution)/shard_map/ppermute | solution.py:128
  209.6 2.8 %collective-permute-start.29 = (bf16[256,128]{1,0:T(8,128)(2,1)S(1)}, bf16[256,128]{1,0:T(8,128)(2,1)S(1)}, u32[]{:S(2)}, u32[]{:S(2)}) collective-permute-start(bf16[256,128]{1,0:T(8,128)(2,1)S(1)} %get-tuple-element.140), channel_id=1, source_target_pairs={{0,4},{2,6},{4,0},{6,2},{1,5},{3,7},{5,1},{7,3},{8,12},{10,14},{12... | collective-permute-start | bytes 196616 | tf_op jit(solution)/shard_map/ppermute | solution.py:128
  214.4 8.2 %local_grads.1 = (bf16[256,2048]{1,0:T(8,128)(2,1)}, bf16[4,256,512]{2,1,0:T(8,128)(2,1)}, bf16[4,256,512]{2,1,0:T(8,128)(2,1)}) custom-call(s32[8]{0:T(128)S(1)} %stack.54.w_ref.i_ref, bf16[256,2048]{1,0:T(8,128)(2,1)S(1)} %bitcast.45, bf16[256,2048]{1,0:T(8,128)(2,1)S(1)} %bitcast.36, bf16[256,2048]{1,0:T(8,128)(2,1)S(1)} %bitcast.40, ...), custom_call_target="tpu_custom_call" | custom-call | flops 1073741824 | bytes 12582912 | tf_op jit(solution)/shard_map/local_grads/pallas_call | solution.py:372
  222.6 10.1 %layer_rows.1 = bf16[256,4096]{1,0:T(8,128)(2,1)} custom-call(s32[8]{0:T(128)S(1)} %stack.54.w_ref.i_ref, bf16[256,1024]{1,0:T(8,128)(2,1)S(1)} %copy-done.17, bf16[256,1024]{1,0:T(8,128)(2,1)S(1)} %copy-done.19, bf16[512,4096]{1,0:T(8,128)(2,1)} %own_ref.1, bf16[32,3,16,4096]{3,2,1,0:T(8,128)(2,1)} %bitcast.61), custom_call_target="tpu_custom_call" | custom-call | flops 4294967296 | bytes 19922944 | tf_op jit(solution)/shard_map/layer_rows/pallas_call | solution.py:456
  233.6 2.0 sum_parts.1
  236.2 1.6 collective-permute-start.34
  237.8 4.9 %later_grads.1 = (bf16[256,2048]{1,0:T(8,128)(2,1)}, bf16[256,2048]{1,0:T(8,128)(2,1)}) custom-call(s32[8]{0:T(128)S(1)} %stack.54.w_ref.i_ref, bf16[256,2048]{1,0:T(8,128)(2,1)S(1)} %bitcast.37, bf16[256,2048]{1,0:T(8,128)(2,1)S(1)} %bitcast.41, bf16[8,128,128]{2,1,0:T(8,128)(2,1)S(1)} %bitcast.56, bf16[8,128,128]{2,1,0:T(8,128)(2,1)S(1)} %bitcast.57, ...), custom_call_target="tpu_custom_call" | custom-call | flops 268435456 | bytes 8388608 | tf_op jit(solution)/shard_map/later_grads/pallas_call | solution.py:413
  242.7 1.3 shard_map.109
  (118 shorter events, 30.9 us)
Async XLA Ops:
  7.2 79.0 %all-gather.2.cloned.1.call-start = ((), (), s32[]{:S(2)}) async-start(), calls=%async_computation.1 | async-start | bytes 12976128 | tf_op jit(solution)/shard_map/all_gather | solution.py:594
  8.1 9.2 %collective-permute-start = (bf16[16,4096]{1,0:T(8,128)(2,1)S(1)}, bf16[16,4096]{1,0:T(8,128)(2,1)S(1)}, u32[]{:S(2)}, u32[]{:S(2)}) collective-permute-start(bf16[16,4096]{1,0:T(8,128)(2,1)S(1)} %constant_dynamic-slice_fusion.2), channel_id=1, source_target_pairs={{32,0},{64,32},{96,64},{0,96},{33,1},{65,33},{97,65},{1,97},{34,2}... | collective-permute-start | bytes 393224 | tf_op jit(solution)/shard_map/ppermute | solution.py:560
  11.1 7.9 %collective-permute-start.1 = (bf16[16,4096]{1,0:T(8,128)(2,1)S(1)}, bf16[16,4096]{1,0:T(8,128)(2,1)S(1)}, u32[]{:S(2)}, u32[]{:S(2)}) collective-permute-start(bf16[16,4096]{1,0:T(8,128)(2,1)S(1)} %constant_dynamic-slice_fusion.2), channel_id=1, source_target_pairs={{64,0},{96,32},{0,64},{32,96},{65,1},{97,33},{1,65},{33,97},{66,2}... | collective-permute-start | bytes 393224 | tf_op jit(solution)/shard_map/ppermute | solution.py:560
  11.9 8.5 %collective-permute-start.2 = (bf16[16,4096]{1,0:T(8,128)(2,1)S(1)}, bf16[16,4096]{1,0:T(8,128)(2,1)S(1)}, u32[]{:S(2)}, u32[]{:S(2)}) collective-permute-start(bf16[16,4096]{1,0:T(8,128)(2,1)S(1)} %constant_dynamic-slice_fusion.2), channel_id=1, source_target_pairs={{96,0},{0,32},{32,64},{64,96},{97,1},{1,33},{33,65},{65,97},{98,2}... | collective-permute-start | bytes 393224 | tf_op jit(solution)/shard_map/ppermute | solution.py:560
  15.2 16.9 %copy-start.1 = (bf16[1,256,2048]{2,1,0:T(8,128)(2,1)S(1)}, bf16[1,256,2048]{2,1,0:T(8,128)(2,1)}, u32[]{:S(2)}) copy-start(bf16[1,256,2048]{2,1,0:T(8,128)(2,1)} %param.7) | copy-start | bytes 3145732
  15.2 16.9 %copy-start.3 = (bf16[1,256,2048]{2,1,0:T(8,128)(2,1)S(1)}, bf16[1,256,2048]{2,1,0:T(8,128)(2,1)}, u32[]{:S(2)}) copy-start(bf16[1,256,2048]{2,1,0:T(8,128)(2,1)} %param.8) | copy-start | bytes 3145732
  15.2 16.9 %copy-start.4 = (bf16[1,256,2048]{2,1,0:T(8,128)(2,1)S(1)}, bf16[1,256,2048]{2,1,0:T(8,128)(2,1)}, u32[]{:S(2)}) copy-start(bf16[1,256,2048]{2,1,0:T(8,128)(2,1)} %param.6) | copy-start | bytes 3145732
  22.8 1.7 collective-permute-start.3
  26.2 9.9 %collective-permute-start.4 = (bf16[256,128]{1,0:T(8,128)(2,1)S(1)}, bf16[256,128]{1,0:T(8,128)(2,1)S(1)}, u32[]{:S(2)}, u32[]{:S(2)}) collective-permute-start(bf16[256,128]{1,0:T(8,128)(2,1)S(1)} %get-tuple-element.84), channel_id=1, source_target_pairs={{0,2},{2,4},{4,6},{6,0},{1,3},{3,5},{5,7},{7,1},{8,10},{10,12},{12... | collective-permute-start | bytes 196616 | tf_op jit(solution)/shard_map/ppermute | solution.py:128
  27.9 8.3 %collective-permute-start.5 = (bf16[256,128]{1,0:T(8,128)(2,1)S(1)}, bf16[256,128]{1,0:T(8,128)(2,1)S(1)}, u32[]{:S(2)}, u32[]{:S(2)}) collective-permute-start(bf16[256,128]{1,0:T(8,128)(2,1)S(1)} %get-tuple-element.85), channel_id=1, source_target_pairs={{0,4},{2,6},{4,0},{6,2},{1,5},{3,7},{5,1},{7,3},{8,12},{10,14},{12... | collective-permute-start | bytes 196616 | tf_op jit(solution)/shard_map/ppermute | solution.py:128
  30.8 5.4 %collective-permute-start.6 = (bf16[256,128]{1,0:T(8,128)(2,1)S(1)}, bf16[256,128]{1,0:T(8,128)(2,1)S(1)}, u32[]{:S(2)}, u32[]{:S(2)}) collective-permute-start(bf16[256,128]{1,0:T(8,128)(2,1)S(1)} %get-tuple-element.86), channel_id=1, source_target_pairs={{0,6},{2,0},{4,2},{6,4},{1,7},{3,1},{5,3},{7,5},{8,14},{10,8},{12,... | collective-permute-start | bytes 196616 | tf_op jit(solution)/shard_map/ppermute | solution.py:128
  36.8 8.4 %collective-permute-start.7 = (bf16[256,128]{1,0:T(8,128)(2,1)S(1)}, bf16[256,128]{1,0:T(8,128)(2,1)S(1)}, u32[]{:S(2)}, u32[]{:S(2)}) collective-permute-start(bf16[256,128]{1,0:T(8,128)(2,1)S(1)} %shard_map.102), channel_id=1, source_target_pairs={{0,8},{8,16},{16,24},{24,0},{1,9},{9,17},{17,25},{25,1},{2,10},{10... | collective-permute-start | bytes 196616 | tf_op jit(solution)/shard_map/ppermute | solution.py:128
  38.9 8.8 %collective-permute-start.8 = (bf16[256,128]{1,0:T(8,128)(2,1)S(1)}, bf16[256,128]{1,0:T(8,128)(2,1)S(1)}, u32[]{:S(2)}, u32[]{:S(2)}) collective-permute-start(bf16[256,128]{1,0:T(8,128)(2,1)S(1)} %shard_map.102), channel_id=1, source_target_pairs={{0,16},{8,24},{16,0},{24,8},{1,17},{9,25},{17,1},{25,9},{2,18},{10... | collective-permute-start | bytes 196616 | tf_op jit(solution)/shard_map/ppermute | solution.py:128
  42.6 5.1 %collective-permute-start.9 = (bf16[256,128]{1,0:T(8,128)(2,1)S(1)}, bf16[256,128]{1,0:T(8,128)(2,1)S(1)}, u32[]{:S(2)}, u32[]{:S(2)}) collective-permute-start(bf16[256,128]{1,0:T(8,128)(2,1)S(1)} %shard_map.102), channel_id=1, source_target_pairs={{0,24},{8,0},{16,8},{24,16},{1,25},{9,1},{17,9},{25,17},{2,26},{10... | collective-permute-start | bytes 196616 | tf_op jit(solution)/shard_map/ppermute | solution.py:128
  49.0 5.8 %collective-permute-start.10 = (bf16[256,128]{1,0:T(8,128)(2,1)}, bf16[256,128]{1,0:T(8,128)(2,1)}, u32[]{:S(2)}, u32[]{:S(2)}) collective-permute-start(bf16[256,128]{1,0:T(8,128)(2,1)} %get-tuple-element.99), channel_id=1, source_target_pairs={{0,2},{2,4},{4,6},{6,0},{1,3},{3,5},{5,7},{7,1},{8,10},{10,12},{12... | collective-permute-start | bytes 196616 | tf_op jit(solution)/shard_map/ppermute | solution.py:128
  49.8 6.1 %collective-permute-start.11 = (bf16[256,128]{1,0:T(8,128)(2,1)}, bf16[256,128]{1,0:T(8,128)(2,1)}, u32[]{:S(2)}, u32[]{:S(2)}) collective-permute-start(bf16[256,128]{1,0:T(8,128)(2,1)} %get-tuple-element.100), channel_id=1, source_target_pairs={{0,4},{2,6},{4,0},{6,2},{1,5},{3,7},{5,1},{7,3},{8,12},{10,14},{12... | collective-permute-start | bytes 196616 | tf_op jit(solution)/shard_map/ppermute | solution.py:128
  52.2 4.6 %collective-permute-start.12 = (bf16[256,128]{1,0:T(8,128)(2,1)}, bf16[256,128]{1,0:T(8,128)(2,1)}, u32[]{:S(2)}, u32[]{:S(2)}) collective-permute-start(bf16[256,128]{1,0:T(8,128)(2,1)} %get-tuple-element.101), channel_id=1, source_target_pairs={{0,6},{2,0},{4,2},{6,4},{1,7},{3,1},{5,3},{7,5},{8,14},{10,8},{12,... | collective-permute-start | bytes 196616 | tf_op jit(solution)/shard_map/ppermute | solution.py:128
  58.9 7.5 %collective-permute-start.13 = (bf16[4,256,128]{2,1,0:T(8,128)(2,1)S(1)}, bf16[4,256,128]{2,1,0:T(8,128)(2,1)S(1)}, u32[]{:S(2)}, u32[]{:S(2)}) collective-permute-start(bf16[4,256,128]{2,1,0:T(8,128)(2,1)S(1)} %get-tuple-element.107), channel_id=1, source_target_pairs={{0,1},{1,0},{2,3},{3,2},{4,5},{5,4},{6,7},{7,6},{8,9},{9,8},{10,11... | collective-permute-start | bytes 786440 | tf_op jit(solution)/shard_map/ppermute | solution.py:128
  59.0 15.5 %copy-start.31 = (bf16[512,4096]{1,0:T(8,128)(2,1)S(1)}, bf16[512,4096]{1,0:T(8,128)(2,1)}, u32[]{:S(2)}) copy-start(bf16[512,4096]{1,0:T(8,128)(2,1)} %own_ref.1) | copy-start | bytes 12582916
  62.3 12.2 %copy-start.30 = (bf16[1,256,4096]{2,1,0:T(8,128)(2,1)S(1)}, bf16[1,256,4096]{2,1,0:T(8,128)(2,1)}, u32[]{:S(2)}) copy-start(bf16[1,256,4096]{2,1,0:T(8,128)(2,1)} %param.11) | copy-start | bytes 6291460
  62.3 85.8 %collective-permute-start.21 = (bf16[256,2048]{1,0:T(8,128)(2,1)}, bf16[256,2048]{1,0:T(8,128)(2,1)}, u32[]{:S(2)}, u32[]{:S(2)}) collective-permute-start(bf16[256,2048]{1,0:T(8,128)(2,1)} %get-tuple-element.161), channel_id=1, source_target_pairs={{0,32},{32,0},{64,96},{96,64},{1,33},{33,1},{65,97},{97,65},{2,34}... | collective-permute-start | bytes 3145736 | tf_op jit(solution)/shard_map/ppermute | solution.py:123
  62.3 85.8 %collective-permute-start.23 = (bf16[256,2048]{1,0:T(8,128)(2,1)}, bf16[256,2048]{1,0:T(8,128)(2,1)}, u32[]{:S(2)}, u32[]{:S(2)}) collective-permute-start(bf16[256,2048]{1,0:T(8,128)(2,1)} %get-tuple-element.161), channel_id=1, source_target_pairs={{0,96},{32,64},{64,32},{96,0},{1,97},{33,65},{65,33},{97,1},{2,98}... | collective-permute-start | bytes 3145736 | tf_op jit(solution)/shard_map/ppermute | solution.py:123
  64.1 84.0 %collective-permute-start.22 = (bf16[256,2048]{1,0:T(8,128)(2,1)}, bf16[256,2048]{1,0:T(8,128)(2,1)}, u32[]{:S(2)}, u32[]{:S(2)}) collective-permute-start(bf16[256,2048]{1,0:T(8,128)(2,1)} %get-tuple-element.162.refs_4_), channel_id=1, source_target_pairs={{0,64},{32,96},{64,0},{96,32},{1,65},{33,97},{65,1},{97,33},{2,66}... | collective-permute-start | bytes 3145736 | tf_op jit(solution)/shard_map/ppermute | solution.py:123
  74.4 47.4 %collective-permute-start.18 = (bf16[1024,256]{1,0:T(8,128)(2,1)}, bf16[1024,256]{1,0:T(8,128)(2,1)}, u32[]{:S(2)}, u32[]{:S(2)}) collective-permute-start(bf16[1024,256]{1,0:T(8,128)(2,1)} %get-tuple-element.132.refs_0_), channel_id=1, source_target_pairs={{0,32},{32,0},{64,96},{96,64},{1,33},{33,1},{65,97},{97,65},{2,34}... | collective-permute-start | bytes 1572872 | tf_op jit(solution)/shard_map/ppermute | solution.py:123
  86.2 35.7 %copy-start.29 = (bf16[1024,256]{1,0:T(8,128)(2,1)S(1)}, bf16[1024,256]{1,0:T(8,128)(2,1)}, u32[]{:S(2)}) copy-start(bf16[1024,256]{1,0:T(8,128)(2,1)} %copy-done.28) | copy-start | bytes 1572868
  97.8 27.1 %copy-start.8 = (bf16[16,128,128]{2,1,0:T(8,128)(2,1)}, bf16[16,128,128]{2,1,0:T(8,128)(2,1)S(1)}, u32[]{:S(2)}) copy-start(bf16[16,128,128]{2,1,0:T(8,128)(2,1)S(1)} %get-tuple-element.117) | copy-start | bytes 1572868
  97.8 25.3 %collective-permute-start.14 = (bf16[4,256,128]{2,1,0:T(8,128)(2,1)S(1)}, bf16[4,256,128]{2,1,0:T(8,128)(2,1)S(1)}, u32[]{:S(2)}, u32[]{:S(2)}) collective-permute-start(bf16[4,256,128]{2,1,0:T(8,128)(2,1)S(1)} %dynamic-slice_bitcast_fusion), channel_id=1, source_target_pairs={{0,1},{1,0},{2,3},{3,2},{4,5},{5,4},{6,7},{7,6},{8,9},{9,8},{10,11... | collective-permute-start | bytes 786440 | tf_op jit(solution)/shard_map/ppermute | solution.py:128
  121.8 15.1 %collective-permute-start.19 = (bf16[1024,256]{1,0:T(8,128)(2,1)S(1)}, bf16[1024,256]{1,0:T(8,128)(2,1)S(1)}, u32[]{:S(2)}, u32[]{:S(2)}) collective-permute-start(bf16[1024,256]{1,0:T(8,128)(2,1)S(1)} %copy-done.29), channel_id=1, source_target_pairs={{0,64},{32,96},{64,0},{96,32},{1,65},{33,97},{65,1},{97,33},{2,66}... | collective-permute-start | bytes 1572872 | tf_op jit(solution)/shard_map/ppermute | solution.py:123
  123.1 30.8 %copy-start.14 = (bf16[4,256,128]{2,1,0:T(8,128)(2,1)}, bf16[4,256,128]{2,1,0:T(8,128)(2,1)S(1)}, u32[]{:S(2)}) copy-start(bf16[4,256,128]{2,1,0:T(8,128)(2,1)S(1)} %collective-permute-done.14.r_ref) | copy-start | bytes 786436
  123.1 24.9 %collective-permute-start.20 = (bf16[1024,256]{1,0:T(8,128)(2,1)S(1)}, bf16[1024,256]{1,0:T(8,128)(2,1)S(1)}, u32[]{:S(2)}, u32[]{:S(2)}) collective-permute-start(bf16[1024,256]{1,0:T(8,128)(2,1)S(1)} %copy-done.29), channel_id=1, source_target_pairs={{0,96},{32,64},{64,32},{96,0},{1,97},{33,65},{65,33},{97,1},{2,98}... | collective-permute-start | bytes 1572872 | tf_op jit(solution)/shard_map/ppermute | solution.py:123
  153.9 10.5 %collective-permute-start.27 = (bf16[16,2,32,1024]{3,2,1,0:T(8,128)(2,1)}, bf16[16,2,32,1024]{3,2,1,0:T(8,128)(2,1)S(1)}, u32[]{:S(2)}, u32[]{:S(2)}) collective-permute-start(bf16[16,2,32,1024]{3,2,1,0:T(8,128)(2,1)} %weight_half.2), channel_id=1, source_target_pairs={{0,1},{1,0},{2,3},{3,2},{4,5},{5,4},{6,7},{7,6},{8,9},{9,8},{10,11... | collective-permute-start | bytes 6291464 | tf_op jit(solution)/shard_map/ppermute | solution.py:128
  154.0 5.7 %collective-permute-start.15 = (bf16[256,128]{1,0:T(8,128)(2,1)S(1)}, bf16[256,128]{1,0:T(8,128)(2,1)S(1)}, u32[]{:S(2)}, u32[]{:S(2)}) collective-permute-start(bf16[256,128]{1,0:T(8,128)(2,1)S(1)} %get-tuple-element.119), channel_id=1, source_target_pairs={{0,2},{2,4},{4,6},{6,0},{1,3},{3,5},{5,7},{7,1},{8,10},{10,12},{12... | collective-permute-start | bytes 196616 | tf_op jit(solution)/shard_map/ppermute | solution.py:128
  155.0 7.1 %collective-permute-start.16 = (bf16[256,128]{1,0:T(8,128)(2,1)S(1)}, bf16[256,128]{1,0:T(8,128)(2,1)S(1)}, u32[]{:S(2)}, u32[]{:S(2)}) collective-permute-start(bf16[256,128]{1,0:T(8,128)(2,1)S(1)} %get-tuple-element.120), channel_id=1, source_target_pairs={{0,4},{2,6},{4,0},{6,2},{1,5},{3,7},{5,1},{7,3},{8,12},{10,14},{12... | collective-permute-start | bytes 196616 | tf_op jit(solution)/shard_map/ppermute | solution.py:128
  158.3 4.3 %collective-permute-start.17 = (bf16[256,128]{1,0:T(8,128)(2,1)S(1)}, bf16[256,128]{1,0:T(8,128)(2,1)S(1)}, u32[]{:S(2)}, u32[]{:S(2)}) collective-permute-start(bf16[256,128]{1,0:T(8,128)(2,1)S(1)} %get-tuple-element.121), channel_id=1, source_target_pairs={{0,6},{2,0},{4,2},{6,4},{1,7},{3,1},{5,3},{7,5},{8,14},{10,8},{12,... | collective-permute-start | bytes 196616 | tf_op jit(solution)/shard_map/ppermute | solution.py:128
  170.4 43.1 %copy-start.11 = (bf16[4,256,128]{2,1,0:T(8,128)(2,1)S(1)}, bf16[4,256,128]{2,1,0:T(8,128)(2,1)}, u32[]{:S(2)}) copy-start(bf16[4,256,128]{2,1,0:T(8,128)(2,1)} %copy-done.10) | copy-start | bytes 786436
  170.4 63.2 %all-to-all-start = ((bf16[16,2,32,1024]{3,2,1,0:T(8,128)(2,1)}), bf16[16,2,32,1024]{3,2,1,0:T(8,128)(2,1)}, u32[]{:S(2)}, u32[]{:S(2)}) async-start(bf16[16,2,32,1024]{3,2,1,0:T(8,128)(2,1)} %weight_half.3), calls=%async_computation | async-start | bytes 4194304 | tf_op jit(solution)/shard_map/all_to_all | solution.py:633
  175.5 25.2 %collective-permute-start.24 = (bf16[256,128]{1,0:T(8,128)(2,1)}, bf16[256,128]{1,0:T(8,128)(2,1)S(1)}, u32[]{:S(2)}, u32[]{:S(2)}) collective-permute-start(bf16[256,128]{1,0:T(8,128)(2,1)} %copy-done.26), channel_id=1, source_target_pairs={{0,8},{8,16},{16,24},{24,0},{1,9},{9,17},{17,25},{25,1},{2,10},{10... | collective-permute-start | bytes 196616 | tf_op jit(solution)/shard_map/ppermute | solution.py:128
  177.4 24.3 %collective-permute-start.25 = (bf16[256,128]{1,0:T(8,128)(2,1)}, bf16[256,128]{1,0:T(8,128)(2,1)S(1)}, u32[]{:S(2)}, u32[]{:S(2)}) collective-permute-start(bf16[256,128]{1,0:T(8,128)(2,1)} %copy-done.26), channel_id=1, source_target_pairs={{0,16},{8,24},{16,0},{24,8},{1,17},{9,25},{17,1},{25,9},{2,18},{10... | collective-permute-start | bytes 196616 | tf_op jit(solution)/shard_map/ppermute | solution.py:128
  180.1 23.0 %collective-permute-start.26 = (bf16[256,128]{1,0:T(8,128)(2,1)}, bf16[256,128]{1,0:T(8,128)(2,1)S(1)}, u32[]{:S(2)}, u32[]{:S(2)}) collective-permute-start(bf16[256,128]{1,0:T(8,128)(2,1)} %copy-done.26), channel_id=1, source_target_pairs={{0,24},{8,0},{16,8},{24,16},{1,25},{9,1},{17,9},{25,17},{2,26},{10... | collective-permute-start | bytes 196616 | tf_op jit(solution)/shard_map/ppermute | solution.py:128
  206.3 26.4 %collective-permute-start.28 = (bf16[256,128]{1,0:T(8,128)(2,1)S(1)}, bf16[256,128]{1,0:T(8,128)(2,1)S(1)}, u32[]{:S(2)}, u32[]{:S(2)}) collective-permute-start(bf16[256,128]{1,0:T(8,128)(2,1)S(1)} %get-tuple-element.139), channel_id=1, source_target_pairs={{0,2},{2,4},{4,6},{6,0},{1,3},{3,5},{5,7},{7,1},{8,10},{10,12},{12... | collective-permute-start | bytes 196616 | tf_op jit(solution)/shard_map/ppermute | solution.py:128
  209.6 23.2 %collective-permute-start.29 = (bf16[256,128]{1,0:T(8,128)(2,1)S(1)}, bf16[256,128]{1,0:T(8,128)(2,1)S(1)}, u32[]{:S(2)}, u32[]{:S(2)}) collective-permute-start(bf16[256,128]{1,0:T(8,128)(2,1)S(1)} %get-tuple-element.140), channel_id=1, source_target_pairs={{0,4},{2,6},{4,0},{6,2},{1,5},{3,7},{5,1},{7,3},{8,12},{10,14},{12... | collective-permute-start | bytes 196616 | tf_op jit(solution)/shard_map/ppermute | solution.py:128
  212.4 20.4 %collective-permute-start.30 = (bf16[256,128]{1,0:T(8,128)(2,1)S(1)}, bf16[256,128]{1,0:T(8,128)(2,1)S(1)}, u32[]{:S(2)}, u32[]{:S(2)}) collective-permute-start(bf16[256,128]{1,0:T(8,128)(2,1)S(1)} %get-tuple-element.141), channel_id=1, source_target_pairs={{0,6},{2,0},{4,2},{6,4},{1,7},{3,1},{5,3},{7,5},{8,14},{10,8},{12,... | collective-permute-start | bytes 196616 | tf_op jit(solution)/shard_map/ppermute | solution.py:128
  222.6 10.2 %copy-start.9 = (bf16[16,128,128]{2,1,0:T(8,128)(2,1)S(1)}, bf16[16,128,128]{2,1,0:T(8,128)(2,1)}, u32[]{:S(2)}) copy-start(bf16[16,128,128]{2,1,0:T(8,128)(2,1)} %copy-done.8) | copy-start | bytes 1572868
  222.6 10.2 %copy-start.15 = (bf16[4,256,128]{2,1,0:T(8,128)(2,1)S(1)}, bf16[4,256,128]{2,1,0:T(8,128)(2,1)}, u32[]{:S(2)}) copy-start(bf16[4,256,128]{2,1,0:T(8,128)(2,1)} %copy-done.14) | copy-start | bytes 786436
  233.5 4.3 %collective-permute-start.31 = (bf16[4,256,128]{2,1,0:T(8,128)(2,1)S(1)}, bf16[4,256,128]{2,1,0:T(8,128)(2,1)S(1)}, u32[]{:S(2)}, u32[]{:S(2)}) collective-permute-start(bf16[4,256,128]{2,1,0:T(8,128)(2,1)S(1)} %get-tuple-element.153), channel_id=1, source_target_pairs={{0,1},{1,0},{2,3},{3,2},{4,5},{5,4},{6,7},{7,6},{8,9},{9,8},{10,11... | collective-permute-start | bytes 786440 | tf_op jit(solution)/shard_map/ppermute | solution.py:128
  235.5 7.1 %collective-permute-start.32 = (f32[16,1024]{1,0:T(8,128)S(1)}, f32[16,1024]{1,0:T(8,128)S(1)}, u32[]{:S(2)}, u32[]{:S(2)}) collective-permute-start(f32[16,1024]{1,0:T(8,128)S(1)} %get-tuple-element.158), channel_id=1, source_target_pairs={{0,32},{32,0},{64,96},{96,64},{1,33},{33,1},{65,97},{97,65},{2,34}... | collective-permute-start | bytes 196616 | tf_op jit(solution)/shard_map/ppermute | solution.py:123
  235.9 6.7 %collective-permute-start.33 = (f32[16,1024]{1,0:T(8,128)S(1)}, f32[16,1024]{1,0:T(8,128)S(1)}, u32[]{:S(2)}, u32[]{:S(2)}) collective-permute-start(f32[16,1024]{1,0:T(8,128)S(1)} %get-tuple-element.159), channel_id=1, source_target_pairs={{0,1},{1,0},{2,3},{3,2},{4,5},{5,4},{6,7},{7,6},{8,9},{9,8},{10,11... | collective-permute-start | bytes 196616 | tf_op jit(solution)/shard_map/ppermute | solution.py:123
  236.2 6.5 %collective-permute-start.34 = (f32[16,1024]{1,0:T(8,128)S(1)}, f32[16,1024]{1,0:T(8,128)S(1)}, u32[]{:S(2)}, u32[]{:S(2)}) collective-permute-start(f32[16,1024]{1,0:T(8,128)S(1)} %get-tuple-element.160), channel_id=1, source_target_pairs={{0,33},{1,32},{32,1},{33,0},{64,97},{65,96},{96,65},{97,64},{2,35}... | collective-permute-start | bytes 196616 | tf_op jit(solution)/shard_map/ppermute | solution.py:647
  (21 other events, 51.1 us)
Sparse Core Ops, SparseCore 0:
  21.3 64.8 all-gather.1
